TPU v7x, 32 devices: a whole 2x2x4 slice. The times are simulated.
32 devices in a mesh: leaf: 4 (over x, core), blk: 8 (over z, y).
Axes of the slice: x: 2, y: 2, z: 4, core: 2. Of those that a mesh axis runs over, the one named last changes fastest.
Arguments:
- right_side: float32 [4, 8, 448, 128], P('leaf', 'blk'), may hold values from -6 to 6
- inverse_blocks: bfloat16 [4, 8, 448, 2048], P('leaf', 'blk'), may hold values from -0.125 to 0.125
- coupling: bfloat16 [4, 8, 640, 1024], P('leaf', 'blk'), may hold values from -0.0625 to 0.0625
- update_rows: int32 [10, 1024], replicated, may hold values from 0 to 2047, as said below
Outputs:
- solution: float32 [4, 8, 448, 128], P('leaf', 'blk')
Inputs may be any that keep to these rules, and one draw needn't show every extreme that they name: `update_rows`: the 1024 entries of each row are distinct.
All inputs are finite; a program needn't handle non-finite values.
Results may differ from a plain program's by a relative error of at most 0.0075.
Values may be sent and summed in bfloat16 or wider, within the bound.
No kernel may reach another device: no remote copies, remote signals or barrier semaphores. Data moves between devices by JAX's collectives and lax.ppermute only.
A program may use at most 64 MiB of HBM per device.

v0:
```python
import functools

import jax
import jax.numpy as jnp
from jax import lax
from jax.experimental import pallas as pl
from jax.experimental.pallas import tpu as pltpu
from jax.sharding import PartitionSpec as P


BF16 = jnp.bfloat16
F32 = jnp.float32


def mm(a, b):
    return jnp.dot(a, b, preferred_element_type=F32)


def mm_tn(a, b):
    return lax.dot_general(a, b, (((0,), (0,)), ((), ())), preferred_element_type=F32)


def mm_nt(a, b):
    return lax.dot_general(a, b, (((1,), (1,)), ((), ())), preferred_element_type=F32)


def shaped(shape, dtype):
    return jax.ShapeDtypeStruct(tuple(shape), dtype)


def kernel_call(body, outs, args, scalars=None, scratch=(), flops=0):
    moved = sum(a.size * a.dtype.itemsize for a in args)
    moved += sum(o.size * o.dtype.itemsize for o in outs)
    specs = [pl.BlockSpec(memory_space=pltpu.VMEM)] * len(args)
    if scalars is not None:
        specs = [pl.BlockSpec(memory_space=pltpu.SMEM)] + specs
        args = [scalars] + list(args)
    return pl.pallas_call(
        body,
        out_shape=list(outs),
        in_specs=specs,
        out_specs=[pl.BlockSpec(memory_space=pltpu.VMEM)] * len(outs),
        scratch_shapes=list(scratch),
        cost_estimate=pl.CostEstimate(flops=flops, bytes_accessed=moved, transcendentals=0),
    )(*args)


class Level:
    def __init__(self, level, leaves, blocks, width, cases):
        self.pair_x = 2 if level >= 2 else 1
        self.his = (1 << level) // (2 * self.pair_x)
        self.zbs = blocks // 2
        self.rows = width // (blocks << level)
        self.cells = self.his * self.zbs
        self.cell_rows = width // self.cells
        self.chunk = cases // (4 * self.pair_x)
        self.targets = self.cells * self.pair_x * 2
        outer = []
        inner = []
        for node in range(leaves >> level):
            base = node << level
            for side in range(2):
                outer.append(
                    [
                        (base + 2 * upper + side) * blocks + b
                        for upper in range(1 << (level - 1))
                        for b in range(blocks)
                    ]
                )
                for xu in range(self.pair_x):
                    for yb in range(2):
                        inner.append(
                            [
                                (base + (hi * self.pair_x + xu) * 2 + side) * blocks + 2 * zb + yb
                                for hi in range(self.his)
                                for zb in range(self.zbs)
                            ]
                        )
        self.outer = outer
        self.inner = inner
        self.inner_blk = [[2 * zb + yb for zb in range(self.zbs)] for yb in range(2)]

    def target(self, hi, xu, zb, yb):
        return ((hi * self.pair_x + xu) * self.zbs + zb) * 2 + yb

    def lanes(self, cell):
        return slice(cell * self.cell_rows, (cell + 1) * self.cell_rows)

    def all_targets(self):
        for hi in range(self.his):
            for xu in range(self.pair_x):
                for zb in range(self.zbs):
                    for yb in range(2):
                        yield hi * self.zbs + zb, xu, yb, self.target(hi, xu, zb, yb)


CORE, YB, XU, SPOT = 0, 1, 2, 3


def expand_kernel(count, spots_ref, *refs):
    blocks, outs = refs[:count], refs[count:]
    width = outs[0].shape[-1]
    step = min(512, width)
    for pair in range(len(outs)):
        listed = spots_ref[pair : pair + 1, :]
        mine = blocks if len(outs) == 1 else (blocks[pair],)
        for begin in range(0, width, step):
            ids = begin + lax.broadcasted_iota(jnp.int32, (step, listed.shape[-1]), 0)
            chosen = jnp.where(ids == listed, 1.0, 0.0).astype(BF16)
            for piece, block in enumerate(mine):
                value = mm_nt(block[...], chosen).astype(BF16)
                outs[pair][piece, :, begin : begin + step] = value


def subtree_kernel(infos, starts, at, full, inverse, rhs, *refs):
    depth = len(infos)
    dense, outs, total = refs[:depth], refs[depth:-1], refs[-1]
    y = mm(inverse[...], full[...])
    outs[0][...] = y
    y_round = y.astype(BF16)
    for n, info in enumerate(infos):
        begin = starts[n]
        own = rhs[begin : begin + info.rows, :].astype(BF16)
        width = info.cells * info.cell_rows
        row_ids = at[SPOT + n] + lax.broadcasted_iota(jnp.int32, (info.rows, width), 0)
        lane_ids = lax.broadcasted_iota(jnp.int32, (info.rows, width), 1)
        spots = jnp.where(row_ids == lane_ids, 1.0, 0.0).astype(BF16)
        total[...] = mm_tn(own, spots) - mm_tn(y_round, dense[n][0])
        mine, other = outs[1 + 2 * n], outs[2 + 2 * n]
        core = at[CORE]
        for cell, xu, yb, target in info.all_targets():
            for side, ref in ((core, mine), (1 - core, other)):
                row = ((yb * 2 + side) * info.pair_x + xu) * info.chunk
                row = pl.multiple_of(row, info.chunk)
                value = total[pl.ds(row, info.chunk), info.lanes(cell)]
                ref[target] = value.astype(ref.dtype)


def sum_spread_kernel(parts, out):
    total = parts[0].astype(F32)
    for n in range(1, parts.shape[0]):
        total = total + parts[n].astype(F32)
    rounded = total.astype(BF16)
    for n in range(out.shape[0]):
        out[n] = rounded


def solve_pieces(info, gathered, pieces):
    ys = []
    for piece in pieces:
        y = None
        for cell in range(info.cells):
            term = mm_nt(gathered[cell], piece[:, info.lanes(cell)])
            y = term if y is None else y + term
        ys.append(y)
    return ys


def forward_kernel(infos, k, at, gathered, mine, received, *refs):
    info, above = infos[k - 1], infos[k]
    count = 4 * info.pair_x
    pieces = refs[:count]
    lower_y = refs[count : count + k - 1]
    dense = refs[count + k - 1 : count + 2 * k - 1]
    y_ref, out, total = refs[count + 2 * k - 1 :]
    ys = solve_pieces(info, gathered, pieces)
    for n, y in enumerate(ys):
        y_ref[n] = y
    same = {}
    for j in range(1, k + 1):
        lower = infos[j - 1]
        values = ys if j == k else [lower_y[j - 1][n] for n in range(4 * lower.pair_x)]
        term = None
        for n, value in enumerate(values):
            product = mm(value.astype(BF16), dense[j - 1][n])
            term = product if term is None else term + product
        same.setdefault(lower.pair_x == above.pair_x, []).append(term)
    if False in same:
        total[...] = functools.reduce(jnp.add, same[False])
    else:
        total[...] = jnp.zeros(total.shape, F32)
    if True in same:
        term = functools.reduce(jnp.add, same[True])
        rows = pl.ds(pl.multiple_of(at[XU] * above.chunk, above.chunk), above.chunk)
        total[rows, :] = total[rows, :] + term
    for cell, xu, yb, target in above.all_targets():
        value = mine[target] + received[target].astype(F32)
        minus = total[xu * above.chunk : (xu + 1) * above.chunk, above.lanes(cell)]
        value = jnp.where(at[YB] == yb, value - minus, value)
        out[target] = value.astype(BF16)


def spread_product(info, zs, pieces, out):
    for cell in range(info.cells):
        total = None
        for z, piece in zip(zs, pieces):
            term = mm(z, piece[:, info.lanes(cell)])
            total = term if total is None else total + term
        out[cell] = total.astype(BF16)


def top_kernel(info, gathered, *refs):
    pieces, out = refs[:-1], refs[-1]
    ys = solve_pieces(info, gathered, pieces)
    spread_product(info, [y.astype(BF16) for y in ys], pieces, out)


def backward_kernel(infos, k, at, y, *refs):
    info = infos[k - 1]
    count = 4 * info.pair_x
    uppers = infos[k:]
    pieces = refs[:count]
    solved = refs[count : count + len(uppers)]
    dense = refs[count + len(uppers) : count + 2 * len(uppers)]
    out = refs[-1]
    zs = [y[n] for n in range(count)]
    for n_up, above in enumerate(uppers):
        for hi in range(above.his):
            for zb in range(above.zbs):
                cell = hi * above.zbs + zb
                if above.pair_x == info.pair_x:
                    slot = ((hi * above.pair_x + at[XU]) * above.zbs + zb) * 2 + at[YB]
                    picked = solved[n_up][slot]
                else:
                    slots = [
                        above.target(hi, xu, zb, 0) + at[YB] for xu in range(above.pair_x)
                    ]
                    picked = jnp.concatenate([solved[n_up][slot] for slot in slots], 0)
                for n in range(count):
                    zs[n] = zs[n] - mm_nt(picked, dense[n_up][n, :, above.lanes(cell)])
    spread_product(info, [z.astype(BF16) for z in zs], pieces, out)


def last_kernel(infos, at, y, inverse, *refs):
    depth = len(infos)
    dense = refs[:depth]
    mine = refs[depth : 2 * depth]
    other = refs[2 * depth : 3 * depth]
    out, full = refs[3 * depth :]
    z = y[...]
    core = at[CORE]
    for n in range(depth - 1, -1, -1):
        info = infos[n]
        for cell, xu, yb, target in info.all_targets():
            for side, ref in ((core, mine[n]), (1 - core, other[n])):
                row = ((yb * 2 + side) * info.pair_x + xu) * info.chunk
                row = pl.multiple_of(row, info.chunk)
                full[pl.ds(row, info.chunk), info.lanes(cell)] = ref[target]
        z = z - mm_nt(dense[n][0], full[...])
    out[...] = mm_tn(inverse[...], z.astype(BF16)).astype(BF16)


def solve(right_side, inverse_blocks, coupling, update_rows):
    leaves = lax.axis_size("leaf")
    blocks = lax.axis_size("blk")
    depth = leaves.bit_length() - 1
    leaf_id = lax.axis_index("leaf")
    blk_id = lax.axis_index("blk")
    core = leaf_id & 1
    yb = blk_id & 1
    zb = blk_id >> 1
    width = inverse_blocks.shape[-1]
    cases = right_side.shape[-1]
    rhs = right_side[0, 0]
    inverse = inverse_blocks[0, 0]
    couple = coupling[0, 0]
    listed_rows = coupling.shape[-1]
    counts = [width // (blocks << level) for level in range(depth + 1)]
    starts = [sum(counts[:level]) for level in range(depth + 1)]
    infos = [Level(l, leaves, blocks, width, cases) for l in range(1, depth + 1)]
    couple_starts = {}
    cursor = 0
    for level in range(depth):
        for above in range(level + 1, depth + 1):
            couple_starts[level, above] = cursor
            cursor += counts[level]
    pair_bases = []
    cursor = 0
    for level in range(depth + 1):
        pair_bases.append(cursor)
        cursor += (leaves >> level) * (depth - level)

    def own_position(level):
        info = infos[level - 1]
        member = leaf_id & ((1 << level) - 1)
        side = member & (2 * info.pair_x - 1)
        cell = member // (2 * info.pair_x) * info.zbs + zb
        return ((cell * 2 * info.pair_x + side) * 2 + yb) * info.rows

    at = jnp.stack(
        [core, yb, (leaf_id >> 1) & 1] + [own_position(l) for l in range(1, depth + 1)]
    ).astype(jnp.int32)

    def swap(value, axis, bit):
        size = leaves if axis == "leaf" else blocks
        return lax.ppermute(value, axis, [(i, i ^ bit) for i in range(size)])

    def cell_position(rows, level):
        info = infos[level - 1]
        t = rows % (2 * info.rows)
        block = rows // (2 * info.rows)
        zpos = block % info.zbs
        block = block // info.zbs
        side = block % (2 * info.pair_x)
        cell = block // (2 * info.pair_x) * info.zbs + zpos
        return (cell * (2 * info.pair_x) + side) * (2 * info.rows) + t

    def cell_columns(rows, level):
        info = infos[level - 1]
        parts = rows.reshape(-1, info.his, 2 * info.pair_x, info.zbs, 2 * info.rows)
        return parts.transpose(0, 1, 3, 2, 4).reshape(-1, width)

    def exchange_outer(value, level):
        if level <= 1:
            return lax.all_to_all(value, "blk", 0, 0, tiled=True)
        return lax.all_to_all(
            value,
            ("leaf", "blk"),
            0,
            0,
            axis_index_groups=infos[level - 1].outer,
            tiled=True,
        )

    def exchange_inner(value, level):
        info = infos[level - 1]
        if info.his == 1:
            return lax.all_to_all(
                value, "blk", 0, 0, axis_index_groups=info.inner_blk, tiled=True
            )
        return lax.all_to_all(
            value, ("leaf", "blk"), 0, 0, axis_index_groups=info.inner, tiled=True
        )

    def positions(level, above):
        node = leaf_id >> level
        pair = pair_bases[level] + node * (depth - level) + (above - level - 1)
        listed = lax.dynamic_index_in_dim(update_rows, pair, 0, keepdims=True)
        return cell_position(listed, above)

    def coupling_block(level, above):
        begin = couple_starts[level, above]
        return couple[begin : begin + counts[level]]

    uppers = range(1, depth + 1)
    lists = jnp.concatenate([positions(0, above) for above in uppers], 0)
    dense = {}
    expanded = kernel_call(
        functools.partial(expand_kernel, depth),
        [shaped((1, counts[0], width), BF16)] * depth,
        [lists] + [coupling_block(0, above) for above in uppers],
        flops=2 * depth * counts[0] * listed_rows * width,
    )
    for above in uppers:
        dense[0, above] = expanded[above - 1]

    spread = jnp.broadcast_to(rhs[: counts[0]].astype(BF16)[None], (blocks, counts[0], cases))
    full = lax.all_to_all(spread, "blk", 0, 0, tiled=True).reshape(width, cases)
    subtree_inverse = inverse[: counts[0]]
    outs = [shaped((counts[0], cases), F32)]
    for info in infos:
        shape = (info.targets, info.chunk, info.cell_rows)
        outs += [shaped(shape, F32), shaped(shape, BF16)]
    y0, *base = kernel_call(
        functools.partial(subtree_kernel, infos, starts[1:]),
        outs,
        [full, subtree_inverse, rhs] + [dense[0, above] for above in uppers],
        scalars=at,
        scratch=[pltpu.VMEM((cases, width), F32)],
        flops=2 * (1 + depth) * counts[0] * width * cases,
    )
    received = []
    for level in uppers:
        received.append(swap(base[2 * level - 1], "leaf", 1))

    def pieces_of(value, level):
        pieces = [value, swap(value, "blk", 1)]
        if infos[level - 1].pair_x == 2:
            pieces += [swap(piece, "leaf", 2) for piece in pieces]
        pieces += [swap(piece, "leaf", 1) for piece in pieces]
        return pieces

    inverse_pieces = {}
    for level in uppers:
        rows = inverse[starts[level] : starts[level] + counts[level]]
        rows = cell_columns(rows, level)
        inverse_pieces[level] = pieces_of(rows, level)
        for above in range(level + 1, depth + 1):
            pieces = pieces_of(coupling_block(level, above), level)
            dense[level, above] = kernel_call(
                functools.partial(expand_kernel, len(pieces)),
                [shaped((len(pieces), counts[level], width), BF16)],
                [positions(level, above)] + pieces,
                flops=2 * len(pieces) * counts[level] * listed_rows * width,
            )[0]

    def sum_spread(parts, copies):
        return kernel_call(
            sum_spread_kernel, [shaped((copies,) + parts.shape[1:], BF16)], [parts]
        )[0]

    ys = {}
    parts = (base[0] + received[0].astype(F32)).astype(BF16)
    for level in uppers:
        info = infos[level - 1]
        parts = exchange_outer(parts, level)
        gathered = exchange_inner(sum_spread(parts, info.cells), level)
        size = info.cell_rows * width * info.chunk
        if level == depth:
            parts = kernel_call(
                functools.partial(top_kernel, info),
                [shaped((info.cells, info.chunk, info.cell_rows), BF16)],
                [gathered] + inverse_pieces[level],
                flops=4 * size,
            )[0]
            break
        above = infos[level]
        lowers = [ys[j] for j in range(1, level)]
        ys[level], parts = kernel_call(
            functools.partial(forward_kernel, infos, level),
            [
                shaped((4 * info.pair_x, info.chunk, info.rows), F32),
                shaped((above.targets, above.chunk, above.cell_rows), BF16),
            ],
            [gathered, base[2 * level], received[level]]
            + inverse_pieces[level]
            + lowers
            + [dense[j, level + 1] for j in range(1, level + 1)],
            scalars=at,
            scratch=[pltpu.VMEM((above.chunk * above.pair_x, width), F32)],
            flops=4 * size,
        )

    solved = {}
    swapped = {}
    for level in range(depth, 0, -1):
        info = infos[level - 1]
        if level < depth:
            higher = range(level + 1, depth + 1)
            parts = kernel_call(
                functools.partial(backward_kernel, infos, level),
                [shaped((info.cells, info.chunk, info.cell_rows), BF16)],
                [ys[level]]
                + inverse_pieces[level]
                + [solved[above] for above in higher]
                + [dense[level, above] for above in higher],
                scalars=at,
                flops=4 * info.cell_rows * width * info.chunk,
            )[0]
        parts = exchange_inner(parts, level)
        solved[level] = exchange_outer(sum_spread(parts, info.targets), level)
        swapped[level] = swap(solved[level], "leaf", 1)

    part = kernel_call(
        functools.partial(last_kernel, infos),
        [shaped((width, cases), BF16)],
        [y0, subtree_inverse]
        + [dense[0, above] for above in uppers]
        + [solved[above] for above in uppers]
        + [swapped[above] for above in uppers],
        scalars=at,
        scratch=[pltpu.VMEM((cases, width), BF16)],
        flops=2 * (1 + depth) * counts[0] * width * cases,
    )[0]
    parts = lax.all_to_all(part, "blk", 0, 0, tiled=True)

    outputs = []
    for level in uppers:
        info = infos[level - 1]
        member = leaf_id & ((1 << level) - 1)
        side = member & (2 * info.pair_x - 1)
        hi = member // (2 * info.pair_x)
        offset = (side * 2 + yb) * info.rows

        def own(value):
            shape = (info.his, info.pair_x, info.zbs, 2, info.chunk, info.cell_rows)
            sizes = (1, info.pair_x, 1, 2, info.chunk, info.rows)
            taken = lax.dynamic_slice(value.reshape(shape), (hi, 0, zb, 0, 0, offset), sizes)
            return taken[0, :, 0].transpose(1, 0, 2, 3)

        mine, other = own(solved[level]), own(swapped[level])
        rows = jnp.where(
            core == 0, jnp.stack([mine, other], 1), jnp.stack([other, mine], 1)
        )
        outputs.append(rows.reshape(cases, info.rows).T.astype(F32))
    top = parts.reshape(-1, counts[0], cases).astype(F32).sum(0)
    return jnp.concatenate([top] + outputs, 0)[None, None]


def solution(mesh):
    spec = P("leaf", "blk", None, None)
    return jax.shard_map(
        solve, mesh=mesh, in_specs=(spec, spec, spec, P()), out_specs=spec, check_vma=False
    )
```

profile of v0, /device:TPU:0, one launch (start us, length us, event | category | flops | bytes accessed | tf_op | source)
XLA Modules:
  0.0 189.6 jit_solution(111881492124853194)
XLA Ops:
  1.9 7.3 %all-to-all-start = ((bf16[8,256,128]{2,1,0:T(8,128)(2,1)}), bf16[8,256,128]{2,1,0:T(8,128)(2,1)S(1)}, u32[]{:S(2)}, u32[]{:S(2)}) async-start(bf16[8,256,128]{2,1,0:T(8,128)(2,1)} %broadcast_in_dim.4), calls=%async_computation | async-start | bytes 1048576 | tf_op jit(solution)/shard_map/all_to_all | solution.py:358
  9.2 1.7 fusion.11
  13.2 4.7 %shard_map.46 = (bf16[1,256,2048]{2,1,0:T(8,128)(2,1)}, bf16[1,256,2048]{2,1,0:T(8,128)(2,1)}) custom-call(s32[2,1024]{1,0:T(2,128)} %pad_add_fusion.spots_ref, bf16[256,1024]{1,0:T(8,128)(2,1)} %get-tuple-element.24.refs_0_, bf16[256,1024]{1,0:T(8,128)(2,1)} %get-tuple-element.23.refs_1_), custom_call_target="tpu_custom_call" | custom-call | flops 2147483648 | bytes 3153920 | tf_op jit(solution)/shard_map/pallas_call | solution.py:38
  19.0 4.7 %all-to-all-done = bf16[8,256,128]{2,1,0:T(8,128)(2,1)S(1)} async-done(((bf16[8,256,128]{2,1,0:T(8,128)(2,1)}), bf16[8,256,128]{2,1,0:T(8,128)(2,1)S(1)}, u32[]{:S(2)}, u32[]{:S(2)}) %all-to-all-start) | async-done | bytes 524320 | tf_op jit(solution)/shard_map/all_to_all | solution.py:358
  24.5 4.2 %shard_map.47 = (f32[256,128]{1,0:T(8,128)}, f32[8,32,512]{2,1,0:T(8,128)}, bf16[8,32,512]{2,1,0:T(8,128)(2,1)}, f32[16,16,512]{2,1,0:T(8,128)}, bf16[16,16,512]{2,1,0:T(8,128)(2,1)}) custom-call(s32[5]{0:T(128)} %stack.47.at, bf16[2048,128]{1,0:T(8,128)(2,1)} %bitcast.65, bf16[256,2048]{1,0:T(8,128)(2,1)} %slice_bitcast_fusion.inverse, ...), custom_call_target="tpu_custom_call" | custom-call | flops 402653184 | bytes 5603328 | tf_op jit(solution)/shard_map/pallas_call | solution.py:38
  31.4 1.7 slice_bitcast_fusion.3.refs_0_
  33.7 1.9 add_convert_fusion
  35.5 3.6 %all-to-all-start.1 = ((bf16[8,32,512]{2,1,0:T(8,128)(2,1)}), bf16[8,32,512]{2,1,0:T(8,128)(2,1)S(1)}, u32[]{:S(2)}, u32[]{:S(2)}) async-start(bf16[8,32,512]{2,1,0:T(8,128)(2,1)} %add_convert_fusion), calls=%async_computation.1 | async-start | bytes 524288 | tf_op jit(solution)/shard_map/all_to_all | solution.py:315
  39.2 7.2 %collective-permute-done.2.refs_1_ = bf16[128,2048]{1,0:T(8,128)(2,1)S(1)} collective-permute-done((bf16[128,2048]{1,0:T(8,128)(2,1)S(1)}, bf16[128,2048]{1,0:T(8,128)(2,1)S(1)}, u32[]{:S(2)}, u32[]{:S(2)}) %collective-permute-start.2) | collective-permute-done | bytes 524320 | tf_op jit(solution)/shard_map/ppermute | solution.py:296
  46.9 5.5 %collective-permute-done.5.refs_1_ = bf16[128,1024]{1,0:T(8,128)(2,1)} collective-permute-done((bf16[128,1024]{1,0:T(8,128)(2,1)}, bf16[128,1024]{1,0:T(8,128)(2,1)}, u32[]{:S(2)}, u32[]{:S(2)}) %collective-permute-start.5) | collective-permute-done | bytes 262176 | tf_op jit(solution)/shard_map/ppermute | solution.py:296
  54.2 1.7 shard_map.48
  55.9 3.3 %all-to-all-start.2 = ((bf16[4,32,512]{2,1,0:T(8,128)(2,1)}), bf16[4,32,512]{2,1,0:T(8,128)(2,1)S(1)}, u32[]{:S(2)}, u32[]{:S(2)}) async-start(bf16[4,32,512]{2,1,0:T(8,128)(2,1)} %shard_map.48), calls=%async_computation.2 | async-start | bytes 262144 | tf_op jit(solution)/shard_map/all_to_all | solution.py:328
  60.8 8.1 %shard_map.49.refs_4_.refs_5_ = bf16[4,128,2048]{2,1,0:T(8,128)(2,1)} custom-call(s32[1,1024]{1,0:T(1,128)} %get-tuple-element.25.spots_ref, bf16[128,1024]{1,0:T(8,128)(2,1)} %slice_bitcast_fusion.3.refs_0_, bf16[128,1024]{1,0:T(8,128)(2,1)} %collective-permute-done.5.refs_1_, bf16[128,1024]{1,0:T(8,128)(2,1)} %collective-permute-done.6.refs_2_, ...), custom_call_target="tpu_custom_call" | custom-call | flops 2147483648 | bytes 3149824 | tf_op jit(solution)/shard_map/pallas_call | solution.py:38
  69.5 4.3 %shard_map.50 = (f32[4,32,128]{2,1,0:T(8,128)}, bf16[16,16,512]{2,1,0:T(8,128)(2,1)}) custom-call(s32[5]{0:T(128)} %stack.47.at, bf16[4,32,512]{2,1,0:T(8,128)(2,1)} %copy-done.10, f32[16,16,512]{2,1,0:T(8,128)} %get-tuple-element.19.mine, bf16[16,16,512]{2,1,0:T(8,128)(2,1)} %collective-permute-done.1.received, bf16[128,2048]{1,0:T(8,128)(2,1)} %copy-done, ...), custom_call_target="tpu_custom_call" | custom-call | flops 134217728 | bytes 5439488 | tf_op jit(solution)/shard_map/pallas_call | solution.py:38
  73.9 6.0 %all-to-all-start.3 = ((bf16[16,16,512]{2,1,0:T(8,128)(2,1)}), bf16[16,16,512]{2,1,0:T(8,128)(2,1)S(1)}, u32[]{:S(2)}, u32[]{:S(2)}) async-start(bf16[16,16,512]{2,1,0:T(8,128)(2,1)} %get-tuple-element.22), calls=%async_computation.3 | async-start | bytes 524288 | tf_op jit(solution)/shard_map/all_to_all | solution.py:316
  79.9 1.9 %collective-permute-start.9 = (bf16[64,2048]{1,0:T(8,128)(2,1)S(1)}, bf16[64,2048]{1,0:T(8,128)(2,1)S(1)}, u32[]{:S(2)}, u32[]{:S(2)}) collective-permute-start(bf16[64,2048]{1,0:T(8,128)(2,1)S(1)} %reshape.81.refs_0_), channel_id=1, source_target_pairs={{0,16},{8,24},{16,0},{24,8},{1,17},{9,25},{17,1},{25,9},{2,18},{10... | collective-permute-start | bytes 786440 | tf_op jit(solution)/shard_map/ppermute | solution.py:296
  82.5 9.1 %collective-permute-done.9.refs_2_ = bf16[64,2048]{1,0:T(8,128)(2,1)S(1)} collective-permute-done((bf16[64,2048]{1,0:T(8,128)(2,1)S(1)}, bf16[64,2048]{1,0:T(8,128)(2,1)S(1)}, u32[]{:S(2)}, u32[]{:S(2)}) %collective-permute-start.9) | collective-permute-done | bytes 262176 | tf_op jit(solution)/shard_map/ppermute | solution.py:296
  91.6 4.2 %collective-permute-done.10.refs_3_ = bf16[64,2048]{1,0:T(8,128)(2,1)S(1)} collective-permute-done((bf16[64,2048]{1,0:T(8,128)(2,1)S(1)}, bf16[64,2048]{1,0:T(8,128)(2,1)S(1)}, u32[]{:S(2)}, u32[]{:S(2)}) %collective-permute-start.10) | collective-permute-done | bytes 262176 | tf_op jit(solution)/shard_map/ppermute | solution.py:296
  98.2 4.5 %all-to-all-start.4 = ((bf16[4,16,512]{2,1,0:T(8,128)(2,1)}), bf16[4,16,512]{2,1,0:T(8,128)(2,1)S(1)}, u32[]{:S(2)}, u32[]{:S(2)}) async-start(bf16[4,16,512]{2,1,0:T(8,128)(2,1)} %shard_map.51), calls=%async_computation.4 | async-start | bytes 131072 | tf_op jit(solution)/shard_map/all_to_all | solution.py:328
  102.8 5.7 %all-to-all-done.4.gathered = bf16[4,16,512]{2,1,0:T(8,128)(2,1)S(1)} async-done(((bf16[4,16,512]{2,1,0:T(8,128)(2,1)}), bf16[4,16,512]{2,1,0:T(8,128)(2,1)S(1)}, u32[]{:S(2)}, u32[]{:S(2)}) %all-to-all-start.4) | async-done | bytes 65568 | tf_op jit(solution)/shard_map/all_to_all | solution.py:328
  109.2 3.1 %shard_map.52 = bf16[4,16,512]{2,1,0:T(8,128)(2,1)} custom-call(bf16[4,16,512]{2,1,0:T(8,128)(2,1)} %copy-done.20, bf16[64,2048]{1,0:T(8,128)(2,1)} %copy-done.7, bf16[64,2048]{1,0:T(8,128)(2,1)} %copy-done.13, bf16[64,2048]{1,0:T(8,128)(2,1)} %copy-done.14, bf16[64,2048]{1,0:T(8,128)(2,1)} %copy-done.15, bf16[64,2048]{1,0:T(8,128)(2,1)} %copy-done.16, ...), custom_call_target="tpu_custom_call" | custom-call | flops 67108864 | bytes 2228224 | tf_op jit(solution)/shard_map/pallas_call | solution.py:38
  112.3 9.7 %all_to_all.54.parts = bf16[4,16,512]{2,1,0:T(8,128)(2,1)} all-to-all(bf16[4,16,512]{2,1,0:T(8,128)(2,1)} %shard_map.52), channel_id=1, replica_groups={{0,2,4,6},{1,3,5,7},{8,10,12,14},{9,11,13,15},{16,18,20,22},{17,19,21,2..., dimensions={0} | all-to-all | bytes 131072 | tf_op jit(solution)/shard_map/all_to_all | solution.py:328
  122.0 1.6 shard_map.53
  123.6 12.7 %all_to_all.55.refs_4_.refs_3_ = bf16[16,16,512]{2,1,0:T(8,128)(2,1)} all-to-all(bf16[16,16,512]{2,1,0:T(8,128)(2,1)} %shard_map.53), channel_id=1, replica_groups={{0,1,2,3,4,5,6,7,16,17,18,19,20,21,22,23},{8,9,10,11,12,13,14,15,24,25,..., dimensions={0} | all-to-all | bytes 524288 | tf_op jit(solution)/shard_map/all_to_all | solution.py:316
  136.3 4.2 %shard_map.54 = bf16[4,32,512]{2,1,0:T(8,128)(2,1)} custom-call(s32[5]{0:T(128)} %stack.47.at, f32[4,32,128]{2,1,0:T(8,128)} %get-tuple-element.21.y, bf16[128,2048]{1,0:T(8,128)(2,1)} %copy-done, bf16[128,2048]{1,0:T(8,128)(2,1)} %copy-done.4, bf16[128,2048]{1,0:T(8,128)(2,1)} %collective-permute-done.3.refs_2_, ...), custom_call_target="tpu_custom_call" | custom-call | flops 134217728 | bytes 4653056 | tf_op jit(solution)/shard_map/pallas_call | solution.py:38
  140.5 9.9 %all_to_all.56.parts = bf16[4,32,512]{2,1,0:T(8,128)(2,1)} all-to-all(bf16[4,32,512]{2,1,0:T(8,128)(2,1)} %shard_map.54), channel_id=1, replica_groups={{0,2,4,6},{1,3,5,7},{8,10,12,14},{9,11,13,15},{16,18,20,22},{17,19,21,2..., dimensions={0} | all-to-all | bytes 262144 | tf_op jit(solution)/shard_map/all_to_all | solution.py:328
  150.4 1.6 shard_map.55
  152.0 3.6 %all-to-all-start.8 = ((bf16[8,32,512]{2,1,0:T(8,128)(2,1)}), bf16[8,32,512]{2,1,0:T(8,128)(2,1)S(1)}, u32[]{:S(2)}, u32[]{:S(2)}) async-start(bf16[8,32,512]{2,1,0:T(8,128)(2,1)} %shard_map.55), calls=%async_computation.8 | async-start | bytes 524288 | tf_op jit(solution)/shard_map/all_to_all | solution.py:315
  155.7 8.1 %all-to-all-done.8.refs_2_ = bf16[8,32,512]{2,1,0:T(8,128)(2,1)S(1)} async-done(((bf16[8,32,512]{2,1,0:T(8,128)(2,1)}), bf16[8,32,512]{2,1,0:T(8,128)(2,1)S(1)}, u32[]{:S(2)}, u32[]{:S(2)}) %all-to-all-start.8) | async-done | bytes 262176 | tf_op jit(solution)/shard_map/all_to_all | solution.py:315
  166.1 4.2 %shard_map.56 = bf16[2048,128]{1,0:T(8,128)(2,1)} custom-call(s32[5]{0:T(128)} %stack.47.at, f32[256,128]{1,0:T(8,128)} %get-tuple-element.16.y, bf16[256,2048]{1,0:T(8,128)(2,1)} %slice_bitcast_fusion.inverse, bf16[1,256,2048]{2,1,0:T(8,128)(2,1)} %get-tuple-element.14.refs_0_, bf16[1,256,2048]{2,1,0:T(8,128)(2,1)} %get-tuple-element.15.refs_1_, ...), custom_call_target="tpu_custom_call" | custom-call | flops 402653184 | bytes 4849664 | tf_op jit(solution)/shard_map/pallas_call | solution.py:38
  170.3 3.5 %all-to-all-start.9 = ((bf16[8,256,128]{2,1,0:T(8,128)(2,1)}), bf16[8,256,128]{2,1,0:T(8,128)(2,1)S(1)}, u32[]{:S(2)}, u32[]{:S(2)}) async-start(bf16[8,256,128]{2,1,0:T(8,128)(2,1)} %bitcast.66), calls=%async_computation.9 | async-start | bytes 1048576 | tf_op jit(solution)/shard_map/all_to_all | solution.py:465
  177.1 11.7 %all-to-all-done.9 = bf16[8,256,128]{2,1,0:T(8,128)(2,1)S(1)} async-done(((bf16[8,256,128]{2,1,0:T(8,128)(2,1)}), bf16[8,256,128]{2,1,0:T(8,128)(2,1)S(1)}, u32[]{:S(2)}, u32[]{:S(2)}) %all-to-all-start.9) | async-done | bytes 524320 | tf_op jit(solution)/shard_map/all_to_all | solution.py:465
  (103 shorter events, 23.8 us)
Async XLA Ops:
  1.9 21.8 %all-to-all-start = ((bf16[8,256,128]{2,1,0:T(8,128)(2,1)}), bf16[8,256,128]{2,1,0:T(8,128)(2,1)S(1)}, u32[]{:S(2)}, u32[]{:S(2)}) async-start(bf16[8,256,128]{2,1,0:T(8,128)(2,1)} %broadcast_in_dim.4), calls=%async_computation | async-start | bytes 1048576 | tf_op jit(solution)/shard_map/all_to_all | solution.py:358
  28.7 5.0 %collective-permute-start = (bf16[8,32,512]{2,1,0:T(8,128)(2,1)}, bf16[8,32,512]{2,1,0:T(8,128)(2,1)}, u32[]{:S(2)}, u32[]{:S(2)}) collective-permute-start(bf16[8,32,512]{2,1,0:T(8,128)(2,1)} %get-tuple-element.18), channel_id=1, source_target_pairs={{0,8},{8,0},{16,24},{24,16},{1,9},{9,1},{17,25},{25,17},{2,10},{10... | collective-permute-start | bytes 786440 | tf_op jit(solution)/shard_map/ppermute | solution.py:296
  29.5 23.5 %slice-start.1 = ((bf16[1,1,448,2048]{3,2,1,0:T(8,128)(2,1)}), bf16[1,1,64,2048]{3,2,1,0:T(8,128)(2,1)S(1)}, s32[]{:S(2)}) async-start(bf16[1,1,448,2048]{3,2,1,0:T(8,128)(2,1)} %param.5), calls=%async_computation.11 | async-start | bytes 524288 | tf_op jit(solution)/shard_map/slice | solution.py:385
  29.9 23.4 %copy-start = (bf16[128,2048]{1,0:T(8,128)(2,1)}, bf16[128,2048]{1,0:T(8,128)(2,1)S(1)}, u32[]{:S(2)}) copy-start(bf16[128,2048]{1,0:T(8,128)(2,1)S(1)} %reshape.79.refs_0_) | copy-start | bytes 1572868
  29.9 16.5 %collective-permute-start.2 = (bf16[128,2048]{1,0:T(8,128)(2,1)S(1)}, bf16[128,2048]{1,0:T(8,128)(2,1)S(1)}, u32[]{:S(2)}, u32[]{:S(2)}) collective-permute-start(bf16[128,2048]{1,0:T(8,128)(2,1)S(1)} %reshape.79.refs_0_), channel_id=1, source_target_pairs={{0,1},{1,0},{2,3},{3,2},{4,5},{5,4},{6,7},{7,6},{8,9},{9,8},{10,11... | collective-permute-start | bytes 1572872 | tf_op jit(solution)/shard_map/ppermute | solution.py:296
  33.1 19.4 %collective-permute-start.5 = (bf16[128,1024]{1,0:T(8,128)(2,1)}, bf16[128,1024]{1,0:T(8,128)(2,1)}, u32[]{:S(2)}, u32[]{:S(2)}) collective-permute-start(bf16[128,1024]{1,0:T(8,128)(2,1)} %slice_bitcast_fusion.3.refs_0_), channel_id=1, source_target_pairs={{0,1},{1,0},{2,3},{3,2},{4,5},{5,4},{6,7},{7,6},{8,9},{9,8},{10,11... | collective-permute-start | bytes 786440 | tf_op jit(solution)/shard_map/ppermute | solution.py:296
  35.5 17.9 %all-to-all-start.1 = ((bf16[8,32,512]{2,1,0:T(8,128)(2,1)}), bf16[8,32,512]{2,1,0:T(8,128)(2,1)S(1)}, u32[]{:S(2)}, u32[]{:S(2)}) async-start(bf16[8,32,512]{2,1,0:T(8,128)(2,1)} %add_convert_fusion), calls=%async_computation.1 | async-start | bytes 524288 | tf_op jit(solution)/shard_map/all_to_all | solution.py:315
  39.2 29.7 %collective-permute-start.3 = (bf16[128,2048]{1,0:T(8,128)(2,1)S(1)}, bf16[128,2048]{1,0:T(8,128)(2,1)}, u32[]{:S(2)}, u32[]{:S(2)}) collective-permute-start(bf16[128,2048]{1,0:T(8,128)(2,1)S(1)} %reshape.79.refs_0_), channel_id=1, source_target_pairs={{0,8},{8,0},{16,24},{24,16},{1,9},{9,1},{17,25},{25,17},{2,10},{10... | collective-permute-start | bytes 1572872 | tf_op jit(solution)/shard_map/ppermute | solution.py:296
  46.4 22.4 %copy-start.4 = (bf16[128,2048]{1,0:T(8,128)(2,1)}, bf16[128,2048]{1,0:T(8,128)(2,1)S(1)}, u32[]{:S(2)}) copy-start(bf16[128,2048]{1,0:T(8,128)(2,1)S(1)} %collective-permute-done.2.refs_1_) | copy-start | bytes 1572868
  46.4 22.4 %collective-permute-start.4 = (bf16[128,2048]{1,0:T(8,128)(2,1)S(1)}, bf16[128,2048]{1,0:T(8,128)(2,1)}, u32[]{:S(2)}, u32[]{:S(2)}) collective-permute-start(bf16[128,2048]{1,0:T(8,128)(2,1)S(1)} %collective-permute-done.2.refs_1_), channel_id=1, source_target_pairs={{0,8},{8,0},{16,24},{24,16},{1,9},{9,1},{17,25},{25,17},{2,10},{10... | collective-permute-start | bytes 1572872 | tf_op jit(solution)/shard_map/ppermute | solution.py:296
  46.4 12.8 %collective-permute-start.6 = (bf16[128,1024]{1,0:T(8,128)(2,1)}, bf16[128,1024]{1,0:T(8,128)(2,1)}, u32[]{:S(2)}, u32[]{:S(2)}) collective-permute-start(bf16[128,1024]{1,0:T(8,128)(2,1)} %slice_bitcast_fusion.3.refs_0_), channel_id=1, source_target_pairs={{0,8},{8,0},{16,24},{24,16},{1,9},{9,1},{17,25},{25,17},{2,10},{10... | collective-permute-start | bytes 786440 | tf_op jit(solution)/shard_map/ppermute | solution.py:296
  52.5 8.3 %collective-permute-start.7 = (bf16[128,1024]{1,0:T(8,128)(2,1)}, bf16[128,1024]{1,0:T(8,128)(2,1)}, u32[]{:S(2)}, u32[]{:S(2)}) collective-permute-start(bf16[128,1024]{1,0:T(8,128)(2,1)} %collective-permute-done.5.refs_1_), channel_id=1, source_target_pairs={{0,8},{8,0},{16,24},{24,16},{1,9},{9,1},{17,25},{25,17},{2,10},{10... | collective-permute-start | bytes 786440 | tf_op jit(solution)/shard_map/ppermute | solution.py:296
  52.5 16.4 %collective-permute-start.1 = (bf16[16,16,512]{2,1,0:T(8,128)(2,1)}, bf16[16,16,512]{2,1,0:T(8,128)(2,1)}, u32[]{:S(2)}, u32[]{:S(2)}) collective-permute-start(bf16[16,16,512]{2,1,0:T(8,128)(2,1)} %get-tuple-element.20), channel_id=1, source_target_pairs={{0,8},{8,0},{16,24},{24,16},{1,9},{9,1},{17,25},{25,17},{2,10},{10... | collective-permute-start | bytes 786440 | tf_op jit(solution)/shard_map/ppermute | solution.py:296
  53.5 28.5 %copy-start.7 = (bf16[64,2048]{1,0:T(8,128)(2,1)}, bf16[64,2048]{1,0:T(8,128)(2,1)S(1)}, u32[]{:S(2)}) copy-start(bf16[64,2048]{1,0:T(8,128)(2,1)S(1)} %reshape.81.refs_0_) | copy-start | bytes 786436
  55.9 13.0 %all-to-all-start.2 = ((bf16[4,32,512]{2,1,0:T(8,128)(2,1)}), bf16[4,32,512]{2,1,0:T(8,128)(2,1)S(1)}, u32[]{:S(2)}, u32[]{:S(2)}) async-start(bf16[4,32,512]{2,1,0:T(8,128)(2,1)} %shard_map.48), calls=%async_computation.2 | async-start | bytes 262144 | tf_op jit(solution)/shard_map/all_to_all | solution.py:328
  59.2 22.6 %collective-permute-start.8 = (bf16[64,2048]{1,0:T(8,128)(2,1)S(1)}, bf16[64,2048]{1,0:T(8,128)(2,1)S(1)}, u32[]{:S(2)}, u32[]{:S(2)}) collective-permute-start(bf16[64,2048]{1,0:T(8,128)(2,1)S(1)} %reshape.81.refs_0_), channel_id=1, source_target_pairs={{0,1},{1,0},{2,3},{3,2},{4,5},{5,4},{6,7},{7,6},{8,9},{9,8},{10,11... | collective-permute-start | bytes 786440 | tf_op jit(solution)/shard_map/ppermute | solution.py:296
  73.9 22.0 %all-to-all-start.3 = ((bf16[16,16,512]{2,1,0:T(8,128)(2,1)}), bf16[16,16,512]{2,1,0:T(8,128)(2,1)S(1)}, u32[]{:S(2)}, u32[]{:S(2)}) async-start(bf16[16,16,512]{2,1,0:T(8,128)(2,1)} %get-tuple-element.22), calls=%async_computation.3 | async-start | bytes 524288 | tf_op jit(solution)/shard_map/all_to_all | solution.py:316
  79.9 11.7 %collective-permute-start.9 = (bf16[64,2048]{1,0:T(8,128)(2,1)S(1)}, bf16[64,2048]{1,0:T(8,128)(2,1)S(1)}, u32[]{:S(2)}, u32[]{:S(2)}) collective-permute-start(bf16[64,2048]{1,0:T(8,128)(2,1)S(1)} %reshape.81.refs_0_), channel_id=1, source_target_pairs={{0,16},{8,24},{16,0},{24,8},{1,17},{9,25},{17,1},{25,9},{2,18},{10... | collective-permute-start | bytes 786440 | tf_op jit(solution)/shard_map/ppermute | solution.py:296
  81.8 26.6 %copy-start.13 = (bf16[64,2048]{1,0:T(8,128)(2,1)}, bf16[64,2048]{1,0:T(8,128)(2,1)S(1)}, u32[]{:S(2)}) copy-start(bf16[64,2048]{1,0:T(8,128)(2,1)S(1)} %collective-permute-done.8.refs_1_) | copy-start | bytes 786436
  81.8 14.0 %collective-permute-start.10 = (bf16[64,2048]{1,0:T(8,128)(2,1)S(1)}, bf16[64,2048]{1,0:T(8,128)(2,1)S(1)}, u32[]{:S(2)}, u32[]{:S(2)}) collective-permute-start(bf16[64,2048]{1,0:T(8,128)(2,1)S(1)} %collective-permute-done.8.refs_1_), channel_id=1, source_target_pairs={{0,16},{8,24},{16,0},{24,8},{1,17},{9,25},{17,1},{25,9},{2,18},{10... | collective-permute-start | bytes 786440 | tf_op jit(solution)/shard_map/ppermute | solution.py:296
  82.0 20.7 %collective-permute-start.11 = (bf16[64,2048]{1,0:T(8,128)(2,1)S(1)}, bf16[64,2048]{1,0:T(8,128)(2,1)S(1)}, u32[]{:S(2)}, u32[]{:S(2)}) collective-permute-start(bf16[64,2048]{1,0:T(8,128)(2,1)S(1)} %reshape.81.refs_0_), channel_id=1, source_target_pairs={{0,8},{8,0},{16,24},{24,16},{1,9},{9,1},{17,25},{25,17},{2,10},{10... | collective-permute-start | bytes 786440 | tf_op jit(solution)/shard_map/ppermute | solution.py:296
  82.0 20.7 %collective-permute-start.12 = (bf16[64,2048]{1,0:T(8,128)(2,1)S(1)}, bf16[64,2048]{1,0:T(8,128)(2,1)S(1)}, u32[]{:S(2)}, u32[]{:S(2)}) collective-permute-start(bf16[64,2048]{1,0:T(8,128)(2,1)S(1)} %collective-permute-done.8.refs_1_), channel_id=1, source_target_pairs={{0,8},{8,0},{16,24},{24,16},{1,9},{9,1},{17,25},{25,17},{2,10},{10... | collective-permute-start | bytes 786440 | tf_op jit(solution)/shard_map/ppermute | solution.py:296
  91.6 16.8 %copy-start.14 = (bf16[64,2048]{1,0:T(8,128)(2,1)}, bf16[64,2048]{1,0:T(8,128)(2,1)S(1)}, u32[]{:S(2)}) copy-start(bf16[64,2048]{1,0:T(8,128)(2,1)S(1)} %collective-permute-done.9.refs_2_) | copy-start | bytes 786436
  91.6 11.1 %collective-permute-start.13 = (bf16[64,2048]{1,0:T(8,128)(2,1)S(1)}, bf16[64,2048]{1,0:T(8,128)(2,1)S(1)}, u32[]{:S(2)}, u32[]{:S(2)}) collective-permute-start(bf16[64,2048]{1,0:T(8,128)(2,1)S(1)} %collective-permute-done.9.refs_2_), channel_id=1, source_target_pairs={{0,8},{8,0},{16,24},{24,16},{1,9},{9,1},{17,25},{25,17},{2,10},{10... | collective-permute-start | bytes 786440 | tf_op jit(solution)/shard_map/ppermute | solution.py:296
  95.8 12.7 %copy-start.15 = (bf16[64,2048]{1,0:T(8,128)(2,1)}, bf16[64,2048]{1,0:T(8,128)(2,1)S(1)}, u32[]{:S(2)}) copy-start(bf16[64,2048]{1,0:T(8,128)(2,1)S(1)} %collective-permute-done.10.refs_3_) | copy-start | bytes 786436
  95.8 7.0 %collective-permute-start.14 = (bf16[64,2048]{1,0:T(8,128)(2,1)S(1)}, bf16[64,2048]{1,0:T(8,128)(2,1)S(1)}, u32[]{:S(2)}, u32[]{:S(2)}) collective-permute-start(bf16[64,2048]{1,0:T(8,128)(2,1)S(1)} %collective-permute-done.10.refs_3_), channel_id=1, source_target_pairs={{0,8},{8,0},{16,24},{24,16},{1,9},{9,1},{17,25},{25,17},{2,10},{10... | collective-permute-start | bytes 786440 | tf_op jit(solution)/shard_map/ppermute | solution.py:296
  98.2 10.3 %all-to-all-start.4 = ((bf16[4,16,512]{2,1,0:T(8,128)(2,1)}), bf16[4,16,512]{2,1,0:T(8,128)(2,1)S(1)}, u32[]{:S(2)}, u32[]{:S(2)}) async-start(bf16[4,16,512]{2,1,0:T(8,128)(2,1)} %shard_map.51), calls=%async_computation.4 | async-start | bytes 131072 | tf_op jit(solution)/shard_map/all_to_all | solution.py:328
  136.3 19.4 %copy-start.1 = (bf16[16,16,512]{2,1,0:T(8,128)(2,1)S(1)}, bf16[16,16,512]{2,1,0:T(8,128)(2,1)}, u32[]{:S(2)}) copy-start(bf16[16,16,512]{2,1,0:T(8,128)(2,1)} %all_to_all.55.refs_4_.refs_3_) | copy-start | bytes 786436
  152.0 11.8 %all-to-all-start.8 = ((bf16[8,32,512]{2,1,0:T(8,128)(2,1)}), bf16[8,32,512]{2,1,0:T(8,128)(2,1)S(1)}, u32[]{:S(2)}, u32[]{:S(2)}) async-start(bf16[8,32,512]{2,1,0:T(8,128)(2,1)} %shard_map.55), calls=%async_computation.8 | async-start | bytes 524288 | tf_op jit(solution)/shard_map/all_to_all | solution.py:315
  155.7 8.2 %collective-permute-start.16 = (bf16[16,16,512]{2,1,0:T(8,128)(2,1)S(1)}, bf16[16,16,512]{2,1,0:T(8,128)(2,1)S(1)}, u32[]{:S(2)}, u32[]{:S(2)}) collective-permute-start(bf16[16,16,512]{2,1,0:T(8,128)(2,1)S(1)} %copy-done.1), channel_id=1, source_target_pairs={{0,8},{8,0},{16,24},{24,16},{1,9},{9,1},{17,25},{25,17},{2,10},{10... | collective-permute-start | bytes 786440 | tf_op jit(solution)/shard_map/ppermute | solution.py:296
  163.9 1.5 collective-permute-start.15
  170.3 18.5 %all-to-all-start.9 = ((bf16[8,256,128]{2,1,0:T(8,128)(2,1)}), bf16[8,256,128]{2,1,0:T(8,128)(2,1)S(1)}, u32[]{:S(2)}, u32[]{:S(2)}) async-start(bf16[8,256,128]{2,1,0:T(8,128)(2,1)} %bitcast.66), calls=%async_computation.9 | async-start | bytes 1048576 | tf_op jit(solution)/shard_map/all_to_all | solution.py:465
  (15 other events, 51.4 us)
where the time goes:
time: 191 us; the launch traced here: 190 us
  waiting for transfers between devices  57.8 us (30%)
  starting transfers between devices  39.3 us (21%)
  Pallas kernels  39.3 us (21%)
  blocking collectives  32.3 us (17%)
  local copies, waits for them, and re-layouts  15.5 us (8%)
  other arithmetic  4.98 us (3%)
    pallas_call x11, Pallas kernels, kernel_call(): pl.pallas_call(body, out_shape=list(outs), in_specs=specs, out_specs=[pl....  39.3 us
    ppermute x17, waiting for transfers between devices, swap(): return lax.ppermute(value, axis, [(i, i ^ bit) for i in range(size)])  27.6 us
    all_to_all x2, blocking collectives, exchange_inner(): lax.all_to_all(value, 'blk', 0, 0, axis_index_groups=info.inner_blk, tile...  19.6 us
    all_to_all x1, blocking collectives, exchange_outer(): lax.all_to_all(value, ('leaf', 'blk'), 0, 0, axis_index_groups=infos[leve...  12.7 us
    all_to_all x1, waiting for transfers between devices, solve(): parts = lax.all_to_all(part, 'blk', 0, 0, tiled=True)  11.7 us
    all_to_all x2, waiting for transfers between devices, exchange_outer(): return lax.all_to_all(value, 'blk', 0, 0, tiled=True)  8.14 us
    all_to_all x2, starting transfers between devices, exchange_inner(): lax.all_to_all(value, 'blk', 0, 0, axis_index_groups=info.inner_blk, tile...  7.86 us
    ppermute x17, starting transfers between devices, swap(): return lax.ppermute(value, axis, [(i, i ^ bit) for i in range(size)])  7.33 us
  transfers between devices with their start and end apart: 24, of which 9 were waited for; matrix products, arithmetic and copies ran while one was open for 7% of the time, Pallas kernels for 11%

commit v1 on v0

v1 whole, which is shorter than its diff:
```python
import functools

import jax
import jax.numpy as jnp
from jax import lax
from jax.experimental import pallas as pl
from jax.experimental.pallas import tpu as pltpu
from jax.sharding import PartitionSpec as P


BF16 = jnp.bfloat16
F32 = jnp.float32


def mm(a, b):
    return jnp.dot(a, b, preferred_element_type=F32)


def mm_tn(a, b):
    return lax.dot_general(a, b, (((0,), (0,)), ((), ())), preferred_element_type=F32)


def mm_nt(a, b):
    return lax.dot_general(a, b, (((1,), (1,)), ((), ())), preferred_element_type=F32)


def shaped(shape, dtype):
    return jax.ShapeDtypeStruct(tuple(shape), dtype)


def kernel_call(body, outs, args, scalars=None, scratch=(), flops=0):
    values = []
    specs = []
    moved = sum(o.size * o.dtype.itemsize for o in outs)
    for arg in args:
        value, spec = arg if isinstance(arg, tuple) else (arg, pl.BlockSpec(memory_space=pltpu.VMEM))
        if spec is None:
            value = pltpu.with_memory_space_constraint(value, pltpu.HBM)
            spec = pl.BlockSpec(memory_space=pltpu.HBM)
        values.append(value)
        specs.append(spec)
        moved += value.size * value.dtype.itemsize
    if scalars is not None:
        specs = [pl.BlockSpec(memory_space=pltpu.SMEM)] + specs
        values = [scalars] + values
    return pl.pallas_call(
        body,
        out_shape=[pltpu.HBM(o.shape, o.dtype) for o in outs],
        in_specs=specs,
        out_specs=[pl.BlockSpec(memory_space=pltpu.VMEM)] * len(outs),
        scratch_shapes=list(scratch),
        compiler_params=pltpu.CompilerParams(vmem_limit_bytes=16 << 20),
        cost_estimate=pl.CostEstimate(flops=flops, bytes_accessed=moved, transcendentals=0),
    )(*values)


def hbm(values):
    return [(value, None) for value in values]


class Loads:
    def __init__(self, sems):
        self.sems = sems
        self.used = 0

    def start(self, pairs):
        copies = []
        for source, target in pairs:
            copies.append(pltpu.make_async_copy(source, target, self.sems.at[self.used]))
            copies[-1].start()
            self.used += 1
        return copies

    def rows(self, sources, target):
        pairs = []
        begin = 0
        for source in sources:
            count = source.shape[0]
            pairs.append((source, target.at[begin : begin + count, :]))
            begin += count
        return self.start(pairs)


def wait(copies):
    for copy in copies:
        copy.wait()


def split_power(value, size):
    bits = size.bit_length() - 1
    if size == 1 << bits:
        return value >> bits, value & (size - 1)
    return value // size, value % size


class Level:
    def __init__(self, level, leaves, blocks, width, cases):
        self.pair_x = 2 if level >= 2 else 1
        self.his = (1 << level) // (2 * self.pair_x)
        self.zbs = blocks // 2
        self.rows = width // (blocks << level)
        self.cells = self.his * self.zbs
        self.cell_rows = width // self.cells
        self.chunk = cases // (4 * self.pair_x)
        self.targets = self.cells * self.pair_x * 2
        outer = []
        inner = []
        for node in range(leaves >> level):
            base = node << level
            for side in range(2):
                outer.append(
                    [
                        (base + 2 * upper + side) * blocks + b
                        for upper in range(1 << (level - 1))
                        for b in range(blocks)
                    ]
                )
                for xu in range(self.pair_x):
                    for yb in range(2):
                        inner.append(
                            [
                                (base + (hi * self.pair_x + xu) * 2 + side) * blocks + 2 * zb + yb
                                for hi in range(self.his)
                                for zb in range(self.zbs)
                            ]
                        )
        self.outer = outer
        self.inner = inner
        self.inner_blk = [[2 * zb + yb for zb in range(self.zbs)] for yb in range(2)]

    @property
    def direct(self):
        return (2 * self.rows) % 128 == 0

    def natural(self):
        if not self.direct:
            return [(c * self.cell_rows, c, 0, self.cell_rows) for c in range(self.cells)]
        size = 2 * self.rows
        return [
            (
                ((hi * 2 * self.pair_x + side) * self.zbs + zb) * size,
                hi * self.zbs + zb,
                side * size,
                size,
            )
            for hi in range(self.his)
            for side in range(2 * self.pair_x)
            for zb in range(self.zbs)
        ]

    def position(self, rows):
        block, t = split_power(rows, 2 * self.rows)
        block, zpos = split_power(block, self.zbs)
        hi, side = split_power(block, 2 * self.pair_x)
        cell = hi * self.zbs + zpos
        return (cell * (2 * self.pair_x) + side) * (2 * self.rows) + t

    def target(self, hi, xu, zb, yb):
        return ((hi * self.pair_x + xu) * self.zbs + zb) * 2 + yb

    def lanes(self, cell):
        return slice(cell * self.cell_rows, (cell + 1) * self.cell_rows)

    def all_targets(self):
        for hi in range(self.his):
            for xu in range(self.pair_x):
                for zb in range(self.zbs):
                    for yb in range(2):
                        yield hi * self.zbs + zb, xu, yb, self.target(hi, xu, zb, yb)


CORE, YB, XU, SPOT = 0, 1, 2, 3


def first_kernel(rhs, out):
    rounded = rhs[0 : out.shape[1], :].astype(BF16)
    for n in range(out.shape[0]):
        out[n] = rounded


def expand_kernel(count, aboves, slots, begins, at, lists, *refs):
    blocks, outs = refs[:count], refs[count:]
    width = outs[0].shape[-1]
    step = min(512, width)
    for n, (info, out) in enumerate(zip(aboves, outs)):
        listed = info.position(lists[pl.ds(at[slots[n]], 1), :])
        if begins is None:
            block = jnp.concatenate([b[...] for b in blocks], 0)
        else:
            block = blocks[0][begins[n] : begins[n] + out.shape[0], :]
        for begin in range(0, width, step):
            ids = begin + lax.broadcasted_iota(jnp.int32, (step, listed.shape[-1]), 0)
            chosen = jnp.where(ids == listed, 1.0, 0.0).astype(BF16)
            out[:, begin : begin + step] = mm_nt(block, chosen).astype(BF16)


def subtree_kernel(infos, starts, at, full, inverse, rhs, *refs):
    depth = len(infos)
    sources = refs[:depth]
    outs = refs[depth : depth + 1 + 2 * depth]
    total, matrix, dense, sems = refs[depth + 1 + 2 * depth :]
    loads = Loads(sems)
    first = loads.start([(inverse.at[0 : matrix.shape[0], :], matrix)])
    later = [loads.start([(sources[n], dense.at[n])]) for n in range(depth)]
    core = at[CORE]
    width = total.shape[-1]
    placed = []
    for n, info in enumerate(infos):
        row_ids = at[SPOT + n] + lax.broadcasted_iota(jnp.int32, (info.rows, width), 0)
        lane_ids = lax.broadcasted_iota(jnp.int32, (info.rows, width), 1)
        spots = jnp.where(row_ids == lane_ids, 1.0, 0.0).astype(BF16)
        own = rhs[starts[n] : starts[n] + info.rows, :].astype(BF16)
        placed.append(mm_tn(own, spots))
    wait(first)
    y = mm(matrix[...], full[...])
    outs[0][...] = y
    y_round = y.astype(BF16)
    for n, info in enumerate(infos):
        wait(later[n])
        total[...] = placed[n] - mm_tn(y_round, dense[n])
        mine, other = outs[1 + 2 * n], outs[2 + 2 * n]
        for cell, xu, yb, target in info.all_targets():
            for side, ref in ((core, mine), (1 - core, other)):
                row = ((yb * 2 + side) * info.pair_x + xu) * info.chunk
                row = pl.multiple_of(row, info.chunk)
                value = total[pl.ds(row, info.chunk), info.lanes(cell)]
                ref[target] = value.astype(ref.dtype)


def sum_spread_kernel(parts, out):
    total = parts[0].astype(F32)
    for n in range(1, parts.shape[0]):
        total = total + parts[n].astype(F32)
    rounded = total.astype(BF16)
    for n in range(out.shape[0]):
        out[n] = rounded


def natural_rows(info, gathered):
    blocks = [
        gathered[cell][:, inside : inside + size]
        for _, cell, inside, size in info.natural()
    ]
    return jnp.concatenate(blocks, 1)


def spread_product(info, z, matrix, out):
    value = mm_tn(z, matrix[...]).astype(BF16)
    for lane, cell, inside, size in info.natural():
        out[cell, :, inside : inside + size] = value[:, lane : lane + size]


def forward_kernel(infos, k, at, gathered, mine, received, *refs):
    info, above = infos[k - 1], infos[k]
    count = 4 * info.pair_x
    pieces = refs[:count]
    lower_y = refs[count : count + k - 1]
    sources = refs[count + k - 1 : count + 2 * k - 1]
    y_ref, out, total, matrix, sems = refs[count + 2 * k - 1 : count + 2 * k + 4]
    dense = refs[count + 2 * k + 4 :]
    loads = Loads(sems)
    first = loads.rows(pieces, matrix)
    later = [loads.start([(source, dense[j])]) for j, source in enumerate(sources)]
    vector = natural_rows(info, gathered)
    wait(first)
    y = mm_nt(matrix[...], vector)
    y_ref[...] = y
    same = {}
    for j in range(1, k + 1):
        wait(later[j - 1])
        value = y if j == k else lower_y[j - 1][...]
        term = mm_tn(value.astype(BF16), dense[j - 1][...])
        same.setdefault(infos[j - 1].pair_x == above.pair_x, []).append(term)
    if False in same:
        total[...] = functools.reduce(jnp.add, same[False])
    else:
        total[...] = jnp.zeros(total.shape, F32)
    if True in same:
        term = functools.reduce(jnp.add, same[True])
        rows = pl.ds(pl.multiple_of(at[XU] * above.chunk, above.chunk), above.chunk)
        total[rows, :] = total[rows, :] + term
    for cell, xu, yb, target in above.all_targets():
        value = mine[target] + received[target].astype(F32)
        minus = total[xu * above.chunk : (xu + 1) * above.chunk, above.lanes(cell)]
        value = jnp.where(at[YB] == yb, value - minus, value)
        out[target] = value.astype(BF16)


def top_kernel(info, gathered, *refs):
    count = 4 * info.pair_x
    pieces = refs[:count]
    out, matrix, sems = refs[count:]
    first = Loads(sems).rows(pieces, matrix)
    vector = natural_rows(info, gathered)
    wait(first)
    y = mm_nt(matrix[...], vector)
    spread_product(info, y.astype(BF16), matrix, out)


def backward_kernel(infos, k, at, y, *refs):
    info = infos[k - 1]
    count = 4 * info.pair_x
    uppers = infos[k:]
    many = len(uppers)
    pieces = refs[:count]
    solved = refs[count : count + many]
    sources = refs[count + many : count + 2 * many]
    out, matrix, sems = refs[count + 2 * many : count + 2 * many + 3]
    dense = refs[count + 2 * many + 3 :]
    loads = Loads(sems)
    first = [loads.start([(source, dense[n])]) for n, source in enumerate(sources)]
    last = loads.rows(pieces, matrix)
    z = y[...]
    for n, above in enumerate(uppers):
        parts = []
        for hi in range(above.his):
            for zb in range(above.zbs):
                if above.pair_x == info.pair_x:
                    slot = ((hi * above.pair_x + at[XU]) * above.zbs + zb) * 2 + at[YB]
                    parts.append(solved[n][slot])
                else:
                    slots = [
                        above.target(hi, xu, zb, 0) + at[YB] for xu in range(above.pair_x)
                    ]
                    parts.append(jnp.concatenate([solved[n][slot] for slot in slots], 0))
        wait(first[n])
        z = z - mm_nt(dense[n][...], jnp.concatenate(parts, 1))
    wait(last)
    spread_product(info, z.astype(BF16), matrix, out)


def last_kernel(infos, at, y, inverse, *refs):
    depth = len(infos)
    sources = refs[:depth]
    mine = refs[depth : 2 * depth]
    other = refs[2 * depth : 3 * depth]
    out, full, matrix, dense, sems = refs[3 * depth :]
    loads = Loads(sems)
    first = {n: loads.start([(sources[n], dense.at[n])]) for n in range(depth - 1, -1, -1)}
    last = loads.start([(inverse.at[0 : matrix.shape[0], :], matrix)])
    z = y[...]
    core = at[CORE]
    for n in range(depth - 1, -1, -1):
        info = infos[n]
        for cell, xu, yb, target in info.all_targets():
            for side, ref in ((core, mine[n]), (1 - core, other[n])):
                row = ((yb * 2 + side) * info.pair_x + xu) * info.chunk
                row = pl.multiple_of(row, info.chunk)
                full[n, pl.ds(row, info.chunk), info.lanes(cell)] = ref[target]
        wait(first[n])
        z = z - mm_nt(dense[n], full[n])
    wait(last)
    value = mm_tn(z.astype(BF16), matrix[...]).astype(BF16)
    size = out.shape[-1]
    for n in range(out.shape[0]):
        out[n] = value[:, n * size : (n + 1) * size]


def output_kernel(parts, *refs):
    rows, out = refs[:-1], refs[-1]
    total = parts[0].astype(F32)
    for n in range(1, parts.shape[0]):
        total = total + parts[n].astype(F32)
    begin = total.shape[1]
    out[0:begin, :] = total.T
    for row in rows:
        out[begin : begin + row.shape[0], :] = row[...].astype(F32)
        begin += row.shape[0]


def solve(right_side, inverse_blocks, coupling, update_rows):
    leaves = lax.axis_size("leaf")
    blocks = lax.axis_size("blk")
    depth = leaves.bit_length() - 1
    leaf_id = lax.axis_index("leaf")
    blk_id = lax.axis_index("blk")
    core = leaf_id & 1
    yb = blk_id & 1
    zb = blk_id >> 1
    width = inverse_blocks.shape[-1]
    cases = right_side.shape[-1]
    rhs = right_side[0, 0]
    inverse = inverse_blocks[0, 0]
    couple = coupling[0, 0]
    listed_rows = coupling.shape[-1]
    counts = [width // (blocks << level) for level in range(depth + 1)]
    starts = [sum(counts[:level]) for level in range(depth + 1)]
    infos = [Level(l, leaves, blocks, width, cases) for l in range(1, depth + 1)]
    couple_starts = {}
    cursor = 0
    for level in range(depth):
        for above in range(level + 1, depth + 1):
            couple_starts[level, above] = cursor
            cursor += counts[level]
    pair_bases = []
    cursor = 0
    for level in range(depth + 1):
        pair_bases.append(cursor)
        cursor += (leaves >> level) * (depth - level)

    def own_position(level):
        info = infos[level - 1]
        member = leaf_id & ((1 << level) - 1)
        side = member & (2 * info.pair_x - 1)
        cell = member // (2 * info.pair_x) * info.zbs + zb
        return ((cell * 2 * info.pair_x + side) * 2 + yb) * info.rows

    pair_slot = {}
    pair_rows = []
    for level in range(depth):
        for above in range(level + 1, depth + 1):
            pair_slot[level, above] = SPOT + depth + len(pair_rows)
            node = leaf_id >> level
            pair_rows.append(pair_bases[level] + node * (depth - level) + (above - level - 1))
    at = jnp.stack(
        [core, yb, (leaf_id >> 1) & 1]
        + [own_position(l) for l in range(1, depth + 1)]
        + pair_rows
    ).astype(jnp.int32)

    def swap(value, axis, bit):
        size = leaves if axis == "leaf" else blocks
        return lax.ppermute(value, axis, [(i, i ^ bit) for i in range(size)])

    def cell_columns(rows, level):
        info = infos[level - 1]
        parts = rows.reshape(-1, info.his, 2 * info.pair_x, info.zbs, 2 * info.rows)
        return parts.transpose(0, 1, 3, 2, 4).reshape(-1, width)

    def exchange_outer(value, level):
        if level <= 1:
            return lax.all_to_all(value, "blk", 0, 0, tiled=True)
        return lax.all_to_all(
            value,
            ("leaf", "blk"),
            0,
            0,
            axis_index_groups=infos[level - 1].outer,
            tiled=True,
        )

    def exchange_inner(value, level):
        info = infos[level - 1]
        if info.his == 1:
            return lax.all_to_all(value, "blk", 0, 0, axis_index_groups=info.inner_blk, tiled=True)
        return lax.all_to_all(
            value, ("leaf", "blk"), 0, 0, axis_index_groups=info.inner, tiled=True
        )

    def coupling_block(level, above):
        begin = couple_starts[level, above]
        return couple[begin : begin + counts[level]]

    uppers = range(1, depth + 1)
    dense = {}
    expanded = kernel_call(
        functools.partial(
            expand_kernel,
            1,
            infos,
            [pair_slot[0, above] for above in uppers],
            [couple_starts[0, above] for above in uppers],
        ),
        [shaped((counts[0], width), BF16)] * depth,
        [update_rows, couple],
        scalars=at,
        flops=2 * depth * counts[0] * listed_rows * width,
    )
    for above in uppers:
        dense[0, above] = expanded[above - 1]

    spread = kernel_call(first_kernel, [shaped((blocks, counts[0], cases), BF16)], [rhs])[0]
    full = lax.all_to_all(spread, "blk", 0, 0, tiled=True).reshape(width, cases)
    outs = [shaped((counts[0], cases), F32)]
    for info in infos:
        shape = (info.targets, info.chunk, info.cell_rows)
        outs += [shaped(shape, F32), shaped(shape, BF16)]
    matrix_scratch = pltpu.VMEM((counts[0], width), BF16)
    dense_scratch = pltpu.VMEM((depth, counts[0], width), BF16)
    y0, *base = kernel_call(
        functools.partial(subtree_kernel, infos, starts[1:]),
        outs,
        [full, (inverse, None), rhs] + hbm([dense[0, above] for above in uppers]),
        scalars=at,
        scratch=[
            pltpu.VMEM((cases, width), F32),
            matrix_scratch,
            dense_scratch,
            pltpu.SemaphoreType.DMA((1 + depth,)),
        ],
        flops=2 * (1 + depth) * counts[0] * width * cases,
    )
    received = []
    for level in uppers:
        received.append(swap(base[2 * level - 1], "leaf", 1))

    def pieces_of(value, level):
        pieces = [value]
        if infos[level - 1].pair_x == 2:
            pieces += [swap(piece, "leaf", 2) for piece in pieces]
        pieces += [swap(piece, "blk", 1) for piece in pieces]
        pieces += [swap(piece, "leaf", 1) for piece in pieces]
        return pieces

    inverse_pieces = {}
    for level in uppers:
        rows = inverse[starts[level] : starts[level] + counts[level]]
        if not infos[level - 1].direct:
            rows = cell_columns(rows, level)
        inverse_pieces[level] = pieces_of(rows, level)
        for above in range(level + 1, depth + 1):
            pieces = pieces_of(coupling_block(level, above), level)
            rows = len(pieces) * counts[level]
            dense[level, above] = kernel_call(
                functools.partial(
                    expand_kernel,
                    len(pieces),
                    [infos[above - 1]],
                    [pair_slot[level, above]],
                    None,
                ),
                [shaped((rows, width), BF16)],
                [update_rows] + pieces,
                scalars=at,
                flops=2 * rows * listed_rows * width,
            )[0]

    def sum_spread(parts, copies):
        return kernel_call(
            sum_spread_kernel, [shaped((copies,) + parts.shape[1:], BF16)], [parts]
        )[0]

    def cell_scratch(info):
        return pltpu.VMEM((info.cell_rows, width), BF16)

    ys = {}
    parts = (base[0] + received[0].astype(F32)).astype(BF16)
    for level in uppers:
        info = infos[level - 1]
        parts = exchange_outer(parts, level)
        gathered = exchange_inner(sum_spread(parts, info.cells), level)
        size = info.cell_rows * width * info.chunk
        count = 4 * info.pair_x
        if level == depth:
            parts = kernel_call(
                functools.partial(top_kernel, info),
                [shaped((info.cells, info.chunk, info.cell_rows), BF16)],
                [gathered] + hbm(inverse_pieces[level]),
                scratch=[cell_scratch(info), pltpu.SemaphoreType.DMA((count,))],
                flops=4 * size,
            )[0]
            break
        above = infos[level]
        ys[level], parts = kernel_call(
            functools.partial(forward_kernel, infos, level),
            [
                shaped((info.cell_rows, info.chunk), F32),
                shaped((above.targets, above.chunk, above.cell_rows), BF16),
            ],
            [gathered, base[2 * level], received[level]]
            + hbm(inverse_pieces[level])
            + [ys[j] for j in range(1, level)]
            + hbm([dense[j, level + 1] for j in range(1, level + 1)]),
            scalars=at,
            scratch=[
                pltpu.VMEM((above.chunk * above.pair_x, width), F32),
                cell_scratch(info),
                pltpu.SemaphoreType.DMA((count + level,)),
            ]
            + [cell_scratch(infos[j - 1]) for j in range(1, level + 1)],
            flops=4 * size,
        )

    solved = {}
    swapped = {}
    for level in range(depth, 0, -1):
        info = infos[level - 1]
        if level < depth:
            higher = range(level + 1, depth + 1)
            count = 4 * info.pair_x
            parts = kernel_call(
                functools.partial(backward_kernel, infos, level),
                [shaped((info.cells, info.chunk, info.cell_rows), BF16)],
                [ys[level]]
                + hbm(inverse_pieces[level])
                + [solved[above] for above in higher]
                + hbm([dense[level, above] for above in higher]),
                scalars=at,
                scratch=[cell_scratch(info), pltpu.SemaphoreType.DMA((count + len(higher),))]
                + [cell_scratch(info)] * len(higher),
                flops=4 * info.cell_rows * width * info.chunk,
            )[0]
        parts = exchange_inner(parts, level)
        solved[level] = exchange_outer(sum_spread(parts, info.targets), level)
        swapped[level] = swap(solved[level], "leaf", 1)

    part = kernel_call(
        functools.partial(last_kernel, infos),
        [shaped((blocks, cases, counts[0]), BF16)],
        [y0, (inverse, None)]
        + hbm([dense[0, above] for above in uppers])
        + [solved[above] for above in uppers]
        + [swapped[above] for above in uppers],
        scalars=at,
        scratch=[
            pltpu.VMEM((depth, cases, width), BF16),
            matrix_scratch,
            dense_scratch,
            pltpu.SemaphoreType.DMA((1 + depth,)),
        ],
        flops=2 * (1 + depth) * counts[0] * width * cases,
    )[0]
    parts = lax.all_to_all(part, "blk", 0, 0, tiled=True)

    outputs = []
    for level in uppers:
        info = infos[level - 1]
        member = leaf_id & ((1 << level) - 1)
        side = member & (2 * info.pair_x - 1)
        hi = member // (2 * info.pair_x)
        offset = (side * 2 + yb) * info.rows

        def own(value):
            shape = (info.his, info.pair_x, info.zbs, 2, info.chunk, info.cell_rows)
            sizes = (1, info.pair_x, 1, 2, info.chunk, info.rows)
            taken = lax.dynamic_slice(value.reshape(shape), (hi, 0, zb, 0, 0, offset), sizes)
            return taken[0, :, 0].transpose(1, 0, 2, 3)

        mine, other = own(solved[level]), own(swapped[level])
        rows = jnp.where(
            core == 0, jnp.stack([mine, other], 1), jnp.stack([other, mine], 1)
        )
        outputs.append(rows.reshape(cases, info.rows).T)
    out = kernel_call(output_kernel, [shaped((sum(counts), cases), F32)], [parts] + outputs)[0]
    return out[None, None]


def solution(mesh):
    spec = P("leaf", "blk", None, None)
    return jax.shard_map(
        solve, mesh=mesh, in_specs=(spec, spec, spec, P()), out_specs=spec, check_vma=False
    )
```

time: 191 us -> 176 us (0.921)
  local copies, waits for them, and re-layouts: 15.5 us -> 4.23 us
  waiting for transfers between devices: 57.8 us -> 64.2 us
  Pallas kernels: 39.3 us -> 33.6 us
  other arithmetic: 4.98 us -> 1.84 us
  blocking collectives: 32.3 us -> 30.2 us
    all_to_all x2, waiting for transfers between devices: 8.14 us -> 16.8 us  [exchange_outer(): return lax.all_to_all(value, 'blk', 0, 0, tiled=True)]
    ppermute x17, waiting for transfers between devices: 27.6 us -> 20.1 us  [swap(): return lax.ppermute(value, axis, [(i, i ^ bit) for i in range(size)])]
    pallas_call x11 -> x13, Pallas kernels: 39.3 us -> 33.6 us  [kernel_call(): pl.pallas_call(body, out_shape=[pltpu.HBM(o.shape, o.dtype) for o in outs...]
    another operation x4 -> x3, local copies, waits for them, and re-layouts: 3.06 us -> 0.12 us  [solve(): jnp.stack([mine, other], 1)]
    all_to_all x1, waiting for transfers between devices: 11.7 us -> 14.6 us  [solve(): parts = lax.all_to_all(part, 'blk', 0, 0, tiled=True)]
    slice x2 -> x1, local copies, waits for them, and re-layouts: 2.71 us -> 0.02 us  [coupling_block(): return couple[begin:begin + counts[level]]]
    unnamed x42 -> x32, local copies, waits for them, and re-layouts: 4.32 us -> 1.76 us
    all_to_all x1, waiting for transfers between devices: 4.71 us -> 7.15 us  [solve(): full = lax.all_to_all(spread, 'blk', 0, 0, tiled=True).reshape(width, cases)]
  transfers between devices with their start and end apart: 24 -> 24, of which waited for: 9 -> 9; matrix products, arithmetic and copies ran while one was open for 7% -> 2% of each run, Pallas kernels for 11% -> 10%
where the time goes in v1:
time: 176 us; the launch traced here: 175 us
  waiting for transfers between devices  64.2 us (36%)
  starting transfers between devices  40.4 us (23%)
  Pallas kernels  33.6 us (19%)
  blocking collectives  30.2 us (17%)
  local copies, waits for them, and re-layouts  4.23 us (2%)
  other arithmetic  1.84 us (1%)
    pallas_call x13, Pallas kernels, kernel_call(): pl.pallas_call(body, out_shape=[pltpu.HBM(o.shape, o.dtype) for o in outs...  33.6 us
    ppermute x17, waiting for transfers between devices, swap(): return lax.ppermute(value, axis, [(i, i ^ bit) for i in range(size)])  20.1 us
    all_to_all x2, blocking collectives, exchange_inner(): lax.all_to_all(value, 'blk', 0, 0, axis_index_groups=info.inner_blk, tile...  18.2 us
    all_to_all x2, waiting for transfers between devices, exchange_outer(): return lax.all_to_all(value, 'blk', 0, 0, tiled=True)  16.8 us
    all_to_all x1, waiting for transfers between devices, solve(): parts = lax.all_to_all(part, 'blk', 0, 0, tiled=True)  14.6 us
    all_to_all x1, blocking collectives, exchange_outer(): lax.all_to_all(value, ('leaf', 'blk'), 0, 0, axis_index_groups=infos[leve...  12 us
    all_to_all x2, starting transfers between devices, exchange_outer(): return lax.all_to_all(value, 'blk', 0, 0, tiled=True)  8.21 us
    all_to_all x2, starting transfers between devices, exchange_inner(): lax.all_to_all(value, 'blk', 0, 0, axis_index_groups=info.inner_blk, tile...  7.86 us
  transfers between devices with their start and end apart: 24, of which 9 were waited for; matrix products, arithmetic and copies ran while one was open for 2% of the time, Pallas kernels for 10%

profile of v1, /device:TPU:0, one launch (start us, length us, event | category | flops | bytes accessed | tf_op | source)
XLA Modules:
  0.0 174.9 jit_solution(1060834156140031220)
XLA Ops:
  1.8 7.3 %all-to-all-start = ((bf16[8,256,128]{2,1,0:T(8,128)(2,1)}), bf16[8,256,128]{2,1,0:T(8,128)(2,1)S(1)}, u32[]{:S(2)}, u32[]{:S(2)}) async-start(bf16[8,256,128]{2,1,0:T(8,128)(2,1)} %shard_map.46), calls=%async_computation | async-start | bytes 1048576 | tf_op jit(solution)/shard_map/all_to_all | solution.py:473
  9.1 1.1 slice_bitcast_fusion.refs_0_
  10.2 2.1 %collective-permute-start.2 = (bf16[128,2048]{1,0:T(8,128)(2,1)S(1)}, bf16[128,2048]{1,0:T(8,128)(2,1)}, u32[]{:S(2)}, u32[]{:S(2)}) collective-permute-start(bf16[128,2048]{1,0:T(8,128)(2,1)S(1)} %slice_bitcast_fusion.refs_0_), channel_id=1, source_target_pairs={{0,1},{1,0},{2,3},{3,2},{4,5},{5,4},{6,7},{7,6},{8,9},{9,8},{10,11... | collective-permute-start | bytes 1572872 | tf_op jit(solution)/shard_map/ppermute | solution.py:423
  12.5 3.9 %shard_map.47 = (bf16[256,2048]{1,0:T(8,128)(2,1)}, bf16[256,2048]{1,0:T(8,128)(2,1)}) custom-call(s32[8]{0:T(128)S(1)} %stack.59.at, s32[10,1024]{1,0:T(8,128)S(1)} %copy-done.6, bf16[640,1024]{1,0:T(8,128)(2,1)S(1)} %bitcast.52), custom_call_target="tpu_custom_call" | custom-call | flops 2147483648 | bytes 3448832 | tf_op jit(solution)/shard_map/pallas_call | solution.py:46
  16.4 7.1 %all-to-all-done = bf16[8,256,128]{2,1,0:T(8,128)(2,1)S(1)} async-done(((bf16[8,256,128]{2,1,0:T(8,128)(2,1)}), bf16[8,256,128]{2,1,0:T(8,128)(2,1)S(1)}, u32[]{:S(2)}, u32[]{:S(2)}) %all-to-all-start) | async-done | bytes 524320 | tf_op jit(solution)/shard_map/all_to_all | solution.py:473
  23.6 3.9 %shard_map.48 = (f32[256,128]{1,0:T(8,128)}, f32[8,32,512]{2,1,0:T(8,128)}, bf16[8,32,512]{2,1,0:T(8,128)(2,1)}, f32[16,16,512]{2,1,0:T(8,128)}, bf16[16,16,512]{2,1,0:T(8,128)(2,1)}) custom-call(s32[8]{0:T(128)S(1)} %stack.59.at, bf16[2048,128]{1,0:T(8,128)(2,1)S(1)} %bitcast.44, bf16[448,2048]{1,0:T(8,128)(2,1)} %bitcast.53, f32[448,128]{1,0:T(8,128)S(1)} %bitcast.47, ...), custom_call_target="tpu_custom_call" | custom-call | flops 402653184 | bytes 6389760 | tf_op jit(solution)/shard_map/pallas_call | solution.py:46
  28.1 6.1 %collective-permute-done.5.refs_1_ = bf16[128,1024]{1,0:T(8,128)(2,1)S(1)} collective-permute-done((bf16[128,1024]{1,0:T(8,128)(2,1)S(1)}, bf16[128,1024]{1,0:T(8,128)(2,1)S(1)}, u32[]{:S(2)}, u32[]{:S(2)}) %collective-permute-start.5) | collective-permute-done | bytes 262176 | tf_op jit(solution)/shard_map/ppermute | solution.py:423
  34.8 1.8 %add_convert_fusion = bf16[8,32,512]{2,1,0:T(8,128)(2,1)} fusion(f32[8,32,512]{2,1,0:T(8,128)} %get-tuple-element.17, bf16[8,32,512]{2,1,0:T(8,128)(2,1)S(1)} %collective-permute-done), kind=kLoop, calls=%fused_computation.1 | loop fusion | flops 393216 | bytes 1048576 | tf_op jit(solution)/shard_map/convert_element_type | solution.py:537
  36.6 4.6 %all-to-all-start.1 = ((bf16[8,32,512]{2,1,0:T(8,128)(2,1)}), bf16[8,32,512]{2,1,0:T(8,128)(2,1)S(1)}, u32[]{:S(2)}, u32[]{:S(2)}) async-start(bf16[8,32,512]{2,1,0:T(8,128)(2,1)} %add_convert_fusion), calls=%async_computation.1 | async-start | bytes 524288 | tf_op jit(solution)/shard_map/all_to_all | solution.py:432
  41.2 1.0 slice_bitcast_fusion.1.refs_0_
  42.2 8.5 %all-to-all-done.1.parts = bf16[8,32,512]{2,1,0:T(8,128)(2,1)S(1)} async-done(((bf16[8,32,512]{2,1,0:T(8,128)(2,1)}), bf16[8,32,512]{2,1,0:T(8,128)(2,1)S(1)}, u32[]{:S(2)}, u32[]{:S(2)}) %all-to-all-start.1) | async-done | bytes 262176 | tf_op jit(solution)/shard_map/all_to_all | solution.py:432
  51.4 3.3 %all-to-all-start.2 = ((bf16[4,32,512]{2,1,0:T(8,128)(2,1)}), bf16[4,32,512]{2,1,0:T(8,128)(2,1)S(1)}, u32[]{:S(2)}, u32[]{:S(2)}) async-start(bf16[4,32,512]{2,1,0:T(8,128)(2,1)} %shard_map.49), calls=%async_computation.2 | async-start | bytes 262144 | tf_op jit(solution)/shard_map/all_to_all | solution.py:445
  54.8 1.6 collective-permute-start.8
  56.3 4.3 %shard_map.50.refs_4_.refs_5_ = bf16[512,2048]{1,0:T(8,128)(2,1)} custom-call(s32[8]{0:T(128)S(1)} %stack.59.at, s32[10,1024]{1,0:T(8,128)S(1)} %copy-done.6, bf16[128,1024]{1,0:T(8,128)(2,1)S(1)} %slice_bitcast_fusion.2.refs_0_, bf16[128,1024]{1,0:T(8,128)(2,1)S(1)} %collective-permute-done.5.refs_1_, bf16[128,1024]{1,0:T(8,128)(2,1)S(1)} %collective-permute-done.6.refs_2_, ...), custom_call_target="tpu_custom_call" | custom-call | flops 2147483648 | bytes 3186688 | tf_op jit(solution)/shard_map/pallas_call | solution.py:46
  61.4 4.4 %shard_map.51 = (f32[512,32]{1,0:T(8,128)}, bf16[16,16,512]{2,1,0:T(8,128)(2,1)}) custom-call(s32[8]{0:T(128)S(1)} %stack.59.at, bf16[4,32,512]{2,1,0:T(8,128)(2,1)S(1)} %all-to-all-done.2.gathered, f32[16,16,512]{2,1,0:T(8,128)S(1)} %copy-done.2, bf16[16,16,512]{2,1,0:T(8,128)(2,1)S(1)} %collective-permute-done.1.received, bf16[128,2048]{1,0:T(8,128)(2,1)} %copy-done.7, ...), custom_call_target="tpu_custom_call" | custom-call | flops 134217728 | bytes 5439488 | tf_op jit(solution)/shard_map/pallas_call | solution.py:46
  65.9 6.0 %all-to-all-start.3 = ((bf16[16,16,512]{2,1,0:T(8,128)(2,1)}), bf16[16,16,512]{2,1,0:T(8,128)(2,1)S(1)}, u32[]{:S(2)}, u32[]{:S(2)}) async-start(bf16[16,16,512]{2,1,0:T(8,128)(2,1)} %get-tuple-element.22), calls=%async_computation.3 | async-start | bytes 524288 | tf_op jit(solution)/shard_map/all_to_all | solution.py:433
  71.8 2.0 %collective-permute-start.9 = (bf16[64,2048]{1,0:T(8,128)(2,1)S(1)}, bf16[64,2048]{1,0:T(8,128)(2,1)S(1)}, u32[]{:S(2)}, u32[]{:S(2)}) collective-permute-start(bf16[64,2048]{1,0:T(8,128)(2,1)S(1)} %slice_bitcast_fusion.1.refs_0_), channel_id=1, source_target_pairs={{0,1},{1,0},{2,3},{3,2},{4,5},{5,4},{6,7},{7,6},{8,9},{9,8},{10,11... | collective-permute-start | bytes 786440 | tf_op jit(solution)/shard_map/ppermute | solution.py:423
  74.5 9.0 %collective-permute-done.9.refs_2_ = bf16[64,2048]{1,0:T(8,128)(2,1)S(1)} collective-permute-done((bf16[64,2048]{1,0:T(8,128)(2,1)S(1)}, bf16[64,2048]{1,0:T(8,128)(2,1)S(1)}, u32[]{:S(2)}, u32[]{:S(2)}) %collective-permute-start.9) | collective-permute-done | bytes 262176 | tf_op jit(solution)/shard_map/ppermute | solution.py:423
  83.4 3.5 %collective-permute-done.10.refs_3_ = bf16[64,2048]{1,0:T(8,128)(2,1)S(1)} collective-permute-done((bf16[64,2048]{1,0:T(8,128)(2,1)}, bf16[64,2048]{1,0:T(8,128)(2,1)S(1)}, u32[]{:S(2)}, u32[]{:S(2)}) %collective-permute-start.10) | collective-permute-done | bytes 262176 | tf_op jit(solution)/shard_map/ppermute | solution.py:423
  87.7 4.5 %all-to-all-start.4 = ((bf16[4,16,512]{2,1,0:T(8,128)(2,1)}), bf16[4,16,512]{2,1,0:T(8,128)(2,1)S(1)}, u32[]{:S(2)}, u32[]{:S(2)}) async-start(bf16[4,16,512]{2,1,0:T(8,128)(2,1)} %shard_map.52), calls=%async_computation.4 | async-start | bytes 131072 | tf_op jit(solution)/shard_map/all_to_all | solution.py:445
  92.2 5.7 %all-to-all-done.4.gathered = bf16[4,16,512]{2,1,0:T(8,128)(2,1)S(1)} async-done(((bf16[4,16,512]{2,1,0:T(8,128)(2,1)}), bf16[4,16,512]{2,1,0:T(8,128)(2,1)S(1)}, u32[]{:S(2)}, u32[]{:S(2)}) %all-to-all-start.4) | async-done | bytes 65568 | tf_op jit(solution)/shard_map/all_to_all | solution.py:445
  98.0 3.8 %shard_map.53 = bf16[4,16,512]{2,1,0:T(8,128)(2,1)} custom-call(bf16[4,16,512]{2,1,0:T(8,128)(2,1)S(1)} %all-to-all-done.4.gathered, bf16[64,2048]{1,0:T(8,128)(2,1)} %copy-done.9, bf16[64,2048]{1,0:T(8,128)(2,1)} %collective-permute-done.8.refs_1_, bf16[64,2048]{1,0:T(8,128)(2,1)} %copy-done.10, bf16[64,2048]{1,0:T(8,128)(2,1)} %copy-done.11, ...), custom_call_target="tpu_custom_call" | custom-call | flops 67108864 | bytes 2228224 | tf_op jit(solution)/shard_map/pallas_call | solution.py:46
  101.7 9.0 %all_to_all.50.parts = bf16[4,16,512]{2,1,0:T(8,128)(2,1)S(1)} all-to-all(bf16[4,16,512]{2,1,0:T(8,128)(2,1)} %shard_map.53), channel_id=1, replica_groups={{0,2,4,6},{1,3,5,7},{8,10,12,14},{9,11,13,15},{16,18,20,22},{17,19,21,2..., dimensions={0} | all-to-all | bytes 131072 | tf_op jit(solution)/shard_map/all_to_all | solution.py:445
  111.5 12.0 %all_to_all.51.refs_4_.refs_3_ = bf16[16,16,512]{2,1,0:T(8,128)(2,1)S(1)} all-to-all(bf16[16,16,512]{2,1,0:T(8,128)(2,1)} %shard_map.54), channel_id=1, replica_groups={{0,1,2,3,4,5,6,7,16,17,18,19,20,21,22,23},{8,9,10,11,12,13,14,15,24,25,..., dimensions={0} | all-to-all | bytes 524288 | tf_op jit(solution)/shard_map/all_to_all | solution.py:433
  123.5 4.4 %shard_map.55 = bf16[4,32,512]{2,1,0:T(8,128)(2,1)} custom-call(s32[8]{0:T(128)S(1)} %stack.59.at, f32[512,32]{1,0:T(8,128)S(1)} %copy-done.3, bf16[128,2048]{1,0:T(8,128)(2,1)} %copy-done.7, bf16[128,2048]{1,0:T(8,128)(2,1)} %collective-permute-done.2.refs_1_, bf16[128,2048]{1,0:T(8,128)(2,1)} %copy-done.8, ...), custom_call_target="tpu_custom_call" | custom-call | flops 134217728 | bytes 4653056 | tf_op jit(solution)/shard_map/pallas_call | solution.py:46
  128.0 9.2 %all_to_all.52.parts = bf16[4,32,512]{2,1,0:T(8,128)(2,1)S(1)} all-to-all(bf16[4,32,512]{2,1,0:T(8,128)(2,1)} %shard_map.55), channel_id=1, replica_groups={{0,2,4,6},{1,3,5,7},{8,10,12,14},{9,11,13,15},{16,18,20,22},{17,19,21,2..., dimensions={0} | all-to-all | bytes 262144 | tf_op jit(solution)/shard_map/all_to_all | solution.py:445
  137.9 3.6 %all-to-all-start.8 = ((bf16[8,32,512]{2,1,0:T(8,128)(2,1)}), bf16[8,32,512]{2,1,0:T(8,128)(2,1)S(1)}, u32[]{:S(2)}, u32[]{:S(2)}) async-start(bf16[8,32,512]{2,1,0:T(8,128)(2,1)} %shard_map.56), calls=%async_computation.8 | async-start | bytes 524288 | tf_op jit(solution)/shard_map/all_to_all | solution.py:432
  141.5 8.2 %all-to-all-done.8.refs_2_ = bf16[8,32,512]{2,1,0:T(8,128)(2,1)S(1)} async-done(((bf16[8,32,512]{2,1,0:T(8,128)(2,1)}), bf16[8,32,512]{2,1,0:T(8,128)(2,1)S(1)}, u32[]{:S(2)}, u32[]{:S(2)}) %all-to-all-start.8) | async-done | bytes 262176 | tf_op jit(solution)/shard_map/all_to_all | solution.py:432
  149.7 1.5 collective-permute-done.15.refs_4_
  151.3 4.3 %shard_map.57 = bf16[8,128,256]{2,1,0:T(8,128)(2,1)} custom-call(s32[8]{0:T(128)S(1)} %stack.59.at, f32[256,128]{1,0:T(8,128)S(1)} %copy-done.4, bf16[448,2048]{1,0:T(8,128)(2,1)} %bitcast.54, bf16[256,2048]{1,0:T(8,128)(2,1)} %get-tuple-element.14.refs_0_, bf16[256,2048]{1,0:T(8,128)(2,1)} %get-tuple-element.15.refs_1_, ...), custom_call_target="tpu_custom_call" | custom-call | flops 402653184 | bytes 5636096 | tf_op jit(solution)/shard_map/pallas_call | solution.py:46
  155.6 3.5 %all-to-all-start.9 = ((bf16[8,128,256]{2,1,0:T(8,128)(2,1)}), bf16[8,128,256]{2,1,0:T(8,128)(2,1)S(1)}, u32[]{:S(2)}, u32[]{:S(2)}) async-start(bf16[8,128,256]{2,1,0:T(8,128)(2,1)} %shard_map.57), calls=%async_computation.9 | async-start | bytes 1048576 | tf_op jit(solution)/shard_map/all_to_all | solution.py:613
  159.5 14.6 %all-to-all-done.9.parts = bf16[8,128,256]{2,1,0:T(8,128)(2,1)S(1)} async-done(((bf16[8,128,256]{2,1,0:T(8,128)(2,1)}), bf16[8,128,256]{2,1,0:T(8,128)(2,1)S(1)}, u32[]{:S(2)}, u32[]{:S(2)}) %all-to-all-start.9) | async-done | bytes 524320 | tf_op jit(solution)/shard_map/all_to_all | solution.py:613
  (77 shorter events, 8.8 us)
Async XLA Ops:
  0.9 11.3 %copy-start.5 = (bf16[1,1,640,1024]{3,2,1,0:T(8,128)(2,1)S(1)}, bf16[1,1,640,1024]{3,2,1,0:T(8,128)(2,1)}, u32[]{:S(2)}) copy-start(bf16[1,1,640,1024]{3,2,1,0:T(8,128)(2,1)} %param.6) | copy-start | bytes 3932164
  0.9 11.6 %copy-start.6 = (s32[10,1024]{1,0:T(8,128)S(1)}, s32[10,1024]{1,0:T(8,128)}, u32[]{:S(2)}) copy-start(s32[10,1024]{1,0:T(8,128)} %lists.3) | copy-start | bytes 122884
  1.8 21.8 %all-to-all-start = ((bf16[8,256,128]{2,1,0:T(8,128)(2,1)}), bf16[8,256,128]{2,1,0:T(8,128)(2,1)S(1)}, u32[]{:S(2)}, u32[]{:S(2)}) async-start(bf16[8,256,128]{2,1,0:T(8,128)(2,1)} %shard_map.46), calls=%async_computation | async-start | bytes 1048576 | tf_op jit(solution)/shard_map/all_to_all | solution.py:473
  10.2 17.4 %copy-start.7 = (bf16[128,2048]{1,0:T(8,128)(2,1)}, bf16[128,2048]{1,0:T(8,128)(2,1)S(1)}, u32[]{:S(2)}) copy-start(bf16[128,2048]{1,0:T(8,128)(2,1)S(1)} %slice_bitcast_fusion.refs_0_) | copy-start | bytes 1572868
  10.2 24.0 %collective-permute-start.2 = (bf16[128,2048]{1,0:T(8,128)(2,1)S(1)}, bf16[128,2048]{1,0:T(8,128)(2,1)}, u32[]{:S(2)}, u32[]{:S(2)}) collective-permute-start(bf16[128,2048]{1,0:T(8,128)(2,1)S(1)} %slice_bitcast_fusion.refs_0_), channel_id=1, source_target_pairs={{0,1},{1,0},{2,3},{3,2},{4,5},{5,4},{6,7},{7,6},{8,9},{9,8},{10,11... | collective-permute-start | bytes 1572872 | tf_op jit(solution)/shard_map/ppermute | solution.py:423
  12.3 21.9 %collective-permute-start.5 = (bf16[128,1024]{1,0:T(8,128)(2,1)S(1)}, bf16[128,1024]{1,0:T(8,128)(2,1)S(1)}, u32[]{:S(2)}, u32[]{:S(2)}) collective-permute-start(bf16[128,1024]{1,0:T(8,128)(2,1)S(1)} %slice_bitcast_fusion.2.refs_0_), channel_id=1, source_target_pairs={{0,1},{1,0},{2,3},{3,2},{4,5},{5,4},{6,7},{7,6},{8,9},{9,8},{10,11... | collective-permute-start | bytes 786440 | tf_op jit(solution)/shard_map/ppermute | solution.py:423
  12.5 11.1 %copy-start.1 = (f32[1,1,448,128]{3,2,1,0:T(8,128)S(1)}, f32[1,1,448,128]{3,2,1,0:T(8,128)}, u32[]{:S(2)}) copy-start(f32[1,1,448,128]{3,2,1,0:T(8,128)} %param.4) | copy-start | bytes 688132
  27.5 7.2 %collective-permute-start = (bf16[8,32,512]{2,1,0:T(8,128)(2,1)}, bf16[8,32,512]{2,1,0:T(8,128)(2,1)S(1)}, u32[]{:S(2)}, u32[]{:S(2)}) collective-permute-start(bf16[8,32,512]{2,1,0:T(8,128)(2,1)} %get-tuple-element.18), channel_id=1, source_target_pairs={{0,8},{8,0},{16,24},{24,16},{1,9},{9,1},{17,25},{25,17},{2,10},{10... | collective-permute-start | bytes 786440 | tf_op jit(solution)/shard_map/ppermute | solution.py:423
  27.5 33.1 %collective-permute-start.3 = (bf16[128,2048]{1,0:T(8,128)(2,1)S(1)}, bf16[128,2048]{1,0:T(8,128)(2,1)S(1)}, u32[]{:S(2)}, u32[]{:S(2)}) collective-permute-start(bf16[128,2048]{1,0:T(8,128)(2,1)S(1)} %slice_bitcast_fusion.refs_0_), channel_id=1, source_target_pairs={{0,8},{8,0},{16,24},{24,16},{1,9},{9,1},{17,25},{25,17},{2,10},{10... | collective-permute-start | bytes 1572872 | tf_op jit(solution)/shard_map/ppermute | solution.py:423
  28.0 26.7 %collective-permute-start.6 = (bf16[128,1024]{1,0:T(8,128)(2,1)S(1)}, bf16[128,1024]{1,0:T(8,128)(2,1)S(1)}, u32[]{:S(2)}, u32[]{:S(2)}) collective-permute-start(bf16[128,1024]{1,0:T(8,128)(2,1)S(1)} %slice_bitcast_fusion.2.refs_0_), channel_id=1, source_target_pairs={{0,8},{8,0},{16,24},{24,16},{1,9},{9,1},{17,25},{25,17},{2,10},{10... | collective-permute-start | bytes 786440 | tf_op jit(solution)/shard_map/ppermute | solution.py:423
  34.2 22.2 %collective-permute-start.7 = (bf16[128,1024]{1,0:T(8,128)(2,1)S(1)}, bf16[128,1024]{1,0:T(8,128)(2,1)S(1)}, u32[]{:S(2)}, u32[]{:S(2)}) collective-permute-start(bf16[128,1024]{1,0:T(8,128)(2,1)S(1)} %collective-permute-done.5.refs_1_), channel_id=1, source_target_pairs={{0,8},{8,0},{16,24},{24,16},{1,9},{9,1},{17,25},{25,17},{2,10},{10... | collective-permute-start | bytes 786440 | tf_op jit(solution)/shard_map/ppermute | solution.py:423
  34.2 26.4 %collective-permute-start.4 = (bf16[128,2048]{1,0:T(8,128)(2,1)}, bf16[128,2048]{1,0:T(8,128)(2,1)}, u32[]{:S(2)}, u32[]{:S(2)}) collective-permute-start(bf16[128,2048]{1,0:T(8,128)(2,1)} %collective-permute-done.2.refs_1_), channel_id=1, source_target_pairs={{0,8},{8,0},{16,24},{24,16},{1,9},{9,1},{17,25},{25,17},{2,10},{10... | collective-permute-start | bytes 1572872 | tf_op jit(solution)/shard_map/ppermute | solution.py:423
  34.7 25.9 %collective-permute-start.1 = (bf16[16,16,512]{2,1,0:T(8,128)(2,1)}, bf16[16,16,512]{2,1,0:T(8,128)(2,1)S(1)}, u32[]{:S(2)}, u32[]{:S(2)}) collective-permute-start(bf16[16,16,512]{2,1,0:T(8,128)(2,1)} %get-tuple-element.20), channel_id=1, source_target_pairs={{0,8},{8,0},{16,24},{24,16},{1,9},{9,1},{17,25},{25,17},{2,10},{10... | collective-permute-start | bytes 786440 | tf_op jit(solution)/shard_map/ppermute | solution.py:423
  36.6 14.1 %all-to-all-start.1 = ((bf16[8,32,512]{2,1,0:T(8,128)(2,1)}), bf16[8,32,512]{2,1,0:T(8,128)(2,1)S(1)}, u32[]{:S(2)}, u32[]{:S(2)}) async-start(bf16[8,32,512]{2,1,0:T(8,128)(2,1)} %add_convert_fusion), calls=%async_computation.1 | async-start | bytes 524288 | tf_op jit(solution)/shard_map/all_to_all | solution.py:432
  42.2 31.8 %copy-start.9 = (bf16[64,2048]{1,0:T(8,128)(2,1)}, bf16[64,2048]{1,0:T(8,128)(2,1)S(1)}, u32[]{:S(2)}) copy-start(bf16[64,2048]{1,0:T(8,128)(2,1)S(1)} %slice_bitcast_fusion.1.refs_0_) | copy-start | bytes 786436
  51.4 9.2 %all-to-all-start.2 = ((bf16[4,32,512]{2,1,0:T(8,128)(2,1)}), bf16[4,32,512]{2,1,0:T(8,128)(2,1)S(1)}, u32[]{:S(2)}, u32[]{:S(2)}) async-start(bf16[4,32,512]{2,1,0:T(8,128)(2,1)} %shard_map.49), calls=%async_computation.2 | async-start | bytes 262144 | tf_op jit(solution)/shard_map/all_to_all | solution.py:445
  54.8 19.1 %collective-permute-start.8 = (bf16[64,2048]{1,0:T(8,128)(2,1)S(1)}, bf16[64,2048]{1,0:T(8,128)(2,1)}, u32[]{:S(2)}, u32[]{:S(2)}) collective-permute-start(bf16[64,2048]{1,0:T(8,128)(2,1)S(1)} %slice_bitcast_fusion.1.refs_0_), channel_id=1, source_target_pairs={{0,16},{8,24},{16,0},{24,8},{1,17},{9,25},{17,1},{25,9},{2,18},{10... | collective-permute-start | bytes 786440 | tf_op jit(solution)/shard_map/ppermute | solution.py:423
  65.9 21.0 %all-to-all-start.3 = ((bf16[16,16,512]{2,1,0:T(8,128)(2,1)}), bf16[16,16,512]{2,1,0:T(8,128)(2,1)S(1)}, u32[]{:S(2)}, u32[]{:S(2)}) async-start(bf16[16,16,512]{2,1,0:T(8,128)(2,1)} %get-tuple-element.22), calls=%async_computation.3 | async-start | bytes 524288 | tf_op jit(solution)/shard_map/all_to_all | solution.py:433
  71.8 51.7 %copy-start.3 = (f32[512,32]{1,0:T(8,128)S(1)}, f32[512,32]{1,0:T(8,128)}, u32[]{:S(2)}) copy-start(f32[512,32]{1,0:T(8,128)} %get-tuple-element.21.y) | copy-start | bytes 196612
  71.8 11.6 %collective-permute-start.9 = (bf16[64,2048]{1,0:T(8,128)(2,1)S(1)}, bf16[64,2048]{1,0:T(8,128)(2,1)S(1)}, u32[]{:S(2)}, u32[]{:S(2)}) collective-permute-start(bf16[64,2048]{1,0:T(8,128)(2,1)S(1)} %slice_bitcast_fusion.1.refs_0_), channel_id=1, source_target_pairs={{0,1},{1,0},{2,3},{3,2},{4,5},{5,4},{6,7},{7,6},{8,9},{9,8},{10,11... | collective-permute-start | bytes 786440 | tf_op jit(solution)/shard_map/ppermute | solution.py:423
  73.8 13.1 %collective-permute-start.10 = (bf16[64,2048]{1,0:T(8,128)(2,1)}, bf16[64,2048]{1,0:T(8,128)(2,1)S(1)}, u32[]{:S(2)}, u32[]{:S(2)}) collective-permute-start(bf16[64,2048]{1,0:T(8,128)(2,1)} %collective-permute-done.8.refs_1_), channel_id=1, source_target_pairs={{0,1},{1,0},{2,3},{3,2},{4,5},{5,4},{6,7},{7,6},{8,9},{9,8},{10,11... | collective-permute-start | bytes 786440 | tf_op jit(solution)/shard_map/ppermute | solution.py:423
  73.9 18.2 %collective-permute-start.11 = (bf16[64,2048]{1,0:T(8,128)(2,1)S(1)}, bf16[64,2048]{1,0:T(8,128)(2,1)S(1)}, u32[]{:S(2)}, u32[]{:S(2)}) collective-permute-start(bf16[64,2048]{1,0:T(8,128)(2,1)S(1)} %slice_bitcast_fusion.1.refs_0_), channel_id=1, source_target_pairs={{0,8},{8,0},{16,24},{24,16},{1,9},{9,1},{17,25},{25,17},{2,10},{10... | collective-permute-start | bytes 786440 | tf_op jit(solution)/shard_map/ppermute | solution.py:423
  73.9 18.2 %collective-permute-start.12 = (bf16[64,2048]{1,0:T(8,128)(2,1)}, bf16[64,2048]{1,0:T(8,128)(2,1)S(1)}, u32[]{:S(2)}, u32[]{:S(2)}) collective-permute-start(bf16[64,2048]{1,0:T(8,128)(2,1)} %collective-permute-done.8.refs_1_), channel_id=1, source_target_pairs={{0,8},{8,0},{16,24},{24,16},{1,9},{9,1},{17,25},{25,17},{2,10},{10... | collective-permute-start | bytes 786440 | tf_op jit(solution)/shard_map/ppermute | solution.py:423
  83.4 14.5 %copy-start.10 = (bf16[64,2048]{1,0:T(8,128)(2,1)}, bf16[64,2048]{1,0:T(8,128)(2,1)S(1)}, u32[]{:S(2)}) copy-start(bf16[64,2048]{1,0:T(8,128)(2,1)S(1)} %collective-permute-done.9.refs_2_) | copy-start | bytes 786436
  83.4 8.8 %collective-permute-start.13 = (bf16[64,2048]{1,0:T(8,128)(2,1)S(1)}, bf16[64,2048]{1,0:T(8,128)(2,1)S(1)}, u32[]{:S(2)}, u32[]{:S(2)}) collective-permute-start(bf16[64,2048]{1,0:T(8,128)(2,1)S(1)} %collective-permute-done.9.refs_2_), channel_id=1, source_target_pairs={{0,8},{8,0},{16,24},{24,16},{1,9},{9,1},{17,25},{25,17},{2,10},{10... | collective-permute-start | bytes 786440 | tf_op jit(solution)/shard_map/ppermute | solution.py:423
  86.9 5.3 %collective-permute-start.14 = (bf16[64,2048]{1,0:T(8,128)(2,1)S(1)}, bf16[64,2048]{1,0:T(8,128)(2,1)S(1)}, u32[]{:S(2)}, u32[]{:S(2)}) collective-permute-start(bf16[64,2048]{1,0:T(8,128)(2,1)S(1)} %collective-permute-done.10.refs_3_), channel_id=1, source_target_pairs={{0,8},{8,0},{16,24},{24,16},{1,9},{9,1},{17,25},{25,17},{2,10},{10... | collective-permute-start | bytes 786440 | tf_op jit(solution)/shard_map/ppermute | solution.py:423
  87.7 10.3 %all-to-all-start.4 = ((bf16[4,16,512]{2,1,0:T(8,128)(2,1)}), bf16[4,16,512]{2,1,0:T(8,128)(2,1)S(1)}, u32[]{:S(2)}, u32[]{:S(2)}) async-start(bf16[4,16,512]{2,1,0:T(8,128)(2,1)} %shard_map.52), calls=%async_computation.4 | async-start | bytes 131072 | tf_op jit(solution)/shard_map/all_to_all | solution.py:445
  123.5 27.8 %copy-start.4 = (f32[256,128]{1,0:T(8,128)S(1)}, f32[256,128]{1,0:T(8,128)}, u32[]{:S(2)}) copy-start(f32[256,128]{1,0:T(8,128)} %get-tuple-element.16.y) | copy-start | bytes 393220
  137.9 11.8 %all-to-all-start.8 = ((bf16[8,32,512]{2,1,0:T(8,128)(2,1)}), bf16[8,32,512]{2,1,0:T(8,128)(2,1)S(1)}, u32[]{:S(2)}, u32[]{:S(2)}) async-start(bf16[8,32,512]{2,1,0:T(8,128)(2,1)} %shard_map.56), calls=%async_computation.8 | async-start | bytes 524288 | tf_op jit(solution)/shard_map/all_to_all | solution.py:432
  141.5 8.2 %collective-permute-start.16 = (bf16[16,16,512]{2,1,0:T(8,128)(2,1)S(1)}, bf16[16,16,512]{2,1,0:T(8,128)(2,1)S(1)}, u32[]{:S(2)}, u32[]{:S(2)}) collective-permute-start(bf16[16,16,512]{2,1,0:T(8,128)(2,1)S(1)} %all_to_all.51.refs_4_.refs_3_), channel_id=1, source_target_pairs={{0,8},{8,0},{16,24},{24,16},{1,9},{9,1},{17,25},{25,17},{2,10},{10... | collective-permute-start | bytes 786440 | tf_op jit(solution)/shard_map/ppermute | solution.py:423
  149.7 1.5 collective-permute-start.15
  155.6 18.5 %all-to-all-start.9 = ((bf16[8,128,256]{2,1,0:T(8,128)(2,1)}), bf16[8,128,256]{2,1,0:T(8,128)(2,1)S(1)}, u32[]{:S(2)}, u32[]{:S(2)}) async-start(bf16[8,128,256]{2,1,0:T(8,128)(2,1)} %shard_map.57), calls=%async_computation.9 | async-start | bytes 1048576 | tf_op jit(solution)/shard_map/all_to_all | solution.py:613
  (8 other events, 42.4 us)

commit v2 on v1

--- a/solution.py
+++ b/solution.py
@@ -28,14 +28,15 @@
     return jax.ShapeDtypeStruct(tuple(shape), dtype)
 
 
-def kernel_call(body, outs, args, scalars=None, scratch=(), flops=0):
+def kernel_call(body, outs, args, scalars=None, scratch=(), flops=0, stay=None):
+    stay = [True] * len(outs) if stay is None else stay
     values = []
     specs = []
     moved = sum(o.size * o.dtype.itemsize for o in outs)
     for arg in args:
-        value, spec = arg if isinstance(arg, tuple) else (arg, pl.BlockSpec(memory_space=pltpu.VMEM))
-        if spec is None:
-            value = pltpu.with_memory_space_constraint(value, pltpu.HBM)
+        value, spec = arg, pl.BlockSpec(memory_space=pltpu.VMEM)
+        if isinstance(arg, tuple):
+            value = pltpu.with_memory_space_constraint(arg[0], pltpu.HBM)
             spec = pl.BlockSpec(memory_space=pltpu.HBM)
         values.append(value)
         specs.append(spec)
@@ -45,7 +46,9 @@
         values = [scalars] + values
     return pl.pallas_call(
         body,
-        out_shape=[pltpu.HBM(o.shape, o.dtype) for o in outs],
+        out_shape=[
+            pltpu.HBM(o.shape, o.dtype) if keep else o for o, keep in zip(outs, stay)
+        ],
         in_specs=specs,
         out_specs=[pl.BlockSpec(memory_space=pltpu.VMEM)] * len(outs),
         scratch_shapes=list(scratch),
@@ -79,6 +82,38 @@
             pairs.append((source, target.at[begin : begin + count, :]))
             begin += count
         return self.start(pairs)
+
+    def groups(self, sources, target, order):
+        rows = target.shape[0] // order
+        if len(sources) == 1:
+            source = sources[0]
+            return [
+                lambda g=g: self.start(
+                    [(source.at[g * rows : (g + 1) * rows, :], target.at[g * rows : (g + 1) * rows, :])]
+                )
+                for g in range(order)
+            ]
+        each = len(sources) // order
+        return [
+            lambda g=g: self.rows(
+                sources[g * each : (g + 1) * each], target.at[g * rows : (g + 1) * rows, :]
+            )
+            for g in range(order)
+        ]
+
+
+GROUPS = 2
+
+
+def group_rows(total):
+    size = total // GROUPS
+    return [slice(g * size, (g + 1) * size) for g in range(GROUPS)]
+
+
+def accumulate(total, left, right):
+    half = right.shape[1] // 2
+    terms = [mm_tn(left, right[:, :half]), mm_tn(left, right[:, half:])]
+    return terms if total is None else [t + term for t, term in zip(total, terms)]
 
 
 def wait(copies):
@@ -200,8 +235,12 @@
     outs = refs[depth : depth + 1 + 2 * depth]
     total, matrix, dense, sems = refs[depth + 1 + 2 * depth :]
     loads = Loads(sems)
-    first = loads.start([(inverse.at[0 : matrix.shape[0], :], matrix)])
-    later = [loads.start([(sources[n], dense.at[n])]) for n in range(depth)]
+    groups = group_rows(matrix.shape[0])
+    first = [start() for start in loads.groups([inverse], matrix, GROUPS)]
+    later = [
+        [start() for start in loads.groups([sources[n]], dense.at[n], GROUPS)]
+        for n in range(depth)
+    ]
     core = at[CORE]
     width = total.shape[-1]
     placed = []
@@ -210,14 +249,21 @@
         lane_ids = lax.broadcasted_iota(jnp.int32, (info.rows, width), 1)
         spots = jnp.where(row_ids == lane_ids, 1.0, 0.0).astype(BF16)
         own = rhs[starts[n] : starts[n] + info.rows, :].astype(BF16)
-        placed.append(mm_tn(own, spots))
-    wait(first)
-    y = mm(matrix[...], full[...])
-    outs[0][...] = y
-    y_round = y.astype(BF16)
+        placed.append(accumulate(None, own, spots))
+    rounded = []
+    for g, rows in enumerate(groups):
+        wait(first[g])
+        y = mm(matrix[rows, :], full[...])
+        outs[0][rows, :] = y
+        rounded.append(y.astype(BF16))
+    half = width // 2
     for n, info in enumerate(infos):
-        wait(later[n])
-        total[...] = placed[n] - mm_tn(y_round, dense[n])
+        term = None
+        for g, rows in enumerate(groups):
+            wait(later[n][g])
+            term = accumulate(term, rounded[g], dense[n, rows, :])
+        total[:, :half] = placed[n][0] - term[0]
+        total[:, half:] = placed[n][1] - term[1]
         mine, other = outs[1 + 2 * n], outs[2 + 2 * n]
         for cell, xu, yb, target in info.all_targets():
             for side, ref in ((core, mine), (1 - core, other)):
@@ -244,8 +290,8 @@
     return jnp.concatenate(blocks, 1)
 
 
-def spread_product(info, z, matrix, out):
-    value = mm_tn(z, matrix[...]).astype(BF16)
+def put_spread(info, halves, out):
+    value = jnp.concatenate(halves, 1).astype(BF16)
     for lane, cell, inside, size in info.natural():
         out[cell, :, inside : inside + size] = value[:, lane : lane + size]
 
@@ -259,17 +305,27 @@
     y_ref, out, total, matrix, sems = refs[count + 2 * k - 1 : count + 2 * k + 4]
     dense = refs[count + 2 * k + 4 :]
     loads = Loads(sems)
-    first = loads.rows(pieces, matrix)
-    later = [loads.start([(source, dense[j])]) for j, source in enumerate(sources)]
+    groups = group_rows(matrix.shape[0])
+    first = [start() for start in loads.groups(pieces, matrix, GROUPS)]
+    later = [
+        [start() for start in loads.groups([source], dense[j], GROUPS)]
+        for j, source in enumerate(sources)
+    ]
     vector = natural_rows(info, gathered)
-    wait(first)
-    y = mm_nt(matrix[...], vector)
-    y_ref[...] = y
+    ys = []
+    for g, rows in enumerate(groups):
+        wait(first[g])
+        y = mm_nt(matrix[rows, :], vector)
+        y_ref[rows, :] = y
+        ys.append(y)
     same = {}
     for j in range(1, k + 1):
-        wait(later[j - 1])
-        value = y if j == k else lower_y[j - 1][...]
-        term = mm_tn(value.astype(BF16), dense[j - 1][...])
+        term = None
+        for g, rows in enumerate(group_rows(dense[j - 1].shape[0])):
+            value = ys[g] if j == k else lower_y[j - 1][rows, :]
+            wait(later[j - 1][g])
+            term = accumulate(term, value.astype(BF16), dense[j - 1][rows, :])
+        term = jnp.concatenate(term, 1)
         same.setdefault(infos[j - 1].pair_x == above.pair_x, []).append(term)
     if False in same:
         total[...] = functools.reduce(jnp.add, same[False])
@@ -280,7 +336,7 @@
         rows = pl.ds(pl.multiple_of(at[XU] * above.chunk, above.chunk), above.chunk)
         total[rows, :] = total[rows, :] + term
     for cell, xu, yb, target in above.all_targets():
-        value = mine[target] + received[target].astype(F32)
+        value = mine[target].astype(F32) + received[target].astype(F32)
         minus = total[xu * above.chunk : (xu + 1) * above.chunk, above.lanes(cell)]
         value = jnp.where(at[YB] == yb, value - minus, value)
         out[target] = value.astype(BF16)
@@ -290,11 +346,14 @@
     count = 4 * info.pair_x
     pieces = refs[:count]
     out, matrix, sems = refs[count:]
-    first = Loads(sems).rows(pieces, matrix)
+    first = [start() for start in Loads(sems).groups(pieces, matrix, GROUPS)]
     vector = natural_rows(info, gathered)
-    wait(first)
-    y = mm_nt(matrix[...], vector)
-    spread_product(info, y.astype(BF16), matrix, out)
+    halves = None
+    for g, rows in enumerate(group_rows(matrix.shape[0])):
+        wait(first[g])
+        y = mm_nt(matrix[rows, :], vector)
+        halves = accumulate(halves, y.astype(BF16), matrix[rows, :])
+    put_spread(info, halves, out)
 
 
 def backward_kernel(infos, k, at, y, *refs):
@@ -308,9 +367,14 @@
     out, matrix, sems = refs[count + 2 * many : count + 2 * many + 3]
     dense = refs[count + 2 * many + 3 :]
     loads = Loads(sems)
-    first = [loads.start([(source, dense[n])]) for n, source in enumerate(sources)]
-    last = loads.rows(pieces, matrix)
-    z = y[...]
+    dense_loads = [loads.groups([source], dense[n], GROUPS) for n, source in enumerate(sources)]
+    matrix_loads = loads.groups(pieces, matrix, GROUPS)
+    first = []
+    last = []
+    for g in range(GROUPS):
+        first.append([start[g]() for start in dense_loads])
+        last.append(matrix_loads[g]())
+    vectors = []
     for n, above in enumerate(uppers):
         parts = []
         for hi in range(above.his):
@@ -323,34 +387,47 @@
                         above.target(hi, xu, zb, 0) + at[YB] for xu in range(above.pair_x)
                     ]
                     parts.append(jnp.concatenate([solved[n][slot] for slot in slots], 0))
-        wait(first[n])
-        z = z - mm_nt(dense[n][...], jnp.concatenate(parts, 1))
-    wait(last)
-    spread_product(info, z.astype(BF16), matrix, out)
-
-
-def last_kernel(infos, at, y, inverse, *refs):
-    depth = len(infos)
-    sources = refs[:depth]
-    mine = refs[depth : 2 * depth]
-    other = refs[2 * depth : 3 * depth]
-    out, full, matrix, dense, sems = refs[3 * depth :]
+        vectors.append(jnp.concatenate(parts, 1))
+    halves = None
+    for g, rows in enumerate(group_rows(matrix.shape[0])):
+        z = y[rows, :]
+        for n in range(many):
+            wait(first[g][n])
+            z = z - mm_nt(dense[n][rows, :], vectors[n])
+        wait(last[g])
+        halves = accumulate(halves, z.astype(BF16), matrix[rows, :])
+    put_spread(info, halves, out)
+
+
+def full_cases(info, core, mine, other, full):
+    for cell, xu, yb, target in info.all_targets():
+        for side, ref in ((core, mine), (1 - core, other)):
+            row = ((yb * 2 + side) * info.pair_x + xu) * info.chunk
+            row = pl.multiple_of(row, info.chunk)
+            full[pl.ds(row, info.chunk), info.lanes(cell)] = ref[target]
+
+
+def subtract_kernel(info, at, y, source, mine, other, out, full, dense, sems):
+    loads = [start() for start in Loads(sems).groups([source], dense, GROUPS)]
+    full_cases(info, at[CORE], mine, other, full)
+    for g, rows in enumerate(group_rows(dense.shape[0])):
+        wait(loads[g])
+        out[rows, :] = y[rows, :] - mm_nt(dense[rows, :], full[...])
+
+
+def last_kernel(info, at, y, source, mine, other, inverse, out, full, dense, matrix, sems):
     loads = Loads(sems)
-    first = {n: loads.start([(sources[n], dense.at[n])]) for n in range(depth - 1, -1, -1)}
-    last = loads.start([(inverse.at[0 : matrix.shape[0], :], matrix)])
-    z = y[...]
-    core = at[CORE]
-    for n in range(depth - 1, -1, -1):
-        info = infos[n]
-        for cell, xu, yb, target in info.all_targets():
-            for side, ref in ((core, mine[n]), (1 - core, other[n])):
-                row = ((yb * 2 + side) * info.pair_x + xu) * info.chunk
-                row = pl.multiple_of(row, info.chunk)
-                full[n, pl.ds(row, info.chunk), info.lanes(cell)] = ref[target]
-        wait(first[n])
-        z = z - mm_nt(dense[n], full[n])
-    wait(last)
-    value = mm_tn(z.astype(BF16), matrix[...]).astype(BF16)
+    dense_loads = loads.groups([source], dense, GROUPS)
+    matrix_loads = loads.groups([inverse], matrix, GROUPS)
+    copies = [(dense_loads[g](), matrix_loads[g]()) for g in range(GROUPS)]
+    full_cases(info, at[CORE], mine, other, full)
+    halves = None
+    for g, rows in enumerate(group_rows(dense.shape[0])):
+        wait(copies[g][0])
+        z = y[rows, :] - mm_nt(dense[rows, :], full[...])
+        wait(copies[g][1])
+        halves = accumulate(halves, z.astype(BF16), matrix[rows, :])
+    value = jnp.concatenate(halves, 1).astype(BF16)
     size = out.shape[-1]
     for n in range(out.shape[0]):
         out[n] = value[:, n * size : (n + 1) * size]
@@ -442,7 +519,9 @@
     def exchange_inner(value, level):
         info = infos[level - 1]
         if info.his == 1:
-            return lax.all_to_all(value, "blk", 0, 0, axis_index_groups=info.inner_blk, tiled=True)
+            return lax.all_to_all(
+                value, "blk", 0, 0, axis_index_groups=info.inner_blk, tiled=True
+            )
         return lax.all_to_all(
             value, ("leaf", "blk"), 0, 0, axis_index_groups=info.inner, tiled=True
         )
@@ -469,14 +548,15 @@
     for above in uppers:
         dense[0, above] = expanded[above - 1]
 
-    spread = kernel_call(first_kernel, [shaped((blocks, counts[0], cases), BF16)], [rhs])[0]
+    spread = kernel_call(
+        first_kernel, [shaped((blocks, counts[0], cases), BF16)], [rhs]
+    )[0]
     full = lax.all_to_all(spread, "blk", 0, 0, tiled=True).reshape(width, cases)
     outs = [shaped((counts[0], cases), F32)]
     for info in infos:
         shape = (info.targets, info.chunk, info.cell_rows)
-        outs += [shaped(shape, F32), shaped(shape, BF16)]
+        outs += [shaped(shape, BF16), shaped(shape, BF16)]
     matrix_scratch = pltpu.VMEM((counts[0], width), BF16)
-    dense_scratch = pltpu.VMEM((depth, counts[0], width), BF16)
     y0, *base = kernel_call(
         functools.partial(subtree_kernel, infos, starts[1:]),
         outs,
@@ -485,10 +565,11 @@
         scratch=[
             pltpu.VMEM((cases, width), F32),
             matrix_scratch,
-            dense_scratch,
-            pltpu.SemaphoreType.DMA((1 + depth,)),
+            pltpu.VMEM((depth, counts[0], width), BF16),
+            pltpu.SemaphoreType.DMA((GROUPS * (1 + depth),)),
         ],
         flops=2 * (1 + depth) * counts[0] * width * cases,
+        stay=[True, False, False] + [True, True] * (depth - 1),
     )
     received = []
     for level in uppers:
@@ -534,7 +615,7 @@
         return pltpu.VMEM((info.cell_rows, width), BF16)
 
     ys = {}
-    parts = (base[0] + received[0].astype(F32)).astype(BF16)
+    parts = (base[0].astype(F32) + received[0].astype(F32)).astype(BF16)
     for level in uppers:
         info = infos[level - 1]
         parts = exchange_outer(parts, level)
@@ -548,6 +629,7 @@
                 [gathered] + hbm(inverse_pieces[level]),
                 scratch=[cell_scratch(info), pltpu.SemaphoreType.DMA((count,))],
                 flops=4 * size,
+                stay=[False],
             )[0]
             break
         above = infos[level]
@@ -565,7 +647,7 @@
             scratch=[
                 pltpu.VMEM((above.chunk * above.pair_x, width), F32),
                 cell_scratch(info),
-                pltpu.SemaphoreType.DMA((count + level,)),
+                pltpu.SemaphoreType.DMA((count + GROUPS * level,)),
             ]
             + [cell_scratch(infos[j - 1]) for j in range(1, level + 1)],
             flops=4 * size,
@@ -573,6 +655,7 @@
 
     solved = {}
     swapped = {}
+    z0 = y0
     for level in range(depth, 0, -1):
         info = infos[level - 1]
         if level < depth:
@@ -586,29 +669,40 @@
                 + [solved[above] for above in higher]
                 + hbm([dense[level, above] for above in higher]),
                 scalars=at,
-                scratch=[cell_scratch(info), pltpu.SemaphoreType.DMA((count + len(higher),))]
+                scratch=[cell_scratch(info), pltpu.SemaphoreType.DMA((count + GROUPS * len(higher),))]
                 + [cell_scratch(info)] * len(higher),
                 flops=4 * info.cell_rows * width * info.chunk,
+                stay=[False],
             )[0]
         parts = exchange_inner(parts, level)
         solved[level] = exchange_outer(sum_spread(parts, info.targets), level)
         swapped[level] = swap(solved[level], "leaf", 1)
+        if level > 1:
+            z0 = kernel_call(
+                functools.partial(subtract_kernel, info),
+                [shaped((counts[0], cases), F32)],
+                [z0, (dense[0, level], None), solved[level], swapped[level]],
+                scalars=at,
+                scratch=[
+                    pltpu.VMEM((cases, width), BF16),
+                    matrix_scratch,
+                    pltpu.SemaphoreType.DMA((GROUPS,)),
+                ],
+                flops=2 * counts[0] * width * cases,
+            )[0]
 
     part = kernel_call(
-        functools.partial(last_kernel, infos),
+        functools.partial(last_kernel, infos[0]),
         [shaped((blocks, cases, counts[0]), BF16)],
-        [y0, (inverse, None)]
-        + hbm([dense[0, above] for above in uppers])
-        + [solved[above] for above in uppers]
-        + [swapped[above] for above in uppers],
+        [z0, (dense[0, 1], None), solved[1], swapped[1], (inverse, None)],
         scalars=at,
         scratch=[
-            pltpu.VMEM((depth, cases, width), BF16),
+            pltpu.VMEM((cases, width), BF16),
             matrix_scratch,
-            dense_scratch,
-            pltpu.SemaphoreType.DMA((1 + depth,)),
+            matrix_scratch,
+            pltpu.SemaphoreType.DMA((2 * GROUPS,)),
         ],
-        flops=2 * (1 + depth) * counts[0] * width * cases,
+        flops=4 * counts[0] * width * cases,
     )[0]
     parts = lax.all_to_all(part, "blk", 0, 0, tiled=True)
 
@@ -631,7 +725,9 @@
             core == 0, jnp.stack([mine, other], 1), jnp.stack([other, mine], 1)
         )
         outputs.append(rows.reshape(cases, info.rows).T)
-    out = kernel_call(output_kernel, [shaped((sum(counts), cases), F32)], [parts] + outputs)[0]
+    out = kernel_call(
+        output_kernel, [shaped((sum(counts), cases), F32)], [parts] + outputs
+    )[0]
     return out[None, None]
 
 

time: 176 us -> 174 us (0.989)
    pallas_call x13 -> x14, Pallas kernels: 33.6 us -> 34.7 us  [kernel_call(): pl.pallas_call(body, out_shape=[pltpu.HBM(o.shape, o.dtype) if keep else...]
  transfers between devices with their start and end apart: 24 -> 24, of which waited for: 9 -> 8; matrix products, arithmetic and copies ran while one was open for 2% -> 2% of each run, Pallas kernels for 10% -> 12%
where the time goes in v2:
time: 174 us; the launch traced here: 173 us
  waiting for transfers between devices  62.8 us (36%)
  starting transfers between devices  40.3 us (23%)
  Pallas kernels  34.7 us (20%)
  blocking collectives  29.1 us (17%)
  local copies, waits for them, and re-layouts  5.13 us (3%)
    pallas_call x14, Pallas kernels, kernel_call(): pl.pallas_call(body, out_shape=[pltpu.HBM(o.shape, o.dtype) if keep else...  34.7 us
    ppermute x17, waiting for transfers between devices, swap(): return lax.ppermute(value, axis, [(i, i ^ bit) for i in range(size)])  18.4 us
    all_to_all x2, blocking collectives, exchange_inner(): lax.all_to_all(value, 'blk', 0, 0, axis_index_groups=info.inner_blk, tile...  17.1 us
    all_to_all x2, waiting for transfers between devices, exchange_outer(): return lax.all_to_all(value, 'blk', 0, 0, tiled=True)  16.6 us
    all_to_all x1, waiting for transfers between devices, solve(): parts = lax.all_to_all(part, 'blk', 0, 0, tiled=True)  15 us
    all_to_all x1, blocking collectives, exchange_outer(): lax.all_to_all(value, ('leaf', 'blk'), 0, 0, axis_index_groups=infos[leve...  12 us
    all_to_all x2, starting transfers between devices, exchange_outer(): return lax.all_to_all(value, 'blk', 0, 0, tiled=True)  8.03 us
    all_to_all x2, starting transfers between devices, exchange_inner(): lax.all_to_all(value, 'blk', 0, 0, axis_index_groups=info.inner_blk, tile...  7.86 us
  transfers between devices with their start and end apart: 24, of which 8 were waited for; matrix products, arithmetic and copies ran while one was open for 2% of the time, Pallas kernels for 12%

profile of v2, /device:TPU:0, one launch (start us, length us, event | category | flops | bytes accessed | tf_op | source)
XLA Modules:
  0.0 173.2 jit_solution(6297087758431467067)
XLA Ops:
  0.0 0.9 copy-done
  1.8 7.3 %all-to-all-start = ((bf16[8,256,128]{2,1,0:T(8,128)(2,1)}), bf16[8,256,128]{2,1,0:T(8,128)(2,1)S(1)}, u32[]{:S(2)}, u32[]{:S(2)}) async-start(bf16[8,256,128]{2,1,0:T(8,128)(2,1)} %shard_map.46), calls=%async_computation | async-start | bytes 1048576 | tf_op jit(solution)/shard_map/all_to_all | solution.py:554
  9.1 1.1 slice_bitcast_fusion.refs_0_
  10.2 2.1 %collective-permute-start.2 = (bf16[128,2048]{1,0:T(8,128)(2,1)S(1)}, bf16[128,2048]{1,0:T(8,128)(2,1)}, u32[]{:S(2)}, u32[]{:S(2)}) collective-permute-start(bf16[128,2048]{1,0:T(8,128)(2,1)S(1)} %slice_bitcast_fusion.refs_0_), channel_id=1, source_target_pairs={{0,1},{1,0},{2,3},{3,2},{4,5},{5,4},{6,7},{7,6},{8,9},{9,8},{10,11... | collective-permute-start | bytes 1572872 | tf_op jit(solution)/shard_map/ppermute | solution.py:500
  12.5 3.9 %shard_map.47 = (bf16[256,2048]{1,0:T(8,128)(2,1)}, bf16[256,2048]{1,0:T(8,128)(2,1)}) custom-call(s32[8]{0:T(128)S(1)} %stack.59.at, s32[10,1024]{1,0:T(8,128)S(1)} %copy-done.7, bf16[640,1024]{1,0:T(8,128)(2,1)S(1)} %bitcast.52), custom_call_target="tpu_custom_call" | custom-call | flops 2147483648 | bytes 3448832 | tf_op jit(solution)/shard_map/pallas_call | solution.py:47
  16.4 7.2 %all-to-all-done = bf16[8,256,128]{2,1,0:T(8,128)(2,1)S(1)} async-done(((bf16[8,256,128]{2,1,0:T(8,128)(2,1)}), bf16[8,256,128]{2,1,0:T(8,128)(2,1)S(1)}, u32[]{:S(2)}, u32[]{:S(2)}) %all-to-all-start) | async-done | bytes 524320 | tf_op jit(solution)/shard_map/all_to_all | solution.py:554
  23.6 4.0 %shard_map.48 = (f32[256,128]{1,0:T(8,128)}, bf16[8,32,512]{2,1,0:T(8,128)(2,1)S(1)}, bf16[8,32,512]{2,1,0:T(8,128)(2,1)S(1)}, bf16[16,16,512]{2,1,0:T(8,128)(2,1)}, bf16[16,16,512]{2,1,0:T(8,128)(2,1)}) custom-call(s32[8]{0:T(128)S(1)} %stack.59.at, bf16[2048,128]{1,0:T(8,128)(2,1)S(1)} %bitcast.44, bf16[448,2048]{1,0:T(8,128)(2,1)} %bitcast.53, ...), custom_call_target="tpu_custom_call" | custom-call | flops 402653184 | bytes 5865472 | tf_op jit(solution)/shard_map/pallas_call | solution.py:47
  28.3 5.9 %collective-permute-done.5.refs_1_ = bf16[128,1024]{1,0:T(8,128)(2,1)S(1)} collective-permute-done((bf16[128,1024]{1,0:T(8,128)(2,1)S(1)}, bf16[128,1024]{1,0:T(8,128)(2,1)S(1)}, u32[]{:S(2)}, u32[]{:S(2)}) %collective-permute-start.5) | collective-permute-done | bytes 262176 | tf_op jit(solution)/shard_map/ppermute | solution.py:500
  35.5 4.6 %all-to-all-start.1 = ((bf16[8,32,512]{2,1,0:T(8,128)(2,1)}), bf16[8,32,512]{2,1,0:T(8,128)(2,1)S(1)}, u32[]{:S(2)}, u32[]{:S(2)}) async-start(bf16[8,32,512]{2,1,0:T(8,128)(2,1)} %add_convert_fusion), calls=%async_computation.1 | async-start | bytes 524288 | tf_op jit(solution)/shard_map/all_to_all | solution.py:509
  40.2 1.0 slice_bitcast_fusion.1.refs_0_
  41.1 8.5 %all-to-all-done.1.parts = bf16[8,32,512]{2,1,0:T(8,128)(2,1)S(1)} async-done(((bf16[8,32,512]{2,1,0:T(8,128)(2,1)}), bf16[8,32,512]{2,1,0:T(8,128)(2,1)S(1)}, u32[]{:S(2)}, u32[]{:S(2)}) %all-to-all-start.1) | async-done | bytes 262176 | tf_op jit(solution)/shard_map/all_to_all | solution.py:509
  50.4 3.3 %all-to-all-start.2 = ((bf16[4,32,512]{2,1,0:T(8,128)(2,1)}), bf16[4,32,512]{2,1,0:T(8,128)(2,1)S(1)}, u32[]{:S(2)}, u32[]{:S(2)}) async-start(bf16[4,32,512]{2,1,0:T(8,128)(2,1)} %shard_map.49), calls=%async_computation.2 | async-start | bytes 262144 | tf_op jit(solution)/shard_map/all_to_all | solution.py:522
  53.7 1.6 collective-permute-start.8
  55.3 4.3 %shard_map.50.refs_4_.refs_5_ = bf16[512,2048]{1,0:T(8,128)(2,1)} custom-call(s32[8]{0:T(128)S(1)} %stack.59.at, s32[10,1024]{1,0:T(8,128)S(1)} %copy-done.7, bf16[128,1024]{1,0:T(8,128)(2,1)S(1)} %slice_bitcast_fusion.2.refs_0_, bf16[128,1024]{1,0:T(8,128)(2,1)S(1)} %collective-permute-done.5.refs_1_, bf16[128,1024]{1,0:T(8,128)(2,1)S(1)} %collective-permute-done.6.refs_2_, ...), custom_call_target="tpu_custom_call" | custom-call | flops 2147483648 | bytes 3186688 | tf_op jit(solution)/shard_map/pallas_call | solution.py:47
  60.4 4.4 %shard_map.51 = (f32[512,32]{1,0:T(8,128)}, bf16[16,16,512]{2,1,0:T(8,128)(2,1)}) custom-call(s32[8]{0:T(128)S(1)} %stack.59.at, bf16[4,32,512]{2,1,0:T(8,128)(2,1)S(1)} %all-to-all-done.2.gathered, bf16[16,16,512]{2,1,0:T(8,128)(2,1)S(1)} %copy-done.4, bf16[16,16,512]{2,1,0:T(8,128)(2,1)S(1)} %collective-permute-done.1.received, ...), custom_call_target="tpu_custom_call" | custom-call | flops 134217728 | bytes 5177344 | tf_op jit(solution)/shard_map/pallas_call | solution.py:47
  64.8 6.0 %all-to-all-start.3 = ((bf16[16,16,512]{2,1,0:T(8,128)(2,1)}), bf16[16,16,512]{2,1,0:T(8,128)(2,1)S(1)}, u32[]{:S(2)}, u32[]{:S(2)}) async-start(bf16[16,16,512]{2,1,0:T(8,128)(2,1)} %get-tuple-element.21), calls=%async_computation.3 | async-start | bytes 524288 | tf_op jit(solution)/shard_map/all_to_all | solution.py:510
  70.7 2.0 %collective-permute-start.9 = (bf16[64,2048]{1,0:T(8,128)(2,1)S(1)}, bf16[64,2048]{1,0:T(8,128)(2,1)S(1)}, u32[]{:S(2)}, u32[]{:S(2)}) collective-permute-start(bf16[64,2048]{1,0:T(8,128)(2,1)S(1)} %slice_bitcast_fusion.1.refs_0_), channel_id=1, source_target_pairs={{0,1},{1,0},{2,3},{3,2},{4,5},{5,4},{6,7},{7,6},{8,9},{9,8},{10,11... | collective-permute-start | bytes 786440 | tf_op jit(solution)/shard_map/ppermute | solution.py:500
  73.4 8.9 %collective-permute-done.9.refs_2_ = bf16[64,2048]{1,0:T(8,128)(2,1)S(1)} collective-permute-done((bf16[64,2048]{1,0:T(8,128)(2,1)S(1)}, bf16[64,2048]{1,0:T(8,128)(2,1)S(1)}, u32[]{:S(2)}, u32[]{:S(2)}) %collective-permute-start.9) | collective-permute-done | bytes 262176 | tf_op jit(solution)/shard_map/ppermute | solution.py:500
  82.3 3.5 %collective-permute-done.10.refs_3_ = bf16[64,2048]{1,0:T(8,128)(2,1)S(1)} collective-permute-done((bf16[64,2048]{1,0:T(8,128)(2,1)S(1)}, bf16[64,2048]{1,0:T(8,128)(2,1)S(1)}, u32[]{:S(2)}, u32[]{:S(2)}) %collective-permute-start.10) | collective-permute-done | bytes 262176 | tf_op jit(solution)/shard_map/ppermute | solution.py:500
  86.6 4.5 %all-to-all-start.4 = ((bf16[4,16,512]{2,1,0:T(8,128)(2,1)}), bf16[4,16,512]{2,1,0:T(8,128)(2,1)S(1)}, u32[]{:S(2)}, u32[]{:S(2)}) async-start(bf16[4,16,512]{2,1,0:T(8,128)(2,1)} %shard_map.52), calls=%async_computation.4 | async-start | bytes 131072 | tf_op jit(solution)/shard_map/all_to_all | solution.py:522
  91.2 5.7 %all-to-all-done.4.gathered = bf16[4,16,512]{2,1,0:T(8,128)(2,1)S(1)} async-done(((bf16[4,16,512]{2,1,0:T(8,128)(2,1)}), bf16[4,16,512]{2,1,0:T(8,128)(2,1)S(1)}, u32[]{:S(2)}, u32[]{:S(2)}) %all-to-all-start.4) | async-done | bytes 65568 | tf_op jit(solution)/shard_map/all_to_all | solution.py:522
  96.9 3.0 %shard_map.53 = bf16[4,16,512]{2,1,0:T(8,128)(2,1)S(1)} custom-call(bf16[4,16,512]{2,1,0:T(8,128)(2,1)S(1)} %all-to-all-done.4.gathered, bf16[64,2048]{1,0:T(8,128)(2,1)} %copy-done.10, bf16[64,2048]{1,0:T(8,128)(2,1)} %copy-done.11, bf16[64,2048]{1,0:T(8,128)(2,1)} %copy-done.12, bf16[64,2048]{1,0:T(8,128)(2,1)} %copy-done.13, bf16[64,2048]{1,0:T(8,128)(2,1)} %copy-done.14, ...), custom_call_target="tpu_custom_call" | custom-call | flops 67108864 | bytes 2228224 | tf_op jit(solution)/shard_map/pallas_call | solution.py:47
  99.9 8.1 %all_to_all.50.parts = bf16[4,16,512]{2,1,0:T(8,128)(2,1)S(1)} all-to-all(bf16[4,16,512]{2,1,0:T(8,128)(2,1)S(1)} %shard_map.53), channel_id=1, replica_groups={{0,2,4,6},{1,3,5,7},{8,10,12,14},{9,11,13,15},{16,18,20,22},{17,19,21,2..., dimensions={0} | all-to-all | bytes 131072 | tf_op jit(solution)/shard_map/all_to_all | solution.py:522
  108.7 12.0 %all_to_all.51.mine.refs_4_ = bf16[16,16,512]{2,1,0:T(8,128)(2,1)S(1)} all-to-all(bf16[16,16,512]{2,1,0:T(8,128)(2,1)} %shard_map.54), channel_id=1, replica_groups={{0,1,2,3,4,5,6,7,16,17,18,19,20,21,22,23},{8,9,10,11,12,13,14,15,24,25,..., dimensions={0} | all-to-all | bytes 524288 | tf_op jit(solution)/shard_map/all_to_all | solution.py:510
  120.7 3.7 %shard_map.56 = bf16[4,32,512]{2,1,0:T(8,128)(2,1)S(1)} custom-call(s32[8]{0:T(128)S(1)} %stack.59.at, f32[512,32]{1,0:T(8,128)S(1)} %copy-done.3, bf16[128,2048]{1,0:T(8,128)(2,1)} %copy-done.8, bf16[128,2048]{1,0:T(8,128)(2,1)} %collective-permute-done.2.refs_1_, bf16[128,2048]{1,0:T(8,128)(2,1)} %copy-done.9, ...), custom_call_target="tpu_custom_call" | custom-call | flops 134217728 | bytes 4653056 | tf_op jit(solution)/shard_map/pallas_call | solution.py:47
  124.5 9.0 %all_to_all.52.parts = bf16[4,32,512]{2,1,0:T(8,128)(2,1)S(1)} all-to-all(bf16[4,32,512]{2,1,0:T(8,128)(2,1)S(1)} %shard_map.56), channel_id=1, replica_groups={{0,2,4,6},{1,3,5,7},{8,10,12,14},{9,11,13,15},{16,18,20,22},{17,19,21,2..., dimensions={0} | all-to-all | bytes 262144 | tf_op jit(solution)/shard_map/all_to_all | solution.py:522
  134.2 3.4 %all-to-all-start.8 = ((bf16[8,32,512]{2,1,0:T(8,128)(2,1)}), bf16[8,32,512]{2,1,0:T(8,128)(2,1)S(1)}, u32[]{:S(2)}, u32[]{:S(2)}) async-start(bf16[8,32,512]{2,1,0:T(8,128)(2,1)} %shard_map.57), calls=%async_computation.8 | async-start | bytes 524288 | tf_op jit(solution)/shard_map/all_to_all | solution.py:509
  137.7 8.1 %all-to-all-done.8.mine = bf16[8,32,512]{2,1,0:T(8,128)(2,1)S(1)} async-done(((bf16[8,32,512]{2,1,0:T(8,128)(2,1)}), bf16[8,32,512]{2,1,0:T(8,128)(2,1)S(1)}, u32[]{:S(2)}, u32[]{:S(2)}) %all-to-all-start.8) | async-done | bytes 262176 | tf_op jit(solution)/shard_map/all_to_all | solution.py:509
  145.8 3.1 %shard_map.55.y = f32[256,128]{1,0:T(8,128)} custom-call(s32[8]{0:T(128)S(1)} %stack.59.at, f32[256,128]{1,0:T(8,128)S(1)} %copy-done.5, bf16[256,2048]{1,0:T(8,128)(2,1)} %get-tuple-element.15.refs_1_.source, bf16[16,16,512]{2,1,0:T(8,128)(2,1)S(1)} %all_to_all.51.mine.refs_4_, bf16[16,16,512]{2,1,0:T(8,128)(2,1)S(1)} %collective-permute-done.15.other), custom_call_target="tpu_custom_call" | custom-call | flops 134217728 | bytes 1835008 | tf_op jit(solution)/shard_map/pallas_call | solution.py:47
  149.8 3.7 %shard_map.58 = bf16[8,128,256]{2,1,0:T(8,128)(2,1)} custom-call(s32[8]{0:T(128)S(1)} %stack.59.at, f32[256,128]{1,0:T(8,128)S(1)} %copy-done.2, bf16[256,2048]{1,0:T(8,128)(2,1)} %get-tuple-element.14.refs_0_.source, bf16[8,32,512]{2,1,0:T(8,128)(2,1)S(1)} %all-to-all-done.8.mine, bf16[8,32,512]{2,1,0:T(8,128)(2,1)S(1)} %collective-permute-done.16.other, ...), custom_call_target="tpu_custom_call" | custom-call | flops 268435456 | bytes 4063232 | tf_op jit(solution)/shard_map/pallas_call | solution.py:47
  153.5 3.5 %all-to-all-start.9 = ((bf16[8,128,256]{2,1,0:T(8,128)(2,1)}), bf16[8,128,256]{2,1,0:T(8,128)(2,1)S(1)}, u32[]{:S(2)}, u32[]{:S(2)}) async-start(bf16[8,128,256]{2,1,0:T(8,128)(2,1)} %shard_map.58), calls=%async_computation.9 | async-start | bytes 1048576 | tf_op jit(solution)/shard_map/all_to_all | solution.py:707
  157.5 15.0 %all-to-all-done.9.parts = bf16[8,128,256]{2,1,0:T(8,128)(2,1)S(1)} async-done(((bf16[8,128,256]{2,1,0:T(8,128)(2,1)}), bf16[8,128,256]{2,1,0:T(8,128)(2,1)S(1)}, u32[]{:S(2)}, u32[]{:S(2)}) %all-to-all-start.9) | async-done | bytes 524320 | tf_op jit(solution)/shard_map/all_to_all | solution.py:707
  (82 shorter events, 9.6 us)
Async XLA Ops:
  0.9 11.3 %copy-start.6 = (bf16[1,1,640,1024]{3,2,1,0:T(8,128)(2,1)S(1)}, bf16[1,1,640,1024]{3,2,1,0:T(8,128)(2,1)}, u32[]{:S(2)}) copy-start(bf16[1,1,640,1024]{3,2,1,0:T(8,128)(2,1)} %param.6) | copy-start | bytes 3932164
  0.9 11.6 %copy-start.7 = (s32[10,1024]{1,0:T(8,128)S(1)}, s32[10,1024]{1,0:T(8,128)}, u32[]{:S(2)}) copy-start(s32[10,1024]{1,0:T(8,128)} %lists.3) | copy-start | bytes 122884
  1.8 21.8 %all-to-all-start = ((bf16[8,256,128]{2,1,0:T(8,128)(2,1)}), bf16[8,256,128]{2,1,0:T(8,128)(2,1)S(1)}, u32[]{:S(2)}, u32[]{:S(2)}) async-start(bf16[8,256,128]{2,1,0:T(8,128)(2,1)} %shard_map.46), calls=%async_computation | async-start | bytes 1048576 | tf_op jit(solution)/shard_map/all_to_all | solution.py:554
  10.2 17.5 %copy-start.8 = (bf16[128,2048]{1,0:T(8,128)(2,1)}, bf16[128,2048]{1,0:T(8,128)(2,1)S(1)}, u32[]{:S(2)}) copy-start(bf16[128,2048]{1,0:T(8,128)(2,1)S(1)} %slice_bitcast_fusion.refs_0_) | copy-start | bytes 1572868
  10.2 24.0 %collective-permute-start.2 = (bf16[128,2048]{1,0:T(8,128)(2,1)S(1)}, bf16[128,2048]{1,0:T(8,128)(2,1)}, u32[]{:S(2)}, u32[]{:S(2)}) collective-permute-start(bf16[128,2048]{1,0:T(8,128)(2,1)S(1)} %slice_bitcast_fusion.refs_0_), channel_id=1, source_target_pairs={{0,1},{1,0},{2,3},{3,2},{4,5},{5,4},{6,7},{7,6},{8,9},{9,8},{10,11... | collective-permute-start | bytes 1572872 | tf_op jit(solution)/shard_map/ppermute | solution.py:500
  12.3 21.9 %collective-permute-start.5 = (bf16[128,1024]{1,0:T(8,128)(2,1)S(1)}, bf16[128,1024]{1,0:T(8,128)(2,1)S(1)}, u32[]{:S(2)}, u32[]{:S(2)}) collective-permute-start(bf16[128,1024]{1,0:T(8,128)(2,1)S(1)} %slice_bitcast_fusion.2.refs_0_), channel_id=1, source_target_pairs={{0,1},{1,0},{2,3},{3,2},{4,5},{5,4},{6,7},{7,6},{8,9},{9,8},{10,11... | collective-permute-start | bytes 786440 | tf_op jit(solution)/shard_map/ppermute | solution.py:500
  27.6 7.1 %collective-permute-start = (bf16[8,32,512]{2,1,0:T(8,128)(2,1)S(1)}, bf16[8,32,512]{2,1,0:T(8,128)(2,1)S(1)}, u32[]{:S(2)}, u32[]{:S(2)}) collective-permute-start(bf16[8,32,512]{2,1,0:T(8,128)(2,1)S(1)} %get-tuple-element.18), channel_id=1, source_target_pairs={{0,8},{8,0},{16,24},{24,16},{1,9},{9,1},{17,25},{25,17},{2,10},{10... | collective-permute-start | bytes 786440 | tf_op jit(solution)/shard_map/ppermute | solution.py:500
  27.7 31.9 %collective-permute-start.3 = (bf16[128,2048]{1,0:T(8,128)(2,1)S(1)}, bf16[128,2048]{1,0:T(8,128)(2,1)S(1)}, u32[]{:S(2)}, u32[]{:S(2)}) collective-permute-start(bf16[128,2048]{1,0:T(8,128)(2,1)S(1)} %slice_bitcast_fusion.refs_0_), channel_id=1, source_target_pairs={{0,8},{8,0},{16,24},{24,16},{1,9},{9,1},{17,25},{25,17},{2,10},{10... | collective-permute-start | bytes 1572872 | tf_op jit(solution)/shard_map/ppermute | solution.py:500
  28.2 25.5 %collective-permute-start.6 = (bf16[128,1024]{1,0:T(8,128)(2,1)S(1)}, bf16[128,1024]{1,0:T(8,128)(2,1)S(1)}, u32[]{:S(2)}, u32[]{:S(2)}) collective-permute-start(bf16[128,1024]{1,0:T(8,128)(2,1)S(1)} %slice_bitcast_fusion.2.refs_0_), channel_id=1, source_target_pairs={{0,8},{8,0},{16,24},{24,16},{1,9},{9,1},{17,25},{25,17},{2,10},{10... | collective-permute-start | bytes 786440 | tf_op jit(solution)/shard_map/ppermute | solution.py:500
  34.2 21.1 %collective-permute-start.7 = (bf16[128,1024]{1,0:T(8,128)(2,1)S(1)}, bf16[128,1024]{1,0:T(8,128)(2,1)S(1)}, u32[]{:S(2)}, u32[]{:S(2)}) collective-permute-start(bf16[128,1024]{1,0:T(8,128)(2,1)S(1)} %collective-permute-done.5.refs_1_), channel_id=1, source_target_pairs={{0,8},{8,0},{16,24},{24,16},{1,9},{9,1},{17,25},{25,17},{2,10},{10... | collective-permute-start | bytes 786440 | tf_op jit(solution)/shard_map/ppermute | solution.py:500
  34.2 25.4 %collective-permute-start.4 = (bf16[128,2048]{1,0:T(8,128)(2,1)}, bf16[128,2048]{1,0:T(8,128)(2,1)}, u32[]{:S(2)}, u32[]{:S(2)}) collective-permute-start(bf16[128,2048]{1,0:T(8,128)(2,1)} %collective-permute-done.2.refs_1_), channel_id=1, source_target_pairs={{0,8},{8,0},{16,24},{24,16},{1,9},{9,1},{17,25},{25,17},{2,10},{10... | collective-permute-start | bytes 1572872 | tf_op jit(solution)/shard_map/ppermute | solution.py:500
  34.7 24.9 %collective-permute-start.1 = (bf16[16,16,512]{2,1,0:T(8,128)(2,1)}, bf16[16,16,512]{2,1,0:T(8,128)(2,1)S(1)}, u32[]{:S(2)}, u32[]{:S(2)}) collective-permute-start(bf16[16,16,512]{2,1,0:T(8,128)(2,1)} %get-tuple-element.20), channel_id=1, source_target_pairs={{0,8},{8,0},{16,24},{24,16},{1,9},{9,1},{17,25},{25,17},{2,10},{10... | collective-permute-start | bytes 786440 | tf_op jit(solution)/shard_map/ppermute | solution.py:500
  35.5 14.1 %all-to-all-start.1 = ((bf16[8,32,512]{2,1,0:T(8,128)(2,1)}), bf16[8,32,512]{2,1,0:T(8,128)(2,1)S(1)}, u32[]{:S(2)}, u32[]{:S(2)}) async-start(bf16[8,32,512]{2,1,0:T(8,128)(2,1)} %add_convert_fusion), calls=%async_computation.1 | async-start | bytes 524288 | tf_op jit(solution)/shard_map/all_to_all | solution.py:509
  41.1 31.7 %copy-start.10 = (bf16[64,2048]{1,0:T(8,128)(2,1)}, bf16[64,2048]{1,0:T(8,128)(2,1)S(1)}, u32[]{:S(2)}) copy-start(bf16[64,2048]{1,0:T(8,128)(2,1)S(1)} %slice_bitcast_fusion.1.refs_0_) | copy-start | bytes 786436
  50.4 9.2 %all-to-all-start.2 = ((bf16[4,32,512]{2,1,0:T(8,128)(2,1)}), bf16[4,32,512]{2,1,0:T(8,128)(2,1)S(1)}, u32[]{:S(2)}, u32[]{:S(2)}) async-start(bf16[4,32,512]{2,1,0:T(8,128)(2,1)} %shard_map.49), calls=%async_computation.2 | async-start | bytes 262144 | tf_op jit(solution)/shard_map/all_to_all | solution.py:522
  53.7 19.0 %collective-permute-start.8 = (bf16[64,2048]{1,0:T(8,128)(2,1)S(1)}, bf16[64,2048]{1,0:T(8,128)(2,1)S(1)}, u32[]{:S(2)}, u32[]{:S(2)}) collective-permute-start(bf16[64,2048]{1,0:T(8,128)(2,1)S(1)} %slice_bitcast_fusion.1.refs_0_), channel_id=1, source_target_pairs={{0,16},{8,24},{16,0},{24,8},{1,17},{9,25},{17,1},{25,9},{2,18},{10... | collective-permute-start | bytes 786440 | tf_op jit(solution)/shard_map/ppermute | solution.py:500
  64.8 21.0 %all-to-all-start.3 = ((bf16[16,16,512]{2,1,0:T(8,128)(2,1)}), bf16[16,16,512]{2,1,0:T(8,128)(2,1)S(1)}, u32[]{:S(2)}, u32[]{:S(2)}) async-start(bf16[16,16,512]{2,1,0:T(8,128)(2,1)} %get-tuple-element.21), calls=%async_computation.3 | async-start | bytes 524288 | tf_op jit(solution)/shard_map/all_to_all | solution.py:510
  70.7 50.0 %copy-start.3 = (f32[512,32]{1,0:T(8,128)S(1)}, f32[512,32]{1,0:T(8,128)}, u32[]{:S(2)}) copy-start(f32[512,32]{1,0:T(8,128)} %get-tuple-element.22.y) | copy-start | bytes 196612
  70.7 11.6 %collective-permute-start.9 = (bf16[64,2048]{1,0:T(8,128)(2,1)S(1)}, bf16[64,2048]{1,0:T(8,128)(2,1)S(1)}, u32[]{:S(2)}, u32[]{:S(2)}) collective-permute-start(bf16[64,2048]{1,0:T(8,128)(2,1)S(1)} %slice_bitcast_fusion.1.refs_0_), channel_id=1, source_target_pairs={{0,1},{1,0},{2,3},{3,2},{4,5},{5,4},{6,7},{7,6},{8,9},{9,8},{10,11... | collective-permute-start | bytes 786440 | tf_op jit(solution)/shard_map/ppermute | solution.py:500
  72.7 24.1 %copy-start.11 = (bf16[64,2048]{1,0:T(8,128)(2,1)}, bf16[64,2048]{1,0:T(8,128)(2,1)S(1)}, u32[]{:S(2)}) copy-start(bf16[64,2048]{1,0:T(8,128)(2,1)S(1)} %collective-permute-done.8.refs_1_) | copy-start | bytes 786436
  72.7 13.1 %collective-permute-start.10 = (bf16[64,2048]{1,0:T(8,128)(2,1)S(1)}, bf16[64,2048]{1,0:T(8,128)(2,1)S(1)}, u32[]{:S(2)}, u32[]{:S(2)}) collective-permute-start(bf16[64,2048]{1,0:T(8,128)(2,1)S(1)} %collective-permute-done.8.refs_1_), channel_id=1, source_target_pairs={{0,1},{1,0},{2,3},{3,2},{4,5},{5,4},{6,7},{7,6},{8,9},{9,8},{10,11... | collective-permute-start | bytes 786440 | tf_op jit(solution)/shard_map/ppermute | solution.py:500
  72.8 18.3 %collective-permute-start.11 = (bf16[64,2048]{1,0:T(8,128)(2,1)S(1)}, bf16[64,2048]{1,0:T(8,128)(2,1)S(1)}, u32[]{:S(2)}, u32[]{:S(2)}) collective-permute-start(bf16[64,2048]{1,0:T(8,128)(2,1)S(1)} %slice_bitcast_fusion.1.refs_0_), channel_id=1, source_target_pairs={{0,8},{8,0},{16,24},{24,16},{1,9},{9,1},{17,25},{25,17},{2,10},{10... | collective-permute-start | bytes 786440 | tf_op jit(solution)/shard_map/ppermute | solution.py:500
  72.9 18.3 %collective-permute-start.12 = (bf16[64,2048]{1,0:T(8,128)(2,1)S(1)}, bf16[64,2048]{1,0:T(8,128)(2,1)S(1)}, u32[]{:S(2)}, u32[]{:S(2)}) collective-permute-start(bf16[64,2048]{1,0:T(8,128)(2,1)S(1)} %collective-permute-done.8.refs_1_), channel_id=1, source_target_pairs={{0,8},{8,0},{16,24},{24,16},{1,9},{9,1},{17,25},{25,17},{2,10},{10... | collective-permute-start | bytes 786440 | tf_op jit(solution)/shard_map/ppermute | solution.py:500
  82.3 14.5 %copy-start.12 = (bf16[64,2048]{1,0:T(8,128)(2,1)}, bf16[64,2048]{1,0:T(8,128)(2,1)S(1)}, u32[]{:S(2)}) copy-start(bf16[64,2048]{1,0:T(8,128)(2,1)S(1)} %collective-permute-done.9.refs_2_) | copy-start | bytes 786436
  82.3 8.8 %collective-permute-start.13 = (bf16[64,2048]{1,0:T(8,128)(2,1)S(1)}, bf16[64,2048]{1,0:T(8,128)(2,1)S(1)}, u32[]{:S(2)}, u32[]{:S(2)}) collective-permute-start(bf16[64,2048]{1,0:T(8,128)(2,1)S(1)} %collective-permute-done.9.refs_2_), channel_id=1, source_target_pairs={{0,8},{8,0},{16,24},{24,16},{1,9},{9,1},{17,25},{25,17},{2,10},{10... | collective-permute-start | bytes 786440 | tf_op jit(solution)/shard_map/ppermute | solution.py:500
  85.8 5.3 %collective-permute-start.14 = (bf16[64,2048]{1,0:T(8,128)(2,1)S(1)}, bf16[64,2048]{1,0:T(8,128)(2,1)S(1)}, u32[]{:S(2)}, u32[]{:S(2)}) collective-permute-start(bf16[64,2048]{1,0:T(8,128)(2,1)S(1)} %collective-permute-done.10.refs_3_), channel_id=1, source_target_pairs={{0,8},{8,0},{16,24},{24,16},{1,9},{9,1},{17,25},{25,17},{2,10},{10... | collective-permute-start | bytes 786440 | tf_op jit(solution)/shard_map/ppermute | solution.py:500
  86.6 10.3 %all-to-all-start.4 = ((bf16[4,16,512]{2,1,0:T(8,128)(2,1)}), bf16[4,16,512]{2,1,0:T(8,128)(2,1)S(1)}, u32[]{:S(2)}, u32[]{:S(2)}) async-start(bf16[4,16,512]{2,1,0:T(8,128)(2,1)} %shard_map.52), calls=%async_computation.4 | async-start | bytes 131072 | tf_op jit(solution)/shard_map/all_to_all | solution.py:522
  120.7 25.0 %copy-start.5 = (f32[256,128]{1,0:T(8,128)S(1)}, f32[256,128]{1,0:T(8,128)}, u32[]{:S(2)}) copy-start(f32[256,128]{1,0:T(8,128)} %get-tuple-element.16.y) | copy-start | bytes 393220
  134.2 11.6 %all-to-all-start.8 = ((bf16[8,32,512]{2,1,0:T(8,128)(2,1)}), bf16[8,32,512]{2,1,0:T(8,128)(2,1)S(1)}, u32[]{:S(2)}, u32[]{:S(2)}) async-start(bf16[8,32,512]{2,1,0:T(8,128)(2,1)} %shard_map.57), calls=%async_computation.8 | async-start | bytes 524288 | tf_op jit(solution)/shard_map/all_to_all | solution.py:509
  137.6 8.2 %collective-permute-start.15 = (bf16[16,16,512]{2,1,0:T(8,128)(2,1)S(1)}, bf16[16,16,512]{2,1,0:T(8,128)(2,1)S(1)}, u32[]{:S(2)}, u32[]{:S(2)}) collective-permute-start(bf16[16,16,512]{2,1,0:T(8,128)(2,1)S(1)} %all_to_all.51.mine.refs_4_), channel_id=1, source_target_pairs={{0,8},{8,0},{16,24},{24,16},{1,9},{9,1},{17,25},{25,17},{2,10},{10... | collective-permute-start | bytes 786440 | tf_op jit(solution)/shard_map/ppermute | solution.py:500
  145.7 3.1 %collective-permute-start.16 = (bf16[8,32,512]{2,1,0:T(8,128)(2,1)S(1)}, bf16[8,32,512]{2,1,0:T(8,128)(2,1)S(1)}, u32[]{:S(2)}, u32[]{:S(2)}) collective-permute-start(bf16[8,32,512]{2,1,0:T(8,128)(2,1)S(1)} %all-to-all-done.8.mine), channel_id=1, source_target_pairs={{0,8},{8,0},{16,24},{24,16},{1,9},{9,1},{17,25},{25,17},{2,10},{10... | collective-permute-start | bytes 786440 | tf_op jit(solution)/shard_map/ppermute | solution.py:500
  153.5 18.9 %all-to-all-start.9 = ((bf16[8,128,256]{2,1,0:T(8,128)(2,1)}), bf16[8,128,256]{2,1,0:T(8,128)(2,1)S(1)}, u32[]{:S(2)}, u32[]{:S(2)}) async-start(bf16[8,128,256]{2,1,0:T(8,128)(2,1)} %shard_map.58), calls=%async_computation.9 | async-start | bytes 1048576 | tf_op jit(solution)/shard_map/all_to_all | solution.py:707
  (10 other events, 54.4 us)

commit v3 on v2

--- a/solution.py
+++ b/solution.py
@@ -37,15 +37,13 @@
         value, spec = arg, pl.BlockSpec(memory_space=pltpu.VMEM)
         if isinstance(arg, tuple):
             value = pltpu.with_memory_space_constraint(arg[0], pltpu.HBM)
-            spec = pl.BlockSpec(memory_space=pltpu.HBM)
+            if arg[1] is None:
+                spec = pl.BlockSpec(memory_space=pltpu.HBM)
         values.append(value)
         specs.append(spec)
         moved += value.size * value.dtype.itemsize
-    if scalars is not None:
-        specs = [pl.BlockSpec(memory_space=pltpu.SMEM)] + specs
-        values = [scalars] + values
     return pl.pallas_call(
-        body,
+        body if scalars is None else lambda *refs: body(scalars(), *refs),
         out_shape=[
             pltpu.HBM(o.shape, o.dtype) if keep else o for o, keep in zip(outs, stay)
         ],
@@ -130,6 +128,7 @@
 
 class Level:
     def __init__(self, level, leaves, blocks, width, cases):
+        self.level = level
         self.pair_x = 2 if level >= 2 else 1
         self.his = (1 << level) // (2 * self.pair_x)
         self.zbs = blocks // 2
@@ -207,8 +206,11 @@
 CORE, YB, XU, SPOT = 0, 1, 2, 3
 
 
-def first_kernel(rhs, out):
-    rounded = rhs[0 : out.shape[1], :].astype(BF16)
+def first_kernel(rhs, out, rows, sem):
+    copy = pltpu.make_async_copy(rhs.at[0 : rows.shape[0], :], rows, sem)
+    copy.start()
+    copy.wait()
+    rounded = rows[...].astype(BF16)
     for n in range(out.shape[0]):
         out[n] = rounded
 
@@ -233,8 +235,9 @@
     depth = len(infos)
     sources = refs[:depth]
     outs = refs[depth : depth + 1 + 2 * depth]
-    total, matrix, dense, sems = refs[depth + 1 + 2 * depth :]
+    total, matrix, dense, rhs_copy, sems = refs[depth + 1 + 2 * depth :]
     loads = Loads(sems)
+    rhs_load = loads.start([(rhs, rhs_copy)])
     groups = group_rows(matrix.shape[0])
     first = [start() for start in loads.groups([inverse], matrix, GROUPS)]
     later = [
@@ -244,11 +247,12 @@
     core = at[CORE]
     width = total.shape[-1]
     placed = []
+    wait(rhs_load)
     for n, info in enumerate(infos):
         row_ids = at[SPOT + n] + lax.broadcasted_iota(jnp.int32, (info.rows, width), 0)
         lane_ids = lax.broadcasted_iota(jnp.int32, (info.rows, width), 1)
         spots = jnp.where(row_ids == lane_ids, 1.0, 0.0).astype(BF16)
-        own = rhs[starts[n] : starts[n] + info.rows, :].astype(BF16)
+        own = rhs_copy[starts[n] : starts[n] + info.rows, :].astype(BF16)
         placed.append(accumulate(None, own, spots))
     rounded = []
     for g, rows in enumerate(groups):
@@ -296,14 +300,15 @@
         out[cell, :, inside : inside + size] = value[:, lane : lane + size]
 
 
-def forward_kernel(infos, k, at, gathered, mine, received, *refs):
+def forward_kernel(infos, k, at, gathered, mine_hbm, received_hbm, *refs):
     info, above = infos[k - 1], infos[k]
     count = 4 * info.pair_x
     pieces = refs[:count]
     lower_y = refs[count : count + k - 1]
     sources = refs[count + k - 1 : count + 2 * k - 1]
-    y_ref, out, total, matrix, sems = refs[count + 2 * k - 1 : count + 2 * k + 4]
-    dense = refs[count + 2 * k + 4 :]
+    y_ref, out, total, matrix, mine, received, sems = refs[count + 2 * k - 1 : count + 2 * k + 6]
+    dense = refs[count + 2 * k + 6 : count + 3 * k + 6]
+    lower_copies = refs[count + 3 * k + 6 :]
     loads = Loads(sems)
     groups = group_rows(matrix.shape[0])
     first = [start() for start in loads.groups(pieces, matrix, GROUPS)]
@@ -311,6 +316,9 @@
         [start() for start in loads.groups([source], dense[j], GROUPS)]
         for j, source in enumerate(sources)
     ]
+    base = loads.start([(mine_hbm, mine), (received_hbm, received)])
+    base += loads.start(list(zip(lower_y, lower_copies)))
+    lower_y = lower_copies
     vector = natural_rows(info, gathered)
     ys = []
     for g, rows in enumerate(groups):
@@ -318,6 +326,7 @@
         y = mm_nt(matrix[rows, :], vector)
         y_ref[rows, :] = y
         ys.append(y)
+    wait(base)
     same = {}
     for j in range(1, k + 1):
         term = None
@@ -343,20 +352,18 @@
 
 
 def top_kernel(info, gathered, *refs):
-    count = 4 * info.pair_x
-    pieces = refs[:count]
-    out, matrix, sems = refs[count:]
-    first = [start() for start in Loads(sems).groups(pieces, matrix, GROUPS)]
+    pieces, out = refs[:-1], refs[-1]
+    each = len(pieces) // GROUPS
     vector = natural_rows(info, gathered)
     halves = None
-    for g, rows in enumerate(group_rows(matrix.shape[0])):
-        wait(first[g])
-        y = mm_nt(matrix[rows, :], vector)
-        halves = accumulate(halves, y.astype(BF16), matrix[rows, :])
+    for g in range(GROUPS):
+        matrix = jnp.concatenate([p[...] for p in pieces[g * each : (g + 1) * each]], 0)
+        y = mm_nt(matrix, vector)
+        halves = accumulate(halves, y.astype(BF16), matrix)
     put_spread(info, halves, out)
 
 
-def backward_kernel(infos, k, at, y, *refs):
+def backward_kernel(infos, k, at, y_hbm, *refs):
     info = infos[k - 1]
     count = 4 * info.pair_x
     uppers = infos[k:]
@@ -364,9 +371,10 @@
     pieces = refs[:count]
     solved = refs[count : count + many]
     sources = refs[count + many : count + 2 * many]
-    out, matrix, sems = refs[count + 2 * many : count + 2 * many + 3]
-    dense = refs[count + 2 * many + 3 :]
+    out, matrix, y, sems = refs[count + 2 * many : count + 2 * many + 4]
+    dense = refs[count + 2 * many + 4 :]
     loads = Loads(sems)
+    y_load = loads.start([(y_hbm, y)])
     dense_loads = [loads.groups([source], dense[n], GROUPS) for n, source in enumerate(sources)]
     matrix_loads = loads.groups(pieces, matrix, GROUPS)
     first = []
@@ -388,6 +396,7 @@
                     ]
                     parts.append(jnp.concatenate([solved[n][slot] for slot in slots], 0))
         vectors.append(jnp.concatenate(parts, 1))
+    wait(y_load)
     halves = None
     for g, rows in enumerate(group_rows(matrix.shape[0])):
         z = y[rows, :]
@@ -407,20 +416,27 @@
             full[pl.ds(row, info.chunk), info.lanes(cell)] = ref[target]
 
 
-def subtract_kernel(info, at, y, source, mine, other, out, full, dense, sems):
-    loads = [start() for start in Loads(sems).groups([source], dense, GROUPS)]
+def subtract_kernel(info, at, y_hbm, source, mine, other, out, full, dense, y, sems):
+    copies = Loads(sems)
+    y_load = copies.start([(y_hbm, y)])
+    loads = [start() for start in copies.groups([source], dense, GROUPS)]
     full_cases(info, at[CORE], mine, other, full)
+    wait(y_load)
     for g, rows in enumerate(group_rows(dense.shape[0])):
         wait(loads[g])
         out[rows, :] = y[rows, :] - mm_nt(dense[rows, :], full[...])
 
 
-def last_kernel(info, at, y, source, mine, other, inverse, out, full, dense, matrix, sems):
+def last_kernel(
+    info, at, y_hbm, source, mine, other, inverse, out, full, dense, matrix, y, sems
+):
     loads = Loads(sems)
+    y_load = loads.start([(y_hbm, y)])
     dense_loads = loads.groups([source], dense, GROUPS)
     matrix_loads = loads.groups([inverse], matrix, GROUPS)
     copies = [(dense_loads[g](), matrix_loads[g]()) for g in range(GROUPS)]
     full_cases(info, at[CORE], mine, other, full)
+    wait(y_load)
     halves = None
     for g, rows in enumerate(group_rows(dense.shape[0])):
         wait(copies[g][0])
@@ -475,25 +491,24 @@
         pair_bases.append(cursor)
         cursor += (leaves >> level) * (depth - level)
 
-    def own_position(level):
-        info = infos[level - 1]
-        member = leaf_id & ((1 << level) - 1)
-        side = member & (2 * info.pair_x - 1)
-        cell = member // (2 * info.pair_x) * info.zbs + zb
-        return ((cell * 2 * info.pair_x + side) * 2 + yb) * info.rows
-
     pair_slot = {}
-    pair_rows = []
     for level in range(depth):
         for above in range(level + 1, depth + 1):
-            pair_slot[level, above] = SPOT + depth + len(pair_rows)
-            node = leaf_id >> level
-            pair_rows.append(pair_bases[level] + node * (depth - level) + (above - level - 1))
-    at = jnp.stack(
-        [core, yb, (leaf_id >> 1) & 1]
-        + [own_position(l) for l in range(1, depth + 1)]
-        + pair_rows
-    ).astype(jnp.int32)
+            pair_slot[level, above] = SPOT + depth + len(pair_slot)
+
+    def at():
+        leaf = lax.axis_index("leaf")
+        blk = lax.axis_index("blk")
+        scalars = [leaf & 1, blk & 1, (leaf >> 1) & 1]
+        for info in infos:
+            member = leaf & ((1 << info.level) - 1)
+            hi, side = split_power(member, 2 * info.pair_x)
+            cell = hi * info.zbs + (blk >> 1)
+            scalars.append(((cell * 2 * info.pair_x + side) * 2 + (blk & 1)) * info.rows)
+        for level, above in pair_slot:
+            node = leaf >> level
+            scalars.append(pair_bases[level] + node * (depth - level) + (above - level - 1))
+        return scalars
 
     def swap(value, axis, bit):
         size = leaves if axis == "leaf" else blocks
@@ -519,9 +534,7 @@
     def exchange_inner(value, level):
         info = infos[level - 1]
         if info.his == 1:
-            return lax.all_to_all(
-                value, "blk", 0, 0, axis_index_groups=info.inner_blk, tiled=True
-            )
+            return lax.all_to_all(value, "blk", 0, 0, axis_index_groups=info.inner_blk, tiled=True)
         return lax.all_to_all(
             value, ("leaf", "blk"), 0, 0, axis_index_groups=info.inner, tiled=True
         )
@@ -549,7 +562,10 @@
         dense[0, above] = expanded[above - 1]
 
     spread = kernel_call(
-        first_kernel, [shaped((blocks, counts[0], cases), BF16)], [rhs]
+        first_kernel,
+        [shaped((blocks, counts[0], cases), BF16)],
+        [(rhs, None)],
+        scratch=[pltpu.VMEM((counts[0], cases), F32), pltpu.SemaphoreType.DMA],
     )[0]
     full = lax.all_to_all(spread, "blk", 0, 0, tiled=True).reshape(width, cases)
     outs = [shaped((counts[0], cases), F32)]
@@ -560,13 +576,14 @@
     y0, *base = kernel_call(
         functools.partial(subtree_kernel, infos, starts[1:]),
         outs,
-        [full, (inverse, None), rhs] + hbm([dense[0, above] for above in uppers]),
+        [full, (inverse, None), (rhs, None)] + hbm([dense[0, above] for above in uppers]),
         scalars=at,
         scratch=[
             pltpu.VMEM((cases, width), F32),
             matrix_scratch,
             pltpu.VMEM((depth, counts[0], width), BF16),
-            pltpu.SemaphoreType.DMA((GROUPS * (1 + depth),)),
+            pltpu.VMEM(rhs.shape, F32),
+            pltpu.SemaphoreType.DMA((1 + GROUPS * (1 + depth),)),
         ],
         flops=2 * (1 + depth) * counts[0] * width * cases,
         stay=[True, False, False] + [True, True] * (depth - 1),
@@ -626,8 +643,7 @@
             parts = kernel_call(
                 functools.partial(top_kernel, info),
                 [shaped((info.cells, info.chunk, info.cell_rows), BF16)],
-                [gathered] + hbm(inverse_pieces[level]),
-                scratch=[cell_scratch(info), pltpu.SemaphoreType.DMA((count,))],
+                [gathered] + [(piece, True) for piece in inverse_pieces[level]],
                 flops=4 * size,
                 stay=[False],
             )[0]
@@ -639,17 +655,23 @@
                 shaped((info.cell_rows, info.chunk), F32),
                 shaped((above.targets, above.chunk, above.cell_rows), BF16),
             ],
-            [gathered, base[2 * level], received[level]]
-            + hbm(inverse_pieces[level])
-            + [ys[j] for j in range(1, level)]
-            + hbm([dense[j, level + 1] for j in range(1, level + 1)]),
+            [gathered]
+            + hbm(
+                [base[2 * level], received[level]]
+                + inverse_pieces[level]
+                + [ys[j] for j in range(1, level)]
+                + [dense[j, level + 1] for j in range(1, level + 1)]
+            ),
             scalars=at,
             scratch=[
                 pltpu.VMEM((above.chunk * above.pair_x, width), F32),
                 cell_scratch(info),
-                pltpu.SemaphoreType.DMA((count + GROUPS * level,)),
+                pltpu.VMEM((above.targets, above.chunk, above.cell_rows), BF16),
+                pltpu.VMEM((above.targets, above.chunk, above.cell_rows), BF16),
+                pltpu.SemaphoreType.DMA((count + GROUPS * level + 1 + level,)),
             ]
-            + [cell_scratch(infos[j - 1]) for j in range(1, level + 1)],
+            + [cell_scratch(infos[j - 1]) for j in range(1, level + 1)]
+            + [pltpu.VMEM(ys[j].shape, F32) for j in range(1, level)],
             flops=4 * size,
         )
 
@@ -664,12 +686,15 @@
             parts = kernel_call(
                 functools.partial(backward_kernel, infos, level),
                 [shaped((info.cells, info.chunk, info.cell_rows), BF16)],
-                [ys[level]]
-                + hbm(inverse_pieces[level])
+                hbm([ys[level]] + inverse_pieces[level])
                 + [solved[above] for above in higher]
                 + hbm([dense[level, above] for above in higher]),
                 scalars=at,
-                scratch=[cell_scratch(info), pltpu.SemaphoreType.DMA((count + GROUPS * len(higher),))]
+                scratch=[
+                    cell_scratch(info),
+                    pltpu.VMEM(ys[level].shape, F32),
+                    pltpu.SemaphoreType.DMA((1 + count + GROUPS * len(higher),)),
+                ]
                 + [cell_scratch(info)] * len(higher),
                 flops=4 * info.cell_rows * width * info.chunk,
                 stay=[False],
@@ -681,12 +706,13 @@
             z0 = kernel_call(
                 functools.partial(subtract_kernel, info),
                 [shaped((counts[0], cases), F32)],
-                [z0, (dense[0, level], None), solved[level], swapped[level]],
+                [(z0, None), (dense[0, level], None), solved[level], swapped[level]],
                 scalars=at,
                 scratch=[
                     pltpu.VMEM((cases, width), BF16),
                     matrix_scratch,
-                    pltpu.SemaphoreType.DMA((GROUPS,)),
+                    pltpu.VMEM((counts[0], cases), F32),
+                    pltpu.SemaphoreType.DMA((1 + GROUPS,)),
                 ],
                 flops=2 * counts[0] * width * cases,
             )[0]
@@ -694,13 +720,14 @@
     part = kernel_call(
         functools.partial(last_kernel, infos[0]),
         [shaped((blocks, cases, counts[0]), BF16)],
-        [z0, (dense[0, 1], None), solved[1], swapped[1], (inverse, None)],
+        [(z0, None), (dense[0, 1], None), solved[1], swapped[1], (inverse, None)],
         scalars=at,
         scratch=[
             pltpu.VMEM((cases, width), BF16),
             matrix_scratch,
             matrix_scratch,
-            pltpu.SemaphoreType.DMA((2 * GROUPS,)),
+            pltpu.VMEM((counts[0], cases), F32),
+            pltpu.SemaphoreType.DMA((1 + 2 * GROUPS,)),
         ],
         flops=4 * counts[0] * width * cases,
     )[0]
@@ -725,9 +752,7 @@
             core == 0, jnp.stack([mine, other], 1), jnp.stack([other, mine], 1)
         )
         outputs.append(rows.reshape(cases, info.rows).T)
-    out = kernel_call(
-        output_kernel, [shaped((sum(counts), cases), F32)], [parts] + outputs
-    )[0]
+    out = kernel_call(output_kernel, [shaped((sum(counts), cases), F32)], [parts] + outputs)[0]
     return out[None, None]
 
 

time: 174 us -> 171 us (0.983)
  Pallas kernels: 34.7 us -> 32.4 us
    pallas_call x14, Pallas kernels: 34.7 us -> 32.4 us  [kernel_call(): pl.pallas_call(body if scalars is None else lambda *refs: body(scalars(),...]
    unnamed x36 -> x26, local copies, waits for them, and re-layouts: 2.66 us -> 0.44 us
  transfers between devices with their start and end apart: 24 -> 24, of which waited for: 8 -> 9; matrix products, arithmetic and copies ran while one was open for 2% -> 2% of each run, Pallas kernels for 12% -> 11%
where the time goes in v3:
time: 171 us; the launch traced here: 170 us
  waiting for transfers between devices  63.3 us (37%)
  starting transfers between devices  40.3 us (24%)
  Pallas kernels  32.4 us (19%)
  blocking collectives  29.1 us (17%)
  local copies, waits for them, and re-layouts  3.52 us (2%)
    pallas_call x14, Pallas kernels, kernel_call(): pl.pallas_call(body if scalars is None else lambda *refs: body(scalars(),...  32.4 us
    ppermute x17, waiting for transfers between devices, swap(): return lax.ppermute(value, axis, [(i, i ^ bit) for i in range(size)])  18.3 us
    all_to_all x2, blocking collectives, exchange_inner(): lax.all_to_all(value, 'blk', 0, 0, axis_index_groups=info.inner_blk, tile...  17.1 us
    all_to_all x2, waiting for transfers between devices, exchange_outer(): return lax.all_to_all(value, 'blk', 0, 0, tiled=True)  15.9 us
    all_to_all x1, waiting for transfers between devices, solve(): parts = lax.all_to_all(part, 'blk', 0, 0, tiled=True)  15 us
    all_to_all x1, blocking collectives, exchange_outer(): lax.all_to_all(value, ('leaf', 'blk'), 0, 0, axis_index_groups=infos[leve...  12 us
    all_to_all x2, starting transfers between devices, exchange_outer(): return lax.all_to_all(value, 'blk', 0, 0, tiled=True)  8.03 us
    all_to_all x2, starting transfers between devices, exchange_inner(): lax.all_to_all(value, 'blk', 0, 0, axis_index_groups=info.inner_blk, tile...  7.86 us
  transfers between devices with their start and end apart: 24, of which 9 were waited for; matrix products, arithmetic and copies ran while one was open for 2% of the time, Pallas kernels for 11%

profile of v3, /device:TPU:0, one launch (start us, length us, event | category | flops | bytes accessed | tf_op | source)
XLA Modules:
  0.0 169.7 jit_solution(13940425680247480972)
XLA Ops:
  0.0 1.9 %shard_map.46 = bf16[8,256,128]{2,1,0:T(8,128)(2,1)} custom-call(f32[448,128]{1,0:T(8,128)} %bitcast.45), custom_call_target="tpu_custom_call" | custom-call | bytes 753664 | tf_op jit(solution)/shard_map/pallas_call | solution.py:45
  1.9 7.3 %all-to-all-start = ((bf16[8,256,128]{2,1,0:T(8,128)(2,1)}), bf16[8,256,128]{2,1,0:T(8,128)(2,1)S(1)}, u32[]{:S(2)}, u32[]{:S(2)}) async-start(bf16[8,256,128]{2,1,0:T(8,128)(2,1)} %shard_map.46), calls=%async_computation | async-start | bytes 1048576 | tf_op jit(solution)/shard_map/all_to_all | solution.py:570
  9.2 1.1 slice_bitcast_fusion.refs_3_.refs_1_
  10.3 2.1 %collective-permute-start.2 = (bf16[128,2048]{1,0:T(8,128)(2,1)S(1)}, bf16[128,2048]{1,0:T(8,128)(2,1)S(1)}, u32[]{:S(2)}, u32[]{:S(2)}) collective-permute-start(bf16[128,2048]{1,0:T(8,128)(2,1)S(1)} %slice_bitcast_fusion.refs_3_.refs_1_), channel_id=1, source_target_pairs={{0,1},{1,0},{2,3},{3,2},{4,5},{5,4},{6,7},{7,6},{8,9},{9,8},{10,11... | collective-permute-start | bytes 1572872 | tf_op jit(solution)/shard_map/ppermute | solution.py:515
  12.5 3.4 %shard_map.47 = (bf16[256,2048]{1,0:T(8,128)(2,1)}, bf16[256,2048]{1,0:T(8,128)(2,1)}) custom-call(s32[10,1024]{1,0:T(8,128)S(1)} %copy-done.1, bf16[640,1024]{1,0:T(8,128)(2,1)S(1)} %bitcast.42), custom_call_target="tpu_custom_call" | custom-call | flops 2147483648 | bytes 3448832 | tf_op jit(solution)/shard_map/pallas_call | solution.py:45
  15.9 7.8 %all-to-all-done = bf16[8,256,128]{2,1,0:T(8,128)(2,1)S(1)} async-done(((bf16[8,256,128]{2,1,0:T(8,128)(2,1)}), bf16[8,256,128]{2,1,0:T(8,128)(2,1)S(1)}, u32[]{:S(2)}, u32[]{:S(2)}) %all-to-all-start) | async-done | bytes 524320 | tf_op jit(solution)/shard_map/all_to_all | solution.py:570
  23.7 4.0 %shard_map.48 = (f32[256,128]{1,0:T(8,128)}, bf16[8,32,512]{2,1,0:T(8,128)(2,1)S(1)}, bf16[8,32,512]{2,1,0:T(8,128)(2,1)S(1)}, bf16[16,16,512]{2,1,0:T(8,128)(2,1)}, bf16[16,16,512]{2,1,0:T(8,128)(2,1)}) custom-call(bf16[2048,128]{1,0:T(8,128)(2,1)S(1)} %bitcast.36, bf16[448,2048]{1,0:T(8,128)(2,1)} %bitcast.43, f32[448,128]{1,0:T(8,128)} %bitcast.46, ...), custom_call_target="tpu_custom_call" | custom-call | flops 402653184 | bytes 5865472 | tf_op jit(solution)/shard_map/pallas_call | solution.py:45
  28.4 5.9 %collective-permute-done.5.refs_2_ = bf16[128,1024]{1,0:T(8,128)(2,1)S(1)} collective-permute-done((bf16[128,1024]{1,0:T(8,128)(2,1)S(1)}, bf16[128,1024]{1,0:T(8,128)(2,1)S(1)}, u32[]{:S(2)}, u32[]{:S(2)}) %collective-permute-start.5) | collective-permute-done | bytes 262176 | tf_op jit(solution)/shard_map/ppermute | solution.py:515
  35.6 4.6 %all-to-all-start.1 = ((bf16[8,32,512]{2,1,0:T(8,128)(2,1)}), bf16[8,32,512]{2,1,0:T(8,128)(2,1)S(1)}, u32[]{:S(2)}, u32[]{:S(2)}) async-start(bf16[8,32,512]{2,1,0:T(8,128)(2,1)} %add_convert_fusion), calls=%async_computation.1 | async-start | bytes 524288 | tf_op jit(solution)/shard_map/all_to_all | solution.py:524
  40.2 1.7 slice_bitcast_fusion.1.refs_0_
  41.9 7.8 %all-to-all-done.1.parts = bf16[8,32,512]{2,1,0:T(8,128)(2,1)S(1)} async-done(((bf16[8,32,512]{2,1,0:T(8,128)(2,1)}), bf16[8,32,512]{2,1,0:T(8,128)(2,1)S(1)}, u32[]{:S(2)}, u32[]{:S(2)}) %all-to-all-start.1) | async-done | bytes 262176 | tf_op jit(solution)/shard_map/all_to_all | solution.py:524
  50.4 3.3 %all-to-all-start.2 = ((bf16[4,32,512]{2,1,0:T(8,128)(2,1)}), bf16[4,32,512]{2,1,0:T(8,128)(2,1)S(1)}, u32[]{:S(2)}, u32[]{:S(2)}) async-start(bf16[4,32,512]{2,1,0:T(8,128)(2,1)} %shard_map.49), calls=%async_computation.2 | async-start | bytes 262144 | tf_op jit(solution)/shard_map/all_to_all | solution.py:537
  53.8 1.6 collective-permute-start.8
  55.3 3.7 %shard_map.50.refs_7_.refs_6_ = bf16[512,2048]{1,0:T(8,128)(2,1)} custom-call(s32[10,1024]{1,0:T(8,128)S(1)} %copy-done.1, bf16[128,1024]{1,0:T(8,128)(2,1)S(1)} %slice_bitcast_fusion.2.refs_1_, bf16[128,1024]{1,0:T(8,128)(2,1)S(1)} %collective-permute-done.5.refs_2_, bf16[128,1024]{1,0:T(8,128)(2,1)S(1)} %collective-permute-done.6.refs_3_, ...), custom_call_target="tpu_custom_call" | custom-call | flops 2147483648 | bytes 3186688 | tf_op jit(solution)/shard_map/pallas_call | solution.py:45
  60.1 3.9 %shard_map.51 = (f32[512,32]{1,0:T(8,128)}, bf16[16,16,512]{2,1,0:T(8,128)(2,1)}) custom-call(bf16[4,32,512]{2,1,0:T(8,128)(2,1)S(1)} %all-to-all-done.2.refs_0_, bf16[16,16,512]{2,1,0:T(8,128)(2,1)} %get-tuple-element.19.refs_1_, bf16[16,16,512]{2,1,0:T(8,128)(2,1)} %collective-permute-done.1.refs_2_, bf16[128,2048]{1,0:T(8,128)(2,1)} %copy-done.2, ...), custom_call_target="tpu_custom_call" | custom-call | flops 134217728 | bytes 5177344 | tf_op jit(solution)/shard_map/pallas_call | solution.py:45
  64.0 6.0 %all-to-all-start.3 = ((bf16[16,16,512]{2,1,0:T(8,128)(2,1)}), bf16[16,16,512]{2,1,0:T(8,128)(2,1)S(1)}, u32[]{:S(2)}, u32[]{:S(2)}) async-start(bf16[16,16,512]{2,1,0:T(8,128)(2,1)} %get-tuple-element.21), calls=%async_computation.3 | async-start | bytes 524288 | tf_op jit(solution)/shard_map/all_to_all | solution.py:525
  70.0 2.0 %collective-permute-start.9 = (bf16[64,2048]{1,0:T(8,128)(2,1)S(1)}, bf16[64,2048]{1,0:T(8,128)(2,1)S(1)}, u32[]{:S(2)}, u32[]{:S(2)}) collective-permute-start(bf16[64,2048]{1,0:T(8,128)(2,1)S(1)} %copy-done.6), channel_id=1, source_target_pairs={{0,1},{1,0},{2,3},{3,2},{4,5},{5,4},{6,7},{7,6},{8,9},{9,8},{10,11... | collective-permute-start | bytes 786440 | tf_op jit(solution)/shard_map/ppermute | solution.py:515
  72.6 9.0 %collective-permute-done.9.refs_2_ = bf16[64,2048]{1,0:T(8,128)(2,1)S(1)} collective-permute-done((bf16[64,2048]{1,0:T(8,128)(2,1)S(1)}, bf16[64,2048]{1,0:T(8,128)(2,1)S(1)}, u32[]{:S(2)}, u32[]{:S(2)}) %collective-permute-start.9) | collective-permute-done | bytes 262176 | tf_op jit(solution)/shard_map/ppermute | solution.py:515
  81.5 3.5 %collective-permute-done.10.refs_3_ = bf16[64,2048]{1,0:T(8,128)(2,1)S(1)} collective-permute-done((bf16[64,2048]{1,0:T(8,128)(2,1)}, bf16[64,2048]{1,0:T(8,128)(2,1)S(1)}, u32[]{:S(2)}, u32[]{:S(2)}) %collective-permute-start.10) | collective-permute-done | bytes 262176 | tf_op jit(solution)/shard_map/ppermute | solution.py:515
  85.7 4.5 %all-to-all-start.4 = ((bf16[4,16,512]{2,1,0:T(8,128)(2,1)}), bf16[4,16,512]{2,1,0:T(8,128)(2,1)S(1)}, u32[]{:S(2)}, u32[]{:S(2)}) async-start(bf16[4,16,512]{2,1,0:T(8,128)(2,1)} %shard_map.52), calls=%async_computation.4 | async-start | bytes 131072 | tf_op jit(solution)/shard_map/all_to_all | solution.py:537
  90.3 5.7 %all-to-all-done.4.gathered = bf16[4,16,512]{2,1,0:T(8,128)(2,1)S(1)} async-done(((bf16[4,16,512]{2,1,0:T(8,128)(2,1)}), bf16[4,16,512]{2,1,0:T(8,128)(2,1)S(1)}, u32[]{:S(2)}, u32[]{:S(2)}) %all-to-all-start.4) | async-done | bytes 65568 | tf_op jit(solution)/shard_map/all_to_all | solution.py:537
  96.1 2.6 %shard_map.53 = bf16[4,16,512]{2,1,0:T(8,128)(2,1)S(1)} custom-call(bf16[4,16,512]{2,1,0:T(8,128)(2,1)S(1)} %all-to-all-done.4.gathered, bf16[64,2048]{1,0:T(8,128)(2,1)} %slice_bitcast_fusion.1.refs_0_, bf16[64,2048]{1,0:T(8,128)(2,1)} %collective-permute-done.8.refs_1_, bf16[64,2048]{1,0:T(8,128)(2,1)} %copy-done.7, bf16[64,2048]{1,0:T(8,128)(2,1)} %copy-done.8, ...), custom_call_target="tpu_custom_call" | custom-call | flops 67108864 | bytes 2228224 | tf_op jit(solution)/shard_map/pallas_call | solution.py:45
  98.6 8.1 %all_to_all.50.parts = bf16[4,16,512]{2,1,0:T(8,128)(2,1)S(1)} all-to-all(bf16[4,16,512]{2,1,0:T(8,128)(2,1)S(1)} %shard_map.53), channel_id=1, replica_groups={{0,2,4,6},{1,3,5,7},{8,10,12,14},{9,11,13,15},{16,18,20,22},{17,19,21,2..., dimensions={0} | all-to-all | bytes 131072 | tf_op jit(solution)/shard_map/all_to_all | solution.py:537
  107.5 12.0 %all_to_all.51.refs_2_.refs_5_ = bf16[16,16,512]{2,1,0:T(8,128)(2,1)S(1)} all-to-all(bf16[16,16,512]{2,1,0:T(8,128)(2,1)} %shard_map.54), channel_id=1, replica_groups={{0,1,2,3,4,5,6,7,16,17,18,19,20,21,22,23},{8,9,10,11,12,13,14,15,24,25,..., dimensions={0} | all-to-all | bytes 524288 | tf_op jit(solution)/shard_map/all_to_all | solution.py:525
  119.5 3.3 %shard_map.56 = bf16[4,32,512]{2,1,0:T(8,128)(2,1)S(1)} custom-call(f32[512,32]{1,0:T(8,128)} %get-tuple-element.22.refs_0_, bf16[128,2048]{1,0:T(8,128)(2,1)} %copy-done.2, bf16[128,2048]{1,0:T(8,128)(2,1)} %copy-done.3, bf16[128,2048]{1,0:T(8,128)(2,1)} %copy-done.4, bf16[128,2048]{1,0:T(8,128)(2,1)} %copy-done.5, ...), custom_call_target="tpu_custom_call" | custom-call | flops 134217728 | bytes 4653056 | tf_op jit(solution)/shard_map/pallas_call | solution.py:45
  122.8 9.0 %all_to_all.52.parts = bf16[4,32,512]{2,1,0:T(8,128)(2,1)S(1)} all-to-all(bf16[4,32,512]{2,1,0:T(8,128)(2,1)S(1)} %shard_map.56), channel_id=1, replica_groups={{0,2,4,6},{1,3,5,7},{8,10,12,14},{9,11,13,15},{16,18,20,22},{17,19,21,2..., dimensions={0} | all-to-all | bytes 262144 | tf_op jit(solution)/shard_map/all_to_all | solution.py:537
  132.5 3.4 %all-to-all-start.8 = ((bf16[8,32,512]{2,1,0:T(8,128)(2,1)}), bf16[8,32,512]{2,1,0:T(8,128)(2,1)S(1)}, u32[]{:S(2)}, u32[]{:S(2)}) async-start(bf16[8,32,512]{2,1,0:T(8,128)(2,1)} %shard_map.57), calls=%async_computation.8 | async-start | bytes 524288 | tf_op jit(solution)/shard_map/all_to_all | solution.py:524
  136.0 8.1 %all-to-all-done.8.refs_2_ = bf16[8,32,512]{2,1,0:T(8,128)(2,1)S(1)} async-done(((bf16[8,32,512]{2,1,0:T(8,128)(2,1)}), bf16[8,32,512]{2,1,0:T(8,128)(2,1)S(1)}, u32[]{:S(2)}, u32[]{:S(2)}) %all-to-all-start.8) | async-done | bytes 262176 | tf_op jit(solution)/shard_map/all_to_all | solution.py:524
  144.1 2.6 %shard_map.55.refs_0_ = f32[256,128]{1,0:T(8,128)} custom-call(f32[256,128]{1,0:T(8,128)} %get-tuple-element.16.refs_0_, bf16[256,2048]{1,0:T(8,128)(2,1)} %get-tuple-element.15.refs_4_.refs_1_, bf16[16,16,512]{2,1,0:T(8,128)(2,1)S(1)} %all_to_all.51.refs_2_.refs_5_, bf16[16,16,512]{2,1,0:T(8,128)(2,1)S(1)} %collective-permute-done.15.refs_3_), custom_call_target="tpu_custom_call" | custom-call | flops 134217728 | bytes 1835008 | tf_op jit(solution)/shard_map/pallas_call | solution.py:45
  146.7 3.3 %shard_map.58 = bf16[8,128,256]{2,1,0:T(8,128)(2,1)} custom-call(f32[256,128]{1,0:T(8,128)} %shard_map.55.refs_0_, bf16[256,2048]{1,0:T(8,128)(2,1)} %get-tuple-element.14.refs_3_.refs_1_, bf16[8,32,512]{2,1,0:T(8,128)(2,1)S(1)} %all-to-all-done.8.refs_2_, bf16[8,32,512]{2,1,0:T(8,128)(2,1)S(1)} %collective-permute-done.16.refs_3_, bf16[448,2048]{1,0:T(8,128)(2,1)} %bitcast.44), custom_call_target="tpu_custom_call" | custom-call | flops 268435456 | bytes 4063232 | tf_op jit(solution)/shard_map/pallas_call | solution.py:45
  150.0 3.5 %all-to-all-start.9 = ((bf16[8,128,256]{2,1,0:T(8,128)(2,1)}), bf16[8,128,256]{2,1,0:T(8,128)(2,1)S(1)}, u32[]{:S(2)}, u32[]{:S(2)}) async-start(bf16[8,128,256]{2,1,0:T(8,128)(2,1)} %shard_map.58), calls=%async_computation.9 | async-start | bytes 1048576 | tf_op jit(solution)/shard_map/all_to_all | solution.py:734
  153.9 15.0 %all-to-all-done.9.parts = bf16[8,128,256]{2,1,0:T(8,128)(2,1)S(1)} async-done(((bf16[8,128,256]{2,1,0:T(8,128)(2,1)}), bf16[8,128,256]{2,1,0:T(8,128)(2,1)S(1)}, u32[]{:S(2)}, u32[]{:S(2)}) %all-to-all-start.9) | async-done | bytes 524320 | tf_op jit(solution)/shard_map/all_to_all | solution.py:734
  (71 shorter events, 7.9 us)
Async XLA Ops:
  0.0 12.4 %copy-start = (bf16[1,1,640,1024]{3,2,1,0:T(8,128)(2,1)S(1)}, bf16[1,1,640,1024]{3,2,1,0:T(8,128)(2,1)}, u32[]{:S(2)}) copy-start(bf16[1,1,640,1024]{3,2,1,0:T(8,128)(2,1)} %param.6) | copy-start | bytes 3932164
  0.0 12.5 %copy-start.1 = (s32[10,1024]{1,0:T(8,128)S(1)}, s32[10,1024]{1,0:T(8,128)}, u32[]{:S(2)}) copy-start(s32[10,1024]{1,0:T(8,128)} %refs_0_.3) | copy-start | bytes 122884
  1.9 21.8 %all-to-all-start = ((bf16[8,256,128]{2,1,0:T(8,128)(2,1)}), bf16[8,256,128]{2,1,0:T(8,128)(2,1)S(1)}, u32[]{:S(2)}, u32[]{:S(2)}) async-start(bf16[8,256,128]{2,1,0:T(8,128)(2,1)} %shard_map.46), calls=%async_computation | async-start | bytes 1048576 | tf_op jit(solution)/shard_map/all_to_all | solution.py:570
  10.3 17.5 %copy-start.2 = (bf16[128,2048]{1,0:T(8,128)(2,1)}, bf16[128,2048]{1,0:T(8,128)(2,1)S(1)}, u32[]{:S(2)}) copy-start(bf16[128,2048]{1,0:T(8,128)(2,1)S(1)} %slice_bitcast_fusion.refs_3_.refs_1_) | copy-start | bytes 1572868
  10.3 24.0 %collective-permute-start.2 = (bf16[128,2048]{1,0:T(8,128)(2,1)S(1)}, bf16[128,2048]{1,0:T(8,128)(2,1)S(1)}, u32[]{:S(2)}, u32[]{:S(2)}) collective-permute-start(bf16[128,2048]{1,0:T(8,128)(2,1)S(1)} %slice_bitcast_fusion.refs_3_.refs_1_), channel_id=1, source_target_pairs={{0,1},{1,0},{2,3},{3,2},{4,5},{5,4},{6,7},{7,6},{8,9},{9,8},{10,11... | collective-permute-start | bytes 1572872 | tf_op jit(solution)/shard_map/ppermute | solution.py:515
  12.4 21.9 %collective-permute-start.5 = (bf16[128,1024]{1,0:T(8,128)(2,1)S(1)}, bf16[128,1024]{1,0:T(8,128)(2,1)S(1)}, u32[]{:S(2)}, u32[]{:S(2)}) collective-permute-start(bf16[128,1024]{1,0:T(8,128)(2,1)S(1)} %slice_bitcast_fusion.2.refs_1_), channel_id=1, source_target_pairs={{0,1},{1,0},{2,3},{3,2},{4,5},{5,4},{6,7},{7,6},{8,9},{9,8},{10,11... | collective-permute-start | bytes 786440 | tf_op jit(solution)/shard_map/ppermute | solution.py:515
  27.7 7.1 %collective-permute-start = (bf16[8,32,512]{2,1,0:T(8,128)(2,1)S(1)}, bf16[8,32,512]{2,1,0:T(8,128)(2,1)S(1)}, u32[]{:S(2)}, u32[]{:S(2)}) collective-permute-start(bf16[8,32,512]{2,1,0:T(8,128)(2,1)S(1)} %get-tuple-element.18), channel_id=1, source_target_pairs={{0,8},{8,0},{16,24},{24,16},{1,9},{9,1},{17,25},{25,17},{2,10},{10... | collective-permute-start | bytes 786440 | tf_op jit(solution)/shard_map/ppermute | solution.py:515
  27.8 31.3 %collective-permute-start.3 = (bf16[128,2048]{1,0:T(8,128)(2,1)S(1)}, bf16[128,2048]{1,0:T(8,128)(2,1)S(1)}, u32[]{:S(2)}, u32[]{:S(2)}) collective-permute-start(bf16[128,2048]{1,0:T(8,128)(2,1)S(1)} %slice_bitcast_fusion.refs_3_.refs_1_), channel_id=1, source_target_pairs={{0,8},{8,0},{16,24},{24,16},{1,9},{9,1},{17,25},{25,17},{2,10},{10... | collective-permute-start | bytes 1572872 | tf_op jit(solution)/shard_map/ppermute | solution.py:515
  28.3 25.5 %collective-permute-start.6 = (bf16[128,1024]{1,0:T(8,128)(2,1)S(1)}, bf16[128,1024]{1,0:T(8,128)(2,1)S(1)}, u32[]{:S(2)}, u32[]{:S(2)}) collective-permute-start(bf16[128,1024]{1,0:T(8,128)(2,1)S(1)} %slice_bitcast_fusion.2.refs_1_), channel_id=1, source_target_pairs={{0,8},{8,0},{16,24},{24,16},{1,9},{9,1},{17,25},{25,17},{2,10},{10... | collective-permute-start | bytes 786440 | tf_op jit(solution)/shard_map/ppermute | solution.py:515
  34.3 21.1 %collective-permute-start.7 = (bf16[128,1024]{1,0:T(8,128)(2,1)S(1)}, bf16[128,1024]{1,0:T(8,128)(2,1)S(1)}, u32[]{:S(2)}, u32[]{:S(2)}) collective-permute-start(bf16[128,1024]{1,0:T(8,128)(2,1)S(1)} %collective-permute-done.5.refs_2_), channel_id=1, source_target_pairs={{0,8},{8,0},{16,24},{24,16},{1,9},{9,1},{17,25},{25,17},{2,10},{10... | collective-permute-start | bytes 786440 | tf_op jit(solution)/shard_map/ppermute | solution.py:515
  34.3 24.8 %copy-start.3 = (bf16[128,2048]{1,0:T(8,128)(2,1)}, bf16[128,2048]{1,0:T(8,128)(2,1)S(1)}, u32[]{:S(2)}) copy-start(bf16[128,2048]{1,0:T(8,128)(2,1)S(1)} %collective-permute-done.2.refs_4_.refs_2_) | copy-start | bytes 1572868
  34.3 24.8 %collective-permute-start.4 = (bf16[128,2048]{1,0:T(8,128)(2,1)S(1)}, bf16[128,2048]{1,0:T(8,128)(2,1)S(1)}, u32[]{:S(2)}, u32[]{:S(2)}) collective-permute-start(bf16[128,2048]{1,0:T(8,128)(2,1)S(1)} %collective-permute-done.2.refs_4_.refs_2_), channel_id=1, source_target_pairs={{0,8},{8,0},{16,24},{24,16},{1,9},{9,1},{17,25},{25,17},{2,10},{10... | collective-permute-start | bytes 1572872 | tf_op jit(solution)/shard_map/ppermute | solution.py:515
  34.8 24.3 %collective-permute-start.1 = (bf16[16,16,512]{2,1,0:T(8,128)(2,1)}, bf16[16,16,512]{2,1,0:T(8,128)(2,1)}, u32[]{:S(2)}, u32[]{:S(2)}) collective-permute-start(bf16[16,16,512]{2,1,0:T(8,128)(2,1)} %get-tuple-element.20), channel_id=1, source_target_pairs={{0,8},{8,0},{16,24},{24,16},{1,9},{9,1},{17,25},{25,17},{2,10},{10... | collective-permute-start | bytes 786440 | tf_op jit(solution)/shard_map/ppermute | solution.py:515
  35.6 14.1 %all-to-all-start.1 = ((bf16[8,32,512]{2,1,0:T(8,128)(2,1)}), bf16[8,32,512]{2,1,0:T(8,128)(2,1)S(1)}, u32[]{:S(2)}, u32[]{:S(2)}) async-start(bf16[8,32,512]{2,1,0:T(8,128)(2,1)} %add_convert_fusion), calls=%async_computation.1 | async-start | bytes 524288 | tf_op jit(solution)/shard_map/all_to_all | solution.py:524
  50.4 9.2 %all-to-all-start.2 = ((bf16[4,32,512]{2,1,0:T(8,128)(2,1)}), bf16[4,32,512]{2,1,0:T(8,128)(2,1)S(1)}, u32[]{:S(2)}, u32[]{:S(2)}) async-start(bf16[4,32,512]{2,1,0:T(8,128)(2,1)} %shard_map.49), calls=%async_computation.2 | async-start | bytes 262144 | tf_op jit(solution)/shard_map/all_to_all | solution.py:537
  53.8 18.2 %collective-permute-start.8 = (bf16[64,2048]{1,0:T(8,128)(2,1)}, bf16[64,2048]{1,0:T(8,128)(2,1)}, u32[]{:S(2)}, u32[]{:S(2)}) collective-permute-start(bf16[64,2048]{1,0:T(8,128)(2,1)} %slice_bitcast_fusion.1.refs_0_), channel_id=1, source_target_pairs={{0,16},{8,24},{16,0},{24,8},{1,17},{9,25},{17,1},{25,9},{2,18},{10... | collective-permute-start | bytes 786440 | tf_op jit(solution)/shard_map/ppermute | solution.py:515
  60.1 9.9 %copy-start.6 = (bf16[64,2048]{1,0:T(8,128)(2,1)S(1)}, bf16[64,2048]{1,0:T(8,128)(2,1)}, u32[]{:S(2)}) copy-start(bf16[64,2048]{1,0:T(8,128)(2,1)} %slice_bitcast_fusion.1.refs_0_) | copy-start | bytes 786436
  64.0 21.0 %all-to-all-start.3 = ((bf16[16,16,512]{2,1,0:T(8,128)(2,1)}), bf16[16,16,512]{2,1,0:T(8,128)(2,1)S(1)}, u32[]{:S(2)}, u32[]{:S(2)}) async-start(bf16[16,16,512]{2,1,0:T(8,128)(2,1)} %get-tuple-element.21), calls=%async_computation.3 | async-start | bytes 524288 | tf_op jit(solution)/shard_map/all_to_all | solution.py:525
  70.0 11.6 %collective-permute-start.9 = (bf16[64,2048]{1,0:T(8,128)(2,1)S(1)}, bf16[64,2048]{1,0:T(8,128)(2,1)S(1)}, u32[]{:S(2)}, u32[]{:S(2)}) collective-permute-start(bf16[64,2048]{1,0:T(8,128)(2,1)S(1)} %copy-done.6), channel_id=1, source_target_pairs={{0,1},{1,0},{2,3},{3,2},{4,5},{5,4},{6,7},{7,6},{8,9},{9,8},{10,11... | collective-permute-start | bytes 786440 | tf_op jit(solution)/shard_map/ppermute | solution.py:515
  71.9 13.1 %collective-permute-start.10 = (bf16[64,2048]{1,0:T(8,128)(2,1)}, bf16[64,2048]{1,0:T(8,128)(2,1)S(1)}, u32[]{:S(2)}, u32[]{:S(2)}) collective-permute-start(bf16[64,2048]{1,0:T(8,128)(2,1)} %collective-permute-done.8.refs_1_), channel_id=1, source_target_pairs={{0,1},{1,0},{2,3},{3,2},{4,5},{5,4},{6,7},{7,6},{8,9},{9,8},{10,11... | collective-permute-start | bytes 786440 | tf_op jit(solution)/shard_map/ppermute | solution.py:515
  72.1 18.2 %collective-permute-start.11 = (bf16[64,2048]{1,0:T(8,128)(2,1)S(1)}, bf16[64,2048]{1,0:T(8,128)(2,1)S(1)}, u32[]{:S(2)}, u32[]{:S(2)}) collective-permute-start(bf16[64,2048]{1,0:T(8,128)(2,1)S(1)} %copy-done.6), channel_id=1, source_target_pairs={{0,8},{8,0},{16,24},{24,16},{1,9},{9,1},{17,25},{25,17},{2,10},{10... | collective-permute-start | bytes 786440 | tf_op jit(solution)/shard_map/ppermute | solution.py:515
  72.1 18.2 %collective-permute-start.12 = (bf16[64,2048]{1,0:T(8,128)(2,1)}, bf16[64,2048]{1,0:T(8,128)(2,1)S(1)}, u32[]{:S(2)}, u32[]{:S(2)}) collective-permute-start(bf16[64,2048]{1,0:T(8,128)(2,1)} %collective-permute-done.8.refs_1_), channel_id=1, source_target_pairs={{0,8},{8,0},{16,24},{24,16},{1,9},{9,1},{17,25},{25,17},{2,10},{10... | collective-permute-start | bytes 786440 | tf_op jit(solution)/shard_map/ppermute | solution.py:515
  81.5 14.5 %copy-start.7 = (bf16[64,2048]{1,0:T(8,128)(2,1)}, bf16[64,2048]{1,0:T(8,128)(2,1)S(1)}, u32[]{:S(2)}) copy-start(bf16[64,2048]{1,0:T(8,128)(2,1)S(1)} %collective-permute-done.9.refs_2_) | copy-start | bytes 786436
  81.5 8.8 %collective-permute-start.13 = (bf16[64,2048]{1,0:T(8,128)(2,1)S(1)}, bf16[64,2048]{1,0:T(8,128)(2,1)S(1)}, u32[]{:S(2)}, u32[]{:S(2)}) collective-permute-start(bf16[64,2048]{1,0:T(8,128)(2,1)S(1)} %collective-permute-done.9.refs_2_), channel_id=1, source_target_pairs={{0,8},{8,0},{16,24},{24,16},{1,9},{9,1},{17,25},{25,17},{2,10},{10... | collective-permute-start | bytes 786440 | tf_op jit(solution)/shard_map/ppermute | solution.py:515
  85.0 11.0 %copy-start.8 = (bf16[64,2048]{1,0:T(8,128)(2,1)}, bf16[64,2048]{1,0:T(8,128)(2,1)S(1)}, u32[]{:S(2)}) copy-start(bf16[64,2048]{1,0:T(8,128)(2,1)S(1)} %collective-permute-done.10.refs_3_) | copy-start | bytes 786436
  85.0 5.3 %collective-permute-start.14 = (bf16[64,2048]{1,0:T(8,128)(2,1)S(1)}, bf16[64,2048]{1,0:T(8,128)(2,1)S(1)}, u32[]{:S(2)}, u32[]{:S(2)}) collective-permute-start(bf16[64,2048]{1,0:T(8,128)(2,1)S(1)} %collective-permute-done.10.refs_3_), channel_id=1, source_target_pairs={{0,8},{8,0},{16,24},{24,16},{1,9},{9,1},{17,25},{25,17},{2,10},{10... | collective-permute-start | bytes 786440 | tf_op jit(solution)/shard_map/ppermute | solution.py:515
  85.7 10.3 %all-to-all-start.4 = ((bf16[4,16,512]{2,1,0:T(8,128)(2,1)}), bf16[4,16,512]{2,1,0:T(8,128)(2,1)S(1)}, u32[]{:S(2)}, u32[]{:S(2)}) async-start(bf16[4,16,512]{2,1,0:T(8,128)(2,1)} %shard_map.52), calls=%async_computation.4 | async-start | bytes 131072 | tf_op jit(solution)/shard_map/all_to_all | solution.py:537
  90.3 5.7 %copy-start.9 = (bf16[64,2048]{1,0:T(8,128)(2,1)}, bf16[64,2048]{1,0:T(8,128)(2,1)S(1)}, u32[]{:S(2)}) copy-start(bf16[64,2048]{1,0:T(8,128)(2,1)S(1)} %collective-permute-done.11.refs_4_) | copy-start | bytes 786436
  132.5 11.6 %all-to-all-start.8 = ((bf16[8,32,512]{2,1,0:T(8,128)(2,1)}), bf16[8,32,512]{2,1,0:T(8,128)(2,1)S(1)}, u32[]{:S(2)}, u32[]{:S(2)}) async-start(bf16[8,32,512]{2,1,0:T(8,128)(2,1)} %shard_map.57), calls=%async_computation.8 | async-start | bytes 524288 | tf_op jit(solution)/shard_map/all_to_all | solution.py:524
  135.9 8.2 %collective-permute-start.15 = (bf16[16,16,512]{2,1,0:T(8,128)(2,1)S(1)}, bf16[16,16,512]{2,1,0:T(8,128)(2,1)S(1)}, u32[]{:S(2)}, u32[]{:S(2)}) collective-permute-start(bf16[16,16,512]{2,1,0:T(8,128)(2,1)S(1)} %all_to_all.51.refs_2_.refs_5_), channel_id=1, source_target_pairs={{0,8},{8,0},{16,24},{24,16},{1,9},{9,1},{17,25},{25,17},{2,10},{10... | collective-permute-start | bytes 786440 | tf_op jit(solution)/shard_map/ppermute | solution.py:515
  144.0 2.6 %collective-permute-start.16 = (bf16[8,32,512]{2,1,0:T(8,128)(2,1)S(1)}, bf16[8,32,512]{2,1,0:T(8,128)(2,1)S(1)}, u32[]{:S(2)}, u32[]{:S(2)}) collective-permute-start(bf16[8,32,512]{2,1,0:T(8,128)(2,1)S(1)} %all-to-all-done.8.refs_2_), channel_id=1, source_target_pairs={{0,8},{8,0},{16,24},{24,16},{1,9},{9,1},{17,25},{25,17},{2,10},{10... | collective-permute-start | bytes 786440 | tf_op jit(solution)/shard_map/ppermute | solution.py:515
  150.0 18.9 %all-to-all-start.9 = ((bf16[8,128,256]{2,1,0:T(8,128)(2,1)}), bf16[8,128,256]{2,1,0:T(8,128)(2,1)S(1)}, u32[]{:S(2)}, u32[]{:S(2)}) async-start(bf16[8,128,256]{2,1,0:T(8,128)(2,1)} %shard_map.58), calls=%async_computation.9 | async-start | bytes 1048576 | tf_op jit(solution)/shard_map/all_to_all | solution.py:734
  (5 other events, 19.0 us)

commit v4 on v3

--- a/solution.py
+++ b/solution.py
@@ -139,6 +139,7 @@
         self.targets = self.cells * self.pair_x * 2
         outer = []
         inner = []
+        middle = []
         for node in range(leaves >> level):
             base = node << level
             for side in range(2):
@@ -149,6 +150,14 @@
                         for b in range(blocks)
                     ]
                 )
+                for yb in range(2):
+                    middle.append(
+                        [
+                            (base + 2 * upper + side) * blocks + 2 * zb + yb
+                            for upper in range(1 << (level - 1))
+                            for zb in range(self.zbs)
+                        ]
+                    )
                 for xu in range(self.pair_x):
                     for yb in range(2):
                         inner.append(
@@ -160,6 +169,7 @@
                         )
         self.outer = outer
         self.inner = inner
+        self.middle = middle
         self.inner_blk = [[2 * zb + yb for zb in range(self.zbs)] for yb in range(2)]
 
     @property
@@ -195,6 +205,13 @@
     def lanes(self, cell):
         return slice(cell * self.cell_rows, (cell + 1) * self.cell_rows)
 
+    def slots(self):
+        for hi in range(self.his):
+            for xu in range(self.pair_x):
+                for zb in range(self.zbs):
+                    index = (hi * self.pair_x + xu) * self.zbs + zb
+                    yield hi * self.zbs + zb, xu, index
+
     def all_targets(self):
         for hi in range(self.his):
             for xu in range(self.pair_x):
@@ -234,8 +251,8 @@
 def subtree_kernel(infos, starts, at, full, inverse, rhs, *refs):
     depth = len(infos)
     sources = refs[:depth]
-    outs = refs[depth : depth + 1 + 2 * depth]
-    total, matrix, dense, rhs_copy, sems = refs[depth + 1 + 2 * depth :]
+    outs = refs[depth : depth + 2 + 2 * depth]
+    total, matrix, dense, rhs_copy, sems = refs[depth + 2 + 2 * depth :]
     loads = Loads(sems)
     rhs_load = loads.start([(rhs, rhs_copy)])
     groups = group_rows(matrix.shape[0])
@@ -258,7 +275,10 @@
     for g, rows in enumerate(groups):
         wait(first[g])
         y = mm(matrix[rows, :], full[...])
-        outs[0][rows, :] = y
+        cut = y.shape[1] // 2
+        low = at[YB] == 0
+        outs[0][rows, :] = jnp.where(low, y[:, :cut], y[:, cut:])
+        outs[1][rows, :] = jnp.where(low, y[:, cut:], y[:, :cut])
         rounded.append(y.astype(BF16))
     half = width // 2
     for n, info in enumerate(infos):
@@ -268,7 +288,7 @@
             term = accumulate(term, rounded[g], dense[n, rows, :])
         total[:, :half] = placed[n][0] - term[0]
         total[:, half:] = placed[n][1] - term[1]
-        mine, other = outs[1 + 2 * n], outs[2 + 2 * n]
+        mine, other = outs[2 + 2 * n], outs[3 + 2 * n]
         for cell, xu, yb, target in info.all_targets():
             for side, ref in ((core, mine), (1 - core, other)):
                 row = ((yb * 2 + side) * info.pair_x + xu) * info.chunk
@@ -387,13 +407,11 @@
         parts = []
         for hi in range(above.his):
             for zb in range(above.zbs):
+                first_slot = hi * above.pair_x * above.zbs + zb
                 if above.pair_x == info.pair_x:
-                    slot = ((hi * above.pair_x + at[XU]) * above.zbs + zb) * 2 + at[YB]
-                    parts.append(solved[n][slot])
+                    parts.append(solved[n][first_slot + at[XU] * above.zbs])
                 else:
-                    slots = [
-                        above.target(hi, xu, zb, 0) + at[YB] for xu in range(above.pair_x)
-                    ]
+                    slots = [first_slot + xu * above.zbs for xu in range(above.pair_x)]
                     parts.append(jnp.concatenate([solved[n][slot] for slot in slots], 0))
         vectors.append(jnp.concatenate(parts, 1))
     wait(y_load)
@@ -409,31 +427,32 @@
 
 
 def full_cases(info, core, mine, other, full):
-    for cell, xu, yb, target in info.all_targets():
+    for cell, xu, index in info.slots():
         for side, ref in ((core, mine), (1 - core, other)):
-            row = ((yb * 2 + side) * info.pair_x + xu) * info.chunk
-            row = pl.multiple_of(row, info.chunk)
-            full[pl.ds(row, info.chunk), info.lanes(cell)] = ref[target]
-
-
-def subtract_kernel(info, at, y_hbm, source, mine, other, out, full, dense, y, sems):
-    copies = Loads(sems)
-    y_load = copies.start([(y_hbm, y)])
-    loads = [start() for start in copies.groups([source], dense, GROUPS)]
+            row = pl.multiple_of((side * info.pair_x + xu) * info.chunk, info.chunk)
+            full[pl.ds(row, info.chunk), info.lanes(cell)] = ref[index]
+
+
+def subtract_kernel(info, count, at, own, near, mine, other, *refs):
+    y_parts = refs[:count]
+    out, full, dense, y, sems = refs[count:]
+    loads = Loads(sems)
+    y_load = loads.rows(y_parts, y)
+    copies = [start() for start in loads.groups([own, near], dense, GROUPS)]
     full_cases(info, at[CORE], mine, other, full)
     wait(y_load)
     for g, rows in enumerate(group_rows(dense.shape[0])):
-        wait(loads[g])
+        wait(copies[g])
         out[rows, :] = y[rows, :] - mm_nt(dense[rows, :], full[...])
 
 
-def last_kernel(
-    info, at, y_hbm, source, mine, other, inverse, out, full, dense, matrix, y, sems
-):
+def last_kernel(info, at, own, near, mine, other, inverse, inverse_near, y_hbm, *refs):
+    out, full, dense, matrix, y, sems = refs
     loads = Loads(sems)
     y_load = loads.start([(y_hbm, y)])
-    dense_loads = loads.groups([source], dense, GROUPS)
-    matrix_loads = loads.groups([inverse], matrix, GROUPS)
+    dense_loads = loads.groups([own, near], dense, GROUPS)
+    inverse_own = inverse.at[0 : inverse_near.shape[0], :]
+    matrix_loads = loads.groups([inverse_own, inverse_near], matrix, GROUPS)
     copies = [(dense_loads[g](), matrix_loads[g]()) for g in range(GROUPS)]
     full_cases(info, at[CORE], mine, other, full)
     wait(y_load)
@@ -451,11 +470,11 @@
 
 def output_kernel(parts, *refs):
     rows, out = refs[:-1], refs[-1]
-    total = parts[0].astype(F32)
-    for n in range(1, parts.shape[0]):
-        total = total + parts[n].astype(F32)
-    begin = total.shape[1]
-    out[0:begin, :] = total.T
+    totals = [parts[0].astype(F32), parts[1].astype(F32)]
+    for n in range(2, parts.shape[0]):
+        totals[n % 2] = totals[n % 2] + parts[n].astype(F32)
+    begin = totals[0].shape[1]
+    out[0:begin, :] = jnp.concatenate(totals, 0).T
     for row in rows:
         out[begin : begin + row.shape[0], :] = row[...].astype(F32)
         begin += row.shape[0]
@@ -531,10 +550,22 @@
             tiled=True,
         )
 
+    def exchange_middle(value, level):
+        info = infos[level - 1]
+        if level <= 1:
+            return lax.all_to_all(
+                value, "blk", 0, 0, axis_index_groups=info.inner_blk, tiled=True
+            )
+        return lax.all_to_all(
+            value, ("leaf", "blk"), 0, 0, axis_index_groups=info.middle, tiled=True
+        )
+
     def exchange_inner(value, level):
         info = infos[level - 1]
         if info.his == 1:
-            return lax.all_to_all(value, "blk", 0, 0, axis_index_groups=info.inner_blk, tiled=True)
+            return lax.all_to_all(
+                value, "blk", 0, 0, axis_index_groups=info.inner_blk, tiled=True
+            )
         return lax.all_to_all(
             value, ("leaf", "blk"), 0, 0, axis_index_groups=info.inner, tiled=True
         )
@@ -568,12 +599,12 @@
         scratch=[pltpu.VMEM((counts[0], cases), F32), pltpu.SemaphoreType.DMA],
     )[0]
     full = lax.all_to_all(spread, "blk", 0, 0, tiled=True).reshape(width, cases)
-    outs = [shaped((counts[0], cases), F32)]
+    outs = [shaped((counts[0], cases // 2), F32)] * 2
     for info in infos:
         shape = (info.targets, info.chunk, info.cell_rows)
         outs += [shaped(shape, BF16), shaped(shape, BF16)]
     matrix_scratch = pltpu.VMEM((counts[0], width), BF16)
-    y0, *base = kernel_call(
+    y_keep, y_send, *base = kernel_call(
         functools.partial(subtree_kernel, infos, starts[1:]),
         outs,
         [full, (inverse, None), (rhs, None)] + hbm([dense[0, above] for above in uppers]),
@@ -586,7 +617,7 @@
             pltpu.SemaphoreType.DMA((1 + GROUPS * (1 + depth),)),
         ],
         flops=2 * (1 + depth) * counts[0] * width * cases,
-        stay=[True, False, False] + [True, True] * (depth - 1),
+        stay=[True, True, False, False] + [True, True] * (depth - 1),
     )
     received = []
     for level in uppers:
@@ -622,6 +653,21 @@
                 scalars=at,
                 flops=2 * rows * listed_rows * width,
             )[0]
+
+    y_near = swap(y_send, "blk", 1)
+    dense_near = {}
+    for above in range(depth, 0, -1):
+        block = swap(coupling_block(0, above), "blk", 1)
+        dense_near[above] = kernel_call(
+            functools.partial(
+                expand_kernel, 1, [infos[above - 1]], [pair_slot[0, above]], None
+            ),
+            [shaped((counts[0], width), BF16)],
+            [update_rows, block],
+            scalars=at,
+            flops=2 * counts[0] * listed_rows * width,
+        )[0]
+    inverse_near = swap(inverse[: counts[0]], "blk", 1)
 
     def sum_spread(parts, copies):
         return kernel_call(
@@ -677,7 +723,9 @@
 
     solved = {}
     swapped = {}
-    z0 = y0
+    pair_scratch = pltpu.VMEM((2 * counts[0], width), BF16)
+    half_cases = cases // 2
+    low = [y_keep, y_near]
     for level in range(depth, 0, -1):
         info = infos[level - 1]
         if level < depth:
@@ -700,59 +748,73 @@
                 stay=[False],
             )[0]
         parts = exchange_inner(parts, level)
-        solved[level] = exchange_outer(sum_spread(parts, info.targets), level)
+        solved[level] = exchange_middle(sum_spread(parts, info.cells * info.pair_x), level)
         swapped[level] = swap(solved[level], "leaf", 1)
         if level > 1:
-            z0 = kernel_call(
-                functools.partial(subtract_kernel, info),
-                [shaped((counts[0], cases), F32)],
-                [(z0, None), (dense[0, level], None), solved[level], swapped[level]],
+            low = kernel_call(
+                functools.partial(subtract_kernel, info, len(low)),
+                [shaped((2 * counts[0], half_cases), F32)],
+                hbm([dense[0, level], dense_near[level]])
+                + [solved[level], swapped[level]]
+                + hbm(low),
                 scalars=at,
                 scratch=[
-                    pltpu.VMEM((cases, width), BF16),
-                    matrix_scratch,
-                    pltpu.VMEM((counts[0], cases), F32),
-                    pltpu.SemaphoreType.DMA((1 + GROUPS,)),
+                    pltpu.VMEM((half_cases, width), BF16),
+                    pair_scratch,
+                    pltpu.VMEM((2 * counts[0], half_cases), F32),
+                    pltpu.SemaphoreType.DMA((2 + GROUPS,)),
                 ],
                 flops=2 * counts[0] * width * cases,
-            )[0]
+            )
 
     part = kernel_call(
         functools.partial(last_kernel, infos[0]),
-        [shaped((blocks, cases, counts[0]), BF16)],
-        [(z0, None), (dense[0, 1], None), solved[1], swapped[1], (inverse, None)],
+        [shaped((blocks, half_cases, counts[0]), BF16)],
+        hbm([dense[0, 1], dense_near[1]])
+        + [solved[1], swapped[1]]
+        + hbm([inverse, inverse_near, low[0]]),
         scalars=at,
         scratch=[
-            pltpu.VMEM((cases, width), BF16),
-            matrix_scratch,
-            matrix_scratch,
-            pltpu.VMEM((counts[0], cases), F32),
+            pltpu.VMEM((half_cases, width), BF16),
+            pair_scratch,
+            pair_scratch,
+            pltpu.VMEM((2 * counts[0], half_cases), F32),
             pltpu.SemaphoreType.DMA((1 + 2 * GROUPS,)),
         ],
         flops=4 * counts[0] * width * cases,
     )[0]
     parts = lax.all_to_all(part, "blk", 0, 0, tiled=True)
 
-    outputs = []
+    keeps = []
+    sends = []
     for level in uppers:
         info = infos[level - 1]
         member = leaf_id & ((1 << level) - 1)
         side = member & (2 * info.pair_x - 1)
         hi = member // (2 * info.pair_x)
-        offset = (side * 2 + yb) * info.rows
 
         def own(value):
-            shape = (info.his, info.pair_x, info.zbs, 2, info.chunk, info.cell_rows)
-            sizes = (1, info.pair_x, 1, 2, info.chunk, info.rows)
-            taken = lax.dynamic_slice(value.reshape(shape), (hi, 0, zb, 0, 0, offset), sizes)
-            return taken[0, :, 0].transpose(1, 0, 2, 3)
+            shape = (info.his, info.pair_x, info.zbs, info.chunk, info.cell_rows)
+            sizes = (1, info.pair_x, 1, info.chunk, 2 * info.rows)
+            start = (hi, 0, zb, 0, side * 2 * info.rows)
+            taken = lax.dynamic_slice(value.reshape(shape), start, sizes)
+            return taken.reshape(half_cases // 2, 2 * info.rows)
 
         mine, other = own(solved[level]), own(swapped[level])
-        rows = jnp.where(
-            core == 0, jnp.stack([mine, other], 1), jnp.stack([other, mine], 1)
+        both = jnp.where(
+            core == 0, jnp.concatenate([mine, other], 0), jnp.concatenate([other, mine], 0)
         )
-        outputs.append(rows.reshape(cases, info.rows).T)
-    out = kernel_call(output_kernel, [shaped((sum(counts), cases), F32)], [parts] + outputs)[0]
+        keeps.append(jnp.where(yb == 0, both[:, : info.rows], both[:, info.rows :]))
+        sends.append(jnp.where(yb == 0, both[:, info.rows :], both[:, : info.rows]))
+    keep = jnp.concatenate(keeps, 1)
+    near = swap(jnp.concatenate(sends, 1), "blk", 1)
+    rows = jnp.where(
+        yb == 0, jnp.concatenate([keep, near], 0), jnp.concatenate([near, keep], 0)
+    )
+    outputs = [rows.T]
+    out = kernel_call(
+        output_kernel, [shaped((sum(counts), cases), F32)], [parts] + outputs
+    )[0]
     return out[None, None]
 
 

time: 171 us -> 177 us (1.035)
  blocking collectives: 29.1 us -> 0 us
  starting transfers between devices: 40.3 us -> 60 us
  Pallas kernels: 32.4 us -> 39.9 us
  waiting for transfers between devices: 63.3 us -> 68.5 us
  local copies, waits for them, and re-layouts: 3.52 us -> 6.38 us
    all_to_all x3 -> x0, blocking collectives: 29.1 us -> none  [the longest x2 17.1 us: exchange_inner(): lax.all_to_all(value, 'blk', 0, 0, axis_index_groups=info.inner_blk, tile...]
    ppermute x17 -> x22, waiting for transfers between devices: 18.3 us -> 31.8 us  [swap(): return lax.ppermute(value, axis, [(i, i ^ bit) for i in range(size)])]
    all_to_all x1, waiting for transfers between devices: 15 us -> 3.46 us  [solve(): parts = lax.all_to_all(part, 'blk', 0, 0, tiled=True)]
    all_to_all x2 -> x4, starting transfers between devices: 7.86 us -> 16.3 us  [exchange_inner(): lax.all_to_all(value, 'blk', 0, 0, axis_index_groups=info.inner_blk, tile...]
    pallas_call x14 -> x16, Pallas kernels: 32.4 us -> 39.9 us  [kernel_call(): pl.pallas_call(body if scalars is None else lambda *refs: body(scalars(),...]
    all_to_all x2 -> x1, waiting for transfers between devices: 15.9 us -> 8.54 us  [exchange_outer(): return lax.all_to_all(value, 'blk', 0, 0, tiled=True)]
    all_to_all x0 -> x2, starting transfers between devices: none -> 6.87 us  [the longest x1 3.55 us: exchange_middle(): lax.all_to_all(value, ('leaf', 'blk'), 0, 0, axis_index_groups=info.middl...]
    ppermute x17 -> x22, starting transfers between devices: 7.65 us -> 14 us  [swap(): return lax.ppermute(value, axis, [(i, i ^ bit) for i in range(size)])]
  transfers between devices with their start and end apart: 24 -> 32, of which waited for: 9 -> 14; matrix products, arithmetic and copies ran while one was open for 2% -> 3% of each run, Pallas kernels for 11% -> 17%
where the time goes in v4:
time: 177 us; the launch traced here: 176 us
  waiting for transfers between devices  68.5 us (39%)
  starting transfers between devices  60 us (34%)
  Pallas kernels  39.9 us (23%)
  local copies, waits for them, and re-layouts  6.38 us (4%)
    pallas_call x16, Pallas kernels, kernel_call(): pl.pallas_call(body if scalars is None else lambda *refs: body(scalars(),...  39.9 us
    ppermute x22, waiting for transfers between devices, swap(): return lax.ppermute(value, axis, [(i, i ^ bit) for i in range(size)])  31.8 us
    all_to_all x4, starting transfers between devices, exchange_inner(): lax.all_to_all(value, 'blk', 0, 0, axis_index_groups=info.inner_blk, tile...  16.3 us
    ppermute x22, starting transfers between devices, swap(): return lax.ppermute(value, axis, [(i, i ^ bit) for i in range(size)])  14 us
    all_to_all x4, waiting for transfers between devices, exchange_inner(): lax.all_to_all(value, 'blk', 0, 0, axis_index_groups=info.inner_blk, tile...  11.1 us
    all_to_all x1, waiting for transfers between devices, exchange_outer(): return lax.all_to_all(value, 'blk', 0, 0, tiled=True)  8.54 us
    all_to_all x1, waiting for transfers between devices, solve(): full = lax.all_to_all(spread, 'blk', 0, 0, tiled=True).reshape(width, cases)  7.83 us
    all_to_all x1, starting transfers between devices, solve(): full = lax.all_to_all(spread, 'blk', 0, 0, tiled=True).reshape(width, cases)  7.32 us
  transfers between devices with their start and end apart: 32, of which 14 were waited for; matrix products, arithmetic and copies ran while one was open for 3% of the time, Pallas kernels for 17%

profile of v4, /device:TPU:0, one launch (start us, length us, event | category | flops | bytes accessed | tf_op | source)
XLA Modules:
  0.0 176.2 jit_solution(11850064578847411883)
XLA Ops:
  1.9 7.3 %all-to-all-start = ((bf16[8,256,128]{2,1,0:T(8,128)(2,1)}), bf16[8,256,128]{2,1,0:T(8,128)(2,1)S(1)}, u32[]{:S(2)}, u32[]{:S(2)}) async-start(bf16[8,256,128]{2,1,0:T(8,128)(2,1)} %shard_map.48), calls=%async_computation | async-start | bytes 1048576 | tf_op jit(solution)/shard_map/all_to_all | solution.py:601
  12.5 3.4 %shard_map.46 = (bf16[256,2048]{1,0:T(8,128)(2,1)}, bf16[256,2048]{1,0:T(8,128)(2,1)}) custom-call(s32[10,1024]{1,0:T(8,128)S(1)} %copy-done.1, bf16[640,1024]{1,0:T(8,128)(2,1)S(1)} %bitcast.30), custom_call_target="tpu_custom_call" | custom-call | flops 2147483648 | bytes 3448832 | tf_op jit(solution)/shard_map/pallas_call | solution.py:45
  15.9 7.8 %all-to-all-done = bf16[8,256,128]{2,1,0:T(8,128)(2,1)S(1)} async-done(((bf16[8,256,128]{2,1,0:T(8,128)(2,1)}), bf16[8,256,128]{2,1,0:T(8,128)(2,1)S(1)}, u32[]{:S(2)}, u32[]{:S(2)}) %all-to-all-start) | async-done | bytes 524320 | tf_op jit(solution)/shard_map/all_to_all | solution.py:601
  23.7 4.3 %shard_map.49 = (f32[256,64]{1,0:T(8,128)}, f32[256,64]{1,0:T(8,128)}, bf16[8,32,512]{2,1,0:T(8,128)(2,1)S(1)}, bf16[8,32,512]{2,1,0:T(8,128)(2,1)S(1)}, bf16[16...) custom-call(bf16[2048,128]{1,0:T(8,128)(2,1)S(1)} %bitcast.29, bf16[448,2048]{1,0:T(8,128)(2,1)} %bitcast.33, ...), custom_call_target="tpu_custom_call" | custom-call | flops 402653184 | bytes 5865472 | tf_op jit(solution)/shard_map/pallas_call | solution.py:45
  28.7 5.6 %collective-permute-done.6.refs_2_ = bf16[128,1024]{1,0:T(8,128)(2,1)S(1)} collective-permute-done((bf16[128,1024]{1,0:T(8,128)(2,1)S(1)}, bf16[128,1024]{1,0:T(8,128)(2,1)S(1)}, u32[]{:S(2)}, u32[]{:S(2)}) %collective-permute-start.6) | collective-permute-done | bytes 262176 | tf_op jit(solution)/shard_map/ppermute | solution.py:534
  35.7 4.6 %all-to-all-start.1 = ((bf16[8,32,512]{2,1,0:T(8,128)(2,1)}), bf16[8,32,512]{2,1,0:T(8,128)(2,1)S(1)}, u32[]{:S(2)}, u32[]{:S(2)}) async-start(bf16[8,32,512]{2,1,0:T(8,128)(2,1)} %add_convert_fusion), calls=%async_computation.1 | async-start | bytes 524288 | tf_op jit(solution)/shard_map/all_to_all | solution.py:543
  41.2 8.5 %all-to-all-done.1.parts = bf16[8,32,512]{2,1,0:T(8,128)(2,1)S(1)} async-done(((bf16[8,32,512]{2,1,0:T(8,128)(2,1)}), bf16[8,32,512]{2,1,0:T(8,128)(2,1)S(1)}, u32[]{:S(2)}, u32[]{:S(2)}) %all-to-all-start.1) | async-done | bytes 262176 | tf_op jit(solution)/shard_map/all_to_all | solution.py:543
  50.5 3.3 %all-to-all-start.2 = ((bf16[4,32,512]{2,1,0:T(8,128)(2,1)}), bf16[4,32,512]{2,1,0:T(8,128)(2,1)S(1)}, u32[]{:S(2)}, u32[]{:S(2)}) async-start(bf16[4,32,512]{2,1,0:T(8,128)(2,1)} %shard_map.50), calls=%async_computation.2 | async-start | bytes 262144 | tf_op jit(solution)/shard_map/all_to_all | solution.py:566
  55.4 3.8 %shard_map.51.refs_7_.refs_6_ = bf16[512,2048]{1,0:T(8,128)(2,1)} custom-call(s32[10,1024]{1,0:T(8,128)S(1)} %copy-done.1, bf16[128,1024]{1,0:T(8,128)(2,1)S(1)} %slice_bitcast_fusion.5.refs_1_, bf16[128,1024]{1,0:T(8,128)(2,1)S(1)} %collective-permute-done.6.refs_2_, bf16[128,1024]{1,0:T(8,128)(2,1)S(1)} %collective-permute-done.7.refs_3_, ...), custom_call_target="tpu_custom_call" | custom-call | flops 2147483648 | bytes 3186688 | tf_op jit(solution)/shard_map/pallas_call | solution.py:45
  59.7 3.9 %shard_map.52 = (f32[512,32]{1,0:T(8,128)}, bf16[16,16,512]{2,1,0:T(8,128)(2,1)}) custom-call(bf16[4,32,512]{2,1,0:T(8,128)(2,1)S(1)} %all-to-all-done.2.refs_0_, bf16[16,16,512]{2,1,0:T(8,128)(2,1)} %get-tuple-element.19.refs_1_, bf16[16,16,512]{2,1,0:T(8,128)(2,1)} %collective-permute-done.2.refs_2_, bf16[128,2048]{1,0:T(8,128)(2,1)} %copy-done.3, ...), custom_call_target="tpu_custom_call" | custom-call | flops 134217728 | bytes 5177344 | tf_op jit(solution)/shard_map/pallas_call | solution.py:45
  63.6 5.4 %all-to-all-start.3 = ((bf16[16,16,512]{2,1,0:T(8,128)(2,1)}), bf16[16,16,512]{2,1,0:T(8,128)(2,1)S(1)}, u32[]{:S(2)}, u32[]{:S(2)}) async-start(bf16[16,16,512]{2,1,0:T(8,128)(2,1)} %get-tuple-element.22), calls=%async_computation.3 | async-start | bytes 524288 | tf_op jit(solution)/shard_map/all_to_all | solution.py:544
  71.6 9.0 %collective-permute-done.10.refs_2_ = bf16[64,2048]{1,0:T(8,128)(2,1)S(1)} collective-permute-done((bf16[64,2048]{1,0:T(8,128)(2,1)S(1)}, bf16[64,2048]{1,0:T(8,128)(2,1)S(1)}, u32[]{:S(2)}, u32[]{:S(2)}) %collective-permute-start.10) | collective-permute-done | bytes 262176 | tf_op jit(solution)/shard_map/ppermute | solution.py:534
  80.6 3.5 %collective-permute-done.11.refs_3_ = bf16[64,2048]{1,0:T(8,128)(2,1)S(1)} collective-permute-done((bf16[64,2048]{1,0:T(8,128)(2,1)}, bf16[64,2048]{1,0:T(8,128)(2,1)S(1)}, u32[]{:S(2)}, u32[]{:S(2)}) %collective-permute-start.11) | collective-permute-done | bytes 262176 | tf_op jit(solution)/shard_map/ppermute | solution.py:534
  84.8 4.5 %all-to-all-start.4 = ((bf16[4,16,512]{2,1,0:T(8,128)(2,1)}), bf16[4,16,512]{2,1,0:T(8,128)(2,1)S(1)}, u32[]{:S(2)}, u32[]{:S(2)}) async-start(bf16[4,16,512]{2,1,0:T(8,128)(2,1)} %shard_map.53), calls=%async_computation.4 | async-start | bytes 131072 | tf_op jit(solution)/shard_map/all_to_all | solution.py:566
  89.4 5.7 %all-to-all-done.4.gathered = bf16[4,16,512]{2,1,0:T(8,128)(2,1)S(1)} async-done(((bf16[4,16,512]{2,1,0:T(8,128)(2,1)}), bf16[4,16,512]{2,1,0:T(8,128)(2,1)S(1)}, u32[]{:S(2)}, u32[]{:S(2)}) %all-to-all-start.4) | async-done | bytes 65568 | tf_op jit(solution)/shard_map/all_to_all | solution.py:566
  95.1 3.2 %shard_map.54 = bf16[4,16,512]{2,1,0:T(8,128)(2,1)} custom-call(bf16[4,16,512]{2,1,0:T(8,128)(2,1)S(1)} %all-to-all-done.4.gathered, bf16[64,2048]{1,0:T(8,128)(2,1)} %copy-done.4, bf16[64,2048]{1,0:T(8,128)(2,1)} %collective-permute-done.9.refs_1_, bf16[64,2048]{1,0:T(8,128)(2,1)} %copy-done.6, bf16[64,2048]{1,0:T(8,128)(2,1)} %copy-done.7, ...), custom_call_target="tpu_custom_call" | custom-call | flops 67108864 | bytes 2228224 | tf_op jit(solution)/shard_map/pallas_call | solution.py:45
  98.3 3.4 %all-to-all-start.5 = ((bf16[4,16,512]{2,1,0:T(8,128)(2,1)}), bf16[4,16,512]{2,1,0:T(8,128)(2,1)S(1)}, u32[]{:S(2)}, u32[]{:S(2)}) async-start(bf16[4,16,512]{2,1,0:T(8,128)(2,1)} %shard_map.54), calls=%async_computation.5 | async-start | bytes 131072 | tf_op jit(solution)/shard_map/all_to_all | solution.py:566
  104.8 2.6 %all-to-all-done.5.parts = bf16[4,16,512]{2,1,0:T(8,128)(2,1)S(1)} async-done(((bf16[4,16,512]{2,1,0:T(8,128)(2,1)}), bf16[4,16,512]{2,1,0:T(8,128)(2,1)S(1)}, u32[]{:S(2)}, u32[]{:S(2)}) %all-to-all-start.5) | async-done | bytes 65568 | tf_op jit(solution)/shard_map/all_to_all | solution.py:566
  108.1 3.5 %all-to-all-start.6 = ((bf16[8,16,512]{2,1,0:T(8,128)(2,1)}), bf16[8,16,512]{2,1,0:T(8,128)(2,1)S(1)}, u32[]{:S(2)}, u32[]{:S(2)}) async-start(bf16[8,16,512]{2,1,0:T(8,128)(2,1)} %shard_map.55), calls=%async_computation.6 | async-start | bytes 262144 | tf_op jit(solution)/shard_map/all_to_all | solution.py:559
  113.9 3.9 %collective-permute-done.18.refs_1_ = bf16[256,1024]{1,0:T(8,128)(2,1)S(1)} collective-permute-done((bf16[256,1024]{1,0:T(8,128)(2,1)}, bf16[256,1024]{1,0:T(8,128)(2,1)S(1)}, u32[]{:S(2)}, u32[]{:S(2)}) %collective-permute-start.18) | collective-permute-done | bytes 524320 | tf_op jit(solution)/shard_map/ppermute | solution.py:534
  117.8 2.3 %shard_map.58.refs_1_ = bf16[256,2048]{1,0:T(8,128)(2,1)} custom-call(s32[10,1024]{1,0:T(8,128)S(1)} %copy-done.1, bf16[256,1024]{1,0:T(8,128)(2,1)S(1)} %collective-permute-done.18.refs_1_), custom_call_target="tpu_custom_call" | custom-call | flops 1073741824 | bytes 1613824 | tf_op jit(solution)/shard_map/pallas_call | solution.py:45
  120.1 3.9 %shard_map.56 = bf16[4,32,512]{2,1,0:T(8,128)(2,1)} custom-call(f32[512,32]{1,0:T(8,128)} %get-tuple-element.21.refs_0_, bf16[128,2048]{1,0:T(8,128)(2,1)} %copy-done.3, bf16[128,2048]{1,0:T(8,128)(2,1)} %collective-permute-done.3.refs_4_.refs_2_, bf16[128,2048]{1,0:T(8,128)(2,1)} %collective-permute-done.4.refs_5_.refs_3_, ...), custom_call_target="tpu_custom_call" | custom-call | flops 134217728 | bytes 4521984 | tf_op jit(solution)/shard_map/pallas_call | solution.py:45
  124.1 5.1 %all-to-all-start.7 = ((bf16[4,32,512]{2,1,0:T(8,128)(2,1)}), bf16[4,32,512]{2,1,0:T(8,128)(2,1)S(1)}, u32[]{:S(2)}, u32[]{:S(2)}) async-start(bf16[4,32,512]{2,1,0:T(8,128)(2,1)} %shard_map.56), calls=%async_computation.7 | async-start | bytes 262144 | tf_op jit(solution)/shard_map/all_to_all | solution.py:566
  129.1 2.3 %shard_map.47.refs_1_ = bf16[256,2048]{1,0:T(8,128)(2,1)} custom-call(s32[10,1024]{1,0:T(8,128)S(1)} %copy-done.1, bf16[256,1024]{1,0:T(8,128)(2,1)S(1)} %collective-permute-done.refs_1_), custom_call_target="tpu_custom_call" | custom-call | flops 1073741824 | bytes 1613824 | tf_op jit(solution)/shard_map/pallas_call | solution.py:45
  135.7 3.3 %all-to-all-start.8 = ((bf16[4,32,512]{2,1,0:T(8,128)(2,1)}), bf16[4,32,512]{2,1,0:T(8,128)(2,1)S(1)}, u32[]{:S(2)}, u32[]{:S(2)}) async-start(bf16[4,32,512]{2,1,0:T(8,128)(2,1)} %shard_map.57), calls=%async_computation.8 | async-start | bytes 262144 | tf_op jit(solution)/shard_map/all_to_all | solution.py:556
  139.3 5.8 %all-to-all-done.8.refs_2_ = bf16[4,32,512]{2,1,0:T(8,128)(2,1)S(1)} async-done(((bf16[4,32,512]{2,1,0:T(8,128)(2,1)}), bf16[4,32,512]{2,1,0:T(8,128)(2,1)S(1)}, u32[]{:S(2)}, u32[]{:S(2)}) %all-to-all-start.8) | async-done | bytes 131104 | tf_op jit(solution)/shard_map/all_to_all | solution.py:556
  145.1 7.4 %collective-permute-done.20.refs_5_ = f32[256,64]{1,0:T(8,128)S(1)} collective-permute-done((f32[256,64]{1,0:T(8,128)S(1)}, f32[256,64]{1,0:T(8,128)S(1)}, u32[]{:S(2)}, u32[]{:S(2)}) %collective-permute-start.20) | collective-permute-done | bytes 65568 | tf_op jit(solution)/shard_map/ppermute | solution.py:534
  153.1 3.4 %shard_map.59.refs_6_ = f32[512,64]{1,0:T(8,128)} custom-call(bf16[256,2048]{1,0:T(8,128)(2,1)} %get-tuple-element.16.refs_4_.refs_0_, bf16[256,2048]{1,0:T(8,128)(2,1)} %shard_map.58.refs_1_, bf16[8,16,512]{2,1,0:T(8,128)(2,1)S(1)} %all-to-all-done.6.refs_5_.refs_2_, bf16[8,16,512]{2,1,0:T(8,128)(2,1)S(1)} %collective-permute-done.19.refs_3_, ...), custom_call_target="tpu_custom_call" | custom-call | flops 134217728 | bytes 2621440 | tf_op jit(solution)/shard_map/pallas_call | solution.py:45
  157.9 4.0 %shard_map.60 = bf16[8,64,256]{2,1,0:T(8,128)(2,1)} custom-call(bf16[256,2048]{1,0:T(8,128)(2,1)} %get-tuple-element.15.refs_3_.refs_0_, bf16[256,2048]{1,0:T(8,128)(2,1)} %shard_map.47.refs_1_, bf16[4,32,512]{2,1,0:T(8,128)(2,1)S(1)} %all-to-all-done.8.refs_2_, bf16[4,32,512]{2,1,0:T(8,128)(2,1)S(1)} %collective-permute-done.16.refs_3_, ...), custom_call_target="tpu_custom_call" | custom-call | flops 268435456 | bytes 5636096 | tf_op jit(solution)/shard_map/pallas_call | solution.py:45
  161.8 5.4 %all-to-all-start.9 = ((bf16[8,64,256]{2,1,0:T(8,128)(2,1)}), bf16[8,64,256]{2,1,0:T(8,128)(2,1)S(1)}, u32[]{:S(2)}, u32[]{:S(2)}) async-start(bf16[8,64,256]{2,1,0:T(8,128)(2,1)} %shard_map.60), calls=%async_computation.9 | async-start | bytes 524288 | tf_op jit(solution)/shard_map/all_to_all | solution.py:786
  169.5 2.4 %collective-permute-done.21 = bf16[64,192]{0,1:T(8,128)(2,1)S(1)} collective-permute-done((bf16[64,192]{0,1:T(8,128)(2,1)S(1)}, bf16[64,192]{0,1:T(8,128)(2,1)S(1)}, u32[]{:S(2)}, u32[]{:S(2)}) %collective-permute-start.21) | collective-permute-done | bytes 24608 | tf_op jit(solution)/shard_map/ppermute | solution.py:534
  172.0 3.5 %all-to-all-done.9.parts = bf16[8,64,256]{2,1,0:T(8,128)(2,1)S(1)} async-done(((bf16[8,64,256]{2,1,0:T(8,128)(2,1)}), bf16[8,64,256]{2,1,0:T(8,128)(2,1)S(1)}, u32[]{:S(2)}, u32[]{:S(2)}) %all-to-all-start.9) | async-done | bytes 262176 | tf_op jit(solution)/shard_map/all_to_all | solution.py:786
  (96 shorter events, 29.8 us)
Async XLA Ops:
  1.9 21.8 %all-to-all-start = ((bf16[8,256,128]{2,1,0:T(8,128)(2,1)}), bf16[8,256,128]{2,1,0:T(8,128)(2,1)S(1)}, u32[]{:S(2)}, u32[]{:S(2)}) async-start(bf16[8,256,128]{2,1,0:T(8,128)(2,1)} %shard_map.48), calls=%async_computation | async-start | bytes 1048576 | tf_op jit(solution)/shard_map/all_to_all | solution.py:601
  10.3 24.0 %collective-permute-start.3 = (bf16[128,2048]{1,0:T(8,128)(2,1)S(1)}, bf16[128,2048]{1,0:T(8,128)(2,1)}, u32[]{:S(2)}, u32[]{:S(2)}) collective-permute-start(bf16[128,2048]{1,0:T(8,128)(2,1)S(1)} %slice_bitcast_fusion.2.refs_3_.refs_1_), channel_id=1, source_target_pairs={{0,1},{1,0},{2,3},{3,2},{4,5},{5,4},{6,7},{7,6},{8,9},{9,8},{10,11... | collective-permute-start | bytes 1572872 | tf_op jit(solution)/shard_map/ppermute | solution.py:534
  12.4 21.9 %collective-permute-start.6 = (bf16[128,1024]{1,0:T(8,128)(2,1)S(1)}, bf16[128,1024]{1,0:T(8,128)(2,1)S(1)}, u32[]{:S(2)}, u32[]{:S(2)}) collective-permute-start(bf16[128,1024]{1,0:T(8,128)(2,1)S(1)} %slice_bitcast_fusion.5.refs_1_), channel_id=1, source_target_pairs={{0,1},{1,0},{2,3},{3,2},{4,5},{5,4},{6,7},{7,6},{8,9},{9,8},{10,11... | collective-permute-start | bytes 786440 | tf_op jit(solution)/shard_map/ppermute | solution.py:534
  28.0 6.8 %collective-permute-start.1 = (bf16[8,32,512]{2,1,0:T(8,128)(2,1)S(1)}, bf16[8,32,512]{2,1,0:T(8,128)(2,1)S(1)}, u32[]{:S(2)}, u32[]{:S(2)}) collective-permute-start(bf16[8,32,512]{2,1,0:T(8,128)(2,1)S(1)} %get-tuple-element.18), channel_id=1, source_target_pairs={{0,8},{8,0},{16,24},{24,16},{1,9},{9,1},{17,25},{25,17},{2,10},{10... | collective-permute-start | bytes 786440 | tf_op jit(solution)/shard_map/ppermute | solution.py:534
  28.1 25.7 %collective-permute-start.7 = (bf16[128,1024]{1,0:T(8,128)(2,1)S(1)}, bf16[128,1024]{1,0:T(8,128)(2,1)S(1)}, u32[]{:S(2)}, u32[]{:S(2)}) collective-permute-start(bf16[128,1024]{1,0:T(8,128)(2,1)S(1)} %slice_bitcast_fusion.5.refs_1_), channel_id=1, source_target_pairs={{0,8},{8,0},{16,24},{24,16},{1,9},{9,1},{17,25},{25,17},{2,10},{10... | collective-permute-start | bytes 786440 | tf_op jit(solution)/shard_map/ppermute | solution.py:534
  28.6 30.6 %collective-permute-start.4 = (bf16[128,2048]{1,0:T(8,128)(2,1)S(1)}, bf16[128,2048]{1,0:T(8,128)(2,1)}, u32[]{:S(2)}, u32[]{:S(2)}) collective-permute-start(bf16[128,2048]{1,0:T(8,128)(2,1)S(1)} %slice_bitcast_fusion.2.refs_3_.refs_1_), channel_id=1, source_target_pairs={{0,8},{8,0},{16,24},{24,16},{1,9},{9,1},{17,25},{25,17},{2,10},{10... | collective-permute-start | bytes 1572872 | tf_op jit(solution)/shard_map/ppermute | solution.py:534
  34.3 21.1 %collective-permute-start.8 = (bf16[128,1024]{1,0:T(8,128)(2,1)S(1)}, bf16[128,1024]{1,0:T(8,128)(2,1)S(1)}, u32[]{:S(2)}, u32[]{:S(2)}) collective-permute-start(bf16[128,1024]{1,0:T(8,128)(2,1)S(1)} %collective-permute-done.6.refs_2_), channel_id=1, source_target_pairs={{0,8},{8,0},{16,24},{24,16},{1,9},{9,1},{17,25},{25,17},{2,10},{10... | collective-permute-start | bytes 786440 | tf_op jit(solution)/shard_map/ppermute | solution.py:534
  34.3 24.9 %collective-permute-start.5 = (bf16[128,2048]{1,0:T(8,128)(2,1)}, bf16[128,2048]{1,0:T(8,128)(2,1)}, u32[]{:S(2)}, u32[]{:S(2)}) collective-permute-start(bf16[128,2048]{1,0:T(8,128)(2,1)} %collective-permute-done.3.refs_4_.refs_2_), channel_id=1, source_target_pairs={{0,8},{8,0},{16,24},{24,16},{1,9},{9,1},{17,25},{25,17},{2,10},{10... | collective-permute-start | bytes 1572872 | tf_op jit(solution)/shard_map/ppermute | solution.py:534
  34.8 24.4 %collective-permute-start.2 = (bf16[16,16,512]{2,1,0:T(8,128)(2,1)}, bf16[16,16,512]{2,1,0:T(8,128)(2,1)}, u32[]{:S(2)}, u32[]{:S(2)}) collective-permute-start(bf16[16,16,512]{2,1,0:T(8,128)(2,1)} %get-tuple-element.20), channel_id=1, source_target_pairs={{0,8},{8,0},{16,24},{24,16},{1,9},{9,1},{17,25},{25,17},{2,10},{10... | collective-permute-start | bytes 786440 | tf_op jit(solution)/shard_map/ppermute | solution.py:534
  35.7 14.1 %all-to-all-start.1 = ((bf16[8,32,512]{2,1,0:T(8,128)(2,1)}), bf16[8,32,512]{2,1,0:T(8,128)(2,1)S(1)}, u32[]{:S(2)}, u32[]{:S(2)}) async-start(bf16[8,32,512]{2,1,0:T(8,128)(2,1)} %add_convert_fusion), calls=%async_computation.1 | async-start | bytes 524288 | tf_op jit(solution)/shard_map/all_to_all | solution.py:543
  50.5 9.2 %all-to-all-start.2 = ((bf16[4,32,512]{2,1,0:T(8,128)(2,1)}), bf16[4,32,512]{2,1,0:T(8,128)(2,1)S(1)}, u32[]{:S(2)}, u32[]{:S(2)}) async-start(bf16[4,32,512]{2,1,0:T(8,128)(2,1)} %shard_map.50), calls=%async_computation.2 | async-start | bytes 262144 | tf_op jit(solution)/shard_map/all_to_all | solution.py:566
  53.8 17.1 %collective-permute-start.9 = (bf16[64,2048]{1,0:T(8,128)(2,1)S(1)}, bf16[64,2048]{1,0:T(8,128)(2,1)}, u32[]{:S(2)}, u32[]{:S(2)}) collective-permute-start(bf16[64,2048]{1,0:T(8,128)(2,1)S(1)} %slice_bitcast_fusion.4.refs_0_), channel_id=1, source_target_pairs={{0,16},{8,24},{16,0},{24,8},{1,17},{9,25},{17,1},{25,9},{2,18},{10... | collective-permute-start | bytes 786440 | tf_op jit(solution)/shard_map/ppermute | solution.py:534
  63.6 20.5 %all-to-all-start.3 = ((bf16[16,16,512]{2,1,0:T(8,128)(2,1)}), bf16[16,16,512]{2,1,0:T(8,128)(2,1)S(1)}, u32[]{:S(2)}, u32[]{:S(2)}) async-start(bf16[16,16,512]{2,1,0:T(8,128)(2,1)} %get-tuple-element.22), calls=%async_computation.3 | async-start | bytes 524288 | tf_op jit(solution)/shard_map/all_to_all | solution.py:544
  69.0 11.6 %collective-permute-start.10 = (bf16[64,2048]{1,0:T(8,128)(2,1)S(1)}, bf16[64,2048]{1,0:T(8,128)(2,1)S(1)}, u32[]{:S(2)}, u32[]{:S(2)}) collective-permute-start(bf16[64,2048]{1,0:T(8,128)(2,1)S(1)} %slice_bitcast_fusion.4.refs_0_), channel_id=1, source_target_pairs={{0,1},{1,0},{2,3},{3,2},{4,5},{5,4},{6,7},{7,6},{8,9},{9,8},{10,11... | collective-permute-start | bytes 786440 | tf_op jit(solution)/shard_map/ppermute | solution.py:534
  70.9 13.1 %collective-permute-start.11 = (bf16[64,2048]{1,0:T(8,128)(2,1)}, bf16[64,2048]{1,0:T(8,128)(2,1)S(1)}, u32[]{:S(2)}, u32[]{:S(2)}) collective-permute-start(bf16[64,2048]{1,0:T(8,128)(2,1)} %collective-permute-done.9.refs_1_), channel_id=1, source_target_pairs={{0,1},{1,0},{2,3},{3,2},{4,5},{5,4},{6,7},{7,6},{8,9},{9,8},{10,11... | collective-permute-start | bytes 786440 | tf_op jit(solution)/shard_map/ppermute | solution.py:534
  71.1 18.3 %collective-permute-start.12 = (bf16[64,2048]{1,0:T(8,128)(2,1)S(1)}, bf16[64,2048]{1,0:T(8,128)(2,1)S(1)}, u32[]{:S(2)}, u32[]{:S(2)}) collective-permute-start(bf16[64,2048]{1,0:T(8,128)(2,1)S(1)} %slice_bitcast_fusion.4.refs_0_), channel_id=1, source_target_pairs={{0,8},{8,0},{16,24},{24,16},{1,9},{9,1},{17,25},{25,17},{2,10},{10... | collective-permute-start | bytes 786440 | tf_op jit(solution)/shard_map/ppermute | solution.py:534
  71.1 18.3 %collective-permute-start.13 = (bf16[64,2048]{1,0:T(8,128)(2,1)}, bf16[64,2048]{1,0:T(8,128)(2,1)S(1)}, u32[]{:S(2)}, u32[]{:S(2)}) collective-permute-start(bf16[64,2048]{1,0:T(8,128)(2,1)} %collective-permute-done.9.refs_1_), channel_id=1, source_target_pairs={{0,8},{8,0},{16,24},{24,16},{1,9},{9,1},{17,25},{25,17},{2,10},{10... | collective-permute-start | bytes 786440 | tf_op jit(solution)/shard_map/ppermute | solution.py:534
  80.6 8.8 %collective-permute-start.14 = (bf16[64,2048]{1,0:T(8,128)(2,1)S(1)}, bf16[64,2048]{1,0:T(8,128)(2,1)S(1)}, u32[]{:S(2)}, u32[]{:S(2)}) collective-permute-start(bf16[64,2048]{1,0:T(8,128)(2,1)S(1)} %collective-permute-done.10.refs_2_), channel_id=1, source_target_pairs={{0,8},{8,0},{16,24},{24,16},{1,9},{9,1},{17,25},{25,17},{2,10},{10... | collective-permute-start | bytes 786440 | tf_op jit(solution)/shard_map/ppermute | solution.py:534
  84.1 5.3 %collective-permute-start.15 = (bf16[64,2048]{1,0:T(8,128)(2,1)S(1)}, bf16[64,2048]{1,0:T(8,128)(2,1)S(1)}, u32[]{:S(2)}, u32[]{:S(2)}) collective-permute-start(bf16[64,2048]{1,0:T(8,128)(2,1)S(1)} %collective-permute-done.11.refs_3_), channel_id=1, source_target_pairs={{0,8},{8,0},{16,24},{24,16},{1,9},{9,1},{17,25},{25,17},{2,10},{10... | collective-permute-start | bytes 786440 | tf_op jit(solution)/shard_map/ppermute | solution.py:534
  84.8 10.3 %all-to-all-start.4 = ((bf16[4,16,512]{2,1,0:T(8,128)(2,1)}), bf16[4,16,512]{2,1,0:T(8,128)(2,1)S(1)}, u32[]{:S(2)}, u32[]{:S(2)}) async-start(bf16[4,16,512]{2,1,0:T(8,128)(2,1)} %shard_map.53), calls=%async_computation.4 | async-start | bytes 131072 | tf_op jit(solution)/shard_map/all_to_all | solution.py:566
  98.3 9.1 %all-to-all-start.5 = ((bf16[4,16,512]{2,1,0:T(8,128)(2,1)}), bf16[4,16,512]{2,1,0:T(8,128)(2,1)S(1)}, u32[]{:S(2)}, u32[]{:S(2)}) async-start(bf16[4,16,512]{2,1,0:T(8,128)(2,1)} %shard_map.54), calls=%async_computation.5 | async-start | bytes 131072 | tf_op jit(solution)/shard_map/all_to_all | solution.py:566
  102.8 15.0 %collective-permute-start.18 = (bf16[256,1024]{1,0:T(8,128)(2,1)}, bf16[256,1024]{1,0:T(8,128)(2,1)S(1)}, u32[]{:S(2)}, u32[]{:S(2)}) collective-permute-start(bf16[256,1024]{1,0:T(8,128)(2,1)} %get-tuple-element.25), channel_id=1, source_target_pairs={{0,1},{1,0},{2,3},{3,2},{4,5},{5,4},{6,7},{7,6},{8,9},{9,8},{10,11... | collective-permute-start | bytes 1572872 | tf_op jit(solution)/shard_map/ppermute | solution.py:534
  104.0 25.2 %collective-permute-start = (bf16[256,1024]{1,0:T(8,128)(2,1)}, bf16[256,1024]{1,0:T(8,128)(2,1)S(1)}, u32[]{:S(2)}, u32[]{:S(2)}) collective-permute-start(bf16[256,1024]{1,0:T(8,128)(2,1)} %get-tuple-element.26), channel_id=1, source_target_pairs={{0,1},{1,0},{2,3},{3,2},{4,5},{5,4},{6,7},{7,6},{8,9},{9,8},{10,11... | collective-permute-start | bytes 1572872 | tf_op jit(solution)/shard_map/ppermute | solution.py:534
  108.1 12.0 %all-to-all-start.6 = ((bf16[8,16,512]{2,1,0:T(8,128)(2,1)}), bf16[8,16,512]{2,1,0:T(8,128)(2,1)S(1)}, u32[]{:S(2)}, u32[]{:S(2)}) async-start(bf16[8,16,512]{2,1,0:T(8,128)(2,1)} %shard_map.55), calls=%async_computation.6 | async-start | bytes 262144 | tf_op jit(solution)/shard_map/all_to_all | solution.py:559
  112.8 44.1 %collective-permute-start.17 = (bf16[256,2048]{1,0:T(8,128)(2,1)}, bf16[256,2048]{1,0:T(8,128)(2,1)S(1)}, u32[]{:S(2)}, u32[]{:S(2)}) collective-permute-start(bf16[256,2048]{1,0:T(8,128)(2,1)} %slice_bitcast_fusion), channel_id=1, source_target_pairs={{0,1},{1,0},{2,3},{3,2},{4,5},{5,4},{6,7},{7,6},{8,9},{9,8},{10,11... | collective-permute-start | bytes 3145736 | tf_op jit(solution)/shard_map/ppermute | solution.py:534
  124.1 11.0 %all-to-all-start.7 = ((bf16[4,32,512]{2,1,0:T(8,128)(2,1)}), bf16[4,32,512]{2,1,0:T(8,128)(2,1)S(1)}, u32[]{:S(2)}, u32[]{:S(2)}) async-start(bf16[4,32,512]{2,1,0:T(8,128)(2,1)} %shard_map.56), calls=%async_computation.7 | async-start | bytes 262144 | tf_op jit(solution)/shard_map/all_to_all | solution.py:566
  129.1 9.9 %collective-permute-start.19 = (bf16[8,16,512]{2,1,0:T(8,128)(2,1)S(1)}, bf16[8,16,512]{2,1,0:T(8,128)(2,1)S(1)}, u32[]{:S(2)}, u32[]{:S(2)}) collective-permute-start(bf16[8,16,512]{2,1,0:T(8,128)(2,1)S(1)} %all-to-all-done.6.refs_5_.refs_2_), channel_id=1, source_target_pairs={{0,8},{8,0},{16,24},{24,16},{1,9},{9,1},{17,25},{25,17},{2,10},{10... | collective-permute-start | bytes 393224 | tf_op jit(solution)/shard_map/ppermute | solution.py:534
  131.5 21.0 %collective-permute-start.20 = (f32[256,64]{1,0:T(8,128)S(1)}, f32[256,64]{1,0:T(8,128)S(1)}, u32[]{:S(2)}, u32[]{:S(2)}) collective-permute-start(f32[256,64]{1,0:T(8,128)S(1)} %copy-done.13), channel_id=1, source_target_pairs={{0,1},{1,0},{2,3},{3,2},{4,5},{5,4},{6,7},{7,6},{8,9},{9,8},{10,11... | collective-permute-start | bytes 196616 | tf_op jit(solution)/shard_map/ppermute | solution.py:534
  135.7 9.4 %all-to-all-start.8 = ((bf16[4,32,512]{2,1,0:T(8,128)(2,1)}), bf16[4,32,512]{2,1,0:T(8,128)(2,1)S(1)}, u32[]{:S(2)}, u32[]{:S(2)}) async-start(bf16[4,32,512]{2,1,0:T(8,128)(2,1)} %shard_map.57), calls=%async_computation.8 | async-start | bytes 262144 | tf_op jit(solution)/shard_map/all_to_all | solution.py:556
  145.1 11.6 %collective-permute-start.16 = (bf16[4,32,512]{2,1,0:T(8,128)(2,1)S(1)}, bf16[4,32,512]{2,1,0:T(8,128)(2,1)S(1)}, u32[]{:S(2)}, u32[]{:S(2)}) collective-permute-start(bf16[4,32,512]{2,1,0:T(8,128)(2,1)S(1)} %all-to-all-done.8.refs_2_), channel_id=1, source_target_pairs={{0,8},{8,0},{16,24},{24,16},{1,9},{9,1},{17,25},{25,17},{2,10},{10... | collective-permute-start | bytes 393224 | tf_op jit(solution)/shard_map/ppermute | solution.py:534
  161.8 13.6 %all-to-all-start.9 = ((bf16[8,64,256]{2,1,0:T(8,128)(2,1)}), bf16[8,64,256]{2,1,0:T(8,128)(2,1)S(1)}, u32[]{:S(2)}, u32[]{:S(2)}) async-start(bf16[8,64,256]{2,1,0:T(8,128)(2,1)} %shard_map.60), calls=%async_computation.9 | async-start | bytes 524288 | tf_op jit(solution)/shard_map/all_to_all | solution.py:786
  167.4 4.5 %collective-permute-start.21 = (bf16[64,192]{0,1:T(8,128)(2,1)S(1)}, bf16[64,192]{0,1:T(8,128)(2,1)S(1)}, u32[]{:S(2)}, u32[]{:S(2)}) collective-permute-start(bf16[64,192]{0,1:T(8,128)(2,1)S(1)} %pad_maximum_fusion), channel_id=1, source_target_pairs={{0,1},{1,0},{2,3},{3,2},{4,5},{5,4},{6,7},{7,6},{8,9},{9,8},{10,11... | collective-permute-start | bytes 73736 | tf_op jit(solution)/shard_map/ppermute | solution.py:534
  (14 other events, 138.9 us)

commit v5 on v4

--- a/solution.py
+++ b/solution.py
@@ -39,6 +39,8 @@
             value = pltpu.with_memory_space_constraint(arg[0], pltpu.HBM)
             if arg[1] is None:
                 spec = pl.BlockSpec(memory_space=pltpu.HBM)
+            elif arg[1] is False:
+                value, spec = arg[0], pl.BlockSpec(memory_space=pl.ANY)
         values.append(value)
         specs.append(spec)
         moved += value.size * value.dtype.itemsize
@@ -364,11 +366,10 @@
         term = functools.reduce(jnp.add, same[True])
         rows = pl.ds(pl.multiple_of(at[XU] * above.chunk, above.chunk), above.chunk)
         total[rows, :] = total[rows, :] + term
-    for cell, xu, yb, target in above.all_targets():
-        value = mine[target].astype(F32) + received[target].astype(F32)
+    for cell, xu, index in above.slots():
+        value = mine[index].astype(F32) + received[index].astype(F32)
         minus = total[xu * above.chunk : (xu + 1) * above.chunk, above.lanes(cell)]
-        value = jnp.where(at[YB] == yb, value - minus, value)
-        out[target] = value.astype(BF16)
+        out[index] = (value - minus).astype(BF16)
 
 
 def top_kernel(info, gathered, *refs):
@@ -622,6 +623,14 @@
     received = []
     for level in uppers:
         received.append(swap(base[2 * level - 1], "leaf", 1))
+    paired = {}
+    for level in range(2, depth + 1):
+        info = infos[level - 1]
+        both = base[2 * level - 2].astype(F32) + received[level - 1].astype(F32)
+        both = both.astype(BF16).reshape(-1, 2, info.chunk, info.cell_rows)
+        keep = lax.dynamic_index_in_dim(both, yb, 1, keepdims=False)
+        send = lax.dynamic_index_in_dim(both, 1 - yb, 1, keepdims=False)
+        paired[level] = keep, swap(send, "blk", 1)
 
     def pieces_of(value, level):
         pieces = [value]
@@ -681,7 +690,7 @@
     parts = (base[0].astype(F32) + received[0].astype(F32)).astype(BF16)
     for level in uppers:
         info = infos[level - 1]
-        parts = exchange_outer(parts, level)
+        parts = (exchange_outer if level == 1 else exchange_middle)(parts, level)
         gathered = exchange_inner(sum_spread(parts, info.cells), level)
         size = info.cell_rows * width * info.chunk
         count = 4 * info.pair_x
@@ -699,11 +708,11 @@
             functools.partial(forward_kernel, infos, level),
             [
                 shaped((info.cell_rows, info.chunk), F32),
-                shaped((above.targets, above.chunk, above.cell_rows), BF16),
+                shaped((above.targets // 2, above.chunk, above.cell_rows), BF16),
             ],
             [gathered]
             + hbm(
-                [base[2 * level], received[level]]
+                list(paired[level + 1])
                 + inverse_pieces[level]
                 + [ys[j] for j in range(1, level)]
                 + [dense[j, level + 1] for j in range(1, level + 1)]
@@ -712,8 +721,8 @@
             scratch=[
                 pltpu.VMEM((above.chunk * above.pair_x, width), F32),
                 cell_scratch(info),
-                pltpu.VMEM((above.targets, above.chunk, above.cell_rows), BF16),
-                pltpu.VMEM((above.targets, above.chunk, above.cell_rows), BF16),
+                pltpu.VMEM((above.targets // 2, above.chunk, above.cell_rows), BF16),
+                pltpu.VMEM((above.targets // 2, above.chunk, above.cell_rows), BF16),
                 pltpu.SemaphoreType.DMA((count + GROUPS * level + 1 + level,)),
             ]
             + [cell_scratch(infos[j - 1]) for j in range(1, level + 1)]
@@ -756,7 +765,8 @@
                 [shaped((2 * counts[0], half_cases), F32)],
                 hbm([dense[0, level], dense_near[level]])
                 + [solved[level], swapped[level]]
-                + hbm(low),
+                + [(low[0], None)]
+                + [(value, False) for value in low[1:]],
                 scalars=at,
                 scratch=[
                     pltpu.VMEM((half_cases, width), BF16),
@@ -772,7 +782,7 @@
         [shaped((blocks, half_cases, counts[0]), BF16)],
         hbm([dense[0, 1], dense_near[1]])
         + [solved[1], swapped[1]]
-        + hbm([inverse, inverse_near, low[0]]),
+        + [(inverse, None), (inverse_near, False), (low[0], None)],
         scalars=at,
         scratch=[
             pltpu.VMEM((half_cases, width), BF16),

time: 177 us -> 175 us (0.989)
  waiting for transfers between devices: 68.5 us -> 62.9 us
  starting transfers between devices: 60 us -> 61.9 us
    all_to_all x1, waiting for transfers between devices: 8.54 us -> 0.01 us  [exchange_outer(): return lax.all_to_all(value, 'blk', 0, 0, tiled=True)]
    all_to_all x1 -> x2, waiting for transfers between devices: 0.01 us -> 6.42 us  [exchange_middle(): lax.all_to_all(value, ('leaf', 'blk'), 0, 0, axis_index_groups=info.middl...]
    all_to_all x1 -> x2, starting transfers between devices: 3.55 us -> 9.21 us  [exchange_middle(): lax.all_to_all(value, ('leaf', 'blk'), 0, 0, axis_index_groups=info.middl...]
    all_to_all x1 -> x0, starting transfers between devices: 5.42 us -> none  [exchange_outer(): lax.all_to_all(value, ('leaf', 'blk'), 0, 0, axis_index_groups=infos[leve...]
    ppermute x22 -> x23, starting transfers between devices: 14 us -> 18 us  [swap(): return lax.ppermute(value, axis, [(i, i ^ bit) for i in range(size)])]
    ppermute x22 -> x23, waiting for transfers between devices: 31.8 us -> 27.9 us  [swap(): return lax.ppermute(value, axis, [(i, i ^ bit) for i in range(size)])]
  transfers between devices with their start and end apart: 32 -> 33, of which waited for: 14 -> 12; matrix products, arithmetic and copies ran while one was open for 3% -> 5% of each run, Pallas kernels for 17% -> 17%
where the time goes in v5:
time: 175 us; the launch traced here: 174 us
  waiting for transfers between devices  62.9 us (36%)
  starting transfers between devices  61.9 us (35%)
  Pallas kernels  39.7 us (23%)
  local copies, waits for them, and re-layouts  6.41 us (4%)
  other arithmetic  2.23 us (1%)
    pallas_call x16, Pallas kernels, kernel_call(): pl.pallas_call(body if scalars is None else lambda *refs: body(scalars(),...  39.7 us
    ppermute x23, waiting for transfers between devices, swap(): return lax.ppermute(value, axis, [(i, i ^ bit) for i in range(size)])  27.9 us
    ppermute x23, starting transfers between devices, swap(): return lax.ppermute(value, axis, [(i, i ^ bit) for i in range(size)])  18 us
    all_to_all x4, starting transfers between devices, exchange_inner(): lax.all_to_all(value, 'blk', 0, 0, axis_index_groups=info.inner_blk, tile...  15 us
    all_to_all x4, waiting for transfers between devices, exchange_inner(): lax.all_to_all(value, 'blk', 0, 0, axis_index_groups=info.inner_blk, tile...  10.2 us
    all_to_all x2, starting transfers between devices, exchange_middle(): lax.all_to_all(value, ('leaf', 'blk'), 0, 0, axis_index_groups=info.middl...  9.21 us
    all_to_all x1, waiting for transfers between devices, solve(): full = lax.all_to_all(spread, 'blk', 0, 0, tiled=True).reshape(width, cases)  9.01 us
    all_to_all x1, starting transfers between devices, solve(): full = lax.all_to_all(spread, 'blk', 0, 0, tiled=True).reshape(width, cases)  7.32 us
  transfers between devices with their start and end apart: 33, of which 12 were waited for; matrix products, arithmetic and copies ran while one was open for 5% of the time, Pallas kernels for 17%

profile of v5, /device:TPU:0, one launch (start us, length us, event | category | flops | bytes accessed | tf_op | source)
XLA Modules:
  0.0 173.5 jit_solution(2590091397154502114)
XLA Ops:
  1.9 7.3 %all-to-all-start = ((bf16[8,256,128]{2,1,0:T(8,128)(2,1)}), bf16[8,256,128]{2,1,0:T(8,128)(2,1)S(1)}, u32[]{:S(2)}, u32[]{:S(2)}) async-start(bf16[8,256,128]{2,1,0:T(8,128)(2,1)} %shard_map.48), calls=%async_computation | async-start | bytes 1048576 | tf_op jit(solution)/shard_map/all_to_all | solution.py:602
  11.3 3.4 %shard_map.46 = (bf16[256,2048]{1,0:T(8,128)(2,1)}, bf16[256,2048]{1,0:T(8,128)(2,1)}) custom-call(s32[10,1024]{1,0:T(8,128)S(1)} %copy-done.1, bf16[640,1024]{1,0:T(8,128)(2,1)S(1)} %bitcast.39), custom_call_target="tpu_custom_call" | custom-call | flops 2147483648 | bytes 3448832 | tf_op jit(solution)/shard_map/pallas_call | solution.py:47
  14.7 9.0 %all-to-all-done = bf16[8,256,128]{2,1,0:T(8,128)(2,1)S(1)} async-done(((bf16[8,256,128]{2,1,0:T(8,128)(2,1)}), bf16[8,256,128]{2,1,0:T(8,128)(2,1)S(1)}, u32[]{:S(2)}, u32[]{:S(2)}) %all-to-all-start) | async-done | bytes 524320 | tf_op jit(solution)/shard_map/all_to_all | solution.py:602
  23.7 4.3 %shard_map.49 = (f32[256,64]{1,0:T(8,128)}, f32[256,64]{1,0:T(8,128)}, bf16[8,32,512]{2,1,0:T(8,128)(2,1)S(1)}, bf16[8,32,512]{2,1,0:T(8,128)(2,1)S(1)}, bf16[16...) custom-call(bf16[2048,128]{1,0:T(8,128)(2,1)S(1)} %bitcast.38, bf16[448,2048]{1,0:T(8,128)(2,1)} %bitcast.42, ...), custom_call_target="tpu_custom_call" | custom-call | flops 402653184 | bytes 5865472 | tf_op jit(solution)/shard_map/pallas_call | solution.py:47
  32.0 3.4 %all-to-all-start.1 = ((bf16[8,32,512]{2,1,0:T(8,128)(2,1)}), bf16[8,32,512]{2,1,0:T(8,128)(2,1)S(1)}, u32[]{:S(2)}, u32[]{:S(2)}) async-start(bf16[8,32,512]{2,1,0:T(8,128)(2,1)} %add_convert_fusion.1), calls=%async_computation.1 | async-start | bytes 524288 | tf_op jit(solution)/shard_map/all_to_all | solution.py:544
  37.9 8.2 %collective-permute-done.4.refs_4_.refs_2_ = bf16[128,2048]{1,0:T(8,128)(2,1)} collective-permute-done((bf16[128,2048]{1,0:T(8,128)(2,1)S(1)}, bf16[128,2048]{1,0:T(8,128)(2,1)}, u32[]{:S(2)}, u32[]{:S(2)}) %collective-permute-start.4) | collective-permute-done | bytes 524320 | tf_op jit(solution)/shard_map/ppermute | solution.py:535
  49.2 3.3 %all-to-all-start.2 = ((bf16[4,32,512]{2,1,0:T(8,128)(2,1)}), bf16[4,32,512]{2,1,0:T(8,128)(2,1)S(1)}, u32[]{:S(2)}, u32[]{:S(2)}) async-start(bf16[4,32,512]{2,1,0:T(8,128)(2,1)} %shard_map.50), calls=%async_computation.2 | async-start | bytes 262144 | tf_op jit(solution)/shard_map/all_to_all | solution.py:567
  56.1 3.7 %shard_map.51.refs_7_.refs_6_ = bf16[512,2048]{1,0:T(8,128)(2,1)} custom-call(s32[10,1024]{1,0:T(8,128)S(1)} %copy-done.1, bf16[128,1024]{1,0:T(8,128)(2,1)S(1)} %slice_bitcast_fusion.5.refs_1_, bf16[128,1024]{1,0:T(8,128)(2,1)S(1)} %collective-permute-done.7.refs_2_, bf16[128,1024]{1,0:T(8,128)(2,1)S(1)} %collective-permute-done.8.refs_3_, ...), custom_call_target="tpu_custom_call" | custom-call | flops 2147483648 | bytes 3186688 | tf_op jit(solution)/shard_map/pallas_call | solution.py:47
  59.8 9.4 %collective-permute-done.3.refs_2_ = bf16[8,16,512]{2,1,0:T(8,128)(2,1)S(1)} collective-permute-done((bf16[8,16,512]{2,1,0:T(8,128)(2,1)}, bf16[8,16,512]{2,1,0:T(8,128)(2,1)S(1)}, u32[]{:S(2)}, u32[]{:S(2)}) %collective-permute-start.3) | collective-permute-done | bytes 131104 | tf_op jit(solution)/shard_map/ppermute | solution.py:535
  69.9 3.8 %shard_map.52 = (f32[512,32]{1,0:T(8,128)}, bf16[8,16,512]{2,1,0:T(8,128)(2,1)}) custom-call(bf16[4,32,512]{2,1,0:T(8,128)(2,1)S(1)} %all-to-all-done.2.refs_0_, bf16[8,16,512]{2,1,0:T(8,128)(2,1)} %get-tuple-element.28.refs_1_, bf16[8,16,512]{2,1,0:T(8,128)(2,1)} %copy-done.8, bf16[128,2048]{1,0:T(8,128)(2,1)} %copy-done.2, ...), custom_call_target="tpu_custom_call" | custom-call | flops 134217728 | bytes 4784128 | tf_op jit(solution)/shard_map/pallas_call | solution.py:47
  73.7 5.7 %all-to-all-start.3 = ((bf16[8,16,512]{2,1,0:T(8,128)(2,1)}), bf16[8,16,512]{2,1,0:T(8,128)(2,1)S(1)}, u32[]{:S(2)}, u32[]{:S(2)}) async-start(bf16[8,16,512]{2,1,0:T(8,128)(2,1)} %get-tuple-element.22), calls=%async_computation.3 | async-start | bytes 262144 | tf_op jit(solution)/shard_map/all_to_all | solution.py:560
  80.5 6.4 %all-to-all-done.3.parts = bf16[8,16,512]{2,1,0:T(8,128)(2,1)S(1)} async-done(((bf16[8,16,512]{2,1,0:T(8,128)(2,1)}), bf16[8,16,512]{2,1,0:T(8,128)(2,1)S(1)}, u32[]{:S(2)}, u32[]{:S(2)}) %all-to-all-start.3) | async-done | bytes 131104 | tf_op jit(solution)/shard_map/all_to_all | solution.py:560
  87.5 3.3 %all-to-all-start.4 = ((bf16[4,16,512]{2,1,0:T(8,128)(2,1)}), bf16[4,16,512]{2,1,0:T(8,128)(2,1)S(1)}, u32[]{:S(2)}, u32[]{:S(2)}) async-start(bf16[4,16,512]{2,1,0:T(8,128)(2,1)} %shard_map.53), calls=%async_computation.4 | async-start | bytes 131072 | tf_op jit(solution)/shard_map/all_to_all | solution.py:567
  90.9 5.6 %all-to-all-done.4.gathered = bf16[4,16,512]{2,1,0:T(8,128)(2,1)S(1)} async-done(((bf16[4,16,512]{2,1,0:T(8,128)(2,1)}), bf16[4,16,512]{2,1,0:T(8,128)(2,1)S(1)}, u32[]{:S(2)}, u32[]{:S(2)}) %all-to-all-start.4) | async-done | bytes 65568 | tf_op jit(solution)/shard_map/all_to_all | solution.py:567
  96.5 3.2 %shard_map.54 = bf16[4,16,512]{2,1,0:T(8,128)(2,1)} custom-call(bf16[4,16,512]{2,1,0:T(8,128)(2,1)S(1)} %all-to-all-done.4.gathered, bf16[64,2048]{1,0:T(8,128)(2,1)} %copy-done.3, bf16[64,2048]{1,0:T(8,128)(2,1)} %collective-permute-done.10.refs_1_, bf16[64,2048]{1,0:T(8,128)(2,1)} %collective-permute-done.11.refs_2_, ...), custom_call_target="tpu_custom_call" | custom-call | flops 67108864 | bytes 2228224 | tf_op jit(solution)/shard_map/pallas_call | solution.py:47
  99.7 3.3 %all-to-all-start.5 = ((bf16[4,16,512]{2,1,0:T(8,128)(2,1)}), bf16[4,16,512]{2,1,0:T(8,128)(2,1)S(1)}, u32[]{:S(2)}, u32[]{:S(2)}) async-start(bf16[4,16,512]{2,1,0:T(8,128)(2,1)} %shard_map.54), calls=%async_computation.5 | async-start | bytes 131072 | tf_op jit(solution)/shard_map/all_to_all | solution.py:567
  106.1 2.6 %all-to-all-done.5.parts = bf16[4,16,512]{2,1,0:T(8,128)(2,1)S(1)} async-done(((bf16[4,16,512]{2,1,0:T(8,128)(2,1)}), bf16[4,16,512]{2,1,0:T(8,128)(2,1)S(1)}, u32[]{:S(2)}, u32[]{:S(2)}) %all-to-all-start.5) | async-done | bytes 65568 | tf_op jit(solution)/shard_map/all_to_all | solution.py:567
  109.4 3.5 %all-to-all-start.6 = ((bf16[8,16,512]{2,1,0:T(8,128)(2,1)}), bf16[8,16,512]{2,1,0:T(8,128)(2,1)S(1)}, u32[]{:S(2)}, u32[]{:S(2)}) async-start(bf16[8,16,512]{2,1,0:T(8,128)(2,1)} %shard_map.55), calls=%async_computation.6 | async-start | bytes 262144 | tf_op jit(solution)/shard_map/all_to_all | solution.py:560
  115.8 3.4 %collective-permute-done.19.refs_1_ = bf16[256,1024]{1,0:T(8,128)(2,1)S(1)} collective-permute-done((bf16[256,1024]{1,0:T(8,128)(2,1)}, bf16[256,1024]{1,0:T(8,128)(2,1)S(1)}, u32[]{:S(2)}, u32[]{:S(2)}) %collective-permute-start.19) | collective-permute-done | bytes 524320 | tf_op jit(solution)/shard_map/ppermute | solution.py:535
  119.1 2.3 %shard_map.58.refs_1_ = bf16[256,2048]{1,0:T(8,128)(2,1)} custom-call(s32[10,1024]{1,0:T(8,128)S(1)} %copy-done.1, bf16[256,1024]{1,0:T(8,128)(2,1)S(1)} %collective-permute-done.19.refs_1_), custom_call_target="tpu_custom_call" | custom-call | flops 1073741824 | bytes 1613824 | tf_op jit(solution)/shard_map/pallas_call | solution.py:47
  121.4 3.9 %shard_map.56 = bf16[4,32,512]{2,1,0:T(8,128)(2,1)} custom-call(f32[512,32]{1,0:T(8,128)} %get-tuple-element.21.refs_0_, bf16[128,2048]{1,0:T(8,128)(2,1)} %copy-done.2, bf16[128,2048]{1,0:T(8,128)(2,1)} %collective-permute-done.4.refs_4_.refs_2_, bf16[128,2048]{1,0:T(8,128)(2,1)} %collective-permute-done.5.refs_5_.refs_3_, ...), custom_call_target="tpu_custom_call" | custom-call | flops 134217728 | bytes 4521984 | tf_op jit(solution)/shard_map/pallas_call | solution.py:47
  125.4 5.1 %all-to-all-start.7 = ((bf16[4,32,512]{2,1,0:T(8,128)(2,1)}), bf16[4,32,512]{2,1,0:T(8,128)(2,1)S(1)}, u32[]{:S(2)}, u32[]{:S(2)}) async-start(bf16[4,32,512]{2,1,0:T(8,128)(2,1)} %shard_map.56), calls=%async_computation.7 | async-start | bytes 262144 | tf_op jit(solution)/shard_map/all_to_all | solution.py:567
  130.4 2.3 %shard_map.47.refs_1_ = bf16[256,2048]{1,0:T(8,128)(2,1)} custom-call(s32[10,1024]{1,0:T(8,128)S(1)} %copy-done.1, bf16[256,1024]{1,0:T(8,128)(2,1)S(1)} %collective-permute-done.refs_1_), custom_call_target="tpu_custom_call" | custom-call | flops 1073741824 | bytes 1613824 | tf_op jit(solution)/shard_map/pallas_call | solution.py:47
  137.0 3.3 %all-to-all-start.8 = ((bf16[4,32,512]{2,1,0:T(8,128)(2,1)}), bf16[4,32,512]{2,1,0:T(8,128)(2,1)S(1)}, u32[]{:S(2)}, u32[]{:S(2)}) async-start(bf16[4,32,512]{2,1,0:T(8,128)(2,1)} %shard_map.57), calls=%async_computation.8 | async-start | bytes 262144 | tf_op jit(solution)/shard_map/all_to_all | solution.py:557
  140.6 5.8 %all-to-all-done.8.refs_2_ = bf16[4,32,512]{2,1,0:T(8,128)(2,1)S(1)} async-done(((bf16[4,32,512]{2,1,0:T(8,128)(2,1)}), bf16[4,32,512]{2,1,0:T(8,128)(2,1)S(1)}, u32[]{:S(2)}, u32[]{:S(2)}) %all-to-all-start.8) | async-done | bytes 131104 | tf_op jit(solution)/shard_map/all_to_all | solution.py:557
  146.4 4.6 %collective-permute-done.21.refs_5_ = f32[256,64]{1,0:T(8,128)S(1)} collective-permute-done((f32[256,64]{1,0:T(8,128)S(1)}, f32[256,64]{1,0:T(8,128)S(1)}, u32[]{:S(2)}, u32[]{:S(2)}) %collective-permute-start.21) | collective-permute-done | bytes 65568 | tf_op jit(solution)/shard_map/ppermute | solution.py:535
  151.1 3.5 %shard_map.59.refs_6_ = f32[512,64]{1,0:T(8,128)} custom-call(bf16[256,2048]{1,0:T(8,128)(2,1)} %get-tuple-element.16.refs_4_.refs_0_, bf16[256,2048]{1,0:T(8,128)(2,1)} %shard_map.58.refs_1_, bf16[8,16,512]{2,1,0:T(8,128)(2,1)S(1)} %all-to-all-done.6.refs_5_.refs_2_, bf16[8,16,512]{2,1,0:T(8,128)(2,1)S(1)} %collective-permute-done.20.refs_3_, ...), custom_call_target="tpu_custom_call" | custom-call | flops 134217728 | bytes 2621440 | tf_op jit(solution)/shard_map/pallas_call | solution.py:47
  154.8 4.0 %shard_map.60 = bf16[8,64,256]{2,1,0:T(8,128)(2,1)} custom-call(bf16[256,2048]{1,0:T(8,128)(2,1)} %get-tuple-element.15.refs_3_.refs_0_, bf16[256,2048]{1,0:T(8,128)(2,1)} %shard_map.47.refs_1_, bf16[4,32,512]{2,1,0:T(8,128)(2,1)S(1)} %all-to-all-done.8.refs_2_, bf16[4,32,512]{2,1,0:T(8,128)(2,1)S(1)} %collective-permute-done.17.refs_3_, ...), custom_call_target="tpu_custom_call" | custom-call | flops 268435456 | bytes 5636096 | tf_op jit(solution)/shard_map/pallas_call | solution.py:47
  158.8 5.7 %all-to-all-start.9 = ((bf16[8,64,256]{2,1,0:T(8,128)(2,1)}), bf16[8,64,256]{2,1,0:T(8,128)(2,1)S(1)}, u32[]{:S(2)}, u32[]{:S(2)}) async-start(bf16[8,64,256]{2,1,0:T(8,128)(2,1)} %shard_map.60), calls=%async_computation.9 | async-start | bytes 524288 | tf_op jit(solution)/shard_map/all_to_all | solution.py:796
  164.7 2.1 %collective-permute-start.22 = (bf16[64,192]{0,1:T(8,128)(2,1)S(1)}, bf16[64,192]{0,1:T(8,128)(2,1)S(1)}, u32[]{:S(2)}, u32[]{:S(2)}) collective-permute-start(bf16[64,192]{0,1:T(8,128)(2,1)S(1)} %pad_maximum_fusion), channel_id=1, source_target_pairs={{0,1},{1,0},{2,3},{3,2},{4,5},{5,4},{6,7},{7,6},{8,9},{9,8},{10,11... | collective-permute-start | bytes 73736 | tf_op jit(solution)/shard_map/ppermute | solution.py:535
  166.7 2.4 %collective-permute-done.22 = bf16[64,192]{0,1:T(8,128)(2,1)S(1)} collective-permute-done((bf16[64,192]{0,1:T(8,128)(2,1)S(1)}, bf16[64,192]{0,1:T(8,128)(2,1)S(1)}, u32[]{:S(2)}, u32[]{:S(2)}) %collective-permute-start.22) | collective-permute-done | bytes 24608 | tf_op jit(solution)/shard_map/ppermute | solution.py:535
  169.2 3.5 %all-to-all-done.9.parts = bf16[8,64,256]{2,1,0:T(8,128)(2,1)S(1)} async-done(((bf16[8,64,256]{2,1,0:T(8,128)(2,1)}), bf16[8,64,256]{2,1,0:T(8,128)(2,1)S(1)}, u32[]{:S(2)}, u32[]{:S(2)}) %all-to-all-start.9) | async-done | bytes 262176 | tf_op jit(solution)/shard_map/all_to_all | solution.py:796
  (92 shorter events, 31.9 us)
Async XLA Ops:
  1.9 21.8 %all-to-all-start = ((bf16[8,256,128]{2,1,0:T(8,128)(2,1)}), bf16[8,256,128]{2,1,0:T(8,128)(2,1)S(1)}, u32[]{:S(2)}, u32[]{:S(2)}) async-start(bf16[8,256,128]{2,1,0:T(8,128)(2,1)} %shard_map.48), calls=%async_computation | async-start | bytes 1048576 | tf_op jit(solution)/shard_map/all_to_all | solution.py:602
  9.2 27.2 %collective-permute-start.7 = (bf16[128,1024]{1,0:T(8,128)(2,1)S(1)}, bf16[128,1024]{1,0:T(8,128)(2,1)S(1)}, u32[]{:S(2)}, u32[]{:S(2)}) collective-permute-start(bf16[128,1024]{1,0:T(8,128)(2,1)S(1)} %slice_bitcast_fusion.5.refs_1_), channel_id=1, source_target_pairs={{0,1},{1,0},{2,3},{3,2},{4,5},{5,4},{6,7},{7,6},{8,9},{9,8},{10,11... | collective-permute-start | bytes 786440 | tf_op jit(solution)/shard_map/ppermute | solution.py:535
  11.3 41.2 %collective-permute-start.8 = (bf16[128,1024]{1,0:T(8,128)(2,1)S(1)}, bf16[128,1024]{1,0:T(8,128)(2,1)S(1)}, u32[]{:S(2)}, u32[]{:S(2)}) collective-permute-start(bf16[128,1024]{1,0:T(8,128)(2,1)S(1)} %slice_bitcast_fusion.5.refs_1_), channel_id=1, source_target_pairs={{0,8},{8,0},{16,24},{24,16},{1,9},{9,1},{17,25},{25,17},{2,10},{10... | collective-permute-start | bytes 786440 | tf_op jit(solution)/shard_map/ppermute | solution.py:535
  29.1 16.9 %collective-permute-start.4 = (bf16[128,2048]{1,0:T(8,128)(2,1)S(1)}, bf16[128,2048]{1,0:T(8,128)(2,1)}, u32[]{:S(2)}, u32[]{:S(2)}) collective-permute-start(bf16[128,2048]{1,0:T(8,128)(2,1)S(1)} %slice_bitcast_fusion.2.refs_3_.refs_1_), channel_id=1, source_target_pairs={{0,1},{1,0},{2,3},{3,2},{4,5},{5,4},{6,7},{7,6},{8,9},{9,8},{10,11... | collective-permute-start | bytes 1572872 | tf_op jit(solution)/shard_map/ppermute | solution.py:535
  30.7 29.1 %collective-permute-start.5 = (bf16[128,2048]{1,0:T(8,128)(2,1)S(1)}, bf16[128,2048]{1,0:T(8,128)(2,1)}, u32[]{:S(2)}, u32[]{:S(2)}) collective-permute-start(bf16[128,2048]{1,0:T(8,128)(2,1)S(1)} %slice_bitcast_fusion.2.refs_3_.refs_1_), channel_id=1, source_target_pairs={{0,8},{8,0},{16,24},{24,16},{1,9},{9,1},{17,25},{25,17},{2,10},{10... | collective-permute-start | bytes 1572872 | tf_op jit(solution)/shard_map/ppermute | solution.py:535
  30.9 15.2 %collective-permute-start.2 = (bf16[16,16,512]{2,1,0:T(8,128)(2,1)}, bf16[16,16,512]{2,1,0:T(8,128)(2,1)}, u32[]{:S(2)}, u32[]{:S(2)}) collective-permute-start(bf16[16,16,512]{2,1,0:T(8,128)(2,1)} %get-tuple-element.20), channel_id=1, source_target_pairs={{0,8},{8,0},{16,24},{24,16},{1,9},{9,1},{17,25},{25,17},{2,10},{10... | collective-permute-start | bytes 786440 | tf_op jit(solution)/shard_map/ppermute | solution.py:535
  32.0 16.5 %all-to-all-start.1 = ((bf16[8,32,512]{2,1,0:T(8,128)(2,1)}), bf16[8,32,512]{2,1,0:T(8,128)(2,1)S(1)}, u32[]{:S(2)}, u32[]{:S(2)}) async-start(bf16[8,32,512]{2,1,0:T(8,128)(2,1)} %add_convert_fusion.1), calls=%async_computation.1 | async-start | bytes 524288 | tf_op jit(solution)/shard_map/all_to_all | solution.py:544
  36.4 17.7 %collective-permute-start.10 = (bf16[64,2048]{1,0:T(8,128)(2,1)S(1)}, bf16[64,2048]{1,0:T(8,128)(2,1)}, u32[]{:S(2)}, u32[]{:S(2)}) collective-permute-start(bf16[64,2048]{1,0:T(8,128)(2,1)S(1)} %slice_bitcast_fusion.4.refs_0_), channel_id=1, source_target_pairs={{0,16},{8,24},{16,0},{24,8},{1,17},{9,25},{17,1},{25,9},{2,18},{10... | collective-permute-start | bytes 786440 | tf_op jit(solution)/shard_map/ppermute | solution.py:535
  46.1 8.5 %collective-permute-start.9 = (bf16[128,1024]{1,0:T(8,128)(2,1)S(1)}, bf16[128,1024]{1,0:T(8,128)(2,1)S(1)}, u32[]{:S(2)}, u32[]{:S(2)}) collective-permute-start(bf16[128,1024]{1,0:T(8,128)(2,1)S(1)} %collective-permute-done.7.refs_2_), channel_id=1, source_target_pairs={{0,8},{8,0},{16,24},{24,16},{1,9},{9,1},{17,25},{25,17},{2,10},{10... | collective-permute-start | bytes 786440 | tf_op jit(solution)/shard_map/ppermute | solution.py:535
  46.1 13.7 %collective-permute-start.6 = (bf16[128,2048]{1,0:T(8,128)(2,1)}, bf16[128,2048]{1,0:T(8,128)(2,1)}, u32[]{:S(2)}, u32[]{:S(2)}) collective-permute-start(bf16[128,2048]{1,0:T(8,128)(2,1)} %collective-permute-done.4.refs_4_.refs_2_), channel_id=1, source_target_pairs={{0,8},{8,0},{16,24},{24,16},{1,9},{9,1},{17,25},{25,17},{2,10},{10... | collective-permute-start | bytes 1572872 | tf_op jit(solution)/shard_map/ppermute | solution.py:535
  49.2 20.1 %all-to-all-start.2 = ((bf16[4,32,512]{2,1,0:T(8,128)(2,1)}), bf16[4,32,512]{2,1,0:T(8,128)(2,1)S(1)}, u32[]{:S(2)}, u32[]{:S(2)}) async-start(bf16[4,32,512]{2,1,0:T(8,128)(2,1)} %shard_map.50), calls=%async_computation.2 | async-start | bytes 262144 | tf_op jit(solution)/shard_map/all_to_all | solution.py:567
  52.5 27.4 %collective-permute-start.11 = (bf16[64,2048]{1,0:T(8,128)(2,1)S(1)}, bf16[64,2048]{1,0:T(8,128)(2,1)}, u32[]{:S(2)}, u32[]{:S(2)}) collective-permute-start(bf16[64,2048]{1,0:T(8,128)(2,1)S(1)} %slice_bitcast_fusion.4.refs_0_), channel_id=1, source_target_pairs={{0,1},{1,0},{2,3},{3,2},{4,5},{5,4},{6,7},{7,6},{8,9},{9,8},{10,11... | collective-permute-start | bytes 786440 | tf_op jit(solution)/shard_map/ppermute | solution.py:535
  54.1 26.0 %collective-permute-start.12 = (bf16[64,2048]{1,0:T(8,128)(2,1)}, bf16[64,2048]{1,0:T(8,128)(2,1)}, u32[]{:S(2)}, u32[]{:S(2)}) collective-permute-start(bf16[64,2048]{1,0:T(8,128)(2,1)} %collective-permute-done.10.refs_1_), channel_id=1, source_target_pairs={{0,1},{1,0},{2,3},{3,2},{4,5},{5,4},{6,7},{7,6},{8,9},{9,8},{10,11... | collective-permute-start | bytes 786440 | tf_op jit(solution)/shard_map/ppermute | solution.py:535
  54.6 14.6 %collective-permute-start.3 = (bf16[8,16,512]{2,1,0:T(8,128)(2,1)}, bf16[8,16,512]{2,1,0:T(8,128)(2,1)S(1)}, u32[]{:S(2)}, u32[]{:S(2)}) collective-permute-start(bf16[8,16,512]{2,1,0:T(8,128)(2,1)} %get-tuple-element.27), channel_id=1, source_target_pairs={{0,1},{1,0},{2,3},{3,2},{4,5},{5,4},{6,7},{7,6},{8,9},{9,8},{10,11... | collective-permute-start | bytes 393224 | tf_op jit(solution)/shard_map/ppermute | solution.py:535
  73.7 13.2 %all-to-all-start.3 = ((bf16[8,16,512]{2,1,0:T(8,128)(2,1)}), bf16[8,16,512]{2,1,0:T(8,128)(2,1)S(1)}, u32[]{:S(2)}, u32[]{:S(2)}) async-start(bf16[8,16,512]{2,1,0:T(8,128)(2,1)} %get-tuple-element.22), calls=%async_computation.3 | async-start | bytes 262144 | tf_op jit(solution)/shard_map/all_to_all | solution.py:560
  79.4 11.4 %collective-permute-start.13 = (bf16[64,2048]{1,0:T(8,128)(2,1)S(1)}, bf16[64,2048]{1,0:T(8,128)(2,1)S(1)}, u32[]{:S(2)}, u32[]{:S(2)}) collective-permute-start(bf16[64,2048]{1,0:T(8,128)(2,1)S(1)} %slice_bitcast_fusion.4.refs_0_), channel_id=1, source_target_pairs={{0,8},{8,0},{16,24},{24,16},{1,9},{9,1},{17,25},{25,17},{2,10},{10... | collective-permute-start | bytes 786440 | tf_op jit(solution)/shard_map/ppermute | solution.py:535
  79.4 11.4 %collective-permute-start.14 = (bf16[64,2048]{1,0:T(8,128)(2,1)}, bf16[64,2048]{1,0:T(8,128)(2,1)S(1)}, u32[]{:S(2)}, u32[]{:S(2)}) collective-permute-start(bf16[64,2048]{1,0:T(8,128)(2,1)} %collective-permute-done.10.refs_1_), channel_id=1, source_target_pairs={{0,8},{8,0},{16,24},{24,16},{1,9},{9,1},{17,25},{25,17},{2,10},{10... | collective-permute-start | bytes 786440 | tf_op jit(solution)/shard_map/ppermute | solution.py:535
  79.9 10.9 %collective-permute-start.15 = (bf16[64,2048]{1,0:T(8,128)(2,1)}, bf16[64,2048]{1,0:T(8,128)(2,1)S(1)}, u32[]{:S(2)}, u32[]{:S(2)}) collective-permute-start(bf16[64,2048]{1,0:T(8,128)(2,1)} %collective-permute-done.11.refs_2_), channel_id=1, source_target_pairs={{0,8},{8,0},{16,24},{24,16},{1,9},{9,1},{17,25},{25,17},{2,10},{10... | collective-permute-start | bytes 786440 | tf_op jit(solution)/shard_map/ppermute | solution.py:535
  80.0 10.8 %collective-permute-start.16 = (bf16[64,2048]{1,0:T(8,128)(2,1)}, bf16[64,2048]{1,0:T(8,128)(2,1)S(1)}, u32[]{:S(2)}, u32[]{:S(2)}) collective-permute-start(bf16[64,2048]{1,0:T(8,128)(2,1)} %collective-permute-done.12.refs_3_), channel_id=1, source_target_pairs={{0,8},{8,0},{16,24},{24,16},{1,9},{9,1},{17,25},{25,17},{2,10},{10... | collective-permute-start | bytes 786440 | tf_op jit(solution)/shard_map/ppermute | solution.py:535
  87.5 9.0 %all-to-all-start.4 = ((bf16[4,16,512]{2,1,0:T(8,128)(2,1)}), bf16[4,16,512]{2,1,0:T(8,128)(2,1)S(1)}, u32[]{:S(2)}, u32[]{:S(2)}) async-start(bf16[4,16,512]{2,1,0:T(8,128)(2,1)} %shard_map.53), calls=%async_computation.4 | async-start | bytes 131072 | tf_op jit(solution)/shard_map/all_to_all | solution.py:567
  99.7 9.0 %all-to-all-start.5 = ((bf16[4,16,512]{2,1,0:T(8,128)(2,1)}), bf16[4,16,512]{2,1,0:T(8,128)(2,1)S(1)}, u32[]{:S(2)}, u32[]{:S(2)}) async-start(bf16[4,16,512]{2,1,0:T(8,128)(2,1)} %shard_map.54), calls=%async_computation.5 | async-start | bytes 131072 | tf_op jit(solution)/shard_map/all_to_all | solution.py:567
  104.1 15.0 %collective-permute-start.19 = (bf16[256,1024]{1,0:T(8,128)(2,1)}, bf16[256,1024]{1,0:T(8,128)(2,1)S(1)}, u32[]{:S(2)}, u32[]{:S(2)}) collective-permute-start(bf16[256,1024]{1,0:T(8,128)(2,1)} %get-tuple-element.25), channel_id=1, source_target_pairs={{0,1},{1,0},{2,3},{3,2},{4,5},{5,4},{6,7},{7,6},{8,9},{9,8},{10,11... | collective-permute-start | bytes 1572872 | tf_op jit(solution)/shard_map/ppermute | solution.py:535
  105.6 24.9 %collective-permute-start = (bf16[256,1024]{1,0:T(8,128)(2,1)}, bf16[256,1024]{1,0:T(8,128)(2,1)S(1)}, u32[]{:S(2)}, u32[]{:S(2)}) collective-permute-start(bf16[256,1024]{1,0:T(8,128)(2,1)} %get-tuple-element.26), channel_id=1, source_target_pairs={{0,1},{1,0},{2,3},{3,2},{4,5},{5,4},{6,7},{7,6},{8,9},{9,8},{10,11... | collective-permute-start | bytes 1572872 | tf_op jit(solution)/shard_map/ppermute | solution.py:535
  109.4 12.0 %all-to-all-start.6 = ((bf16[8,16,512]{2,1,0:T(8,128)(2,1)}), bf16[8,16,512]{2,1,0:T(8,128)(2,1)S(1)}, u32[]{:S(2)}, u32[]{:S(2)}) async-start(bf16[8,16,512]{2,1,0:T(8,128)(2,1)} %shard_map.55), calls=%async_computation.6 | async-start | bytes 262144 | tf_op jit(solution)/shard_map/all_to_all | solution.py:560
  114.2 40.6 %collective-permute-start.18 = (bf16[256,2048]{1,0:T(8,128)(2,1)S(1)}, bf16[256,2048]{1,0:T(8,128)(2,1)S(1)}, u32[]{:S(2)}, u32[]{:S(2)}) collective-permute-start(bf16[256,2048]{1,0:T(8,128)(2,1)S(1)} %slice_bitcast_fusion), channel_id=1, source_target_pairs={{0,1},{1,0},{2,3},{3,2},{4,5},{5,4},{6,7},{7,6},{8,9},{9,8},{10,11... | collective-permute-start | bytes 3145736 | tf_op jit(solution)/shard_map/ppermute | solution.py:535
  125.4 11.0 %all-to-all-start.7 = ((bf16[4,32,512]{2,1,0:T(8,128)(2,1)}), bf16[4,32,512]{2,1,0:T(8,128)(2,1)S(1)}, u32[]{:S(2)}, u32[]{:S(2)}) async-start(bf16[4,32,512]{2,1,0:T(8,128)(2,1)} %shard_map.56), calls=%async_computation.7 | async-start | bytes 262144 | tf_op jit(solution)/shard_map/all_to_all | solution.py:567
  130.4 9.9 %collective-permute-start.20 = (bf16[8,16,512]{2,1,0:T(8,128)(2,1)S(1)}, bf16[8,16,512]{2,1,0:T(8,128)(2,1)S(1)}, u32[]{:S(2)}, u32[]{:S(2)}) collective-permute-start(bf16[8,16,512]{2,1,0:T(8,128)(2,1)S(1)} %all-to-all-done.6.refs_5_.refs_2_), channel_id=1, source_target_pairs={{0,8},{8,0},{16,24},{24,16},{1,9},{9,1},{17,25},{25,17},{2,10},{10... | collective-permute-start | bytes 393224 | tf_op jit(solution)/shard_map/ppermute | solution.py:535
  132.8 18.3 %collective-permute-start.21 = (f32[256,64]{1,0:T(8,128)S(1)}, f32[256,64]{1,0:T(8,128)S(1)}, u32[]{:S(2)}, u32[]{:S(2)}) collective-permute-start(f32[256,64]{1,0:T(8,128)S(1)} %copy-done.9), channel_id=1, source_target_pairs={{0,1},{1,0},{2,3},{3,2},{4,5},{5,4},{6,7},{7,6},{8,9},{9,8},{10,11... | collective-permute-start | bytes 196616 | tf_op jit(solution)/shard_map/ppermute | solution.py:535
  137.0 9.4 %all-to-all-start.8 = ((bf16[4,32,512]{2,1,0:T(8,128)(2,1)}), bf16[4,32,512]{2,1,0:T(8,128)(2,1)S(1)}, u32[]{:S(2)}, u32[]{:S(2)}) async-start(bf16[4,32,512]{2,1,0:T(8,128)(2,1)} %shard_map.57), calls=%async_computation.8 | async-start | bytes 262144 | tf_op jit(solution)/shard_map/all_to_all | solution.py:557
  146.4 8.2 %collective-permute-start.17 = (bf16[4,32,512]{2,1,0:T(8,128)(2,1)S(1)}, bf16[4,32,512]{2,1,0:T(8,128)(2,1)S(1)}, u32[]{:S(2)}, u32[]{:S(2)}) collective-permute-start(bf16[4,32,512]{2,1,0:T(8,128)(2,1)S(1)} %all-to-all-done.8.refs_2_), channel_id=1, source_target_pairs={{0,8},{8,0},{16,24},{24,16},{1,9},{9,1},{17,25},{25,17},{2,10},{10... | collective-permute-start | bytes 393224 | tf_op jit(solution)/shard_map/ppermute | solution.py:535
  158.8 13.9 %all-to-all-start.9 = ((bf16[8,64,256]{2,1,0:T(8,128)(2,1)}), bf16[8,64,256]{2,1,0:T(8,128)(2,1)S(1)}, u32[]{:S(2)}, u32[]{:S(2)}) async-start(bf16[8,64,256]{2,1,0:T(8,128)(2,1)} %shard_map.60), calls=%async_computation.9 | async-start | bytes 524288 | tf_op jit(solution)/shard_map/all_to_all | solution.py:796
  164.7 4.5 %collective-permute-start.22 = (bf16[64,192]{0,1:T(8,128)(2,1)S(1)}, bf16[64,192]{0,1:T(8,128)(2,1)S(1)}, u32[]{:S(2)}, u32[]{:S(2)}) collective-permute-start(bf16[64,192]{0,1:T(8,128)(2,1)S(1)} %pad_maximum_fusion), channel_id=1, source_target_pairs={{0,1},{1,0},{2,3},{3,2},{4,5},{5,4},{6,7},{7,6},{8,9},{9,8},{10,11... | collective-permute-start | bytes 73736 | tf_op jit(solution)/shard_map/ppermute | solution.py:535
  (11 other events, 112.2 us)

commit v6 on v5

--- a/solution.py
+++ b/solution.py
@@ -308,6 +308,16 @@
         out[n] = rounded
 
 
+def sum_parts_kernel(*refs):
+    parts, out = refs[:-1], refs[-1]
+    total = parts[0][...].astype(F32)
+    for part in parts[1:]:
+        total = total + part[...].astype(F32)
+    rounded = total.astype(BF16)
+    for n in range(out.shape[0]):
+        out[n] = rounded
+
+
 def natural_rows(info, gathered):
     blocks = [
         gathered[cell][:, inside : inside + size]
@@ -316,10 +326,12 @@
     return jnp.concatenate(blocks, 1)
 
 
-def put_spread(info, halves, out):
+def put_spread(info, halves, stage, own_cell, outs):
     value = jnp.concatenate(halves, 1).astype(BF16)
     for lane, cell, inside, size in info.natural():
-        out[cell, :, inside : inside + size] = value[:, lane : lane + size]
+        stage[cell, :, inside : inside + size] = value[:, lane : lane + size]
+    for d, out in enumerate(outs):
+        out[...] = stage[own_cell ^ d]
 
 
 def forward_kernel(infos, k, at, gathered, mine_hbm, received_hbm, *refs):
@@ -372,8 +384,9 @@
         out[index] = (value - minus).astype(BF16)
 
 
-def top_kernel(info, gathered, *refs):
-    pieces, out = refs[:-1], refs[-1]
+def top_kernel(info, at, gathered, *refs):
+    pieces = refs[: 4 * info.pair_x]
+    outs, stage = refs[4 * info.pair_x : -1], refs[-1]
     each = len(pieces) // GROUPS
     vector = natural_rows(info, gathered)
     halves = None
@@ -381,7 +394,7 @@
         matrix = jnp.concatenate([p[...] for p in pieces[g * each : (g + 1) * each]], 0)
         y = mm_nt(matrix, vector)
         halves = accumulate(halves, y.astype(BF16), matrix)
-    put_spread(info, halves, out)
+    put_spread(info, halves, stage, at[info.cell_slot], outs)
 
 
 def backward_kernel(infos, k, at, y_hbm, *refs):
@@ -392,8 +405,10 @@
     pieces = refs[:count]
     solved = refs[count : count + many]
     sources = refs[count + many : count + 2 * many]
-    out, matrix, y, sems = refs[count + 2 * many : count + 2 * many + 4]
-    dense = refs[count + 2 * many + 4 :]
+    begin = count + 2 * many
+    outs = refs[begin : begin + info.cells]
+    stage, matrix, y, sems = refs[begin + info.cells : begin + info.cells + 4]
+    dense = refs[begin + info.cells + 4 :]
     loads = Loads(sems)
     y_load = loads.start([(y_hbm, y)])
     dense_loads = [loads.groups([source], dense[n], GROUPS) for n, source in enumerate(sources)]
@@ -424,7 +439,7 @@
             z = z - mm_nt(dense[n][rows, :], vectors[n])
         wait(last[g])
         halves = accumulate(halves, z.astype(BF16), matrix[rows, :])
-    put_spread(info, halves, out)
+    put_spread(info, halves, stage, at[info.cell_slot], outs)
 
 
 def full_cases(info, core, mine, other, full):
@@ -520,15 +535,20 @@
         leaf = lax.axis_index("leaf")
         blk = lax.axis_index("blk")
         scalars = [leaf & 1, blk & 1, (leaf >> 1) & 1]
+        own_cells = []
         for info in infos:
             member = leaf & ((1 << info.level) - 1)
             hi, side = split_power(member, 2 * info.pair_x)
             cell = hi * info.zbs + (blk >> 1)
+            own_cells.append(cell)
             scalars.append(((cell * 2 * info.pair_x + side) * 2 + (blk & 1)) * info.rows)
         for level, above in pair_slot:
             node = leaf >> level
             scalars.append(pair_bases[level] + node * (depth - level) + (above - level - 1))
-        return scalars
+        return scalars + own_cells
+
+    for n, info in enumerate(infos):
+        info.cell_slot = SPOT + depth + len(pair_slot) + n
 
     def swap(value, axis, bit):
         size = leaves if axis == "leaf" else blocks
@@ -570,6 +590,13 @@
         return lax.all_to_all(
             value, ("leaf", "blk"), 0, 0, axis_index_groups=info.inner, tiled=True
         )
+
+    def swap_inner(value, level, d):
+        info = infos[level - 1]
+        groups = info.inner_blk if info.his == 1 else info.inner
+        axes = "blk" if info.his == 1 else ("leaf", "blk")
+        pairs = [(device, group[i ^ d]) for group in groups for i, device in enumerate(group)]
+        return lax.ppermute(value, axes, pairs)
 
     def coupling_block(level, above):
         begin = couple_starts[level, above]
@@ -683,6 +710,14 @@
             sum_spread_kernel, [shaped((copies,) + parts.shape[1:], BF16)], [parts]
         )[0]
 
+    def sum_parts(parts, copies):
+        return kernel_call(
+            sum_parts_kernel, [shaped((copies,) + parts[0].shape, BF16)], parts
+        )[0]
+
+    def stage_scratch(info):
+        return pltpu.VMEM((info.cells, info.chunk, info.cell_rows), BF16)
+
     def cell_scratch(info):
         return pltpu.VMEM((info.cell_rows, width), BF16)
 
@@ -697,11 +732,13 @@
         if level == depth:
             parts = kernel_call(
                 functools.partial(top_kernel, info),
-                [shaped((info.cells, info.chunk, info.cell_rows), BF16)],
+                [shaped((info.chunk, info.cell_rows), BF16)] * info.cells,
                 [gathered] + [(piece, True) for piece in inverse_pieces[level]],
+                scalars=at,
+                scratch=[stage_scratch(info)],
                 flops=4 * size,
-                stay=[False],
-            )[0]
+                stay=[False] * info.cells,
+            )
             break
         above = infos[level]
         ys[level], parts = kernel_call(
@@ -742,22 +779,25 @@
             count = 4 * info.pair_x
             parts = kernel_call(
                 functools.partial(backward_kernel, infos, level),
-                [shaped((info.cells, info.chunk, info.cell_rows), BF16)],
+                [shaped((info.chunk, info.cell_rows), BF16)] * info.cells,
                 hbm([ys[level]] + inverse_pieces[level])
                 + [solved[above] for above in higher]
                 + hbm([dense[level, above] for above in higher]),
                 scalars=at,
                 scratch=[
+                    stage_scratch(info),
                     cell_scratch(info),
                     pltpu.VMEM(ys[level].shape, F32),
                     pltpu.SemaphoreType.DMA((1 + count + GROUPS * len(higher),)),
                 ]
                 + [cell_scratch(info)] * len(higher),
                 flops=4 * info.cell_rows * width * info.chunk,
-                stay=[False],
-            )[0]
-        parts = exchange_inner(parts, level)
-        solved[level] = exchange_middle(sum_spread(parts, info.cells * info.pair_x), level)
+                stay=[False] * info.cells,
+            )
+        parts = [parts[0]] + [
+            swap_inner(parts[d], level, d) for d in range(1, info.cells)
+        ]
+        solved[level] = exchange_middle(sum_parts(parts, info.cells * info.pair_x), level)
         swapped[level] = swap(solved[level], "leaf", 1)
         if level > 1:
             low = kernel_call(

time: 175 us -> 177 us (1.011)
  waiting for transfers between devices: 62.9 us -> 67.6 us
    ppermute x0 -> x6, starting transfers between devices: none -> 8.9 us  [swap_inner(): return lax.ppermute(value, axes, pairs)]
    all_to_all x4 -> x2, starting transfers between devices: 15 us -> 6.61 us  [exchange_inner(): lax.all_to_all(value, 'blk', 0, 0, axis_index_groups=info.inner_blk, tile...]
    ppermute x23, waiting for transfers between devices: 27.9 us -> 36 us  [swap(): return lax.ppermute(value, axis, [(i, i ^ bit) for i in range(size)])]
    all_to_all x4 -> x2, waiting for transfers between devices: 10.2 us -> 5.63 us  [exchange_inner(): lax.all_to_all(value, 'blk', 0, 0, axis_index_groups=info.inner_blk, tile...]
    all_to_all x1, starting transfers between devices: 5.69 us -> 3.6 us  [solve(): parts = lax.all_to_all(part, 'blk', 0, 0, tiled=True)]
  transfers between devices with their start and end apart: 33 -> 37, of which waited for: 12 -> 11; matrix products, arithmetic and copies ran while one was open for 5% -> 4% of each run, Pallas kernels for 17% -> 17%
where the time goes in v6:
time: 177 us; the launch traced here: 176 us
  waiting for transfers between devices  67.6 us (38%)
  starting transfers between devices  61.3 us (35%)
  Pallas kernels  38.5 us (22%)
  local copies, waits for them, and re-layouts  6.34 us (4%)
  other arithmetic  2.23 us (1%)
    pallas_call x16, Pallas kernels, kernel_call(): pl.pallas_call(body if scalars is None else lambda *refs: body(scalars(),...  38.5 us
    ppermute x23, waiting for transfers between devices, swap(): return lax.ppermute(value, axis, [(i, i ^ bit) for i in range(size)])  36 us
    ppermute x23, starting transfers between devices, swap(): return lax.ppermute(value, axis, [(i, i ^ bit) for i in range(size)])  18.1 us
    all_to_all x2, starting transfers between devices, exchange_middle(): lax.all_to_all(value, ('leaf', 'blk'), 0, 0, axis_index_groups=info.middl...  9.37 us
    all_to_all x1, waiting for transfers between devices, solve(): full = lax.all_to_all(spread, 'blk', 0, 0, tiled=True).reshape(width, cases)  9 us
    ppermute x6, starting transfers between devices, swap_inner(): return lax.ppermute(value, axes, pairs)  8.9 us
    all_to_all x1, starting transfers between devices, solve(): full = lax.all_to_all(spread, 'blk', 0, 0, tiled=True).reshape(width, cases)  7.32 us
    all_to_all x2, starting transfers between devices, exchange_inner(): lax.all_to_all(value, 'blk', 0, 0, axis_index_groups=info.inner_blk, tile...  6.61 us
  transfers between devices with their start and end apart: 37, of which 11 were waited for; matrix products, arithmetic and copies ran while one was open for 4% of the time, Pallas kernels for 17%

profile of v6, /device:TPU:0, one launch (start us, length us, event | category | flops | bytes accessed | tf_op | source)
XLA Modules:
  0.0 176.4 jit_solution(9721430928864193122)
XLA Ops:
  1.9 7.3 %all-to-all-start = ((bf16[8,256,128]{2,1,0:T(8,128)(2,1)}), bf16[8,256,128]{2,1,0:T(8,128)(2,1)S(1)}, u32[]{:S(2)}, u32[]{:S(2)}) async-start(bf16[8,256,128]{2,1,0:T(8,128)(2,1)} %shard_map.48), calls=%async_computation | async-start | bytes 1048576 | tf_op jit(solution)/shard_map/all_to_all | solution.py:629
  9.2 2.1 %collective-permute-start.7 = (bf16[128,1024]{1,0:T(8,128)(2,1)S(1)}, bf16[128,1024]{1,0:T(8,128)(2,1)S(1)}, u32[]{:S(2)}, u32[]{:S(2)}) collective-permute-start(bf16[128,1024]{1,0:T(8,128)(2,1)S(1)} %slice_bitcast_fusion.5.refs_1_), channel_id=1, source_target_pairs={{0,1},{1,0},{2,3},{3,2},{4,5},{5,4},{6,7},{7,6},{8,9},{9,8},{10,11... | collective-permute-start | bytes 786440 | tf_op jit(solution)/shard_map/ppermute | solution.py:555
  11.3 3.4 %shard_map.46 = (bf16[256,2048]{1,0:T(8,128)(2,1)}, bf16[256,2048]{1,0:T(8,128)(2,1)}) custom-call(s32[10,1024]{1,0:T(8,128)S(1)} %copy-done.1, bf16[640,1024]{1,0:T(8,128)(2,1)S(1)} %bitcast.39), custom_call_target="tpu_custom_call" | custom-call | flops 2147483648 | bytes 3448832 | tf_op jit(solution)/shard_map/pallas_call | solution.py:47
  14.7 9.0 %all-to-all-done = bf16[8,256,128]{2,1,0:T(8,128)(2,1)S(1)} async-done(((bf16[8,256,128]{2,1,0:T(8,128)(2,1)}), bf16[8,256,128]{2,1,0:T(8,128)(2,1)S(1)}, u32[]{:S(2)}, u32[]{:S(2)}) %all-to-all-start) | async-done | bytes 524320 | tf_op jit(solution)/shard_map/all_to_all | solution.py:629
  23.7 4.3 %shard_map.49 = (f32[256,64]{1,0:T(8,128)}, f32[256,64]{1,0:T(8,128)}, bf16[8,32,512]{2,1,0:T(8,128)(2,1)S(1)}, bf16[8,32,512]{2,1,0:T(8,128)(2,1)S(1)}, bf16[16...) custom-call(bf16[2048,128]{1,0:T(8,128)(2,1)S(1)} %bitcast.38, bf16[448,2048]{1,0:T(8,128)(2,1)} %bitcast.42, ...), custom_call_target="tpu_custom_call" | custom-call | flops 402653184 | bytes 5865472 | tf_op jit(solution)/shard_map/pallas_call | solution.py:47
  32.0 3.4 %all-to-all-start.1 = ((bf16[8,32,512]{2,1,0:T(8,128)(2,1)}), bf16[8,32,512]{2,1,0:T(8,128)(2,1)S(1)}, u32[]{:S(2)}, u32[]{:S(2)}) async-start(bf16[8,32,512]{2,1,0:T(8,128)(2,1)} %add_convert_fusion.1), calls=%async_computation.1 | async-start | bytes 524288 | tf_op jit(solution)/shard_map/all_to_all | solution.py:564
  38.0 8.2 %collective-permute-done.4.refs_4_.refs_2_ = bf16[128,2048]{1,0:T(8,128)(2,1)} collective-permute-done((bf16[128,2048]{1,0:T(8,128)(2,1)S(1)}, bf16[128,2048]{1,0:T(8,128)(2,1)}, u32[]{:S(2)}, u32[]{:S(2)}) %collective-permute-start.4) | collective-permute-done | bytes 524320 | tf_op jit(solution)/shard_map/ppermute | solution.py:555
  49.2 3.3 %all-to-all-start.2 = ((bf16[4,32,512]{2,1,0:T(8,128)(2,1)}), bf16[4,32,512]{2,1,0:T(8,128)(2,1)S(1)}, u32[]{:S(2)}, u32[]{:S(2)}) async-start(bf16[4,32,512]{2,1,0:T(8,128)(2,1)} %shard_map.50), calls=%async_computation.2 | async-start | bytes 262144 | tf_op jit(solution)/shard_map/all_to_all | solution.py:587
  56.1 3.7 %shard_map.51.refs_7_.refs_6_ = bf16[512,2048]{1,0:T(8,128)(2,1)} custom-call(s32[10,1024]{1,0:T(8,128)S(1)} %copy-done.1, bf16[128,1024]{1,0:T(8,128)(2,1)S(1)} %slice_bitcast_fusion.5.refs_1_, bf16[128,1024]{1,0:T(8,128)(2,1)S(1)} %collective-permute-done.7.refs_2_, bf16[128,1024]{1,0:T(8,128)(2,1)S(1)} %collective-permute-done.8.refs_3_, ...), custom_call_target="tpu_custom_call" | custom-call | flops 2147483648 | bytes 3186688 | tf_op jit(solution)/shard_map/pallas_call | solution.py:47
  59.8 9.4 %collective-permute-done.3.refs_2_ = bf16[8,16,512]{2,1,0:T(8,128)(2,1)S(1)} collective-permute-done((bf16[8,16,512]{2,1,0:T(8,128)(2,1)}, bf16[8,16,512]{2,1,0:T(8,128)(2,1)S(1)}, u32[]{:S(2)}, u32[]{:S(2)}) %collective-permute-start.3) | collective-permute-done | bytes 131104 | tf_op jit(solution)/shard_map/ppermute | solution.py:555
  69.9 3.8 %shard_map.52 = (f32[512,32]{1,0:T(8,128)}, bf16[8,16,512]{2,1,0:T(8,128)(2,1)}) custom-call(bf16[4,32,512]{2,1,0:T(8,128)(2,1)S(1)} %all-to-all-done.2.refs_0_, bf16[8,16,512]{2,1,0:T(8,128)(2,1)} %get-tuple-element.44.refs_1_, bf16[8,16,512]{2,1,0:T(8,128)(2,1)} %copy-done.8, bf16[128,2048]{1,0:T(8,128)(2,1)} %copy-done.2, ...), custom_call_target="tpu_custom_call" | custom-call | flops 134217728 | bytes 4784128 | tf_op jit(solution)/shard_map/pallas_call | solution.py:47
  73.7 5.7 %all-to-all-start.3 = ((bf16[8,16,512]{2,1,0:T(8,128)(2,1)}), bf16[8,16,512]{2,1,0:T(8,128)(2,1)S(1)}, u32[]{:S(2)}, u32[]{:S(2)}) async-start(bf16[8,16,512]{2,1,0:T(8,128)(2,1)} %get-tuple-element.30), calls=%async_computation.3 | async-start | bytes 262144 | tf_op jit(solution)/shard_map/all_to_all | solution.py:580
  80.4 6.4 %all-to-all-done.3.parts = bf16[8,16,512]{2,1,0:T(8,128)(2,1)S(1)} async-done(((bf16[8,16,512]{2,1,0:T(8,128)(2,1)}), bf16[8,16,512]{2,1,0:T(8,128)(2,1)S(1)}, u32[]{:S(2)}, u32[]{:S(2)}) %all-to-all-start.3) | async-done | bytes 131104 | tf_op jit(solution)/shard_map/all_to_all | solution.py:580
  87.5 3.3 %all-to-all-start.4 = ((bf16[4,16,512]{2,1,0:T(8,128)(2,1)}), bf16[4,16,512]{2,1,0:T(8,128)(2,1)S(1)}, u32[]{:S(2)}, u32[]{:S(2)}) async-start(bf16[4,16,512]{2,1,0:T(8,128)(2,1)} %shard_map.53), calls=%async_computation.4 | async-start | bytes 131072 | tf_op jit(solution)/shard_map/all_to_all | solution.py:587
  90.9 5.6 %all-to-all-done.4.refs_0_ = bf16[4,16,512]{2,1,0:T(8,128)(2,1)S(1)} async-done(((bf16[4,16,512]{2,1,0:T(8,128)(2,1)}), bf16[4,16,512]{2,1,0:T(8,128)(2,1)S(1)}, u32[]{:S(2)}, u32[]{:S(2)}) %all-to-all-start.4) | async-done | bytes 65568 | tf_op jit(solution)/shard_map/all_to_all | solution.py:587
  96.5 2.6 %shard_map.54 = (bf16[16,512]{1,0:T(8,128)(2,1)S(1)}, bf16[16,512]{1,0:T(8,128)(2,1)S(1)}, bf16[16,512]{1,0:T(8,128)(2,1)S(1)}, bf16[16,512]{1,0:T(8,128)(2,1)S(1)}) custom-call(bf16[4,16,512]{2,1,0:T(8,128)(2,1)S(1)} %all-to-all-done.4.refs_0_, bf16[64,2048]{1,0:T(8,128)(2,1)} %copy-done.3, bf16[64,2048]{1,0:T(8,128)(2,1)} %collective-permute-done.10.refs_2_, ...), custom_call_target="tpu_custom_call" | custom-call | flops 67108864 | bytes 2228224 | tf_op jit(solution)/shard_map/pallas_call | solution.py:47
  100.5 3.1 %collective-permute-start.19 = (bf16[16,512]{1,0:T(8,128)(2,1)S(1)}, bf16[16,512]{1,0:T(8,128)(2,1)S(1)}, u32[]{:S(2)}, u32[]{:S(2)}) collective-permute-start(bf16[16,512]{1,0:T(8,128)(2,1)S(1)} %get-tuple-element.34), channel_id=1, source_target_pairs={{0,6},{2,4},{4,2},{6,0},{1,7},{3,5},{5,3},{7,1},{8,14},{10,12},{12... | collective-permute-start | bytes 49160 | tf_op jit(solution)/shard_map/ppermute | solution.py:599
  107.3 3.7 %all-to-all-start.5 = ((bf16[8,16,512]{2,1,0:T(8,128)(2,1)}), bf16[8,16,512]{2,1,0:T(8,128)(2,1)S(1)}, u32[]{:S(2)}, u32[]{:S(2)}) async-start(bf16[8,16,512]{2,1,0:T(8,128)(2,1)} %shard_map.55), calls=%async_computation.5 | async-start | bytes 262144 | tf_op jit(solution)/shard_map/all_to_all | solution.py:580
  113.9 5.8 %collective-permute-done.25.refs_1_ = bf16[256,1024]{1,0:T(8,128)(2,1)S(1)} collective-permute-done((bf16[256,1024]{1,0:T(8,128)(2,1)}, bf16[256,1024]{1,0:T(8,128)(2,1)S(1)}, u32[]{:S(2)}, u32[]{:S(2)}) %collective-permute-start.25) | collective-permute-done | bytes 524320 | tf_op jit(solution)/shard_map/ppermute | solution.py:555
  119.6 2.3 %shard_map.58.refs_1_ = bf16[256,2048]{1,0:T(8,128)(2,1)} custom-call(s32[10,1024]{1,0:T(8,128)S(1)} %copy-done.1, bf16[256,1024]{1,0:T(8,128)(2,1)S(1)} %collective-permute-done.25.refs_1_), custom_call_target="tpu_custom_call" | custom-call | flops 1073741824 | bytes 1613824 | tf_op jit(solution)/shard_map/pallas_call | solution.py:47
  121.9 8.9 %collective-permute-done.refs_1_ = bf16[256,1024]{1,0:T(8,128)(2,1)S(1)} collective-permute-done((bf16[256,1024]{1,0:T(8,128)(2,1)}, bf16[256,1024]{1,0:T(8,128)(2,1)S(1)}, u32[]{:S(2)}, u32[]{:S(2)}) %collective-permute-start) | collective-permute-done | bytes 524320 | tf_op jit(solution)/shard_map/ppermute | solution.py:555
  130.9 2.3 %shard_map.47.refs_1_ = bf16[256,2048]{1,0:T(8,128)(2,1)} custom-call(s32[10,1024]{1,0:T(8,128)S(1)} %copy-done.1, bf16[256,1024]{1,0:T(8,128)(2,1)S(1)} %collective-permute-done.refs_1_), custom_call_target="tpu_custom_call" | custom-call | flops 1073741824 | bytes 1613824 | tf_op jit(solution)/shard_map/pallas_call | solution.py:47
  133.2 3.3 %shard_map.56 = (bf16[32,512]{1,0:T(8,128)(2,1)S(1)}, bf16[32,512]{1,0:T(8,128)(2,1)S(1)}, bf16[32,512]{1,0:T(8,128)(2,1)S(1)}, bf16[32,512]{1,0:T(8,128)(2,1)S(1)}) custom-call(f32[512,32]{1,0:T(8,128)} %get-tuple-element.29.refs_0_, bf16[128,2048]{1,0:T(8,128)(2,1)} %copy-done.2, bf16[128,2048]{1,0:T(8,128)(2,1)} %collective-permute-done.4.refs_4_.refs_2_, ...), custom_call_target="tpu_custom_call" | custom-call | flops 134217728 | bytes 4521984 | tf_op jit(solution)/shard_map/pallas_call | solution.py:47
  137.9 3.1 %collective-permute-start.22 = (bf16[32,512]{1,0:T(8,128)(2,1)S(1)}, bf16[32,512]{1,0:T(8,128)(2,1)S(1)}, u32[]{:S(2)}, u32[]{:S(2)}) collective-permute-start(bf16[32,512]{1,0:T(8,128)(2,1)S(1)} %get-tuple-element.38), channel_id=1, source_target_pairs={{0,6},{2,4},{4,2},{6,0},{1,7},{3,5},{5,3},{7,1},{8,14},{10,12},{12... | collective-permute-start | bytes 98312 | tf_op jit(solution)/shard_map/ppermute | solution.py:599
  144.6 4.0 %all-to-all-start.6 = ((bf16[4,32,512]{2,1,0:T(8,128)(2,1)}), bf16[4,32,512]{2,1,0:T(8,128)(2,1)S(1)}, u32[]{:S(2)}, u32[]{:S(2)}) async-start(bf16[4,32,512]{2,1,0:T(8,128)(2,1)} %shard_map.57), calls=%async_computation.6 | async-start | bytes 262144 | tf_op jit(solution)/shard_map/all_to_all | solution.py:577
  148.8 5.7 %all-to-all-done.6.refs_2_ = bf16[4,32,512]{2,1,0:T(8,128)(2,1)S(1)} async-done(((bf16[4,32,512]{2,1,0:T(8,128)(2,1)}), bf16[4,32,512]{2,1,0:T(8,128)(2,1)S(1)}, u32[]{:S(2)}, u32[]{:S(2)}) %all-to-all-start.6) | async-done | bytes 131104 | tf_op jit(solution)/shard_map/all_to_all | solution.py:577
  154.5 3.5 %shard_map.59.refs_6_ = f32[512,64]{1,0:T(8,128)} custom-call(bf16[256,2048]{1,0:T(8,128)(2,1)} %get-tuple-element.24.refs_4_.refs_0_, bf16[256,2048]{1,0:T(8,128)(2,1)} %shard_map.58.refs_1_, bf16[8,16,512]{2,1,0:T(8,128)(2,1)S(1)} %all-to-all-done.5.refs_5_.refs_2_, bf16[8,16,512]{2,1,0:T(8,128)(2,1)S(1)} %collective-permute-done.26.refs_3_, ...), custom_call_target="tpu_custom_call" | custom-call | flops 134217728 | bytes 2621440 | tf_op jit(solution)/shard_map/pallas_call | solution.py:47
  158.4 4.0 %shard_map.60 = bf16[8,64,256]{2,1,0:T(8,128)(2,1)} custom-call(bf16[256,2048]{1,0:T(8,128)(2,1)} %get-tuple-element.23.refs_3_.refs_0_, bf16[256,2048]{1,0:T(8,128)(2,1)} %shard_map.47.refs_1_, bf16[4,32,512]{2,1,0:T(8,128)(2,1)S(1)} %all-to-all-done.6.refs_2_, bf16[4,32,512]{2,1,0:T(8,128)(2,1)S(1)} %collective-permute-done.23.refs_3_, ...), custom_call_target="tpu_custom_call" | custom-call | flops 268435456 | bytes 5636096 | tf_op jit(solution)/shard_map/pallas_call | solution.py:47
  162.3 3.6 %all-to-all-start.7 = ((bf16[8,64,256]{2,1,0:T(8,128)(2,1)}), bf16[8,64,256]{2,1,0:T(8,128)(2,1)S(1)}, u32[]{:S(2)}, u32[]{:S(2)}) async-start(bf16[8,64,256]{2,1,0:T(8,128)(2,1)} %shard_map.60), calls=%async_computation.7 | async-start | bytes 524288 | tf_op jit(solution)/shard_map/all_to_all | solution.py:836
  166.1 2.1 %collective-permute-start.28 = (bf16[64,192]{0,1:T(8,128)(2,1)S(1)}, bf16[64,192]{0,1:T(8,128)(2,1)S(1)}, u32[]{:S(2)}, u32[]{:S(2)}) collective-permute-start(bf16[64,192]{0,1:T(8,128)(2,1)S(1)} %pad_maximum_fusion), channel_id=1, source_target_pairs={{0,1},{1,0},{2,3},{3,2},{4,5},{5,4},{6,7},{7,6},{8,9},{9,8},{10,11... | collective-permute-start | bytes 73736 | tf_op jit(solution)/shard_map/ppermute | solution.py:555
  168.2 3.7 %collective-permute-done.28 = bf16[64,192]{0,1:T(8,128)(2,1)S(1)} collective-permute-done((bf16[64,192]{0,1:T(8,128)(2,1)S(1)}, bf16[64,192]{0,1:T(8,128)(2,1)S(1)}, u32[]{:S(2)}, u32[]{:S(2)}) %collective-permute-start.28) | collective-permute-done | bytes 24608 | tf_op jit(solution)/shard_map/ppermute | solution.py:555
  172.0 3.5 %all-to-all-done.7.parts = bf16[8,64,256]{2,1,0:T(8,128)(2,1)S(1)} async-done(((bf16[8,64,256]{2,1,0:T(8,128)(2,1)}), bf16[8,64,256]{2,1,0:T(8,128)(2,1)S(1)}, u32[]{:S(2)}, u32[]{:S(2)}) %all-to-all-start.7) | async-done | bytes 262176 | tf_op jit(solution)/shard_map/all_to_all | solution.py:836
  (100 shorter events, 31.9 us)
Async XLA Ops:
  1.9 21.8 %all-to-all-start = ((bf16[8,256,128]{2,1,0:T(8,128)(2,1)}), bf16[8,256,128]{2,1,0:T(8,128)(2,1)S(1)}, u32[]{:S(2)}, u32[]{:S(2)}) async-start(bf16[8,256,128]{2,1,0:T(8,128)(2,1)} %shard_map.48), calls=%async_computation | async-start | bytes 1048576 | tf_op jit(solution)/shard_map/all_to_all | solution.py:629
  9.2 27.2 %collective-permute-start.7 = (bf16[128,1024]{1,0:T(8,128)(2,1)S(1)}, bf16[128,1024]{1,0:T(8,128)(2,1)S(1)}, u32[]{:S(2)}, u32[]{:S(2)}) collective-permute-start(bf16[128,1024]{1,0:T(8,128)(2,1)S(1)} %slice_bitcast_fusion.5.refs_1_), channel_id=1, source_target_pairs={{0,1},{1,0},{2,3},{3,2},{4,5},{5,4},{6,7},{7,6},{8,9},{9,8},{10,11... | collective-permute-start | bytes 786440 | tf_op jit(solution)/shard_map/ppermute | solution.py:555
  11.3 41.2 %collective-permute-start.8 = (bf16[128,1024]{1,0:T(8,128)(2,1)S(1)}, bf16[128,1024]{1,0:T(8,128)(2,1)S(1)}, u32[]{:S(2)}, u32[]{:S(2)}) collective-permute-start(bf16[128,1024]{1,0:T(8,128)(2,1)S(1)} %slice_bitcast_fusion.5.refs_1_), channel_id=1, source_target_pairs={{0,8},{8,0},{16,24},{24,16},{1,9},{9,1},{17,25},{25,17},{2,10},{10... | collective-permute-start | bytes 786440 | tf_op jit(solution)/shard_map/ppermute | solution.py:555
  29.2 16.9 %collective-permute-start.4 = (bf16[128,2048]{1,0:T(8,128)(2,1)S(1)}, bf16[128,2048]{1,0:T(8,128)(2,1)}, u32[]{:S(2)}, u32[]{:S(2)}) collective-permute-start(bf16[128,2048]{1,0:T(8,128)(2,1)S(1)} %slice_bitcast_fusion.2.refs_3_.refs_1_), channel_id=1, source_target_pairs={{0,1},{1,0},{2,3},{3,2},{4,5},{5,4},{6,7},{7,6},{8,9},{9,8},{10,11... | collective-permute-start | bytes 1572872 | tf_op jit(solution)/shard_map/ppermute | solution.py:555
  30.7 29.1 %collective-permute-start.5 = (bf16[128,2048]{1,0:T(8,128)(2,1)S(1)}, bf16[128,2048]{1,0:T(8,128)(2,1)}, u32[]{:S(2)}, u32[]{:S(2)}) collective-permute-start(bf16[128,2048]{1,0:T(8,128)(2,1)S(1)} %slice_bitcast_fusion.2.refs_3_.refs_1_), channel_id=1, source_target_pairs={{0,8},{8,0},{16,24},{24,16},{1,9},{9,1},{17,25},{25,17},{2,10},{10... | collective-permute-start | bytes 1572872 | tf_op jit(solution)/shard_map/ppermute | solution.py:555
  30.9 15.2 %collective-permute-start.2 = (bf16[16,16,512]{2,1,0:T(8,128)(2,1)}, bf16[16,16,512]{2,1,0:T(8,128)(2,1)}, u32[]{:S(2)}, u32[]{:S(2)}) collective-permute-start(bf16[16,16,512]{2,1,0:T(8,128)(2,1)} %get-tuple-element.28), channel_id=1, source_target_pairs={{0,8},{8,0},{16,24},{24,16},{1,9},{9,1},{17,25},{25,17},{2,10},{10... | collective-permute-start | bytes 786440 | tf_op jit(solution)/shard_map/ppermute | solution.py:555
  32.0 16.5 %all-to-all-start.1 = ((bf16[8,32,512]{2,1,0:T(8,128)(2,1)}), bf16[8,32,512]{2,1,0:T(8,128)(2,1)S(1)}, u32[]{:S(2)}, u32[]{:S(2)}) async-start(bf16[8,32,512]{2,1,0:T(8,128)(2,1)} %add_convert_fusion.1), calls=%async_computation.1 | async-start | bytes 524288 | tf_op jit(solution)/shard_map/all_to_all | solution.py:564
  36.4 17.6 %collective-permute-start.10 = (bf16[64,2048]{1,0:T(8,128)(2,1)S(1)}, bf16[64,2048]{1,0:T(8,128)(2,1)}, u32[]{:S(2)}, u32[]{:S(2)}) collective-permute-start(bf16[64,2048]{1,0:T(8,128)(2,1)S(1)} %slice_bitcast_fusion.4.refs_1_), channel_id=1, source_target_pairs={{0,16},{8,24},{16,0},{24,8},{1,17},{9,25},{17,1},{25,9},{2,18},{10... | collective-permute-start | bytes 786440 | tf_op jit(solution)/shard_map/ppermute | solution.py:555
  46.1 8.5 %collective-permute-start.9 = (bf16[128,1024]{1,0:T(8,128)(2,1)S(1)}, bf16[128,1024]{1,0:T(8,128)(2,1)S(1)}, u32[]{:S(2)}, u32[]{:S(2)}) collective-permute-start(bf16[128,1024]{1,0:T(8,128)(2,1)S(1)} %collective-permute-done.7.refs_2_), channel_id=1, source_target_pairs={{0,8},{8,0},{16,24},{24,16},{1,9},{9,1},{17,25},{25,17},{2,10},{10... | collective-permute-start | bytes 786440 | tf_op jit(solution)/shard_map/ppermute | solution.py:555
  46.1 13.7 %collective-permute-start.6 = (bf16[128,2048]{1,0:T(8,128)(2,1)}, bf16[128,2048]{1,0:T(8,128)(2,1)}, u32[]{:S(2)}, u32[]{:S(2)}) collective-permute-start(bf16[128,2048]{1,0:T(8,128)(2,1)} %collective-permute-done.4.refs_4_.refs_2_), channel_id=1, source_target_pairs={{0,8},{8,0},{16,24},{24,16},{1,9},{9,1},{17,25},{25,17},{2,10},{10... | collective-permute-start | bytes 1572872 | tf_op jit(solution)/shard_map/ppermute | solution.py:555
  49.2 20.1 %all-to-all-start.2 = ((bf16[4,32,512]{2,1,0:T(8,128)(2,1)}), bf16[4,32,512]{2,1,0:T(8,128)(2,1)S(1)}, u32[]{:S(2)}, u32[]{:S(2)}) async-start(bf16[4,32,512]{2,1,0:T(8,128)(2,1)} %shard_map.50), calls=%async_computation.2 | async-start | bytes 262144 | tf_op jit(solution)/shard_map/all_to_all | solution.py:587
  52.5 27.4 %collective-permute-start.11 = (bf16[64,2048]{1,0:T(8,128)(2,1)S(1)}, bf16[64,2048]{1,0:T(8,128)(2,1)}, u32[]{:S(2)}, u32[]{:S(2)}) collective-permute-start(bf16[64,2048]{1,0:T(8,128)(2,1)S(1)} %slice_bitcast_fusion.4.refs_1_), channel_id=1, source_target_pairs={{0,1},{1,0},{2,3},{3,2},{4,5},{5,4},{6,7},{7,6},{8,9},{9,8},{10,11... | collective-permute-start | bytes 786440 | tf_op jit(solution)/shard_map/ppermute | solution.py:555
  54.0 26.0 %collective-permute-start.12 = (bf16[64,2048]{1,0:T(8,128)(2,1)}, bf16[64,2048]{1,0:T(8,128)(2,1)}, u32[]{:S(2)}, u32[]{:S(2)}) collective-permute-start(bf16[64,2048]{1,0:T(8,128)(2,1)} %collective-permute-done.10.refs_2_), channel_id=1, source_target_pairs={{0,1},{1,0},{2,3},{3,2},{4,5},{5,4},{6,7},{7,6},{8,9},{9,8},{10,11... | collective-permute-start | bytes 786440 | tf_op jit(solution)/shard_map/ppermute | solution.py:555
  54.6 14.6 %collective-permute-start.3 = (bf16[8,16,512]{2,1,0:T(8,128)(2,1)}, bf16[8,16,512]{2,1,0:T(8,128)(2,1)S(1)}, u32[]{:S(2)}, u32[]{:S(2)}) collective-permute-start(bf16[8,16,512]{2,1,0:T(8,128)(2,1)} %get-tuple-element.43), channel_id=1, source_target_pairs={{0,1},{1,0},{2,3},{3,2},{4,5},{5,4},{6,7},{7,6},{8,9},{9,8},{10,11... | collective-permute-start | bytes 393224 | tf_op jit(solution)/shard_map/ppermute | solution.py:555
  73.7 13.2 %all-to-all-start.3 = ((bf16[8,16,512]{2,1,0:T(8,128)(2,1)}), bf16[8,16,512]{2,1,0:T(8,128)(2,1)S(1)}, u32[]{:S(2)}, u32[]{:S(2)}) async-start(bf16[8,16,512]{2,1,0:T(8,128)(2,1)} %get-tuple-element.30), calls=%async_computation.3 | async-start | bytes 262144 | tf_op jit(solution)/shard_map/all_to_all | solution.py:580
  79.3 11.4 %collective-permute-start.13 = (bf16[64,2048]{1,0:T(8,128)(2,1)S(1)}, bf16[64,2048]{1,0:T(8,128)(2,1)S(1)}, u32[]{:S(2)}, u32[]{:S(2)}) collective-permute-start(bf16[64,2048]{1,0:T(8,128)(2,1)S(1)} %slice_bitcast_fusion.4.refs_1_), channel_id=1, source_target_pairs={{0,8},{8,0},{16,24},{24,16},{1,9},{9,1},{17,25},{25,17},{2,10},{10... | collective-permute-start | bytes 786440 | tf_op jit(solution)/shard_map/ppermute | solution.py:555
  79.4 11.4 %collective-permute-start.14 = (bf16[64,2048]{1,0:T(8,128)(2,1)}, bf16[64,2048]{1,0:T(8,128)(2,1)S(1)}, u32[]{:S(2)}, u32[]{:S(2)}) collective-permute-start(bf16[64,2048]{1,0:T(8,128)(2,1)} %collective-permute-done.10.refs_2_), channel_id=1, source_target_pairs={{0,8},{8,0},{16,24},{24,16},{1,9},{9,1},{17,25},{25,17},{2,10},{10... | collective-permute-start | bytes 786440 | tf_op jit(solution)/shard_map/ppermute | solution.py:555
  79.9 10.9 %collective-permute-start.15 = (bf16[64,2048]{1,0:T(8,128)(2,1)}, bf16[64,2048]{1,0:T(8,128)(2,1)S(1)}, u32[]{:S(2)}, u32[]{:S(2)}) collective-permute-start(bf16[64,2048]{1,0:T(8,128)(2,1)} %collective-permute-done.11.refs_3_), channel_id=1, source_target_pairs={{0,8},{8,0},{16,24},{24,16},{1,9},{9,1},{17,25},{25,17},{2,10},{10... | collective-permute-start | bytes 786440 | tf_op jit(solution)/shard_map/ppermute | solution.py:555
  80.0 10.8 %collective-permute-start.16 = (bf16[64,2048]{1,0:T(8,128)(2,1)}, bf16[64,2048]{1,0:T(8,128)(2,1)S(1)}, u32[]{:S(2)}, u32[]{:S(2)}) collective-permute-start(bf16[64,2048]{1,0:T(8,128)(2,1)} %collective-permute-done.12.refs_4_), channel_id=1, source_target_pairs={{0,8},{8,0},{16,24},{24,16},{1,9},{9,1},{17,25},{25,17},{2,10},{10... | collective-permute-start | bytes 786440 | tf_op jit(solution)/shard_map/ppermute | solution.py:555
  87.5 9.0 %all-to-all-start.4 = ((bf16[4,16,512]{2,1,0:T(8,128)(2,1)}), bf16[4,16,512]{2,1,0:T(8,128)(2,1)S(1)}, u32[]{:S(2)}, u32[]{:S(2)}) async-start(bf16[4,16,512]{2,1,0:T(8,128)(2,1)} %shard_map.53), calls=%async_computation.4 | async-start | bytes 131072 | tf_op jit(solution)/shard_map/all_to_all | solution.py:587
  99.1 7.5 %collective-permute-start.17 = (bf16[16,512]{1,0:T(8,128)(2,1)S(1)}, bf16[16,512]{1,0:T(8,128)(2,1)S(1)}, u32[]{:S(2)}, u32[]{:S(2)}) collective-permute-start(bf16[16,512]{1,0:T(8,128)(2,1)S(1)} %get-tuple-element.32), channel_id=1, source_target_pairs={{0,2},{2,0},{4,6},{6,4},{1,3},{3,1},{5,7},{7,5},{8,10},{10,8},{12,... | collective-permute-start | bytes 49160 | tf_op jit(solution)/shard_map/ppermute | solution.py:599
  100.1 6.6 %collective-permute-start.18 = (bf16[16,512]{1,0:T(8,128)(2,1)S(1)}, bf16[16,512]{1,0:T(8,128)(2,1)S(1)}, u32[]{:S(2)}, u32[]{:S(2)}) collective-permute-start(bf16[16,512]{1,0:T(8,128)(2,1)S(1)} %get-tuple-element.33), channel_id=1, source_target_pairs={{0,4},{2,6},{4,0},{6,2},{1,5},{3,7},{5,1},{7,3},{8,12},{10,14},{12... | collective-permute-start | bytes 49160 | tf_op jit(solution)/shard_map/ppermute | solution.py:599
  100.5 6.2 %collective-permute-start.19 = (bf16[16,512]{1,0:T(8,128)(2,1)S(1)}, bf16[16,512]{1,0:T(8,128)(2,1)S(1)}, u32[]{:S(2)}, u32[]{:S(2)}) collective-permute-start(bf16[16,512]{1,0:T(8,128)(2,1)S(1)} %get-tuple-element.34), channel_id=1, source_target_pairs={{0,6},{2,4},{4,2},{6,0},{1,7},{3,5},{5,3},{7,1},{8,14},{10,12},{12... | collective-permute-start | bytes 49160 | tf_op jit(solution)/shard_map/ppermute | solution.py:599
  104.6 15.0 %collective-permute-start.25 = (bf16[256,1024]{1,0:T(8,128)(2,1)}, bf16[256,1024]{1,0:T(8,128)(2,1)S(1)}, u32[]{:S(2)}, u32[]{:S(2)}) collective-permute-start(bf16[256,1024]{1,0:T(8,128)(2,1)} %get-tuple-element.41), channel_id=1, source_target_pairs={{0,1},{1,0},{2,3},{3,2},{4,5},{5,4},{6,7},{7,6},{8,9},{9,8},{10,11... | collective-permute-start | bytes 1572872 | tf_op jit(solution)/shard_map/ppermute | solution.py:555
  106.1 24.8 %collective-permute-start = (bf16[256,1024]{1,0:T(8,128)(2,1)}, bf16[256,1024]{1,0:T(8,128)(2,1)S(1)}, u32[]{:S(2)}, u32[]{:S(2)}) collective-permute-start(bf16[256,1024]{1,0:T(8,128)(2,1)} %get-tuple-element.42), channel_id=1, source_target_pairs={{0,1},{1,0},{2,3},{3,2},{4,5},{5,4},{6,7},{7,6},{8,9},{9,8},{10,11... | collective-permute-start | bytes 1572872 | tf_op jit(solution)/shard_map/ppermute | solution.py:555
  107.3 14.6 %all-to-all-start.5 = ((bf16[8,16,512]{2,1,0:T(8,128)(2,1)}), bf16[8,16,512]{2,1,0:T(8,128)(2,1)S(1)}, u32[]{:S(2)}, u32[]{:S(2)}) async-start(bf16[8,16,512]{2,1,0:T(8,128)(2,1)} %shard_map.55), calls=%async_computation.5 | async-start | bytes 262144 | tf_op jit(solution)/shard_map/all_to_all | solution.py:580
  112.3 46.0 %collective-permute-start.24 = (bf16[256,2048]{1,0:T(8,128)(2,1)S(1)}, bf16[256,2048]{1,0:T(8,128)(2,1)S(1)}, u32[]{:S(2)}, u32[]{:S(2)}) collective-permute-start(bf16[256,2048]{1,0:T(8,128)(2,1)S(1)} %slice_bitcast_fusion), channel_id=1, source_target_pairs={{0,1},{1,0},{2,3},{3,2},{4,5},{5,4},{6,7},{7,6},{8,9},{9,8},{10,11... | collective-permute-start | bytes 3145736 | tf_op jit(solution)/shard_map/ppermute | solution.py:555
  121.9 26.7 %collective-permute-start.26 = (bf16[8,16,512]{2,1,0:T(8,128)(2,1)S(1)}, bf16[8,16,512]{2,1,0:T(8,128)(2,1)S(1)}, u32[]{:S(2)}, u32[]{:S(2)}) collective-permute-start(bf16[8,16,512]{2,1,0:T(8,128)(2,1)S(1)} %all-to-all-done.5.refs_5_.refs_2_), channel_id=1, source_target_pairs={{0,8},{8,0},{16,24},{24,16},{1,9},{9,1},{17,25},{25,17},{2,10},{10... | collective-permute-start | bytes 393224 | tf_op jit(solution)/shard_map/ppermute | solution.py:555
  137.9 6.1 %collective-permute-start.22 = (bf16[32,512]{1,0:T(8,128)(2,1)S(1)}, bf16[32,512]{1,0:T(8,128)(2,1)S(1)}, u32[]{:S(2)}, u32[]{:S(2)}) collective-permute-start(bf16[32,512]{1,0:T(8,128)(2,1)S(1)} %get-tuple-element.38), channel_id=1, source_target_pairs={{0,6},{2,4},{4,2},{6,0},{1,7},{3,5},{5,3},{7,1},{8,14},{10,12},{12... | collective-permute-start | bytes 98312 | tf_op jit(solution)/shard_map/ppermute | solution.py:599
  141.1 13.4 %collective-permute-start.27 = (f32[256,64]{1,0:T(8,128)S(1)}, f32[256,64]{1,0:T(8,128)S(1)}, u32[]{:S(2)}, u32[]{:S(2)}) collective-permute-start(f32[256,64]{1,0:T(8,128)S(1)} %copy-done.9), channel_id=1, source_target_pairs={{0,1},{1,0},{2,3},{3,2},{4,5},{5,4},{6,7},{7,6},{8,9},{9,8},{10,11... | collective-permute-start | bytes 196616 | tf_op jit(solution)/shard_map/ppermute | solution.py:555
  144.6 9.9 %all-to-all-start.6 = ((bf16[4,32,512]{2,1,0:T(8,128)(2,1)}), bf16[4,32,512]{2,1,0:T(8,128)(2,1)S(1)}, u32[]{:S(2)}, u32[]{:S(2)}) async-start(bf16[4,32,512]{2,1,0:T(8,128)(2,1)} %shard_map.57), calls=%async_computation.6 | async-start | bytes 262144 | tf_op jit(solution)/shard_map/all_to_all | solution.py:577
  162.3 13.2 %all-to-all-start.7 = ((bf16[8,64,256]{2,1,0:T(8,128)(2,1)}), bf16[8,64,256]{2,1,0:T(8,128)(2,1)S(1)}, u32[]{:S(2)}, u32[]{:S(2)}) async-start(bf16[8,64,256]{2,1,0:T(8,128)(2,1)} %shard_map.60), calls=%async_computation.7 | async-start | bytes 524288 | tf_op jit(solution)/shard_map/all_to_all | solution.py:836
  (15 other events, 137.8 us)

commit v7 on v6

--- a/solution.py
+++ b/solution.py
@@ -334,8 +334,11 @@
         out[...] = stage[own_cell ^ d]
 
 
-def forward_kernel(infos, k, at, gathered, mine_hbm, received_hbm, *refs):
+def forward_kernel(infos, k, at, *refs):
     info, above = infos[k - 1], infos[k]
+    near = refs[: info.cells]
+    mine_hbm, received_hbm = refs[info.cells : info.cells + 2]
+    gathered, refs = refs[-1], refs[info.cells + 2 : -1]
     count = 4 * info.pair_x
     pieces = refs[:count]
     lower_y = refs[count : count + k - 1]
@@ -353,6 +356,8 @@
     base = loads.start([(mine_hbm, mine), (received_hbm, received)])
     base += loads.start(list(zip(lower_y, lower_copies)))
     lower_y = lower_copies
+    for d, value in enumerate(near):
+        gathered[at[info.cell_slot] ^ d] = value[0]
     vector = natural_rows(info, gathered)
     ys = []
     for g, rows in enumerate(groups):
@@ -726,7 +731,13 @@
     for level in uppers:
         info = infos[level - 1]
         parts = (exchange_outer if level == 1 else exchange_middle)(parts, level)
-        gathered = exchange_inner(sum_spread(parts, info.cells), level)
+        if level == depth:
+            gathered = exchange_inner(sum_spread(parts, info.cells), level)
+        else:
+            own = sum_spread(parts, 1)
+            gathered = [own] + [
+                swap_inner(own, level, d) for d in range(info.cells - 1, 0, -1)
+            ][::-1]
         size = info.cell_rows * width * info.chunk
         count = 4 * info.pair_x
         if level == depth:
@@ -747,7 +758,7 @@
                 shaped((info.cell_rows, info.chunk), F32),
                 shaped((above.targets // 2, above.chunk, above.cell_rows), BF16),
             ],
-            [gathered]
+            gathered
             + hbm(
                 list(paired[level + 1])
                 + inverse_pieces[level]
@@ -763,7 +774,8 @@
                 pltpu.SemaphoreType.DMA((count + GROUPS * level + 1 + level,)),
             ]
             + [cell_scratch(infos[j - 1]) for j in range(1, level + 1)]
-            + [pltpu.VMEM(ys[j].shape, F32) for j in range(1, level)],
+            + [pltpu.VMEM(ys[j].shape, F32) for j in range(1, level)]
+            + [stage_scratch(info)],
             flops=4 * size,
         )
 

time: 177 us -> 167 us (0.944)
  waiting for transfers between devices: 67.6 us -> 57.3 us
    ppermute x23, waiting for transfers between devices: 36 us -> 23.7 us  [swap(): return lax.ppermute(value, axis, [(i, i ^ bit) for i in range(size)])]
    ppermute x6 -> x9, starting transfers between devices: 8.9 us -> 13.3 us  [swap_inner(): return lax.ppermute(value, axes, pairs)]
    all_to_all x1, waiting for transfers between devices: 0.01 us -> 3.8 us  [exchange_outer(): return lax.all_to_all(value, 'blk', 0, 0, tiled=True)]
    all_to_all x2 -> x1, starting transfers between devices: 6.61 us -> 3.28 us  [exchange_inner(): lax.all_to_all(value, 'blk', 0, 0, axis_index_groups=info.inner_blk, tile...]
    all_to_all x1, waiting for transfers between devices: 9 us -> 7.05 us  [solve(): full = lax.all_to_all(spread, 'blk', 0, 0, tiled=True).reshape(width, cases)]
    ppermute x23, starting transfers between devices: 18.1 us -> 16.2 us  [swap(): return lax.ppermute(value, axis, [(i, i ^ bit) for i in range(size)])]
    all_to_all x2 -> x1, waiting for transfers between devices: 5.63 us -> 5.72 us  [exchange_inner(): lax.all_to_all(value, 'blk', 0, 0, axis_index_groups=info.inner_blk, tile...]
  transfers between devices with their start and end apart: 37 -> 39, of which waited for: 11 -> 12; matrix products, arithmetic and copies ran while one was open for 4% -> 6% of each run, Pallas kernels for 17% -> 18%
where the time goes in v7:
time: 167 us; the launch traced here: 166 us
  starting transfers between devices  60.4 us (36%)
  waiting for transfers between devices  57.3 us (34%)
  Pallas kernels  38.5 us (23%)
  local copies, waits for them, and re-layouts  6.49 us (4%)
  other arithmetic  3.19 us (2%)
    pallas_call x16, Pallas kernels, kernel_call(): pl.pallas_call(body if scalars is None else lambda *refs: body(scalars(),...  38.5 us
    ppermute x23, waiting for transfers between devices, swap(): return lax.ppermute(value, axis, [(i, i ^ bit) for i in range(size)])  23.7 us
    ppermute x23, starting transfers between devices, swap(): return lax.ppermute(value, axis, [(i, i ^ bit) for i in range(size)])  16.2 us
    ppermute x9, starting transfers between devices, swap_inner(): return lax.ppermute(value, axes, pairs)  13.3 us
    all_to_all x2, starting transfers between devices, exchange_middle(): lax.all_to_all(value, ('leaf', 'blk'), 0, 0, axis_index_groups=info.middl...  8.23 us
    all_to_all x1, starting transfers between devices, solve(): full = lax.all_to_all(spread, 'blk', 0, 0, tiled=True).reshape(width, cases)  7.32 us
    all_to_all x1, waiting for transfers between devices, solve(): full = lax.all_to_all(spread, 'blk', 0, 0, tiled=True).reshape(width, cases)  7.05 us
    all_to_all x2, waiting for transfers between devices, exchange_middle(): lax.all_to_all(value, ('leaf', 'blk'), 0, 0, axis_index_groups=info.middl...  6.42 us
  transfers between devices with their start and end apart: 39, of which 12 were waited for; matrix products, arithmetic and copies ran while one was open for 6% of the time, Pallas kernels for 18%

profile of v7, /device:TPU:0, one launch (start us, length us, event | category | flops | bytes accessed | tf_op | source)
XLA Modules:
  0.0 166.3 jit_solution(16530246340021779125)
XLA Ops:
  1.9 7.3 %all-to-all-start = ((bf16[8,256,128]{2,1,0:T(8,128)(2,1)}), bf16[8,256,128]{2,1,0:T(8,128)(2,1)S(1)}, u32[]{:S(2)}, u32[]{:S(2)}) async-start(bf16[8,256,128]{2,1,0:T(8,128)(2,1)} %shard_map.48), calls=%async_computation | async-start | bytes 1048576 | tf_op jit(solution)/shard_map/all_to_all | solution.py:634
  9.2 2.1 %collective-permute-start.10 = (bf16[128,1024]{1,0:T(8,128)(2,1)S(1)}, bf16[128,1024]{1,0:T(8,128)(2,1)S(1)}, u32[]{:S(2)}, u32[]{:S(2)}) collective-permute-start(bf16[128,1024]{1,0:T(8,128)(2,1)S(1)} %slice_bitcast_fusion.5.refs_1_), channel_id=1, source_target_pairs={{0,1},{1,0},{2,3},{3,2},{4,5},{5,4},{6,7},{7,6},{8,9},{9,8},{10,11... | collective-permute-start | bytes 786440 | tf_op jit(solution)/shard_map/ppermute | solution.py:560
  13.3 3.4 %shard_map.46 = (bf16[256,2048]{1,0:T(8,128)(2,1)}, bf16[256,2048]{1,0:T(8,128)(2,1)}) custom-call(s32[10,1024]{1,0:T(8,128)S(1)} %copy-done.2, bf16[640,1024]{1,0:T(8,128)(2,1)S(1)} %bitcast.39), custom_call_target="tpu_custom_call" | custom-call | flops 2147483648 | bytes 3448832 | tf_op jit(solution)/shard_map/pallas_call | solution.py:47
  16.6 7.1 %all-to-all-done = bf16[8,256,128]{2,1,0:T(8,128)(2,1)S(1)} async-done(((bf16[8,256,128]{2,1,0:T(8,128)(2,1)}), bf16[8,256,128]{2,1,0:T(8,128)(2,1)S(1)}, u32[]{:S(2)}, u32[]{:S(2)}) %all-to-all-start) | async-done | bytes 524320 | tf_op jit(solution)/shard_map/all_to_all | solution.py:634
  23.7 4.3 %shard_map.49 = (f32[256,64]{1,0:T(8,128)}, f32[256,64]{1,0:T(8,128)}, bf16[8,32,512]{2,1,0:T(8,128)(2,1)S(1)}, bf16[8,32,512]{2,1,0:T(8,128)(2,1)S(1)}, bf16[16...) custom-call(bf16[2048,128]{1,0:T(8,128)(2,1)S(1)} %bitcast.38, bf16[448,2048]{1,0:T(8,128)(2,1)} %bitcast.42, ...), custom_call_target="tpu_custom_call" | custom-call | flops 402653184 | bytes 5865472 | tf_op jit(solution)/shard_map/pallas_call | solution.py:47
  29.6 4.6 %collective-permute-done.7.refs_7_.refs_2_ = bf16[128,2048]{1,0:T(8,128)(2,1)} collective-permute-done((bf16[128,2048]{1,0:T(8,128)(2,1)}, bf16[128,2048]{1,0:T(8,128)(2,1)}, u32[]{:S(2)}, u32[]{:S(2)}) %collective-permute-start.7) | collective-permute-done | bytes 524320 | tf_op jit(solution)/shard_map/ppermute | solution.py:560
  36.4 4.5 %all-to-all-start.1 = ((bf16[8,32,512]{2,1,0:T(8,128)(2,1)}), bf16[8,32,512]{2,1,0:T(8,128)(2,1)S(1)}, u32[]{:S(2)}, u32[]{:S(2)}) async-start(bf16[8,32,512]{2,1,0:T(8,128)(2,1)} %add_convert_fusion.1), calls=%async_computation.1 | async-start | bytes 524288 | tf_op jit(solution)/shard_map/all_to_all | solution.py:569
  46.3 3.8 %all-to-all-done.1.parts = bf16[8,32,512]{2,1,0:T(8,128)(2,1)S(1)} async-done(((bf16[8,32,512]{2,1,0:T(8,128)(2,1)}), bf16[8,32,512]{2,1,0:T(8,128)(2,1)S(1)}, u32[]{:S(2)}, u32[]{:S(2)}) %all-to-all-start.1) | async-done | bytes 262176 | tf_op jit(solution)/shard_map/all_to_all | solution.py:569
  55.1 2.1 %collective-permute-start.4 = (bf16[1,32,512]{2,1,0:T(8,128)(2,1)}, bf16[1,32,512]{2,1,0:T(8,128)(2,1)S(1)}, u32[]{:S(2)}, u32[]{:S(2)}) collective-permute-start(bf16[1,32,512]{2,1,0:T(8,128)(2,1)} %shard_map.50.refs_0_), channel_id=1, source_target_pairs={{0,6},{2,4},{4,2},{6,0},{1,7},{3,5},{5,3},{7,1},{8,14},{10,12},{12... | collective-permute-start | bytes 98312 | tf_op jit(solution)/shard_map/ppermute | solution.py:604
  57.2 3.7 %shard_map.51.refs_10_.refs_6_ = bf16[512,2048]{1,0:T(8,128)(2,1)} custom-call(s32[10,1024]{1,0:T(8,128)S(1)} %copy-done.2, bf16[128,1024]{1,0:T(8,128)(2,1)S(1)} %slice_bitcast_fusion.5.refs_1_, bf16[128,1024]{1,0:T(8,128)(2,1)S(1)} %collective-permute-done.10.refs_2_, bf16[128,1024]{1,0:T(8,128)(2,1)S(1)} %collective-permute-done.11.refs_3_, ...), custom_call_target="tpu_custom_call" | custom-call | flops 2147483648 | bytes 3186688 | tf_op jit(solution)/shard_map/pallas_call | solution.py:47
  61.0 3.8 %shard_map.52 = (f32[512,32]{1,0:T(8,128)}, bf16[8,16,512]{2,1,0:T(8,128)(2,1)}) custom-call(bf16[1,32,512]{2,1,0:T(8,128)(2,1)S(1)} %copy-done.1, bf16[1,32,512]{2,1,0:T(8,128)(2,1)S(1)} %collective-permute-done.2.refs_1_, bf16[1,32,512]{2,1,0:T(8,128)(2,1)S(1)} %collective-permute-done.3.refs_2_, bf16[1,32,512]{2,1,0:T(8,128)(2,1)S(1)} %collective-permute-done.4.refs_3_, ...), custom_call_target="tpu_custom_call" | custom-call | flops 134217728 | bytes 4784128 | tf_op jit(solution)/shard_map/pallas_call | solution.py:47
  64.9 4.3 %all-to-all-start.2 = ((bf16[8,16,512]{2,1,0:T(8,128)(2,1)}), bf16[8,16,512]{2,1,0:T(8,128)(2,1)S(1)}, u32[]{:S(2)}, u32[]{:S(2)}) async-start(bf16[8,16,512]{2,1,0:T(8,128)(2,1)} %get-tuple-element.30), calls=%async_computation.2 | async-start | bytes 262144 | tf_op jit(solution)/shard_map/all_to_all | solution.py:585
  70.2 6.4 %all-to-all-done.2.parts = bf16[8,16,512]{2,1,0:T(8,128)(2,1)S(1)} async-done(((bf16[8,16,512]{2,1,0:T(8,128)(2,1)}), bf16[8,16,512]{2,1,0:T(8,128)(2,1)S(1)}, u32[]{:S(2)}, u32[]{:S(2)}) %all-to-all-start.2) | async-done | bytes 131104 | tf_op jit(solution)/shard_map/all_to_all | solution.py:585
  77.3 3.3 %all-to-all-start.3 = ((bf16[4,16,512]{2,1,0:T(8,128)(2,1)}), bf16[4,16,512]{2,1,0:T(8,128)(2,1)S(1)}, u32[]{:S(2)}, u32[]{:S(2)}) async-start(bf16[4,16,512]{2,1,0:T(8,128)(2,1)} %shard_map.53), calls=%async_computation.3 | async-start | bytes 131072 | tf_op jit(solution)/shard_map/all_to_all | solution.py:592
  80.7 5.7 %all-to-all-done.3.refs_0_ = bf16[4,16,512]{2,1,0:T(8,128)(2,1)S(1)} async-done(((bf16[4,16,512]{2,1,0:T(8,128)(2,1)}), bf16[4,16,512]{2,1,0:T(8,128)(2,1)S(1)}, u32[]{:S(2)}, u32[]{:S(2)}) %all-to-all-start.3) | async-done | bytes 65568 | tf_op jit(solution)/shard_map/all_to_all | solution.py:592
  86.4 2.6 %shard_map.54 = (bf16[16,512]{1,0:T(8,128)(2,1)S(1)}, bf16[16,512]{1,0:T(8,128)(2,1)S(1)}, bf16[16,512]{1,0:T(8,128)(2,1)S(1)}, bf16[16,512]{1,0:T(8,128)(2,1)S(1)}) custom-call(bf16[4,16,512]{2,1,0:T(8,128)(2,1)S(1)} %all-to-all-done.3.refs_0_, bf16[64,2048]{1,0:T(8,128)(2,1)} %copy-done.4, bf16[64,2048]{1,0:T(8,128)(2,1)} %collective-permute-done.13.refs_2_, ...), custom_call_target="tpu_custom_call" | custom-call | flops 67108864 | bytes 2228224 | tf_op jit(solution)/shard_map/pallas_call | solution.py:47
  90.3 3.2 %collective-permute-start.22 = (bf16[16,512]{1,0:T(8,128)(2,1)S(1)}, bf16[16,512]{1,0:T(8,128)(2,1)S(1)}, u32[]{:S(2)}, u32[]{:S(2)}) collective-permute-start(bf16[16,512]{1,0:T(8,128)(2,1)S(1)} %get-tuple-element.34), channel_id=1, source_target_pairs={{0,6},{2,4},{4,2},{6,0},{1,7},{3,5},{5,3},{7,1},{8,14},{10,12},{12... | collective-permute-start | bytes 49160 | tf_op jit(solution)/shard_map/ppermute | solution.py:604
  97.2 3.9 %all-to-all-start.4 = ((bf16[8,16,512]{2,1,0:T(8,128)(2,1)}), bf16[8,16,512]{2,1,0:T(8,128)(2,1)S(1)}, u32[]{:S(2)}, u32[]{:S(2)}) async-start(bf16[8,16,512]{2,1,0:T(8,128)(2,1)} %shard_map.55), calls=%async_computation.4 | async-start | bytes 262144 | tf_op jit(solution)/shard_map/all_to_all | solution.py:585
  103.5 6.0 %collective-permute-done.28.refs_1_ = bf16[256,1024]{1,0:T(8,128)(2,1)S(1)} collective-permute-done((bf16[256,1024]{1,0:T(8,128)(2,1)}, bf16[256,1024]{1,0:T(8,128)(2,1)S(1)}, u32[]{:S(2)}, u32[]{:S(2)}) %collective-permute-start.28) | collective-permute-done | bytes 524320 | tf_op jit(solution)/shard_map/ppermute | solution.py:560
  109.5 2.3 %shard_map.58.refs_1_ = bf16[256,2048]{1,0:T(8,128)(2,1)} custom-call(s32[10,1024]{1,0:T(8,128)S(1)} %copy-done.2, bf16[256,1024]{1,0:T(8,128)(2,1)S(1)} %collective-permute-done.28.refs_1_), custom_call_target="tpu_custom_call" | custom-call | flops 1073741824 | bytes 1613824 | tf_op jit(solution)/shard_map/pallas_call | solution.py:47
  111.8 8.9 %collective-permute-done.refs_1_ = bf16[256,1024]{1,0:T(8,128)(2,1)S(1)} collective-permute-done((bf16[256,1024]{1,0:T(8,128)(2,1)}, bf16[256,1024]{1,0:T(8,128)(2,1)S(1)}, u32[]{:S(2)}, u32[]{:S(2)}) %collective-permute-start) | collective-permute-done | bytes 524320 | tf_op jit(solution)/shard_map/ppermute | solution.py:560
  120.8 2.3 %shard_map.47.refs_1_ = bf16[256,2048]{1,0:T(8,128)(2,1)} custom-call(s32[10,1024]{1,0:T(8,128)S(1)} %copy-done.2, bf16[256,1024]{1,0:T(8,128)(2,1)S(1)} %collective-permute-done.refs_1_), custom_call_target="tpu_custom_call" | custom-call | flops 1073741824 | bytes 1613824 | tf_op jit(solution)/shard_map/pallas_call | solution.py:47
  123.1 3.3 %shard_map.56 = (bf16[32,512]{1,0:T(8,128)(2,1)S(1)}, bf16[32,512]{1,0:T(8,128)(2,1)S(1)}, bf16[32,512]{1,0:T(8,128)(2,1)S(1)}, bf16[32,512]{1,0:T(8,128)(2,1)S(1)}) custom-call(f32[512,32]{1,0:T(8,128)} %get-tuple-element.29.refs_0_, bf16[128,2048]{1,0:T(8,128)(2,1)} %slice_bitcast_fusion.2.refs_6_.refs_1_, ...), custom_call_target="tpu_custom_call" | custom-call | flops 134217728 | bytes 4521984 | tf_op jit(solution)/shard_map/pallas_call | solution.py:47
  127.7 3.2 %collective-permute-start.25 = (bf16[32,512]{1,0:T(8,128)(2,1)S(1)}, bf16[32,512]{1,0:T(8,128)(2,1)S(1)}, u32[]{:S(2)}, u32[]{:S(2)}) collective-permute-start(bf16[32,512]{1,0:T(8,128)(2,1)S(1)} %get-tuple-element.38), channel_id=1, source_target_pairs={{0,6},{2,4},{4,2},{6,0},{1,7},{3,5},{5,3},{7,1},{8,14},{10,12},{12... | collective-permute-start | bytes 98312 | tf_op jit(solution)/shard_map/ppermute | solution.py:604
  134.4 4.1 %all-to-all-start.5 = ((bf16[4,32,512]{2,1,0:T(8,128)(2,1)}), bf16[4,32,512]{2,1,0:T(8,128)(2,1)S(1)}, u32[]{:S(2)}, u32[]{:S(2)}) async-start(bf16[4,32,512]{2,1,0:T(8,128)(2,1)} %shard_map.57), calls=%async_computation.5 | async-start | bytes 262144 | tf_op jit(solution)/shard_map/all_to_all | solution.py:582
  138.7 5.7 %all-to-all-done.5.refs_2_ = bf16[4,32,512]{2,1,0:T(8,128)(2,1)S(1)} async-done(((bf16[4,32,512]{2,1,0:T(8,128)(2,1)}), bf16[4,32,512]{2,1,0:T(8,128)(2,1)S(1)}, u32[]{:S(2)}, u32[]{:S(2)}) %all-to-all-start.5) | async-done | bytes 131104 | tf_op jit(solution)/shard_map/all_to_all | solution.py:582
  144.4 3.5 %shard_map.59.refs_6_ = f32[512,64]{1,0:T(8,128)} custom-call(bf16[256,2048]{1,0:T(8,128)(2,1)} %get-tuple-element.24.refs_4_.refs_0_, bf16[256,2048]{1,0:T(8,128)(2,1)} %shard_map.58.refs_1_, bf16[8,16,512]{2,1,0:T(8,128)(2,1)S(1)} %all-to-all-done.4.refs_5_.refs_2_, bf16[8,16,512]{2,1,0:T(8,128)(2,1)S(1)} %collective-permute-done.29.refs_3_, ...), custom_call_target="tpu_custom_call" | custom-call | flops 134217728 | bytes 2621440 | tf_op jit(solution)/shard_map/pallas_call | solution.py:47
  148.3 4.0 %shard_map.60 = bf16[8,64,256]{2,1,0:T(8,128)(2,1)} custom-call(bf16[256,2048]{1,0:T(8,128)(2,1)} %get-tuple-element.23.refs_3_.refs_0_, bf16[256,2048]{1,0:T(8,128)(2,1)} %shard_map.47.refs_1_, bf16[4,32,512]{2,1,0:T(8,128)(2,1)S(1)} %all-to-all-done.5.refs_2_, bf16[4,32,512]{2,1,0:T(8,128)(2,1)S(1)} %collective-permute-done.26.refs_3_, ...), custom_call_target="tpu_custom_call" | custom-call | flops 268435456 | bytes 5636096 | tf_op jit(solution)/shard_map/pallas_call | solution.py:47
  152.2 3.4 %all-to-all-start.6 = ((bf16[8,64,256]{2,1,0:T(8,128)(2,1)}), bf16[8,64,256]{2,1,0:T(8,128)(2,1)S(1)}, u32[]{:S(2)}, u32[]{:S(2)}) async-start(bf16[8,64,256]{2,1,0:T(8,128)(2,1)} %shard_map.60), calls=%async_computation.6 | async-start | bytes 524288 | tf_op jit(solution)/shard_map/all_to_all | solution.py:848
  155.8 2.0 %collective-permute-start.31 = (bf16[64,192]{0,1:T(8,128)(2,1)S(1)}, bf16[64,192]{0,1:T(8,128)(2,1)S(1)}, u32[]{:S(2)}, u32[]{:S(2)}) collective-permute-start(bf16[64,192]{0,1:T(8,128)(2,1)S(1)} %pad_maximum_fusion), channel_id=1, source_target_pairs={{0,1},{1,0},{2,3},{3,2},{4,5},{5,4},{6,7},{7,6},{8,9},{9,8},{10,11... | collective-permute-start | bytes 73736 | tf_op jit(solution)/shard_map/ppermute | solution.py:560
  157.8 4.1 %collective-permute-done.31 = bf16[64,192]{0,1:T(8,128)(2,1)S(1)} collective-permute-done((bf16[64,192]{0,1:T(8,128)(2,1)S(1)}, bf16[64,192]{0,1:T(8,128)(2,1)S(1)}, u32[]{:S(2)}, u32[]{:S(2)}) %collective-permute-start.31) | collective-permute-done | bytes 24608 | tf_op jit(solution)/shard_map/ppermute | solution.py:560
  162.0 3.4 %all-to-all-done.6.parts = bf16[8,64,256]{2,1,0:T(8,128)(2,1)S(1)} async-done(((bf16[8,64,256]{2,1,0:T(8,128)(2,1)}), bf16[8,64,256]{2,1,0:T(8,128)(2,1)S(1)}, u32[]{:S(2)}, u32[]{:S(2)}) %all-to-all-start.6) | async-done | bytes 262176 | tf_op jit(solution)/shard_map/all_to_all | solution.py:848
  (106 shorter events, 33.6 us)
Async XLA Ops:
  1.9 21.8 %all-to-all-start = ((bf16[8,256,128]{2,1,0:T(8,128)(2,1)}), bf16[8,256,128]{2,1,0:T(8,128)(2,1)S(1)}, u32[]{:S(2)}, u32[]{:S(2)}) async-start(bf16[8,256,128]{2,1,0:T(8,128)(2,1)} %shard_map.48), calls=%async_computation | async-start | bytes 1048576 | tf_op jit(solution)/shard_map/all_to_all | solution.py:634
  9.2 31.7 %collective-permute-start.10 = (bf16[128,1024]{1,0:T(8,128)(2,1)S(1)}, bf16[128,1024]{1,0:T(8,128)(2,1)S(1)}, u32[]{:S(2)}, u32[]{:S(2)}) collective-permute-start(bf16[128,1024]{1,0:T(8,128)(2,1)S(1)} %slice_bitcast_fusion.5.refs_1_), channel_id=1, source_target_pairs={{0,1},{1,0},{2,3},{3,2},{4,5},{5,4},{6,7},{7,6},{8,9},{9,8},{10,11... | collective-permute-start | bytes 786440 | tf_op jit(solution)/shard_map/ppermute | solution.py:560
  11.3 33.0 %collective-permute-start.11 = (bf16[128,1024]{1,0:T(8,128)(2,1)S(1)}, bf16[128,1024]{1,0:T(8,128)(2,1)S(1)}, u32[]{:S(2)}, u32[]{:S(2)}) collective-permute-start(bf16[128,1024]{1,0:T(8,128)(2,1)S(1)} %slice_bitcast_fusion.5.refs_1_), channel_id=1, source_target_pairs={{0,8},{8,0},{16,24},{24,16},{1,9},{9,1},{17,25},{25,17},{2,10},{10... | collective-permute-start | bytes 786440 | tf_op jit(solution)/shard_map/ppermute | solution.py:560
  13.2 20.9 %collective-permute-start.7 = (bf16[128,2048]{1,0:T(8,128)(2,1)}, bf16[128,2048]{1,0:T(8,128)(2,1)}, u32[]{:S(2)}, u32[]{:S(2)}) collective-permute-start(bf16[128,2048]{1,0:T(8,128)(2,1)} %slice_bitcast_fusion.2.refs_6_.refs_1_), channel_id=1, source_target_pairs={{0,1},{1,0},{2,3},{3,2},{4,5},{5,4},{6,7},{7,6},{8,9},{9,8},{10,11... | collective-permute-start | bytes 1572872 | tf_op jit(solution)/shard_map/ppermute | solution.py:560
  28.0 14.5 %collective-permute-start.5 = (bf16[16,16,512]{2,1,0:T(8,128)(2,1)}, bf16[16,16,512]{2,1,0:T(8,128)(2,1)}, u32[]{:S(2)}, u32[]{:S(2)}) collective-permute-start(bf16[16,16,512]{2,1,0:T(8,128)(2,1)} %get-tuple-element.28), channel_id=1, source_target_pairs={{0,8},{8,0},{16,24},{24,16},{1,9},{9,1},{17,25},{25,17},{2,10},{10... | collective-permute-start | bytes 786440 | tf_op jit(solution)/shard_map/ppermute | solution.py:560
  34.1 18.6 %collective-permute-start.8 = (bf16[128,2048]{1,0:T(8,128)(2,1)}, bf16[128,2048]{1,0:T(8,128)(2,1)S(1)}, u32[]{:S(2)}, u32[]{:S(2)}) collective-permute-start(bf16[128,2048]{1,0:T(8,128)(2,1)} %slice_bitcast_fusion.2.refs_6_.refs_1_), channel_id=1, source_target_pairs={{0,8},{8,0},{16,24},{24,16},{1,9},{9,1},{17,25},{25,17},{2,10},{10... | collective-permute-start | bytes 1572872 | tf_op jit(solution)/shard_map/ppermute | solution.py:560
  34.1 19.7 %collective-permute-start.9 = (bf16[128,2048]{1,0:T(8,128)(2,1)}, bf16[128,2048]{1,0:T(8,128)(2,1)}, u32[]{:S(2)}, u32[]{:S(2)}) collective-permute-start(bf16[128,2048]{1,0:T(8,128)(2,1)} %collective-permute-done.7.refs_7_.refs_2_), channel_id=1, source_target_pairs={{0,8},{8,0},{16,24},{24,16},{1,9},{9,1},{17,25},{25,17},{2,10},{10... | collective-permute-start | bytes 1572872 | tf_op jit(solution)/shard_map/ppermute | solution.py:560
  36.4 13.7 %all-to-all-start.1 = ((bf16[8,32,512]{2,1,0:T(8,128)(2,1)}), bf16[8,32,512]{2,1,0:T(8,128)(2,1)S(1)}, u32[]{:S(2)}, u32[]{:S(2)}) async-start(bf16[8,32,512]{2,1,0:T(8,128)(2,1)} %add_convert_fusion.1), calls=%async_computation.1 | async-start | bytes 524288 | tf_op jit(solution)/shard_map/all_to_all | solution.py:569
  40.9 9.8 %collective-permute-start.13 = (bf16[64,2048]{1,0:T(8,128)(2,1)S(1)}, bf16[64,2048]{1,0:T(8,128)(2,1)}, u32[]{:S(2)}, u32[]{:S(2)}) collective-permute-start(bf16[64,2048]{1,0:T(8,128)(2,1)S(1)} %slice_bitcast_fusion.4.refs_1_), channel_id=1, source_target_pairs={{0,16},{8,24},{16,0},{24,8},{1,17},{9,25},{17,1},{25,9},{2,18},{10... | collective-permute-start | bytes 786440 | tf_op jit(solution)/shard_map/ppermute | solution.py:560
  42.5 9.6 %collective-permute-start.12 = (bf16[128,1024]{1,0:T(8,128)(2,1)S(1)}, bf16[128,1024]{1,0:T(8,128)(2,1)S(1)}, u32[]{:S(2)}, u32[]{:S(2)}) collective-permute-start(bf16[128,1024]{1,0:T(8,128)(2,1)S(1)} %collective-permute-done.10.refs_2_), channel_id=1, source_target_pairs={{0,8},{8,0},{16,24},{24,16},{1,9},{9,1},{17,25},{25,17},{2,10},{10... | collective-permute-start | bytes 786440 | tf_op jit(solution)/shard_map/ppermute | solution.py:560
  44.3 10.8 %collective-permute-start.6 = (bf16[8,16,512]{2,1,0:T(8,128)(2,1)}, bf16[8,16,512]{2,1,0:T(8,128)(2,1)}, u32[]{:S(2)}, u32[]{:S(2)}) collective-permute-start(bf16[8,16,512]{2,1,0:T(8,128)(2,1)} %get-tuple-element.43), channel_id=1, source_target_pairs={{0,1},{1,0},{2,3},{3,2},{4,5},{5,4},{6,7},{7,6},{8,9},{9,8},{10,11... | collective-permute-start | bytes 393224 | tf_op jit(solution)/shard_map/ppermute | solution.py:560
  50.7 19.0 %collective-permute-start.14 = (bf16[64,2048]{1,0:T(8,128)(2,1)S(1)}, bf16[64,2048]{1,0:T(8,128)(2,1)S(1)}, u32[]{:S(2)}, u32[]{:S(2)}) collective-permute-start(bf16[64,2048]{1,0:T(8,128)(2,1)S(1)} %slice_bitcast_fusion.4.refs_1_), channel_id=1, source_target_pairs={{0,1},{1,0},{2,3},{3,2},{4,5},{5,4},{6,7},{7,6},{8,9},{9,8},{10,11... | collective-permute-start | bytes 786440 | tf_op jit(solution)/shard_map/ppermute | solution.py:560
  52.1 17.7 %collective-permute-start.15 = (bf16[64,2048]{1,0:T(8,128)(2,1)}, bf16[64,2048]{1,0:T(8,128)(2,1)}, u32[]{:S(2)}, u32[]{:S(2)}) collective-permute-start(bf16[64,2048]{1,0:T(8,128)(2,1)} %collective-permute-done.13.refs_2_), channel_id=1, source_target_pairs={{0,1},{1,0},{2,3},{3,2},{4,5},{5,4},{6,7},{7,6},{8,9},{9,8},{10,11... | collective-permute-start | bytes 786440 | tf_op jit(solution)/shard_map/ppermute | solution.py:560
  52.8 8.1 %collective-permute-start.2 = (bf16[1,32,512]{2,1,0:T(8,128)(2,1)}, bf16[1,32,512]{2,1,0:T(8,128)(2,1)S(1)}, u32[]{:S(2)}, u32[]{:S(2)}) collective-permute-start(bf16[1,32,512]{2,1,0:T(8,128)(2,1)} %shard_map.50.refs_0_), channel_id=1, source_target_pairs={{0,2},{2,0},{4,6},{6,4},{1,3},{3,1},{5,7},{7,5},{8,10},{10,8},{12,... | collective-permute-start | bytes 98312 | tf_op jit(solution)/shard_map/ppermute | solution.py:604
  53.8 7.1 %collective-permute-start.3 = (bf16[1,32,512]{2,1,0:T(8,128)(2,1)}, bf16[1,32,512]{2,1,0:T(8,128)(2,1)S(1)}, u32[]{:S(2)}, u32[]{:S(2)}) collective-permute-start(bf16[1,32,512]{2,1,0:T(8,128)(2,1)} %shard_map.50.refs_0_), channel_id=1, source_target_pairs={{0,4},{2,6},{4,0},{6,2},{1,5},{3,7},{5,1},{7,3},{8,12},{10,14},{12... | collective-permute-start | bytes 98312 | tf_op jit(solution)/shard_map/ppermute | solution.py:604
  64.9 11.8 %all-to-all-start.2 = ((bf16[8,16,512]{2,1,0:T(8,128)(2,1)}), bf16[8,16,512]{2,1,0:T(8,128)(2,1)S(1)}, u32[]{:S(2)}, u32[]{:S(2)}) async-start(bf16[8,16,512]{2,1,0:T(8,128)(2,1)} %get-tuple-element.30), calls=%async_computation.2 | async-start | bytes 262144 | tf_op jit(solution)/shard_map/all_to_all | solution.py:585
  69.1 11.5 %collective-permute-start.16 = (bf16[64,2048]{1,0:T(8,128)(2,1)S(1)}, bf16[64,2048]{1,0:T(8,128)(2,1)S(1)}, u32[]{:S(2)}, u32[]{:S(2)}) collective-permute-start(bf16[64,2048]{1,0:T(8,128)(2,1)S(1)} %slice_bitcast_fusion.4.refs_1_), channel_id=1, source_target_pairs={{0,8},{8,0},{16,24},{24,16},{1,9},{9,1},{17,25},{25,17},{2,10},{10... | collective-permute-start | bytes 786440 | tf_op jit(solution)/shard_map/ppermute | solution.py:560
  69.2 11.4 %collective-permute-start.17 = (bf16[64,2048]{1,0:T(8,128)(2,1)}, bf16[64,2048]{1,0:T(8,128)(2,1)S(1)}, u32[]{:S(2)}, u32[]{:S(2)}) collective-permute-start(bf16[64,2048]{1,0:T(8,128)(2,1)} %collective-permute-done.13.refs_2_), channel_id=1, source_target_pairs={{0,8},{8,0},{16,24},{24,16},{1,9},{9,1},{17,25},{25,17},{2,10},{10... | collective-permute-start | bytes 786440 | tf_op jit(solution)/shard_map/ppermute | solution.py:560
  69.7 10.9 %collective-permute-start.18 = (bf16[64,2048]{1,0:T(8,128)(2,1)S(1)}, bf16[64,2048]{1,0:T(8,128)(2,1)S(1)}, u32[]{:S(2)}, u32[]{:S(2)}) collective-permute-start(bf16[64,2048]{1,0:T(8,128)(2,1)S(1)} %collective-permute-done.14.refs_3_), channel_id=1, source_target_pairs={{0,8},{8,0},{16,24},{24,16},{1,9},{9,1},{17,25},{25,17},{2,10},{10... | collective-permute-start | bytes 786440 | tf_op jit(solution)/shard_map/ppermute | solution.py:560
  69.8 10.8 %collective-permute-start.19 = (bf16[64,2048]{1,0:T(8,128)(2,1)}, bf16[64,2048]{1,0:T(8,128)(2,1)S(1)}, u32[]{:S(2)}, u32[]{:S(2)}) collective-permute-start(bf16[64,2048]{1,0:T(8,128)(2,1)} %collective-permute-done.15.refs_4_), channel_id=1, source_target_pairs={{0,8},{8,0},{16,24},{24,16},{1,9},{9,1},{17,25},{25,17},{2,10},{10... | collective-permute-start | bytes 786440 | tf_op jit(solution)/shard_map/ppermute | solution.py:560
  77.3 9.1 %all-to-all-start.3 = ((bf16[4,16,512]{2,1,0:T(8,128)(2,1)}), bf16[4,16,512]{2,1,0:T(8,128)(2,1)S(1)}, u32[]{:S(2)}, u32[]{:S(2)}) async-start(bf16[4,16,512]{2,1,0:T(8,128)(2,1)} %shard_map.53), calls=%async_computation.3 | async-start | bytes 131072 | tf_op jit(solution)/shard_map/all_to_all | solution.py:592
  89.0 7.5 %collective-permute-start.20 = (bf16[16,512]{1,0:T(8,128)(2,1)S(1)}, bf16[16,512]{1,0:T(8,128)(2,1)S(1)}, u32[]{:S(2)}, u32[]{:S(2)}) collective-permute-start(bf16[16,512]{1,0:T(8,128)(2,1)S(1)} %get-tuple-element.32), channel_id=1, source_target_pairs={{0,2},{2,0},{4,6},{6,4},{1,3},{3,1},{5,7},{7,5},{8,10},{10,8},{12,... | collective-permute-start | bytes 49160 | tf_op jit(solution)/shard_map/ppermute | solution.py:604
  90.1 6.5 %collective-permute-start.21 = (bf16[16,512]{1,0:T(8,128)(2,1)S(1)}, bf16[16,512]{1,0:T(8,128)(2,1)S(1)}, u32[]{:S(2)}, u32[]{:S(2)}) collective-permute-start(bf16[16,512]{1,0:T(8,128)(2,1)S(1)} %get-tuple-element.33), channel_id=1, source_target_pairs={{0,4},{2,6},{4,0},{6,2},{1,5},{3,7},{5,1},{7,3},{8,12},{10,14},{12... | collective-permute-start | bytes 49160 | tf_op jit(solution)/shard_map/ppermute | solution.py:604
  90.3 6.3 %collective-permute-start.22 = (bf16[16,512]{1,0:T(8,128)(2,1)S(1)}, bf16[16,512]{1,0:T(8,128)(2,1)S(1)}, u32[]{:S(2)}, u32[]{:S(2)}) collective-permute-start(bf16[16,512]{1,0:T(8,128)(2,1)S(1)} %get-tuple-element.34), channel_id=1, source_target_pairs={{0,6},{2,4},{4,2},{6,0},{1,7},{3,5},{5,3},{7,1},{8,14},{10,12},{12... | collective-permute-start | bytes 49160 | tf_op jit(solution)/shard_map/ppermute | solution.py:604
  94.5 15.0 %collective-permute-start.28 = (bf16[256,1024]{1,0:T(8,128)(2,1)}, bf16[256,1024]{1,0:T(8,128)(2,1)S(1)}, u32[]{:S(2)}, u32[]{:S(2)}) collective-permute-start(bf16[256,1024]{1,0:T(8,128)(2,1)} %get-tuple-element.41), channel_id=1, source_target_pairs={{0,1},{1,0},{2,3},{3,2},{4,5},{5,4},{6,7},{7,6},{8,9},{9,8},{10,11... | collective-permute-start | bytes 1572872 | tf_op jit(solution)/shard_map/ppermute | solution.py:560
  95.7 25.0 %collective-permute-start = (bf16[256,1024]{1,0:T(8,128)(2,1)}, bf16[256,1024]{1,0:T(8,128)(2,1)S(1)}, u32[]{:S(2)}, u32[]{:S(2)}) collective-permute-start(bf16[256,1024]{1,0:T(8,128)(2,1)} %get-tuple-element.42), channel_id=1, source_target_pairs={{0,1},{1,0},{2,3},{3,2},{4,5},{5,4},{6,7},{7,6},{8,9},{9,8},{10,11... | collective-permute-start | bytes 1572872 | tf_op jit(solution)/shard_map/ppermute | solution.py:560
  97.2 14.6 %all-to-all-start.4 = ((bf16[8,16,512]{2,1,0:T(8,128)(2,1)}), bf16[8,16,512]{2,1,0:T(8,128)(2,1)S(1)}, u32[]{:S(2)}, u32[]{:S(2)}) async-start(bf16[8,16,512]{2,1,0:T(8,128)(2,1)} %shard_map.55), calls=%async_computation.4 | async-start | bytes 262144 | tf_op jit(solution)/shard_map/all_to_all | solution.py:585
  102.5 45.8 %collective-permute-start.27 = (bf16[256,2048]{1,0:T(8,128)(2,1)S(1)}, bf16[256,2048]{1,0:T(8,128)(2,1)S(1)}, u32[]{:S(2)}, u32[]{:S(2)}) collective-permute-start(bf16[256,2048]{1,0:T(8,128)(2,1)S(1)} %slice_bitcast_fusion), channel_id=1, source_target_pairs={{0,1},{1,0},{2,3},{3,2},{4,5},{5,4},{6,7},{7,6},{8,9},{9,8},{10,11... | collective-permute-start | bytes 3145736 | tf_op jit(solution)/shard_map/ppermute | solution.py:560
  111.8 26.7 %collective-permute-start.29 = (bf16[8,16,512]{2,1,0:T(8,128)(2,1)S(1)}, bf16[8,16,512]{2,1,0:T(8,128)(2,1)S(1)}, u32[]{:S(2)}, u32[]{:S(2)}) collective-permute-start(bf16[8,16,512]{2,1,0:T(8,128)(2,1)S(1)} %all-to-all-done.4.refs_5_.refs_2_), channel_id=1, source_target_pairs={{0,8},{8,0},{16,24},{24,16},{1,9},{9,1},{17,25},{25,17},{2,10},{10... | collective-permute-start | bytes 393224 | tf_op jit(solution)/shard_map/ppermute | solution.py:560
  131.0 13.4 %collective-permute-start.30 = (f32[256,64]{1,0:T(8,128)S(1)}, f32[256,64]{1,0:T(8,128)S(1)}, u32[]{:S(2)}, u32[]{:S(2)}) collective-permute-start(f32[256,64]{1,0:T(8,128)S(1)} %copy-done.10), channel_id=1, source_target_pairs={{0,1},{1,0},{2,3},{3,2},{4,5},{5,4},{6,7},{7,6},{8,9},{9,8},{10,11... | collective-permute-start | bytes 196616 | tf_op jit(solution)/shard_map/ppermute | solution.py:560
  134.4 10.0 %all-to-all-start.5 = ((bf16[4,32,512]{2,1,0:T(8,128)(2,1)}), bf16[4,32,512]{2,1,0:T(8,128)(2,1)S(1)}, u32[]{:S(2)}, u32[]{:S(2)}) async-start(bf16[4,32,512]{2,1,0:T(8,128)(2,1)} %shard_map.57), calls=%async_computation.5 | async-start | bytes 262144 | tf_op jit(solution)/shard_map/all_to_all | solution.py:582
  152.2 13.2 %all-to-all-start.6 = ((bf16[8,64,256]{2,1,0:T(8,128)(2,1)}), bf16[8,64,256]{2,1,0:T(8,128)(2,1)S(1)}, u32[]{:S(2)}, u32[]{:S(2)}) async-start(bf16[8,64,256]{2,1,0:T(8,128)(2,1)} %shard_map.60), calls=%async_computation.6 | async-start | bytes 524288 | tf_op jit(solution)/shard_map/all_to_all | solution.py:848
  (18 other events, 166.3 us)

commit v8 on v7

--- a/solution.py
+++ b/solution.py
@@ -712,7 +712,10 @@
 
     def sum_spread(parts, copies):
         return kernel_call(
-            sum_spread_kernel, [shaped((copies,) + parts.shape[1:], BF16)], [parts]
+            sum_spread_kernel,
+            [shaped((copies,) + parts.shape[1:], BF16)],
+            [parts],
+            stay=[copies > 1],
         )[0]
 
     def sum_parts(parts, copies):

time: 167 us -> 167 us (level)
  transfers between devices with their start and end apart: 39 -> 39, of which waited for: 12 -> 12; matrix products, arithmetic and copies ran while one was open for 6% -> 6% of each run, Pallas kernels for 18% -> 17%
where the time goes in v8:
time: 167 us; the launch traced here: 166 us
  starting transfers between devices  61.2 us (37%)
  waiting for transfers between devices  56.6 us (34%)
  Pallas kernels  37.9 us (23%)
  local copies, waits for them, and re-layouts  6.49 us (4%)
  other arithmetic  3.19 us (2%)
    pallas_call x16, Pallas kernels, kernel_call(): pl.pallas_call(body if scalars is None else lambda *refs: body(scalars(),...  37.9 us
    ppermute x23, waiting for transfers between devices, swap(): return lax.ppermute(value, axis, [(i, i ^ bit) for i in range(size)])  22.8 us
    ppermute x23, starting transfers between devices, swap(): return lax.ppermute(value, axis, [(i, i ^ bit) for i in range(size)])  17.1 us
    ppermute x9, starting transfers between devices, swap_inner(): return lax.ppermute(value, axes, pairs)  13.3 us
    all_to_all x2, starting transfers between devices, exchange_middle(): lax.all_to_all(value, ('leaf', 'blk'), 0, 0, axis_index_groups=info.middl...  8 us
    all_to_all x1, starting transfers between devices, solve(): full = lax.all_to_all(spread, 'blk', 0, 0, tiled=True).reshape(width, cases)  7.32 us
    all_to_all x1, waiting for transfers between devices, solve(): full = lax.all_to_all(spread, 'blk', 0, 0, tiled=True).reshape(width, cases)  7.04 us
    all_to_all x2, waiting for transfers between devices, exchange_middle(): lax.all_to_all(value, ('leaf', 'blk'), 0, 0, axis_index_groups=info.middl...  6.42 us
  transfers between devices with their start and end apart: 39, of which 12 were waited for; matrix products, arithmetic and copies ran while one was open for 6% of the time, Pallas kernels for 17%

profile of v8, /device:TPU:0, one launch (start us, length us, event | category | flops | bytes accessed | tf_op | source)
XLA Modules:
  0.0 165.8 jit_solution(15013633980537247074)
XLA Ops:
  1.9 7.3 %all-to-all-start = ((bf16[8,256,128]{2,1,0:T(8,128)(2,1)}), bf16[8,256,128]{2,1,0:T(8,128)(2,1)S(1)}, u32[]{:S(2)}, u32[]{:S(2)}) async-start(bf16[8,256,128]{2,1,0:T(8,128)(2,1)} %shard_map.48), calls=%async_computation | async-start | bytes 1048576 | tf_op jit(solution)/shard_map/all_to_all | solution.py:634
  9.2 2.1 %collective-permute-start.10 = (bf16[128,1024]{1,0:T(8,128)(2,1)S(1)}, bf16[128,1024]{1,0:T(8,128)(2,1)S(1)}, u32[]{:S(2)}, u32[]{:S(2)}) collective-permute-start(bf16[128,1024]{1,0:T(8,128)(2,1)S(1)} %slice_bitcast_fusion.5.refs_1_), channel_id=1, source_target_pairs={{0,1},{1,0},{2,3},{3,2},{4,5},{5,4},{6,7},{7,6},{8,9},{9,8},{10,11... | collective-permute-start | bytes 786440 | tf_op jit(solution)/shard_map/ppermute | solution.py:560
  13.3 3.4 %shard_map.46 = (bf16[256,2048]{1,0:T(8,128)(2,1)}, bf16[256,2048]{1,0:T(8,128)(2,1)}) custom-call(s32[10,1024]{1,0:T(8,128)S(1)} %copy-done.1, bf16[640,1024]{1,0:T(8,128)(2,1)S(1)} %bitcast.39), custom_call_target="tpu_custom_call" | custom-call | flops 2147483648 | bytes 3448832 | tf_op jit(solution)/shard_map/pallas_call | solution.py:47
  16.7 7.0 %all-to-all-done = bf16[8,256,128]{2,1,0:T(8,128)(2,1)S(1)} async-done(((bf16[8,256,128]{2,1,0:T(8,128)(2,1)}), bf16[8,256,128]{2,1,0:T(8,128)(2,1)S(1)}, u32[]{:S(2)}, u32[]{:S(2)}) %all-to-all-start) | async-done | bytes 524320 | tf_op jit(solution)/shard_map/all_to_all | solution.py:634
  23.7 4.3 %shard_map.49 = (f32[256,64]{1,0:T(8,128)}, f32[256,64]{1,0:T(8,128)}, bf16[8,32,512]{2,1,0:T(8,128)(2,1)S(1)}, bf16[8,32,512]{2,1,0:T(8,128)(2,1)S(1)}, bf16[16...) custom-call(bf16[2048,128]{1,0:T(8,128)(2,1)S(1)} %bitcast.38, bf16[448,2048]{1,0:T(8,128)(2,1)} %bitcast.42, ...), custom_call_target="tpu_custom_call" | custom-call | flops 402653184 | bytes 5865472 | tf_op jit(solution)/shard_map/pallas_call | solution.py:47
  29.6 4.6 %collective-permute-done.7.refs_7_.refs_2_ = bf16[128,2048]{1,0:T(8,128)(2,1)} collective-permute-done((bf16[128,2048]{1,0:T(8,128)(2,1)}, bf16[128,2048]{1,0:T(8,128)(2,1)}, u32[]{:S(2)}, u32[]{:S(2)}) %collective-permute-start.7) | collective-permute-done | bytes 524320 | tf_op jit(solution)/shard_map/ppermute | solution.py:560
  36.4 4.5 %all-to-all-start.1 = ((bf16[8,32,512]{2,1,0:T(8,128)(2,1)}), bf16[8,32,512]{2,1,0:T(8,128)(2,1)S(1)}, u32[]{:S(2)}, u32[]{:S(2)}) async-start(bf16[8,32,512]{2,1,0:T(8,128)(2,1)} %add_convert_fusion.1), calls=%async_computation.1 | async-start | bytes 524288 | tf_op jit(solution)/shard_map/all_to_all | solution.py:569
  44.4 2.0 %collective-permute-start.6 = (bf16[8,16,512]{2,1,0:T(8,128)(2,1)}, bf16[8,16,512]{2,1,0:T(8,128)(2,1)}, u32[]{:S(2)}, u32[]{:S(2)}) collective-permute-start(bf16[8,16,512]{2,1,0:T(8,128)(2,1)} %get-tuple-element.43), channel_id=1, source_target_pairs={{0,1},{1,0},{2,3},{3,2},{4,5},{5,4},{6,7},{7,6},{8,9},{9,8},{10,11... | collective-permute-start | bytes 393224 | tf_op jit(solution)/shard_map/ppermute | solution.py:560
  46.3 3.8 %all-to-all-done.1.parts = bf16[8,32,512]{2,1,0:T(8,128)(2,1)S(1)} async-done(((bf16[8,32,512]{2,1,0:T(8,128)(2,1)}), bf16[8,32,512]{2,1,0:T(8,128)(2,1)S(1)}, u32[]{:S(2)}, u32[]{:S(2)}) %all-to-all-start.1) | async-done | bytes 262176 | tf_op jit(solution)/shard_map/all_to_all | solution.py:569
  56.7 3.7 %shard_map.51.refs_10_.refs_6_ = bf16[512,2048]{1,0:T(8,128)(2,1)} custom-call(s32[10,1024]{1,0:T(8,128)S(1)} %copy-done.1, bf16[128,1024]{1,0:T(8,128)(2,1)S(1)} %slice_bitcast_fusion.5.refs_1_, bf16[128,1024]{1,0:T(8,128)(2,1)S(1)} %collective-permute-done.10.refs_2_, bf16[128,1024]{1,0:T(8,128)(2,1)S(1)} %collective-permute-done.11.refs_3_, ...), custom_call_target="tpu_custom_call" | custom-call | flops 2147483648 | bytes 3186688 | tf_op jit(solution)/shard_map/pallas_call | solution.py:47
  60.8 3.8 %shard_map.52 = (f32[512,32]{1,0:T(8,128)}, bf16[8,16,512]{2,1,0:T(8,128)(2,1)}) custom-call(bf16[1,32,512]{2,1,0:T(8,128)(2,1)S(1)} %shard_map.50.refs_0_, bf16[1,32,512]{2,1,0:T(8,128)(2,1)S(1)} %collective-permute-done.2.refs_1_, bf16[1,32,512]{2,1,0:T(8,128)(2,1)S(1)} %collective-permute-done.3.refs_2_, ...), custom_call_target="tpu_custom_call" | custom-call | flops 134217728 | bytes 4784128 | tf_op jit(solution)/shard_map/pallas_call | solution.py:47
  64.7 4.1 %all-to-all-start.2 = ((bf16[8,16,512]{2,1,0:T(8,128)(2,1)}), bf16[8,16,512]{2,1,0:T(8,128)(2,1)S(1)}, u32[]{:S(2)}, u32[]{:S(2)}) async-start(bf16[8,16,512]{2,1,0:T(8,128)(2,1)} %get-tuple-element.30), calls=%async_computation.2 | async-start | bytes 262144 | tf_op jit(solution)/shard_map/all_to_all | solution.py:585
  69.8 6.4 %all-to-all-done.2.parts = bf16[8,16,512]{2,1,0:T(8,128)(2,1)S(1)} async-done(((bf16[8,16,512]{2,1,0:T(8,128)(2,1)}), bf16[8,16,512]{2,1,0:T(8,128)(2,1)S(1)}, u32[]{:S(2)}, u32[]{:S(2)}) %all-to-all-start.2) | async-done | bytes 131104 | tf_op jit(solution)/shard_map/all_to_all | solution.py:585
  76.9 3.3 %all-to-all-start.3 = ((bf16[4,16,512]{2,1,0:T(8,128)(2,1)}), bf16[4,16,512]{2,1,0:T(8,128)(2,1)S(1)}, u32[]{:S(2)}, u32[]{:S(2)}) async-start(bf16[4,16,512]{2,1,0:T(8,128)(2,1)} %shard_map.53), calls=%async_computation.3 | async-start | bytes 131072 | tf_op jit(solution)/shard_map/all_to_all | solution.py:592
  80.3 5.6 %all-to-all-done.3.refs_0_ = bf16[4,16,512]{2,1,0:T(8,128)(2,1)S(1)} async-done(((bf16[4,16,512]{2,1,0:T(8,128)(2,1)}), bf16[4,16,512]{2,1,0:T(8,128)(2,1)S(1)}, u32[]{:S(2)}, u32[]{:S(2)}) %all-to-all-start.3) | async-done | bytes 65568 | tf_op jit(solution)/shard_map/all_to_all | solution.py:592
  86.0 2.6 %shard_map.54 = (bf16[16,512]{1,0:T(8,128)(2,1)S(1)}, bf16[16,512]{1,0:T(8,128)(2,1)S(1)}, bf16[16,512]{1,0:T(8,128)(2,1)S(1)}, bf16[16,512]{1,0:T(8,128)(2,1)S(1)}) custom-call(bf16[4,16,512]{2,1,0:T(8,128)(2,1)S(1)} %all-to-all-done.3.refs_0_, bf16[64,2048]{1,0:T(8,128)(2,1)} %copy-done.3, bf16[64,2048]{1,0:T(8,128)(2,1)} %collective-permute-done.13.refs_2_, ...), custom_call_target="tpu_custom_call" | custom-call | flops 67108864 | bytes 2228224 | tf_op jit(solution)/shard_map/pallas_call | solution.py:47
  89.9 3.1 %collective-permute-start.22 = (bf16[16,512]{1,0:T(8,128)(2,1)S(1)}, bf16[16,512]{1,0:T(8,128)(2,1)S(1)}, u32[]{:S(2)}, u32[]{:S(2)}) collective-permute-start(bf16[16,512]{1,0:T(8,128)(2,1)S(1)} %get-tuple-element.34), channel_id=1, source_target_pairs={{0,6},{2,4},{4,2},{6,0},{1,7},{3,5},{5,3},{7,1},{8,14},{10,12},{12... | collective-permute-start | bytes 49160 | tf_op jit(solution)/shard_map/ppermute | solution.py:604
  96.8 3.9 %all-to-all-start.4 = ((bf16[8,16,512]{2,1,0:T(8,128)(2,1)}), bf16[8,16,512]{2,1,0:T(8,128)(2,1)S(1)}, u32[]{:S(2)}, u32[]{:S(2)}) async-start(bf16[8,16,512]{2,1,0:T(8,128)(2,1)} %shard_map.55), calls=%async_computation.4 | async-start | bytes 262144 | tf_op jit(solution)/shard_map/all_to_all | solution.py:585
  103.5 5.5 %collective-permute-done.28.refs_1_ = bf16[256,1024]{1,0:T(8,128)(2,1)S(1)} collective-permute-done((bf16[256,1024]{1,0:T(8,128)(2,1)}, bf16[256,1024]{1,0:T(8,128)(2,1)S(1)}, u32[]{:S(2)}, u32[]{:S(2)}) %collective-permute-start.28) | collective-permute-done | bytes 524320 | tf_op jit(solution)/shard_map/ppermute | solution.py:560
  109.0 2.3 %shard_map.58.refs_1_ = bf16[256,2048]{1,0:T(8,128)(2,1)} custom-call(s32[10,1024]{1,0:T(8,128)S(1)} %copy-done.1, bf16[256,1024]{1,0:T(8,128)(2,1)S(1)} %collective-permute-done.28.refs_1_), custom_call_target="tpu_custom_call" | custom-call | flops 1073741824 | bytes 1613824 | tf_op jit(solution)/shard_map/pallas_call | solution.py:47
  111.4 8.9 %collective-permute-done.refs_1_ = bf16[256,1024]{1,0:T(8,128)(2,1)S(1)} collective-permute-done((bf16[256,1024]{1,0:T(8,128)(2,1)}, bf16[256,1024]{1,0:T(8,128)(2,1)S(1)}, u32[]{:S(2)}, u32[]{:S(2)}) %collective-permute-start) | collective-permute-done | bytes 524320 | tf_op jit(solution)/shard_map/ppermute | solution.py:560
  120.3 2.3 %shard_map.47.refs_1_ = bf16[256,2048]{1,0:T(8,128)(2,1)} custom-call(s32[10,1024]{1,0:T(8,128)S(1)} %copy-done.1, bf16[256,1024]{1,0:T(8,128)(2,1)S(1)} %collective-permute-done.refs_1_), custom_call_target="tpu_custom_call" | custom-call | flops 1073741824 | bytes 1613824 | tf_op jit(solution)/shard_map/pallas_call | solution.py:47
  122.6 3.3 %shard_map.56 = (bf16[32,512]{1,0:T(8,128)(2,1)S(1)}, bf16[32,512]{1,0:T(8,128)(2,1)S(1)}, bf16[32,512]{1,0:T(8,128)(2,1)S(1)}, bf16[32,512]{1,0:T(8,128)(2,1)S(1)}) custom-call(f32[512,32]{1,0:T(8,128)} %get-tuple-element.29.refs_0_, bf16[128,2048]{1,0:T(8,128)(2,1)} %slice_bitcast_fusion.2.refs_6_.refs_1_, ...), custom_call_target="tpu_custom_call" | custom-call | flops 134217728 | bytes 4521984 | tf_op jit(solution)/shard_map/pallas_call | solution.py:47
  127.3 3.1 %collective-permute-start.25 = (bf16[32,512]{1,0:T(8,128)(2,1)S(1)}, bf16[32,512]{1,0:T(8,128)(2,1)S(1)}, u32[]{:S(2)}, u32[]{:S(2)}) collective-permute-start(bf16[32,512]{1,0:T(8,128)(2,1)S(1)} %get-tuple-element.38), channel_id=1, source_target_pairs={{0,6},{2,4},{4,2},{6,0},{1,7},{3,5},{5,3},{7,1},{8,14},{10,12},{12... | collective-permute-start | bytes 98312 | tf_op jit(solution)/shard_map/ppermute | solution.py:604
  134.0 4.0 %all-to-all-start.5 = ((bf16[4,32,512]{2,1,0:T(8,128)(2,1)}), bf16[4,32,512]{2,1,0:T(8,128)(2,1)S(1)}, u32[]{:S(2)}, u32[]{:S(2)}) async-start(bf16[4,32,512]{2,1,0:T(8,128)(2,1)} %shard_map.57), calls=%async_computation.5 | async-start | bytes 262144 | tf_op jit(solution)/shard_map/all_to_all | solution.py:582
  138.3 5.7 %all-to-all-done.5.refs_2_ = bf16[4,32,512]{2,1,0:T(8,128)(2,1)S(1)} async-done(((bf16[4,32,512]{2,1,0:T(8,128)(2,1)}), bf16[4,32,512]{2,1,0:T(8,128)(2,1)S(1)}, u32[]{:S(2)}, u32[]{:S(2)}) %all-to-all-start.5) | async-done | bytes 131104 | tf_op jit(solution)/shard_map/all_to_all | solution.py:582
  144.0 3.5 %shard_map.59.refs_6_ = f32[512,64]{1,0:T(8,128)} custom-call(bf16[256,2048]{1,0:T(8,128)(2,1)} %get-tuple-element.24.refs_4_.refs_0_, bf16[256,2048]{1,0:T(8,128)(2,1)} %shard_map.58.refs_1_, bf16[8,16,512]{2,1,0:T(8,128)(2,1)S(1)} %all-to-all-done.4.refs_5_.refs_2_, bf16[8,16,512]{2,1,0:T(8,128)(2,1)S(1)} %collective-permute-done.29.refs_3_, ...), custom_call_target="tpu_custom_call" | custom-call | flops 134217728 | bytes 2621440 | tf_op jit(solution)/shard_map/pallas_call | solution.py:47
  147.8 4.0 %shard_map.60 = bf16[8,64,256]{2,1,0:T(8,128)(2,1)} custom-call(bf16[256,2048]{1,0:T(8,128)(2,1)} %get-tuple-element.23.refs_3_.refs_0_, bf16[256,2048]{1,0:T(8,128)(2,1)} %shard_map.47.refs_1_, bf16[4,32,512]{2,1,0:T(8,128)(2,1)S(1)} %all-to-all-done.5.refs_2_, bf16[4,32,512]{2,1,0:T(8,128)(2,1)S(1)} %collective-permute-done.26.refs_3_, ...), custom_call_target="tpu_custom_call" | custom-call | flops 268435456 | bytes 5636096 | tf_op jit(solution)/shard_map/pallas_call | solution.py:47
  151.8 3.6 %all-to-all-start.6 = ((bf16[8,64,256]{2,1,0:T(8,128)(2,1)}), bf16[8,64,256]{2,1,0:T(8,128)(2,1)S(1)}, u32[]{:S(2)}, u32[]{:S(2)}) async-start(bf16[8,64,256]{2,1,0:T(8,128)(2,1)} %shard_map.60), calls=%async_computation.6 | async-start | bytes 524288 | tf_op jit(solution)/shard_map/all_to_all | solution.py:851
  155.5 2.1 %collective-permute-start.31 = (bf16[64,192]{0,1:T(8,128)(2,1)S(1)}, bf16[64,192]{0,1:T(8,128)(2,1)S(1)}, u32[]{:S(2)}, u32[]{:S(2)}) collective-permute-start(bf16[64,192]{0,1:T(8,128)(2,1)S(1)} %pad_maximum_fusion), channel_id=1, source_target_pairs={{0,1},{1,0},{2,3},{3,2},{4,5},{5,4},{6,7},{7,6},{8,9},{9,8},{10,11... | collective-permute-start | bytes 73736 | tf_op jit(solution)/shard_map/ppermute | solution.py:560
  157.6 3.7 %collective-permute-done.31 = bf16[64,192]{0,1:T(8,128)(2,1)S(1)} collective-permute-done((bf16[64,192]{0,1:T(8,128)(2,1)S(1)}, bf16[64,192]{0,1:T(8,128)(2,1)S(1)}, u32[]{:S(2)}, u32[]{:S(2)}) %collective-permute-start.31) | collective-permute-done | bytes 24608 | tf_op jit(solution)/shard_map/ppermute | solution.py:560
  161.4 3.5 %all-to-all-done.6.parts = bf16[8,64,256]{2,1,0:T(8,128)(2,1)S(1)} async-done(((bf16[8,64,256]{2,1,0:T(8,128)(2,1)}), bf16[8,64,256]{2,1,0:T(8,128)(2,1)S(1)}, u32[]{:S(2)}, u32[]{:S(2)}) %all-to-all-start.6) | async-done | bytes 262176 | tf_op jit(solution)/shard_map/all_to_all | solution.py:851
  (104 shorter events, 34.3 us)
Async XLA Ops:
  1.9 21.8 %all-to-all-start = ((bf16[8,256,128]{2,1,0:T(8,128)(2,1)}), bf16[8,256,128]{2,1,0:T(8,128)(2,1)S(1)}, u32[]{:S(2)}, u32[]{:S(2)}) async-start(bf16[8,256,128]{2,1,0:T(8,128)(2,1)} %shard_map.48), calls=%async_computation | async-start | bytes 1048576 | tf_op jit(solution)/shard_map/all_to_all | solution.py:634
  9.2 31.7 %collective-permute-start.10 = (bf16[128,1024]{1,0:T(8,128)(2,1)S(1)}, bf16[128,1024]{1,0:T(8,128)(2,1)S(1)}, u32[]{:S(2)}, u32[]{:S(2)}) collective-permute-start(bf16[128,1024]{1,0:T(8,128)(2,1)S(1)} %slice_bitcast_fusion.5.refs_1_), channel_id=1, source_target_pairs={{0,1},{1,0},{2,3},{3,2},{4,5},{5,4},{6,7},{7,6},{8,9},{9,8},{10,11... | collective-permute-start | bytes 786440 | tf_op jit(solution)/shard_map/ppermute | solution.py:560
  11.3 33.0 %collective-permute-start.11 = (bf16[128,1024]{1,0:T(8,128)(2,1)S(1)}, bf16[128,1024]{1,0:T(8,128)(2,1)S(1)}, u32[]{:S(2)}, u32[]{:S(2)}) collective-permute-start(bf16[128,1024]{1,0:T(8,128)(2,1)S(1)} %slice_bitcast_fusion.5.refs_1_), channel_id=1, source_target_pairs={{0,8},{8,0},{16,24},{24,16},{1,9},{9,1},{17,25},{25,17},{2,10},{10... | collective-permute-start | bytes 786440 | tf_op jit(solution)/shard_map/ppermute | solution.py:560
  13.2 20.9 %collective-permute-start.7 = (bf16[128,2048]{1,0:T(8,128)(2,1)}, bf16[128,2048]{1,0:T(8,128)(2,1)}, u32[]{:S(2)}, u32[]{:S(2)}) collective-permute-start(bf16[128,2048]{1,0:T(8,128)(2,1)} %slice_bitcast_fusion.2.refs_6_.refs_1_), channel_id=1, source_target_pairs={{0,1},{1,0},{2,3},{3,2},{4,5},{5,4},{6,7},{7,6},{8,9},{9,8},{10,11... | collective-permute-start | bytes 1572872 | tf_op jit(solution)/shard_map/ppermute | solution.py:560
  28.0 14.5 %collective-permute-start.5 = (bf16[16,16,512]{2,1,0:T(8,128)(2,1)}, bf16[16,16,512]{2,1,0:T(8,128)(2,1)}, u32[]{:S(2)}, u32[]{:S(2)}) collective-permute-start(bf16[16,16,512]{2,1,0:T(8,128)(2,1)} %get-tuple-element.28), channel_id=1, source_target_pairs={{0,8},{8,0},{16,24},{24,16},{1,9},{9,1},{17,25},{25,17},{2,10},{10... | collective-permute-start | bytes 786440 | tf_op jit(solution)/shard_map/ppermute | solution.py:560
  34.1 18.1 %collective-permute-start.8 = (bf16[128,2048]{1,0:T(8,128)(2,1)}, bf16[128,2048]{1,0:T(8,128)(2,1)S(1)}, u32[]{:S(2)}, u32[]{:S(2)}) collective-permute-start(bf16[128,2048]{1,0:T(8,128)(2,1)} %slice_bitcast_fusion.2.refs_6_.refs_1_), channel_id=1, source_target_pairs={{0,8},{8,0},{16,24},{24,16},{1,9},{9,1},{17,25},{25,17},{2,10},{10... | collective-permute-start | bytes 1572872 | tf_op jit(solution)/shard_map/ppermute | solution.py:560
  34.1 19.2 %collective-permute-start.9 = (bf16[128,2048]{1,0:T(8,128)(2,1)}, bf16[128,2048]{1,0:T(8,128)(2,1)}, u32[]{:S(2)}, u32[]{:S(2)}) collective-permute-start(bf16[128,2048]{1,0:T(8,128)(2,1)} %collective-permute-done.7.refs_7_.refs_2_), channel_id=1, source_target_pairs={{0,8},{8,0},{16,24},{24,16},{1,9},{9,1},{17,25},{25,17},{2,10},{10... | collective-permute-start | bytes 1572872 | tf_op jit(solution)/shard_map/ppermute | solution.py:560
  36.4 13.7 %all-to-all-start.1 = ((bf16[8,32,512]{2,1,0:T(8,128)(2,1)}), bf16[8,32,512]{2,1,0:T(8,128)(2,1)S(1)}, u32[]{:S(2)}, u32[]{:S(2)}) async-start(bf16[8,32,512]{2,1,0:T(8,128)(2,1)} %add_convert_fusion.1), calls=%async_computation.1 | async-start | bytes 524288 | tf_op jit(solution)/shard_map/all_to_all | solution.py:569
  40.9 9.2 %collective-permute-start.13 = (bf16[64,2048]{1,0:T(8,128)(2,1)S(1)}, bf16[64,2048]{1,0:T(8,128)(2,1)}, u32[]{:S(2)}, u32[]{:S(2)}) collective-permute-start(bf16[64,2048]{1,0:T(8,128)(2,1)S(1)} %slice_bitcast_fusion.4.refs_1_), channel_id=1, source_target_pairs={{0,16},{8,24},{16,0},{24,8},{1,17},{9,25},{17,1},{25,9},{2,18},{10... | collective-permute-start | bytes 786440 | tf_op jit(solution)/shard_map/ppermute | solution.py:560
  42.5 9.1 %collective-permute-start.12 = (bf16[128,1024]{1,0:T(8,128)(2,1)S(1)}, bf16[128,1024]{1,0:T(8,128)(2,1)S(1)}, u32[]{:S(2)}, u32[]{:S(2)}) collective-permute-start(bf16[128,1024]{1,0:T(8,128)(2,1)S(1)} %collective-permute-done.10.refs_2_), channel_id=1, source_target_pairs={{0,8},{8,0},{16,24},{24,16},{1,9},{9,1},{17,25},{25,17},{2,10},{10... | collective-permute-start | bytes 786440 | tf_op jit(solution)/shard_map/ppermute | solution.py:560
  44.4 10.8 %collective-permute-start.6 = (bf16[8,16,512]{2,1,0:T(8,128)(2,1)}, bf16[8,16,512]{2,1,0:T(8,128)(2,1)}, u32[]{:S(2)}, u32[]{:S(2)}) collective-permute-start(bf16[8,16,512]{2,1,0:T(8,128)(2,1)} %get-tuple-element.43), channel_id=1, source_target_pairs={{0,1},{1,0},{2,3},{3,2},{4,5},{5,4},{6,7},{7,6},{8,9},{9,8},{10,11... | collective-permute-start | bytes 393224 | tf_op jit(solution)/shard_map/ppermute | solution.py:560
  50.2 19.2 %collective-permute-start.14 = (bf16[64,2048]{1,0:T(8,128)(2,1)S(1)}, bf16[64,2048]{1,0:T(8,128)(2,1)S(1)}, u32[]{:S(2)}, u32[]{:S(2)}) collective-permute-start(bf16[64,2048]{1,0:T(8,128)(2,1)S(1)} %slice_bitcast_fusion.4.refs_1_), channel_id=1, source_target_pairs={{0,1},{1,0},{2,3},{3,2},{4,5},{5,4},{6,7},{7,6},{8,9},{9,8},{10,11... | collective-permute-start | bytes 786440 | tf_op jit(solution)/shard_map/ppermute | solution.py:560
  51.5 17.9 %collective-permute-start.15 = (bf16[64,2048]{1,0:T(8,128)(2,1)}, bf16[64,2048]{1,0:T(8,128)(2,1)}, u32[]{:S(2)}, u32[]{:S(2)}) collective-permute-start(bf16[64,2048]{1,0:T(8,128)(2,1)} %collective-permute-done.13.refs_2_), channel_id=1, source_target_pairs={{0,1},{1,0},{2,3},{3,2},{4,5},{5,4},{6,7},{7,6},{8,9},{9,8},{10,11... | collective-permute-start | bytes 786440 | tf_op jit(solution)/shard_map/ppermute | solution.py:560
  52.3 8.1 %collective-permute-start.2 = (bf16[1,32,512]{2,1,0:T(8,128)(2,1)S(1)}, bf16[1,32,512]{2,1,0:T(8,128)(2,1)S(1)}, u32[]{:S(2)}, u32[]{:S(2)}) collective-permute-start(bf16[1,32,512]{2,1,0:T(8,128)(2,1)S(1)} %shard_map.50.refs_0_), channel_id=1, source_target_pairs={{0,2},{2,0},{4,6},{6,4},{1,3},{3,1},{5,7},{7,5},{8,10},{10,8},{12,... | collective-permute-start | bytes 98312 | tf_op jit(solution)/shard_map/ppermute | solution.py:604
  53.3 7.1 %collective-permute-start.3 = (bf16[1,32,512]{2,1,0:T(8,128)(2,1)S(1)}, bf16[1,32,512]{2,1,0:T(8,128)(2,1)S(1)}, u32[]{:S(2)}, u32[]{:S(2)}) collective-permute-start(bf16[1,32,512]{2,1,0:T(8,128)(2,1)S(1)} %shard_map.50.refs_0_), channel_id=1, source_target_pairs={{0,4},{2,6},{4,0},{6,2},{1,5},{3,7},{5,1},{7,3},{8,12},{10,14},{12... | collective-permute-start | bytes 98312 | tf_op jit(solution)/shard_map/ppermute | solution.py:604
  64.7 11.6 %all-to-all-start.2 = ((bf16[8,16,512]{2,1,0:T(8,128)(2,1)}), bf16[8,16,512]{2,1,0:T(8,128)(2,1)S(1)}, u32[]{:S(2)}, u32[]{:S(2)}) async-start(bf16[8,16,512]{2,1,0:T(8,128)(2,1)} %get-tuple-element.30), calls=%async_computation.2 | async-start | bytes 262144 | tf_op jit(solution)/shard_map/all_to_all | solution.py:585
  68.8 11.5 %collective-permute-start.16 = (bf16[64,2048]{1,0:T(8,128)(2,1)S(1)}, bf16[64,2048]{1,0:T(8,128)(2,1)S(1)}, u32[]{:S(2)}, u32[]{:S(2)}) collective-permute-start(bf16[64,2048]{1,0:T(8,128)(2,1)S(1)} %slice_bitcast_fusion.4.refs_1_), channel_id=1, source_target_pairs={{0,8},{8,0},{16,24},{24,16},{1,9},{9,1},{17,25},{25,17},{2,10},{10... | collective-permute-start | bytes 786440 | tf_op jit(solution)/shard_map/ppermute | solution.py:560
  68.8 11.4 %collective-permute-start.17 = (bf16[64,2048]{1,0:T(8,128)(2,1)}, bf16[64,2048]{1,0:T(8,128)(2,1)S(1)}, u32[]{:S(2)}, u32[]{:S(2)}) collective-permute-start(bf16[64,2048]{1,0:T(8,128)(2,1)} %collective-permute-done.13.refs_2_), channel_id=1, source_target_pairs={{0,8},{8,0},{16,24},{24,16},{1,9},{9,1},{17,25},{25,17},{2,10},{10... | collective-permute-start | bytes 786440 | tf_op jit(solution)/shard_map/ppermute | solution.py:560
  69.3 10.9 %collective-permute-start.18 = (bf16[64,2048]{1,0:T(8,128)(2,1)S(1)}, bf16[64,2048]{1,0:T(8,128)(2,1)S(1)}, u32[]{:S(2)}, u32[]{:S(2)}) collective-permute-start(bf16[64,2048]{1,0:T(8,128)(2,1)S(1)} %collective-permute-done.14.refs_3_), channel_id=1, source_target_pairs={{0,8},{8,0},{16,24},{24,16},{1,9},{9,1},{17,25},{25,17},{2,10},{10... | collective-permute-start | bytes 786440 | tf_op jit(solution)/shard_map/ppermute | solution.py:560
  69.4 10.9 %collective-permute-start.19 = (bf16[64,2048]{1,0:T(8,128)(2,1)}, bf16[64,2048]{1,0:T(8,128)(2,1)S(1)}, u32[]{:S(2)}, u32[]{:S(2)}) collective-permute-start(bf16[64,2048]{1,0:T(8,128)(2,1)} %collective-permute-done.15.refs_4_), channel_id=1, source_target_pairs={{0,8},{8,0},{16,24},{24,16},{1,9},{9,1},{17,25},{25,17},{2,10},{10... | collective-permute-start | bytes 786440 | tf_op jit(solution)/shard_map/ppermute | solution.py:560
  76.9 9.0 %all-to-all-start.3 = ((bf16[4,16,512]{2,1,0:T(8,128)(2,1)}), bf16[4,16,512]{2,1,0:T(8,128)(2,1)S(1)}, u32[]{:S(2)}, u32[]{:S(2)}) async-start(bf16[4,16,512]{2,1,0:T(8,128)(2,1)} %shard_map.53), calls=%async_computation.3 | async-start | bytes 131072 | tf_op jit(solution)/shard_map/all_to_all | solution.py:592
  88.5 7.5 %collective-permute-start.20 = (bf16[16,512]{1,0:T(8,128)(2,1)S(1)}, bf16[16,512]{1,0:T(8,128)(2,1)S(1)}, u32[]{:S(2)}, u32[]{:S(2)}) collective-permute-start(bf16[16,512]{1,0:T(8,128)(2,1)S(1)} %get-tuple-element.32), channel_id=1, source_target_pairs={{0,2},{2,0},{4,6},{6,4},{1,3},{3,1},{5,7},{7,5},{8,10},{10,8},{12,... | collective-permute-start | bytes 49160 | tf_op jit(solution)/shard_map/ppermute | solution.py:604
  89.7 6.4 %collective-permute-start.21 = (bf16[16,512]{1,0:T(8,128)(2,1)S(1)}, bf16[16,512]{1,0:T(8,128)(2,1)S(1)}, u32[]{:S(2)}, u32[]{:S(2)}) collective-permute-start(bf16[16,512]{1,0:T(8,128)(2,1)S(1)} %get-tuple-element.33), channel_id=1, source_target_pairs={{0,4},{2,6},{4,0},{6,2},{1,5},{3,7},{5,1},{7,3},{8,12},{10,14},{12... | collective-permute-start | bytes 49160 | tf_op jit(solution)/shard_map/ppermute | solution.py:604
  89.9 6.2 %collective-permute-start.22 = (bf16[16,512]{1,0:T(8,128)(2,1)S(1)}, bf16[16,512]{1,0:T(8,128)(2,1)S(1)}, u32[]{:S(2)}, u32[]{:S(2)}) collective-permute-start(bf16[16,512]{1,0:T(8,128)(2,1)S(1)} %get-tuple-element.34), channel_id=1, source_target_pairs={{0,6},{2,4},{4,2},{6,0},{1,7},{3,5},{5,3},{7,1},{8,14},{10,12},{12... | collective-permute-start | bytes 49160 | tf_op jit(solution)/shard_map/ppermute | solution.py:604
  94.0 15.0 %collective-permute-start.28 = (bf16[256,1024]{1,0:T(8,128)(2,1)}, bf16[256,1024]{1,0:T(8,128)(2,1)S(1)}, u32[]{:S(2)}, u32[]{:S(2)}) collective-permute-start(bf16[256,1024]{1,0:T(8,128)(2,1)} %get-tuple-element.41), channel_id=1, source_target_pairs={{0,1},{1,0},{2,3},{3,2},{4,5},{5,4},{6,7},{7,6},{8,9},{9,8},{10,11... | collective-permute-start | bytes 1572872 | tf_op jit(solution)/shard_map/ppermute | solution.py:560
  95.5 24.8 %collective-permute-start = (bf16[256,1024]{1,0:T(8,128)(2,1)}, bf16[256,1024]{1,0:T(8,128)(2,1)S(1)}, u32[]{:S(2)}, u32[]{:S(2)}) collective-permute-start(bf16[256,1024]{1,0:T(8,128)(2,1)} %get-tuple-element.42), channel_id=1, source_target_pairs={{0,1},{1,0},{2,3},{3,2},{4,5},{5,4},{6,7},{7,6},{8,9},{9,8},{10,11... | collective-permute-start | bytes 1572872 | tf_op jit(solution)/shard_map/ppermute | solution.py:560
  96.8 14.6 %all-to-all-start.4 = ((bf16[8,16,512]{2,1,0:T(8,128)(2,1)}), bf16[8,16,512]{2,1,0:T(8,128)(2,1)S(1)}, u32[]{:S(2)}, u32[]{:S(2)}) async-start(bf16[8,16,512]{2,1,0:T(8,128)(2,1)} %shard_map.55), calls=%async_computation.4 | async-start | bytes 262144 | tf_op jit(solution)/shard_map/all_to_all | solution.py:585
  102.0 45.8 %collective-permute-start.27 = (bf16[256,2048]{1,0:T(8,128)(2,1)S(1)}, bf16[256,2048]{1,0:T(8,128)(2,1)S(1)}, u32[]{:S(2)}, u32[]{:S(2)}) collective-permute-start(bf16[256,2048]{1,0:T(8,128)(2,1)S(1)} %slice_bitcast_fusion), channel_id=1, source_target_pairs={{0,1},{1,0},{2,3},{3,2},{4,5},{5,4},{6,7},{7,6},{8,9},{9,8},{10,11... | collective-permute-start | bytes 3145736 | tf_op jit(solution)/shard_map/ppermute | solution.py:560
  111.4 26.7 %collective-permute-start.29 = (bf16[8,16,512]{2,1,0:T(8,128)(2,1)S(1)}, bf16[8,16,512]{2,1,0:T(8,128)(2,1)S(1)}, u32[]{:S(2)}, u32[]{:S(2)}) collective-permute-start(bf16[8,16,512]{2,1,0:T(8,128)(2,1)S(1)} %all-to-all-done.4.refs_5_.refs_2_), channel_id=1, source_target_pairs={{0,8},{8,0},{16,24},{24,16},{1,9},{9,1},{17,25},{25,17},{2,10},{10... | collective-permute-start | bytes 393224 | tf_op jit(solution)/shard_map/ppermute | solution.py:560
  130.5 13.4 %collective-permute-start.30 = (f32[256,64]{1,0:T(8,128)S(1)}, f32[256,64]{1,0:T(8,128)S(1)}, u32[]{:S(2)}, u32[]{:S(2)}) collective-permute-start(f32[256,64]{1,0:T(8,128)S(1)} %copy-done.9), channel_id=1, source_target_pairs={{0,1},{1,0},{2,3},{3,2},{4,5},{5,4},{6,7},{7,6},{8,9},{9,8},{10,11... | collective-permute-start | bytes 196616 | tf_op jit(solution)/shard_map/ppermute | solution.py:560
  134.0 9.9 %all-to-all-start.5 = ((bf16[4,32,512]{2,1,0:T(8,128)(2,1)}), bf16[4,32,512]{2,1,0:T(8,128)(2,1)S(1)}, u32[]{:S(2)}, u32[]{:S(2)}) async-start(bf16[4,32,512]{2,1,0:T(8,128)(2,1)} %shard_map.57), calls=%async_computation.5 | async-start | bytes 262144 | tf_op jit(solution)/shard_map/all_to_all | solution.py:582
  151.8 13.2 %all-to-all-start.6 = ((bf16[8,64,256]{2,1,0:T(8,128)(2,1)}), bf16[8,64,256]{2,1,0:T(8,128)(2,1)S(1)}, u32[]{:S(2)}, u32[]{:S(2)}) async-start(bf16[8,64,256]{2,1,0:T(8,128)(2,1)} %shard_map.60), calls=%async_computation.6 | async-start | bytes 524288 | tf_op jit(solution)/shard_map/all_to_all | solution.py:851
  (17 other events, 154.9 us)
